TPU v7x, 32 devices: a whole 2x2x4 slice. The times are simulated.
32 devices in a mesh: groups: 1, ctx: 32 (over z, y, x, core).
Axes of the slice: x: 2, y: 2, z: 4, core: 2. Of those that a mesh axis runs over, the one named last changes fastest.
Arguments:
- queries: bfloat16 [4096, 2048], P(('groups', 'ctx')), may hold values from -120 to 120
- self_keys: bfloat16 [4096, 2048], P(('groups', 'ctx')), may hold values from -6 to 6
- self_values: bfloat16 [4096, 2048], P(('groups', 'ctx')), may hold values from -6 to 6
- cross_queries: bfloat16 [4096, 2048], P(('groups', 'ctx')), may hold values from -6 to 6
- encoded: bfloat16 [4096, 896], P(('groups', 'ctx')), may hold values from -6 to 6
- neighbour_weight: bfloat16 [896, 4096], replicated, may hold values from -1 to 1
- counts: int32 [64], P(('groups', 'ctx')), may hold values from 0 to 2
- sources: int32 [64, 2], P(('groups', 'ctx')), may hold values from 0 to 61, as said below
Outputs:
- attended: bfloat16 [4096, 2048], P(('groups', 'ctx'))
Inputs may be any that keep to these rules, and one draw needn't show every extreme that they name: sources[c, j] equals max(c - 1 - r, 0) for some r with 1 <= r <= 29.
All inputs are finite; a program needn't handle non-finite values.
Results may differ from a plain program's by a relative error of at most 0.0061.
Values may be sent and summed in bfloat16 or wider, within the bound.
No kernel may reach another device: no remote copies, remote signals or barrier semaphores. Data moves between devices by JAX's collectives and lax.ppermute only.
A program may use at most 128 MiB of HBM per device.

v0:
```python
import functools

import jax
import jax.numpy as jnp
from jax import lax
from jax.experimental import pallas as pl
from jax.experimental.pallas import tpu as pltpu
from jax.sharding import PartitionSpec as P


HEADS = 16
HEAD_DIM = 128
SPAN = 64
PLANE = 8
LEFT = 6

MASKED_SCORE = -1e30
LOG2E = 1.4426950408889634


def shifted(value, axis, steps):
    count = lax.axis_size(axis)
    first, last = (max(0, -steps), min(count, count - steps))
    return lax.ppermute(value, axis, [(source, source + steps) for source in range(first, last)])


def swapped(value, axis, bit):
    count = lax.axis_size(axis)
    return lax.ppermute(value, axis, [(source, source ^ bit) for source in range(count)])


def pack_kernel(*refs):
    *in_refs, out_ref = refs
    rows = in_refs[0].shape[0]
    for head in range(out_ref.shape[0]):
        columns = slice(head * HEAD_DIM, (head + 1) * HEAD_DIM)
        for n, ref in enumerate(in_refs):
            out_ref[head, n * rows : (n + 1) * rows, :] = ref[:, columns]


def packed(*arrays):
    rows, width = arrays[0].shape
    return pl.pallas_call(
        pack_kernel,
        out_shape=jax.ShapeDtypeStruct(
            (width // HEAD_DIM, len(arrays) * rows, HEAD_DIM), arrays[0].dtype
        ),
        cost_estimate=pl.CostEstimate(
            flops=0, bytes_accessed=4 * len(arrays) * rows * width, transcendentals=0
        ),
        name="pack",
    )(*arrays)


def scores_of(q, k):
    return lax.dot_general(q, k, (((1,), (1,)), ((), ())), preferred_element_type=jnp.float32)


def softmax_parts(q, pieces, scale):
    scores = []
    for k, _, mask in pieces:
        s = scores_of(q, k)
        scores.append(s if mask is None else jnp.where(mask, s, MASKED_SCORE))
    largest = functools.reduce(
        jnp.maximum, [jnp.max(s, axis=1, keepdims=True) for s in scores]
    )
    total, out = None, None
    for s, (_, v, _) in zip(scores, pieces):
        p = jnp.exp2((s - largest) * scale)
        t = jnp.sum(p, axis=1, keepdims=True)
        o = jnp.dot(p.astype(jnp.bfloat16), v, preferred_element_type=jnp.float32)
        total = t if total is None else total + t
        out = o if out is None else out + o
    return out, largest, total


def with_stats(largest, total):
    lane = lax.broadcasted_iota(jnp.int32, (largest.shape[0], 128), 1)
    return jnp.where(lane < 64, largest, total)


def halves(stat):
    return stat[:, 0:1], stat[:, 64:65]


def thirds(x):
    high = x.astype(jnp.bfloat16)
    rest = x - high.astype(jnp.float32)
    middle = rest.astype(jnp.bfloat16)
    low = (rest - middle.astype(jnp.float32)).astype(jnp.bfloat16)
    return high, middle, low


def taken(ref, first, count, start, rows):
    return ref[first : first + count, start : start + rows, :].reshape(count * rows, ref.shape[2])


def triangle(size, keep):
    row = lax.broadcasted_iota(jnp.int32, (size, size), 0)
    column = lax.broadcasted_iota(jnp.int32, (size, size), 1)
    return keep(column, row)


def own_kernel(scale, q_ref, kv_ref, out_ref, stat_ref):
    blocks, rows, dim = q_ref.shape
    causal = triangle(2 * rows, lambda column, row: column <= row)
    for i in range(0, blocks, 2):
        pieces = [(taken(kv_ref, i, 2, 0, rows), taken(kv_ref, i, 2, rows, rows), causal)]
        if i:
            pieces.append((taken(kv_ref, 0, i, 0, rows), taken(kv_ref, 0, i, rows, rows), None))
        out, largest, total = softmax_parts(taken(q_ref, i, 2, 0, rows), pieces, scale)
        out_ref[i : i + 2] = out.reshape(2, rows, dim)
        stat_ref[i : i + 2] = with_stats(largest, total).reshape(2, rows, 128)


def later_kernel(scale, q_ref, kv_ref, out_ref):
    blocks, rows, dim = q_ref.shape
    later = triangle(2 * rows, lambda column, row: column > row)
    out_ref[blocks] = jnp.zeros((rows, dim), out_ref.dtype)
    for i in range(0, blocks, 2):
        pieces = [(taken(kv_ref, i, 2, 0, rows), taken(kv_ref, i, 2, rows, rows), later)]
        rest = blocks - i - 2
        if rest:
            pieces.append(
                (taken(kv_ref, i + 2, rest, 0, rows), taken(kv_ref, i + 2, rest, rows, rows), None)
            )
        out, largest, total = softmax_parts(taken(q_ref, i, 2, 0, rows), pieces, scale)
        out_ref[i : i + 2] = out.reshape(2, rows, dim).astype(out_ref.dtype)
        stat = with_stats(largest, total)
        for n in range(2):
            turned = stat[n * rows : (n + 1) * rows].T
            for m, row in enumerate((turned[0:1], turned[64:65])):
                for k, part in enumerate(thirds(row)):
                    place = ((i + n) * 2 + m) * 3 + k
                    out_ref[blocks, place : place + 1, :] = part


def sent_stats(ref, block, rows):
    values = []
    for m in range(2):
        place = (block * 2 + m) * 3
        three = ref[ref.shape[0] - 1, place : place + 3, :].astype(jnp.float32)
        values.append(three[0:1] + three[1:2] + three[2:3])
    sublane = lax.broadcasted_iota(jnp.int32, (rows, 128), 0)
    return jnp.where(sublane < 64, values[0], values[1]).T


def previous_kernel(scale, flag_ref, q_ref, kv_ref, back_ref, out1_ref, stat_ref, out_ref):
    blocks, rows, dim = q_ref.shape
    sent = back_ref.shape[0] - 1
    later = triangle(2 * rows, lambda column, row: column > row)

    def store(i, parts):
        top = functools.reduce(jnp.maximum, [largest for _, largest, _ in parts])
        weights = [jnp.exp2((largest - top) * scale) for _, largest, _ in parts]
        inverse = 1.0 / sum(w * total for w, (_, _, total) in zip(weights, parts))
        merged = sum((w * inverse) * out for w, (out, _, _) in zip(weights, parts))
        out_ref[i : i + 2] = merged.reshape(2, rows, dim).astype(out_ref.dtype)

    def own_part(i):
        stat = stat_ref[i : i + 2].reshape(2 * rows, 128)
        return (out1_ref[i : i + 2].reshape(2 * rows, dim), *halves(stat))

    @pl.when(flag_ref[0] > 0)
    def _():
        for i in range(0, blocks, 2):
            pieces = []
            first = max(i - sent, 0)
            if i >= sent:
                pieces.append(
                    (taken(kv_ref, first, 2, 0, rows), taken(kv_ref, first, 2, rows, rows), later)
                )
                first += 2
            rest = kv_ref.shape[0] - first
            if rest:
                pieces.append(
                    (
                        taken(kv_ref, first, rest, 0, rows),
                        taken(kv_ref, first, rest, rows, rows),
                        None,
                    )
                )
            parts = [softmax_parts(taken(q_ref, i, 2, 0, rows), pieces, scale), own_part(i)]
            if i < sent:
                stat = jnp.concatenate([sent_stats(back_ref, i + n, rows) for n in range(2)], axis=0)
                parts.append((taken(back_ref, i, 2, 0, rows).astype(jnp.float32), *halves(stat)))
            store(i, parts)

    @pl.when(flag_ref[0] == 0)
    def _():
        for i in range(0, blocks, 2):
            store(i, [own_part(i)])


def estimate(area, arrays):
    return pl.CostEstimate(
        flops=4 * HEAD_DIM * area,
        bytes_accessed=sum(2 * a.size for a in arrays),
        transcendentals=area,
    )


def self_attention(queries, keys, values, chunk, groups):
    rows, width = queries.shape
    heads = width // HEAD_DIM
    scale = HEAD_DIM ** (-0.5) * LOG2E
    kv = lax.all_to_all(
        packed(keys, values), "ctx", 0, 0, axis_index_groups=groups, tiled=True
    )
    q = lax.all_to_all(packed(queries), "ctx", 0, 0, axis_index_groups=groups, tiled=True)
    arriving = shifted(kv[LEFT:], "ctx", heads)
    asked = shifted(q[:LEFT], "ctx", -heads)
    area = (heads * rows) ** 2 // 2
    small = (LEFT * rows) ** 2 // 2
    out1, stat = pl.pallas_call(
        functools.partial(own_kernel, scale),
        out_shape=(
            jax.ShapeDtypeStruct((heads, rows, HEAD_DIM), jnp.float32),
            jax.ShapeDtypeStruct((heads, rows, 128), jnp.float32),
        ),
        cost_estimate=estimate(area, (q, kv)),
        name="own",
    )(q, kv)
    answer = pl.pallas_call(
        functools.partial(later_kernel, scale),
        out_shape=jax.ShapeDtypeStruct((LEFT + 1, rows, HEAD_DIM), jnp.bfloat16),
        cost_estimate=estimate(small, (asked,)),
        name="later",
    )(asked, kv[:LEFT])
    back = shifted(answer, "ctx", heads)
    vmem = pl.BlockSpec(memory_space=pltpu.VMEM)
    return pl.pallas_call(
        functools.partial(previous_kernel, scale),
        out_shape=jax.ShapeDtypeStruct((heads, rows, HEAD_DIM), jnp.bfloat16),
        in_specs=[pl.BlockSpec(memory_space=pltpu.SMEM)] + [vmem] * 5,
        cost_estimate=estimate(area - small, (q, kv, out1, stat)),
        name="previous",
    )(chunk.reshape(1), q, arriving, back, out1, stat)


def gather_kernel(mine_ref, theirs_ref, *refs):
    *in_refs, mine_out, theirs_out, window_ref = refs
    start = 0
    for ref in in_refs:
        window_ref[start : start + ref.shape[0], :] = ref[...]
        start += ref.shape[0]
    for piece_ref, out_ref in ((mine_ref, mine_out), (theirs_ref, theirs_out)):
        pieces = piece_ref.shape[0]
        size = out_ref.shape[0] // pieces
        for n in range(pieces):
            place = pl.multiple_of(piece_ref[n], size)
            out_ref[n * size : (n + 1) * size, :] = window_ref[pl.ds(place, size), :]


def cross_kernel(
    scale, span_count, here_ref, count_ref, mine_ref, theirs_ref, q_ref, wk_ref, wv_ref, out_ref, rows_ref
):
    span = q_ref.shape[0] // span_count
    keys_of_span = rows_ref.shape[0] // span_count
    pieces = rows_ref.shape[0] // span

    @pl.when(pl.program_id(0) == 0)
    def _():
        for n in range(pieces):
            place = slice(n * span, (n + 1) * span)

            @pl.when(here_ref[n] > 0)
            def _():
                rows_ref[place, :] = mine_ref[place, :]

            @pl.when(here_ref[n] == 0)
            def _():
                rows_ref[place, :] = theirs_ref[place, :]

    rows = rows_ref[...]
    keys = jnp.dot(rows, wk_ref[...], preferred_element_type=jnp.float32).astype(jnp.bfloat16)
    values = jnp.dot(rows, wv_ref[...], preferred_element_type=jnp.float32).astype(jnp.bfloat16)
    slot = lax.broadcasted_iota(jnp.int32, (span, keys_of_span), 1) // (2 * span)
    for c in range(span_count):
        valid = slot < count_ref[c]
        none = jnp.where(count_ref[c] > 0, 0.0, 1.0)
        here = slice(c * keys_of_span, (c + 1) * keys_of_span)
        for h in range(q_ref.shape[1] // HEAD_DIM):
            lanes = slice(h * HEAD_DIM, (h + 1) * HEAD_DIM)
            s = scores_of(q_ref[c * span : (c + 1) * span, lanes], keys[here, lanes])
            s = jnp.where(valid, s, MASKED_SCORE)
            largest = jnp.max(s, axis=1, keepdims=True)
            p = jnp.where(valid, jnp.exp2((s - largest) * scale), 0.0)
            total = jnp.sum(p, axis=1, keepdims=True) + none
            o = jnp.dot(
                p.astype(jnp.bfloat16), values[here, lanes], preferred_element_type=jnp.float32
            )
            out_ref[c * span : (c + 1) * span, lanes] = o * (1.0 / total)


def cross_attention(cross_queries, encoded, weight, counts, sources, position):
    rows, width = cross_queries.shape
    span_count = counts.shape[0]
    depth = encoded.shape[1]
    place, plane = position % PLANE, position // PLANE
    one_back = shifted(encoded, "ctx", PLANE)
    before = shifted(jnp.concatenate([counts[-1:], sources[-1]]), "ctx", 1)
    count_rows = jnp.concatenate([before[:1], counts[:-1]])
    source_rows = jnp.concatenate([before[1:][None], sources[:-1]], axis=0)
    spans = (source_rows[:, :, None] + jnp.arange(2, dtype=jnp.int32)).reshape(-1)
    their_spans = swapped(spans, "ctx", 1)
    two_back = shifted(one_back, "ctx", PLANE)

    near = []
    for bit in (2, 4, 6):
        other = jnp.where(place < (place ^ bit), encoded, two_back)
        near.append(swapped(jnp.concatenate([one_back, other], axis=0), "ctx", bit))

    def places(wanted):
        block, half = wanted // span_count, wanted % span_count
        relative = (block % PLANE) ^ place
        away = plane - block // PLANE
        column = relative // 2
        slot = jnp.where(column == 0, away, 1 + 2 * column + jnp.where(away == 1, 0, 1))
        start = jnp.where(relative % 2 == 0, slot * rows + half * SPAN, 0)
        return jnp.clip(start, 0, 9 * rows - SPAN), (relative % 2 == 0).astype(jnp.int32)

    my_places, here = places(spans)
    picked = span_count * 4 * SPAN
    smem, vmem = (pl.BlockSpec(memory_space=m) for m in (pltpu.SMEM, pltpu.VMEM))
    mine, theirs = pl.pallas_call(
        gather_kernel,
        out_shape=(jax.ShapeDtypeStruct((picked, depth), encoded.dtype),) * 2,
        in_specs=[smem] * 2 + [vmem] * 6,
        scratch_shapes=[pltpu.VMEM((9 * rows, depth), encoded.dtype)],
        cost_estimate=pl.CostEstimate(
            flops=0, bytes_accessed=8 * picked * depth, transcendentals=0
        ),
        name="gather",
    )(my_places, places(their_spans)[0], encoded, one_back, two_back, *near)
    theirs = swapped(theirs, "ctx", 1)

    block = 4 * HEAD_DIM
    steps = width // block
    cost = pl.CostEstimate(
        flops=2 * picked * depth * 2 * width,
        bytes_accessed=weight.size * 2 + picked * depth * 4,
        transcendentals=picked * SPAN * HEADS,
    )
    return pl.pallas_call(
        functools.partial(cross_kernel, HEAD_DIM ** (-0.5) * LOG2E, span_count),
        out_shape=jax.ShapeDtypeStruct((rows, width), jnp.float32),
        grid_spec=pltpu.PrefetchScalarGridSpec(
            num_scalar_prefetch=2,
            grid=(steps,),
            in_specs=[
                pl.BlockSpec((picked, depth), lambda g, *_: (0, 0), pipeline_mode=pl.Buffered(1)),
                pl.BlockSpec((picked, depth), lambda g, *_: (0, 0), pipeline_mode=pl.Buffered(1)),
                pl.BlockSpec((rows, block), lambda g, *_: (0, g)),
                pl.BlockSpec((depth, block), lambda g, *_: (0, g)),
                pl.BlockSpec((depth, block), lambda g, *_: (0, g + steps)),
            ],
            out_specs=pl.BlockSpec((rows, block), lambda g, *_: (0, g)),
            scratch_shapes=[pltpu.VMEM((picked, depth), encoded.dtype)],
        ),
        cost_estimate=cost,
        name="cross",
    )(here, count_rows, mine, theirs, cross_queries, weight, weight)


def sum_kernel(self_ref, cross_ref, out_ref):
    for head in range(self_ref.shape[0]):
        lanes = slice(head * HEAD_DIM, (head + 1) * HEAD_DIM)
        out_ref[:, lanes] = (self_ref[head].astype(jnp.float32) + cross_ref[:, lanes]).astype(
            out_ref.dtype
        )


def per_device(
    queries, self_keys, self_values, cross_queries, encoded, neighbour_weight, counts, sources
):
    position = lax.axis_index("ctx")
    count = lax.axis_size("ctx")
    groups = [list(range(first, first + HEADS)) for first in range(0, count, HEADS)]
    cross_part = cross_attention(
        cross_queries, encoded, neighbour_weight, counts, sources, position
    )
    by_head = self_attention(queries, self_keys, self_values, position // HEADS, groups)
    self_part = lax.all_to_all(by_head, "ctx", 0, 0, axis_index_groups=groups, tiled=True)
    return pl.pallas_call(
        sum_kernel,
        out_shape=jax.ShapeDtypeStruct(queries.shape, jnp.bfloat16),
        name="total",
    )(self_part, cross_part)


def solution(mesh):
    return jax.shard_map(
        per_device,
        mesh=mesh,
        in_specs=(
            P(("groups", "ctx"), None),
            P(("groups", "ctx"), None),
            P(("groups", "ctx"), None),
            P(("groups", "ctx"), None),
            P(("groups", "ctx"), None),
            P(),
            P(("groups", "ctx")),
            P(("groups", "ctx"), None),
        ),
        out_specs=P(("groups", "ctx"), None),
        check_vma=False,
    )
```

profile of v0, /device:TPU:23, one launch (start us, length us, event | category | flops | bytes accessed | tf_op | source)
XLA Modules:
  0.0 132.5 jit_solution(4896848666546290137)
XLA Ops:
  0.0 1.9 %pack.2 = bf16[16,128,128]{2,1,0:T(8,128)(2,1)} custom-call(bf16[128,2048]{1,0:T(8,128)(2,1)} %refs_0_.3), custom_call_target="tpu_custom_call" | custom-call | bytes 1048576 | tf_op jit(solution)/shard_map/pack/pallas_call | solution.py:43
  1.9 5.5 %all-to-all-start = ((bf16[16,128,128]{2,1,0:T(8,128)(2,1)}), bf16[16,128,128]{2,1,0:T(8,128)(2,1)S(1)}, u32[]{:S(2)}, u32[]{:S(2)}) async-start(bf16[16,128,128]{2,1,0:T(8,128)(2,1)} %pack.2), calls=%async_computation | async-start | bytes 1048576 | tf_op jit(solution)/shard_map/all_to_all | solution.py:210
  7.4 2.3 %pack.3 = bf16[16,256,128]{2,1,0:T(8,128)(2,1)} custom-call(bf16[128,2048]{1,0:T(8,128)(2,1)} %refs_0_.4, bf16[128,2048]{1,0:T(8,128)(2,1)} %refs_1_.1), custom_call_target="tpu_custom_call" | custom-call | bytes 2097152 | tf_op jit(solution)/shard_map/pack/pallas_call | solution.py:43
  9.8 6.0 %all-to-all-done.q_ref = bf16[16,128,128]{2,1,0:T(8,128)(2,1)S(1)} async-done(((bf16[16,128,128]{2,1,0:T(8,128)(2,1)}), bf16[16,128,128]{2,1,0:T(8,128)(2,1)S(1)}, u32[]{:S(2)}, u32[]{:S(2)}) %all-to-all-start) | async-done | bytes 524320 | tf_op jit(solution)/shard_map/all_to_all | solution.py:210
  15.7 0.0 copy-start.1
  15.7 5.8 %all-to-all-start.1 = ((bf16[16,256,128]{2,1,0:T(8,128)(2,1)}), bf16[16,256,128]{2,1,0:T(8,128)(2,1)S(1)}, u32[]{:S(2)}, u32[]{:S(2)}) async-start(bf16[16,256,128]{2,1,0:T(8,128)(2,1)} %pack.3), calls=%async_computation.1 | async-start | bytes 2097152 | tf_op jit(solution)/shard_map/all_to_all | solution.py:207
  21.5 3.1 %collective-permute-start.5 = (bf16[128,896]{1,0:T(8,128)(2,1)}, bf16[128,896]{1,0:T(8,128)(2,1)S(1)}, u32[]{:S(2)}, u32[]{:S(2)}) collective-permute-start(bf16[128,896]{1,0:T(8,128)(2,1)} %refs_0_.5), channel_id=1, source_target_pairs={{0,8},{1,9},{2,10},{3,11},{4,12},{5,13},{6,14},{7,15},{8,16},{9,17... | collective-permute-start | bytes 688136 | tf_op jit(solution)/shard_map/ppermute | solution.py:24
  24.7 1.3 %fusion.13 = (s32[1]{0:T(128)}, s32[1]{0:T(128)}) fusion(s32[2]{0:T(128)} %param.14), kind=kLoop, calls=%fused_computation.61 | loop fusion | bytes 16 | tf_op jit(solution)/shard_map/slice | solution.py:303
  26.0 0.8 slice_bitcast_fusion.1
  26.8 0.7 pad_add_fusion.1
  27.5 1.9 %collective-permute-start.3 = (s32[3]{0:T(128)S(1)}, s32[3]{0:T(128)S(1)}, u32[]{:S(2)}, u32[]{:S(2)}) collective-permute-start(s32[3]{0:T(128)S(1)} %pad_add_fusion.1), channel_id=1, source_target_pairs={{0,1},{1,2},{2,3},{3,4},{4,5},{5,6},{6,7},{7,8},{8,9},{9,10},{10,1... | collective-permute-start | bytes 44 | tf_op jit(solution)/shard_map/ppermute | solution.py:24
  29.4 8.5 %collective-permute-done.3 = s32[3]{0:T(128)S(1)} collective-permute-done((s32[3]{0:T(128)S(1)}, s32[3]{0:T(128)S(1)}, u32[]{:S(2)}, u32[]{:S(2)}) %collective-permute-start.3) | collective-permute-done | bytes 44 | tf_op jit(solution)/shard_map/ppermute | solution.py:24
  37.9 0.1 slice_bitcast_fusion
  38.0 0.0 collective-permute-done.5.refs_1_
  38.0 0.0 copy-start.3
  38.0 3.9 %collective-permute-start.6 = (bf16[128,896]{1,0:T(8,128)(2,1)S(1)}, bf16[128,896]{1,0:T(8,128)(2,1)S(1)}, u32[]{:S(2)}, u32[]{:S(2)}) collective-permute-start(bf16[128,896]{1,0:T(8,128)(2,1)S(1)} %collective-permute-done.5.refs_1_), channel_id=1, source_target_pairs={{0,8},{1,9},{2,10},{3,11},{4,12},{5,13},{6,14},{7,15},{8,16},{9,17... | collective-permute-start | bytes 688136 | tf_op jit(solution)/shard_map/ppermute | solution.py:24
  41.9 0.1 iota_add_fusion
  42.0 0.1 add.78
  42.1 4.1 %collective-permute-done.6.refs_2_ = bf16[128,896]{1,0:T(8,128)(2,1)S(1)} collective-permute-done((bf16[128,896]{1,0:T(8,128)(2,1)S(1)}, bf16[128,896]{1,0:T(8,128)(2,1)S(1)}, u32[]{:S(2)}, u32[]{:S(2)}) %collective-permute-start.6) | collective-permute-done | bytes 229408 | tf_op jit(solution)/shard_map/ppermute | solution.py:24
  46.2 1.1 broadcast_select_fusion
  47.3 1.2 pad_maximum_fusion
  48.4 0.1 collective-permute-start.7
  48.5 0.0 collective-permute-start.8
  48.5 2.5 %collective-permute-start.9 = (bf16[256,896]{1,0:T(8,128)(2,1)}, bf16[256,896]{1,0:T(8,128)(2,1)}, u32[]{:S(2)}, u32[]{:S(2)}) collective-permute-start(bf16[256,896]{1,0:T(8,128)(2,1)} %get-tuple-element.18), channel_id=1, source_target_pairs={{0,6},{1,7},{2,4},{3,5},{4,2},{5,3},{6,0},{7,1},{8,14},{9,15},{10,... | collective-permute-start | bytes 1376264 | tf_op jit(solution)/shard_map/ppermute | solution.py:29
  51.1 1.7 %collective-permute-start.1 = (bf16[6,128,128]{2,1,0:T(8,128)(2,1)S(1)}, bf16[6,128,128]{2,1,0:T(8,128)(2,1)S(1)}, u32[]{:S(2)}, u32[]{:S(2)}) collective-permute-start(bf16[6,128,128]{2,1,0:T(8,128)(2,1)S(1)} %slice.37), channel_id=1, source_target_pairs={{16,0},{17,1},{18,2},{19,3},{20,4},{21,5},{22,6},{23,7},{24,8},{25... | collective-permute-start | bytes 589832 | tf_op jit(solution)/shard_map/ppermute | solution.py:24
  52.8 0.0 all-to-all-done.1.kv_ref
  52.8 0.0 copy-start
  52.8 1.0 slice.36
  53.8 1.3 collective-permute-start
  55.1 0.6 fusion
  55.7 0.8 slice.38.kv_ref
  56.5 0.0 collective-permute-done.1.q_ref
  56.5 5.6 %collective-permute-start.4 = (s32[8]{0:T(128)S(1)}, s32[8]{0:T(128)S(1)}, u32[]{:S(2)}, u32[]{:S(2)}) collective-permute-start(s32[8]{0:T(128)S(1)} %add.78), channel_id=1, source_target_pairs={{0,1},{1,0},{2,3},{3,2},{4,5},{5,4},{6,7},{7,6},{8,9},{9,8},{10,11... | collective-permute-start | bytes 104 | tf_op jit(solution)/shard_map/ppermute | solution.py:29
  62.1 0.0 copy-done.9
  62.1 3.2 %later.1 = bf16[7,128,128]{2,1,0:T(8,128)(2,1)} custom-call(bf16[6,128,128]{2,1,0:T(8,128)(2,1)} %copy-done.9, bf16[6,256,128]{2,1,0:T(8,128)(2,1)} %slice.38.kv_ref), custom_call_target="tpu_custom_call" | custom-call | flops 150994944 | bytes 196608 | tf_op jit(solution)/shard_map/later/pallas_call | solution.py:224
  65.3 0.0 collective-permute-done.4
  65.3 1.3 collective-permute-start.2
  66.6 0.6 fusion.11.theirs_ref
  67.1 0.0 collective-permute-done.7.refs_3_
  67.1 0.0 collective-permute-done.8.refs_4_
  67.2 1.5 %collective-permute-done.9.refs_5_ = bf16[256,896]{1,0:T(8,128)(2,1)} collective-permute-done((bf16[256,896]{1,0:T(8,128)(2,1)}, bf16[256,896]{1,0:T(8,128)(2,1)}, u32[]{:S(2)}, u32[]{:S(2)}) %collective-permute-start.9) | collective-permute-done | bytes 458784 | tf_op jit(solution)/shard_map/ppermute | solution.py:29
  68.7 0.0 copy-done.3
  68.7 0.0 copy-done.4
  68.7 0.0 copy-done.7
  68.7 3.1 %gather.1 = (bf16[512,896]{1,0:T(8,128)(2,1)}, bf16[512,896]{1,0:T(8,128)(2,1)}) custom-call(s32[8]{0:T(128)} %get-tuple-element.13.mine_ref, s32[8]{0:T(128)} %fusion.11.theirs_ref, bf16[128,896]{1,0:T(8,128)(2,1)} %refs_0_.5, bf16[128,896]{1,0:T(8,128)(2,1)} %copy-done.3, bf16[128,896]{1,0:T(8,128)(2,1)} %copy-done.4, bf16[256,896]{1,0:T(8,128)(2,1)} %copy-done.7, ...), custom_call_target="tpu_custom_call" | custom-call | bytes 3670016 | tf_op jit(solution)/shard_map/gather/pallas_call | solution.py:326
  71.8 2.9 %collective-permute-start.10 = (bf16[512,896]{1,0:T(8,128)(2,1)}, bf16[512,896]{1,0:T(8,128)(2,1)S(1)}, u32[]{:S(2)}, u32[]{:S(2)}) collective-permute-start(bf16[512,896]{1,0:T(8,128)(2,1)} %get-tuple-element.12), channel_id=1, source_target_pairs={{0,1},{1,0},{2,3},{3,2},{4,5},{5,4},{6,7},{7,6},{8,9},{9,8},{10,11... | collective-permute-start | bytes 2752520 | tf_op jit(solution)/shard_map/ppermute | solution.py:29
  74.7 0.0 copy-done.1
  74.7 0.0 copy-done
  74.7 7.3 %own.1 = (f32[16,128,128]{2,1,0:T(8,128)}, f32[16,128,128]{2,1,0:T(8,128)}) custom-call(bf16[16,128,128]{2,1,0:T(8,128)(2,1)} %copy-done.1, bf16[16,256,128]{2,1,0:T(8,128)(2,1)} %copy-done), custom_call_target="tpu_custom_call" | custom-call | flops 1073741824 | bytes 1572864 | tf_op jit(solution)/shard_map/own/pallas_call | solution.py:215
  82.0 0.0 collective-permute-done.2.back_ref
  82.0 0.0 collective-permute-done.kv_ref
  82.0 0.0 copy-start.6
  82.0 0.7 copy-done.8
  82.7 0.2 copy-done.6
  82.9 7.4 %previous.1 = bf16[16,128,128]{2,1,0:T(8,128)(2,1)} custom-call(s32[1]{0:T(128)} %bitcast.flag_ref, bf16[16,128,128]{2,1,0:T(8,128)(2,1)} %copy-done.1, bf16[10,256,128]{2,1,0:T(8,128)(2,1)} %copy-done.6, bf16[7,128,128]{2,1,0:T(8,128)(2,1)} %copy-done.8, f32[16,128,128]{2,1,0:T(8,128)} %get-tuple-element.9.out1_ref, f32[16,128,128]{2,1,0:T(8,128)} %get-tuple-element.10.stat_ref), custom_call_target="tpu_custom_call" | custom-call | flops 922746880 | bytes 2621440 | tf_op jit(solution)/shard_map/previous/pallas_call | solution.py:232
  90.3 20.6 %all-to-all-start.2 = ((bf16[16,128,128]{2,1,0:T(8,128)(2,1)}), bf16[16,128,128]{2,1,0:T(8,128)(2,1)S(1)}, u32[]{:S(2)}, u32[]{:S(2)}) async-start(bf16[16,128,128]{2,1,0:T(8,128)(2,1)} %previous.1), calls=%async_computation.2 | async-start | bytes 1048576 | tf_op jit(solution)/shard_map/all_to_all | solution.py:384
  110.8 1.3 pad_add_fusion.2.count_ref
  112.1 0.5 compare_convert_fusion.here_ref
  112.7 0.0 collective-permute-done.10.theirs_ref
  112.7 0.9 copy-done.5
  113.6 15.8 %cross.1.cross_ref = f32[128,2048]{1,0:T(8,128)} custom-call(s32[8]{0:T(128)} %compare_convert_fusion.here_ref, s32[2]{0:T(128)} %pad_add_fusion.2.count_ref, bf16[512,896]{1,0:T(8,128)(2,1)} %get-tuple-element.11.mine_ref, bf16[512,896]{1,0:T(8,128)(2,1)} %copy-done.5, bf16[128,2048]{1,0:T(8,128)(2,1)} %q_ref.1, bf16[896,4096]{1,0:T(8,128)(2,1)} %wv_ref.1, ...), custom_call_target="tpu_custom_call" | custom-call | flops 3758096384 | bytes 9175040 | tf_op jit(solution)/shard_map/cross/pallas_call | solution.py:345
  129.4 0.0 all-to-all-done.2.self_ref
  129.4 0.8 copy-done.2
  130.2 2.3 %total.1 = bf16[128,2048]{1,0:T(8,128)(2,1)} custom-call(bf16[16,128,128]{2,1,0:T(8,128)(2,1)} %copy-done.2, f32[128,2048]{1,0:T(8,128)} %cross.1.cross_ref), custom_call_target="tpu_custom_call" | custom-call | tf_op jit(solution)/shard_map/total/pallas_call | solution.py:385
  (8 shorter events, 0.0 us)
Async XLA Ops:
  1.9 13.8 %all-to-all-start = ((bf16[16,128,128]{2,1,0:T(8,128)(2,1)}), bf16[16,128,128]{2,1,0:T(8,128)(2,1)S(1)}, u32[]{:S(2)}, u32[]{:S(2)}) async-start(bf16[16,128,128]{2,1,0:T(8,128)(2,1)} %pack.2), calls=%async_computation | async-start | bytes 1048576 | tf_op jit(solution)/shard_map/all_to_all | solution.py:210
  15.7 59.0 %copy-start.1 = (bf16[16,128,128]{2,1,0:T(8,128)(2,1)}, bf16[16,128,128]{2,1,0:T(8,128)(2,1)S(1)}, u32[]{:S(2)}) copy-start(bf16[16,128,128]{2,1,0:T(8,128)(2,1)S(1)} %all-to-all-done.q_ref) | copy-start | bytes 1572868
  15.7 37.1 %all-to-all-start.1 = ((bf16[16,256,128]{2,1,0:T(8,128)(2,1)}), bf16[16,256,128]{2,1,0:T(8,128)(2,1)S(1)}, u32[]{:S(2)}, u32[]{:S(2)}) async-start(bf16[16,256,128]{2,1,0:T(8,128)(2,1)} %pack.3), calls=%async_computation.1 | async-start | bytes 2097152 | tf_op jit(solution)/shard_map/all_to_all | solution.py:207
  21.5 16.5 %collective-permute-start.5 = (bf16[128,896]{1,0:T(8,128)(2,1)}, bf16[128,896]{1,0:T(8,128)(2,1)S(1)}, u32[]{:S(2)}, u32[]{:S(2)}) collective-permute-start(bf16[128,896]{1,0:T(8,128)(2,1)} %refs_0_.5), channel_id=1, source_target_pairs={{0,8},{1,9},{2,10},{3,11},{4,12},{5,13},{6,14},{7,15},{8,16},{9,17... | collective-permute-start | bytes 688136 | tf_op jit(solution)/shard_map/ppermute | solution.py:24
  27.5 10.5 %collective-permute-start.3 = (s32[3]{0:T(128)S(1)}, s32[3]{0:T(128)S(1)}, u32[]{:S(2)}, u32[]{:S(2)}) collective-permute-start(s32[3]{0:T(128)S(1)} %pad_add_fusion.1), channel_id=1, source_target_pairs={{0,1},{1,2},{2,3},{3,4},{4,5},{5,6},{6,7},{7,8},{8,9},{9,10},{10,1... | collective-permute-start | bytes 44 | tf_op jit(solution)/shard_map/ppermute | solution.py:24
  38.0 30.7 %copy-start.3 = (bf16[128,896]{1,0:T(8,128)(2,1)}, bf16[128,896]{1,0:T(8,128)(2,1)S(1)}, u32[]{:S(2)}) copy-start(bf16[128,896]{1,0:T(8,128)(2,1)S(1)} %collective-permute-done.5.refs_1_) | copy-start | bytes 688132
  38.0 8.2 %collective-permute-start.6 = (bf16[128,896]{1,0:T(8,128)(2,1)S(1)}, bf16[128,896]{1,0:T(8,128)(2,1)S(1)}, u32[]{:S(2)}, u32[]{:S(2)}) collective-permute-start(bf16[128,896]{1,0:T(8,128)(2,1)S(1)} %collective-permute-done.5.refs_1_), channel_id=1, source_target_pairs={{0,8},{1,9},{2,10},{3,11},{4,12},{5,13},{6,14},{7,15},{8,16},{9,17... | collective-permute-start | bytes 688136 | tf_op jit(solution)/shard_map/ppermute | solution.py:24
  46.2 22.5 %copy-start.4 = (bf16[128,896]{1,0:T(8,128)(2,1)}, bf16[128,896]{1,0:T(8,128)(2,1)S(1)}, u32[]{:S(2)}) copy-start(bf16[128,896]{1,0:T(8,128)(2,1)S(1)} %collective-permute-done.6.refs_2_) | copy-start | bytes 688132
  48.4 18.7 %collective-permute-start.7 = (bf16[256,896]{1,0:T(8,128)(2,1)}, bf16[256,896]{1,0:T(8,128)(2,1)S(1)}, u32[]{:S(2)}, u32[]{:S(2)}) collective-permute-start(bf16[256,896]{1,0:T(8,128)(2,1)} %get-tuple-element.20), channel_id=1, source_target_pairs={{0,2},{1,3},{2,0},{3,1},{4,6},{5,7},{6,4},{7,5},{8,10},{9,11},{10,... | collective-permute-start | bytes 1376264 | tf_op jit(solution)/shard_map/ppermute | solution.py:29
  48.5 18.6 %collective-permute-start.8 = (bf16[256,896]{1,0:T(8,128)(2,1)}, bf16[256,896]{1,0:T(8,128)(2,1)}, u32[]{:S(2)}, u32[]{:S(2)}) collective-permute-start(bf16[256,896]{1,0:T(8,128)(2,1)} %get-tuple-element.19), channel_id=1, source_target_pairs={{0,4},{1,5},{2,6},{3,7},{4,0},{5,1},{6,2},{7,3},{8,12},{9,13},{10,... | collective-permute-start | bytes 1376264 | tf_op jit(solution)/shard_map/ppermute | solution.py:29
  48.5 20.1 %collective-permute-start.9 = (bf16[256,896]{1,0:T(8,128)(2,1)}, bf16[256,896]{1,0:T(8,128)(2,1)}, u32[]{:S(2)}, u32[]{:S(2)}) collective-permute-start(bf16[256,896]{1,0:T(8,128)(2,1)} %get-tuple-element.18), channel_id=1, source_target_pairs={{0,6},{1,7},{2,4},{3,5},{4,2},{5,3},{6,0},{7,1},{8,14},{9,15},{10,... | collective-permute-start | bytes 1376264 | tf_op jit(solution)/shard_map/ppermute | solution.py:29
  51.1 5.4 %collective-permute-start.1 = (bf16[6,128,128]{2,1,0:T(8,128)(2,1)S(1)}, bf16[6,128,128]{2,1,0:T(8,128)(2,1)S(1)}, u32[]{:S(2)}, u32[]{:S(2)}) collective-permute-start(bf16[6,128,128]{2,1,0:T(8,128)(2,1)S(1)} %slice.37), channel_id=1, source_target_pairs={{16,0},{17,1},{18,2},{19,3},{20,4},{21,5},{22,6},{23,7},{24,8},{25... | collective-permute-start | bytes 589832 | tf_op jit(solution)/shard_map/ppermute | solution.py:24
  52.8 21.9 %copy-start = (bf16[16,256,128]{2,1,0:T(8,128)(2,1)}, bf16[16,256,128]{2,1,0:T(8,128)(2,1)S(1)}, u32[]{:S(2)}) copy-start(bf16[16,256,128]{2,1,0:T(8,128)(2,1)S(1)} %all-to-all-done.1.kv_ref) | copy-start | bytes 3145732
  53.8 28.2 %collective-permute-start = (bf16[10,256,128]{2,1,0:T(8,128)(2,1)}, bf16[10,256,128]{2,1,0:T(8,128)(2,1)S(1)}, u32[]{:S(2)}, u32[]{:S(2)}) collective-permute-start(bf16[10,256,128]{2,1,0:T(8,128)(2,1)} %slice.36), channel_id=1, source_target_pairs={{0,16},{1,17},{2,18},{3,19},{4,20},{5,21},{6,22},{7,23},{8,24},{9,... | collective-permute-start | bytes 1966088 | tf_op jit(solution)/shard_map/ppermute | solution.py:24
  56.5 5.6 %copy-start.9 = (bf16[6,128,128]{2,1,0:T(8,128)(2,1)}, bf16[6,128,128]{2,1,0:T(8,128)(2,1)S(1)}, u32[]{:S(2)}) copy-start(bf16[6,128,128]{2,1,0:T(8,128)(2,1)S(1)} %collective-permute-done.1.q_ref) | copy-start | bytes 589828
  56.5 8.8 %collective-permute-start.4 = (s32[8]{0:T(128)S(1)}, s32[8]{0:T(128)S(1)}, u32[]{:S(2)}, u32[]{:S(2)}) collective-permute-start(s32[8]{0:T(128)S(1)} %add.78), channel_id=1, source_target_pairs={{0,1},{1,0},{2,3},{3,2},{4,5},{5,4},{6,7},{7,6},{8,9},{9,8},{10,11... | collective-permute-start | bytes 104 | tf_op jit(solution)/shard_map/ppermute | solution.py:29
  65.3 16.7 %collective-permute-start.2 = (bf16[7,128,128]{2,1,0:T(8,128)(2,1)}, bf16[7,128,128]{2,1,0:T(8,128)(2,1)S(1)}, u32[]{:S(2)}, u32[]{:S(2)}) collective-permute-start(bf16[7,128,128]{2,1,0:T(8,128)(2,1)} %later.1), channel_id=1, source_target_pairs={{0,16},{1,17},{2,18},{3,19},{4,20},{5,21},{6,22},{7,23},{8,24},{9,... | collective-permute-start | bytes 688136 | tf_op jit(solution)/shard_map/ppermute | solution.py:24
  67.1 1.5 %copy-start.7 = (bf16[256,896]{1,0:T(8,128)(2,1)}, bf16[256,896]{1,0:T(8,128)(2,1)S(1)}, u32[]{:S(2)}) copy-start(bf16[256,896]{1,0:T(8,128)(2,1)S(1)} %collective-permute-done.7.refs_3_) | copy-start | bytes 1376260
  71.8 40.9 %collective-permute-start.10 = (bf16[512,896]{1,0:T(8,128)(2,1)}, bf16[512,896]{1,0:T(8,128)(2,1)S(1)}, u32[]{:S(2)}, u32[]{:S(2)}) collective-permute-start(bf16[512,896]{1,0:T(8,128)(2,1)} %get-tuple-element.12), channel_id=1, source_target_pairs={{0,1},{1,0},{2,3},{3,2},{4,5},{5,4},{6,7},{7,6},{8,9},{9,8},{10,11... | collective-permute-start | bytes 2752520 | tf_op jit(solution)/shard_map/ppermute | solution.py:29
  82.0 0.7 copy-start.8
  82.0 0.9 copy-start.6
  90.3 39.1 %all-to-all-start.2 = ((bf16[16,128,128]{2,1,0:T(8,128)(2,1)}), bf16[16,128,128]{2,1,0:T(8,128)(2,1)S(1)}, u32[]{:S(2)}, u32[]{:S(2)}) async-start(bf16[16,128,128]{2,1,0:T(8,128)(2,1)} %previous.1), calls=%async_computation.2 | async-start | bytes 1048576 | tf_op jit(solution)/shard_map/all_to_all | solution.py:384
  112.7 0.9 copy-start.5
  129.4 0.8 copy-start.2
where the time goes:
time: 133 us
  starting transfers between devices  56.3 us (42%)
  Pallas kernels  43.3 us (33%)
  waiting for transfers between devices  20.1 us (15%)
  local copies, waits for them, and re-layouts  6.66 us (5%)
  other arithmetic  6 us (5%)
    all_to_all x1, starting transfers between devices, per_device(): lax.all_to_all(by_head, 'ctx', 0, 0, axis_index_groups=groups, tiled=True)  20.6 us
    pallas_call x1, Pallas kernels, cross_attention(): pl.pallas_call(functools.partial(cross_kernel, HEAD_DIM ** (-0.5) * LOG2E...  15.8 us
    ppermute x6, starting transfers between devices, shifted(): lax.ppermute(value, axis, [(source, source + steps) for source in range(f...  13.2 us
    ppermute x6, waiting for transfers between devices, shifted(): lax.ppermute(value, axis, [(source, source + steps) for source in range(f...  12.6 us
    ppermute x5, starting transfers between devices, swapped(): lax.ppermute(value, axis, [(source, source ^ bit) for source in range(cou...  11.2 us
    pallas_call x1, Pallas kernels, self_attention(): pl.pallas_call(functools.partial(previous_kernel, scale), out_shape=jax.S...  7.39 us
    pallas_call x1, Pallas kernels, self_attention(): pl.pallas_call(functools.partial(own_kernel, scale), out_shape=(jax.Shape...  7.25 us
    all_to_all x1, waiting for transfers between devices, self_attention(): lax.all_to_all(packed(queries), 'ctx', 0, 0, axis_index_groups=groups, ti...  5.96 us
  transfers between devices with their start and end apart: 14, of which 4 were waited for; matrix products, arithmetic and copies ran while one was open for 8% of the time, Pallas kernels for 29%

commit v1 on v0

--- a/solution.py
+++ b/solution.py
@@ -12,7 +12,7 @@
 HEAD_DIM = 128
 SPAN = 64
 PLANE = 8
-LEFT = 6
+LEFT = 8
 
 MASKED_SCORE = -1e30
 LOG2E = 1.4426950408889634
@@ -226,7 +226,7 @@
         out_shape=jax.ShapeDtypeStruct((LEFT + 1, rows, HEAD_DIM), jnp.bfloat16),
         cost_estimate=estimate(small, (asked,)),
         name="later",
-    )(asked, kv[:LEFT])
+    )(asked, kv)
     back = shifted(answer, "ctx", heads)
     vmem = pl.BlockSpec(memory_space=pltpu.VMEM)
     return pl.pallas_call(
@@ -238,72 +238,134 @@
     )(chunk.reshape(1), q, arriving, back, out1, stat)
 
 
-def gather_kernel(mine_ref, theirs_ref, *refs):
-    *in_refs, mine_out, theirs_out, window_ref = refs
-    start = 0
-    for ref in in_refs:
-        window_ref[start : start + ref.shape[0], :] = ref[...]
-        start += ref.shape[0]
-    for piece_ref, out_ref in ((mine_ref, mine_out), (theirs_ref, theirs_out)):
-        pieces = piece_ref.shape[0]
-        size = out_ref.shape[0] // pieces
-        for n in range(pieces):
-            place = pl.multiple_of(piece_ref[n], size)
-            out_ref[n * size : (n + 1) * size, :] = window_ref[pl.ds(place, size), :]
-
-
-def cross_kernel(
-    scale, span_count, here_ref, count_ref, mine_ref, theirs_ref, q_ref, wk_ref, wv_ref, out_ref, rows_ref
-):
-    span = q_ref.shape[0] // span_count
+def wanted_pieces(table_ref, position, span_count):
+    pieces = []
+    place, plane = position % PLANE, position // PLANE
+    for c in range(span_count):
+        for slot in range(2):
+            source = table_ref[c, slot] // 4
+            for later in range(2):
+                block = (source + later) // span_count
+                relative = (block % PLANE) ^ place
+                away = plane - block // PLANE
+                column = relative // 2
+                index = jnp.where(
+                    column == 0, away, 1 + 2 * column + jnp.where(away == 1, 0, 1)
+                )
+                pieces.append((relative % 2 == 0, index, (source + later) % span_count))
+    return pieces
+
+
+def fetch(refs, rows, index, half, target, sem):
+    size = target.shape[0]
+    first = 0
+    for ref in refs:
+        count = ref.shape[0] // rows
+
+        @pl.when((index >= first) & (index < first + count))
+        def _(ref=ref, first=first):
+            start = pl.multiple_of((index - first) * rows + half * size, size)
+            pltpu.make_async_copy(ref.at[pl.ds(start, size), :], target, sem).start()
+
+        first += count
+
+
+def gather_kernel(span_count, position_ref, theirs_ref, *refs):
+    *in_refs, out_ref, sems = refs
+    rows = in_refs[0].shape[0]
+    pieces = wanted_pieces(theirs_ref, position_ref[0], span_count)
+    size = out_ref.shape[0] // len(pieces)
+    targets = [out_ref.at[n * size : (n + 1) * size, :] for n in range(len(pieces))]
+    for n, (here, index, half) in enumerate(pieces):
+        fetch(in_refs, rows, jnp.where(here, index, -1), half, targets[n], sems.at[n])
+    for n, (here, _, _) in enumerate(pieces):
+
+        @pl.when(here)
+        def _(n=n):
+            pltpu.make_async_copy(in_refs[0].at[0:size, :], targets[n], sems.at[n]).wait()
+
+
+def cross_kernel(scale, span_count, position_ref, table_ref, *refs):
+    *in_refs, theirs_ref, q_ref, weight_ref, out_ref, rows_ref, weights_ref, sems, weight_sems = refs
+    rows, width = q_ref.shape
+    span = rows // span_count
+    steps, _, _, block = weights_ref.shape
+    weight_copies = [
+        [
+            pltpu.make_async_copy(
+                weight_ref.at[:, n * width + g * block : n * width + (g + 1) * block],
+                weights_ref.at[g, n],
+                weight_sems.at[g, n],
+            )
+            for n in range(2)
+        ]
+        for g in range(steps)
+    ]
+    pieces = wanted_pieces(table_ref, position_ref[0], span_count)
+    targets = [rows_ref.at[n * span : (n + 1) * span, :] for n in range(len(pieces))]
+    held = sum(ref.shape[0] for ref in in_refs) // rows
+    for n, (here, index, half) in enumerate(pieces):
+        fetch(in_refs, rows, jnp.where(here, index, held), half, targets[n], sems.at[n])
+
+        @pl.when(jnp.logical_not(here))
+        def _(n=n):
+            source = theirs_ref.at[n * span : (n + 1) * span, :]
+            pltpu.make_async_copy(source, targets[n], sems.at[n]).start()
+
+    for g in range(steps):
+        for copy in weight_copies[g]:
+            copy.start()
+    for n in range(len(pieces)):
+        pltpu.make_async_copy(theirs_ref.at[0:span, :], targets[n], sems.at[n]).wait()
+
     keys_of_span = rows_ref.shape[0] // span_count
-    pieces = rows_ref.shape[0] // span
-
-    @pl.when(pl.program_id(0) == 0)
-    def _():
-        for n in range(pieces):
-            place = slice(n * span, (n + 1) * span)
-
-            @pl.when(here_ref[n] > 0)
-            def _():
-                rows_ref[place, :] = mine_ref[place, :]
-
-            @pl.when(here_ref[n] == 0)
-            def _():
-                rows_ref[place, :] = theirs_ref[place, :]
-
-    rows = rows_ref[...]
-    keys = jnp.dot(rows, wk_ref[...], preferred_element_type=jnp.float32).astype(jnp.bfloat16)
-    values = jnp.dot(rows, wv_ref[...], preferred_element_type=jnp.float32).astype(jnp.bfloat16)
     slot = lax.broadcasted_iota(jnp.int32, (span, keys_of_span), 1) // (2 * span)
-    for c in range(span_count):
-        valid = slot < count_ref[c]
-        none = jnp.where(count_ref[c] > 0, 0.0, 1.0)
-        here = slice(c * keys_of_span, (c + 1) * keys_of_span)
-        for h in range(q_ref.shape[1] // HEAD_DIM):
-            lanes = slice(h * HEAD_DIM, (h + 1) * HEAD_DIM)
-            s = scores_of(q_ref[c * span : (c + 1) * span, lanes], keys[here, lanes])
-            s = jnp.where(valid, s, MASKED_SCORE)
-            largest = jnp.max(s, axis=1, keepdims=True)
-            p = jnp.where(valid, jnp.exp2((s - largest) * scale), 0.0)
-            total = jnp.sum(p, axis=1, keepdims=True) + none
-            o = jnp.dot(
-                p.astype(jnp.bfloat16), values[here, lanes], preferred_element_type=jnp.float32
-            )
-            out_ref[c * span : (c + 1) * span, lanes] = o * (1.0 / total)
+    counts = [table_ref[c, 0] % 4 for c in range(span_count)]
+    valid = [slot < count for count in counts]
+    none = [jnp.where(count > 0, 0.0, 1.0) for count in counts]
+
+    def attend(g, keys, values):
+        for h in range(block // HEAD_DIM):
+            inner = slice(h * HEAD_DIM, (h + 1) * HEAD_DIM)
+            lanes = slice(g * block + h * HEAD_DIM, g * block + (h + 1) * HEAD_DIM)
+            for c in range(span_count):
+                here = slice(c * keys_of_span, (c + 1) * keys_of_span)
+                mine = slice(c * span, (c + 1) * span)
+                s = jnp.where(valid[c], scores_of(q_ref[mine, lanes], keys[here, inner]), MASKED_SCORE)
+                largest = jnp.max(s, axis=1, keepdims=True)
+                p = jnp.where(valid[c], jnp.exp2((s - largest) * scale), 0.0)
+                total = jnp.sum(p, axis=1, keepdims=True) + none[c]
+                o = jnp.dot(
+                    p.astype(jnp.bfloat16), values[here, inner], preferred_element_type=jnp.float32
+                )
+                out_ref[mine, lanes] = o * (1.0 / total)
+
+    waiting = None
+    for g in range(steps):
+        for copy in weight_copies[g]:
+            copy.wait()
+        projected = [
+            jnp.dot(
+                rows_ref[...], weights_ref[g, n], preferred_element_type=jnp.float32
+            ).astype(jnp.bfloat16)
+            for n in range(2)
+        ]
+        if waiting is not None:
+            attend(*waiting)
+        waiting = (g, *projected)
+    attend(*waiting)
 
 
 def cross_attention(cross_queries, encoded, weight, counts, sources, position):
     rows, width = cross_queries.shape
     span_count = counts.shape[0]
     depth = encoded.shape[1]
-    place, plane = position % PLANE, position // PLANE
+    place = position % PLANE
     one_back = shifted(encoded, "ctx", PLANE)
-    before = shifted(jnp.concatenate([counts[-1:], sources[-1]]), "ctx", 1)
-    count_rows = jnp.concatenate([before[:1], counts[:-1]])
-    source_rows = jnp.concatenate([before[1:][None], sources[:-1]], axis=0)
-    spans = (source_rows[:, :, None] + jnp.arange(2, dtype=jnp.int32)).reshape(-1)
-    their_spans = swapped(spans, "ctx", 1)
+    table = sources * 4 + counts[:, None]
+    before = shifted(table, "ctx", 1)
+    table = jnp.concatenate([before[-1:], table[:-1]], axis=0)
+    their_table = swapped(table, "ctx", 1)
     two_back = shifted(one_back, "ctx", PLANE)
 
     near = []
@@ -311,28 +373,23 @@
         other = jnp.where(place < (place ^ bit), encoded, two_back)
         near.append(swapped(jnp.concatenate([one_back, other], axis=0), "ctx", bit))
 
-    def places(wanted):
-        block, half = wanted // span_count, wanted % span_count
-        relative = (block % PLANE) ^ place
-        away = plane - block // PLANE
-        column = relative // 2
-        slot = jnp.where(column == 0, away, 1 + 2 * column + jnp.where(away == 1, 0, 1))
-        start = jnp.where(relative % 2 == 0, slot * rows + half * SPAN, 0)
-        return jnp.clip(start, 0, 9 * rows - SPAN), (relative % 2 == 0).astype(jnp.int32)
-
-    my_places, here = places(spans)
+    held = [encoded, one_back, two_back, *near]
+    where = position.reshape(1)
     picked = span_count * 4 * SPAN
-    smem, vmem = (pl.BlockSpec(memory_space=m) for m in (pltpu.SMEM, pltpu.VMEM))
-    mine, theirs = pl.pallas_call(
-        gather_kernel,
-        out_shape=(jax.ShapeDtypeStruct((picked, depth), encoded.dtype),) * 2,
-        in_specs=[smem] * 2 + [vmem] * 6,
-        scratch_shapes=[pltpu.VMEM((9 * rows, depth), encoded.dtype)],
+    pieces = picked // SPAN
+    smem, anywhere = (pl.BlockSpec(memory_space=m) for m in (pltpu.SMEM, pl.ANY))
+    vmem = pl.BlockSpec(memory_space=pltpu.VMEM)
+    theirs = pl.pallas_call(
+        functools.partial(gather_kernel, span_count),
+        out_shape=jax.ShapeDtypeStruct((picked, depth), encoded.dtype),
+        in_specs=[smem] * 2 + [anywhere] * len(held),
+        out_specs=vmem,
+        scratch_shapes=[pltpu.SemaphoreType.DMA((pieces,))],
         cost_estimate=pl.CostEstimate(
             flops=0, bytes_accessed=8 * picked * depth, transcendentals=0
         ),
         name="gather",
-    )(my_places, places(their_spans)[0], encoded, one_back, two_back, *near)
+    )(where, their_table, *held)
     theirs = swapped(theirs, "ctx", 1)
 
     block = 4 * HEAD_DIM
@@ -345,22 +402,17 @@
     return pl.pallas_call(
         functools.partial(cross_kernel, HEAD_DIM ** (-0.5) * LOG2E, span_count),
         out_shape=jax.ShapeDtypeStruct((rows, width), jnp.float32),
-        grid_spec=pltpu.PrefetchScalarGridSpec(
-            num_scalar_prefetch=2,
-            grid=(steps,),
-            in_specs=[
-                pl.BlockSpec((picked, depth), lambda g, *_: (0, 0), pipeline_mode=pl.Buffered(1)),
-                pl.BlockSpec((picked, depth), lambda g, *_: (0, 0), pipeline_mode=pl.Buffered(1)),
-                pl.BlockSpec((rows, block), lambda g, *_: (0, g)),
-                pl.BlockSpec((depth, block), lambda g, *_: (0, g)),
-                pl.BlockSpec((depth, block), lambda g, *_: (0, g + steps)),
-            ],
-            out_specs=pl.BlockSpec((rows, block), lambda g, *_: (0, g)),
-            scratch_shapes=[pltpu.VMEM((picked, depth), encoded.dtype)],
-        ),
+        in_specs=[smem] * 2 + [anywhere] * (len(held) + 1) + [vmem, anywhere],
+        out_specs=vmem,
+        scratch_shapes=[
+            pltpu.VMEM((picked, depth), encoded.dtype),
+            pltpu.VMEM((steps, 2, depth, block), weight.dtype),
+            pltpu.SemaphoreType.DMA((pieces,)),
+            pltpu.SemaphoreType.DMA((steps, 2)),
+        ],
         cost_estimate=cost,
         name="cross",
-    )(here, count_rows, mine, theirs, cross_queries, weight, weight)
+    )(where, table, *held, theirs, cross_queries, weight)
 
 
 def sum_kernel(self_ref, cross_ref, out_ref):

time: 133 us -> 142 us (1.068)
  starting transfers between devices: 56.3 us -> 65.9 us
  waiting for transfers between devices: 20.1 us -> 24.1 us
  other arithmetic: 6 us -> 2.33 us
  local copies, waits for them, and re-layouts: 6.66 us -> 3.23 us
  Pallas kernels: 43.3 us -> 45.5 us
    ppermute x6, starting transfers between devices: 13.2 us -> 19.2 us  [shifted(): lax.ppermute(value, axis, [(source, source + steps) for source in range(f...]
    ppermute x6, waiting for transfers between devices: 12.6 us -> 18.2 us  [shifted(): lax.ppermute(value, axis, [(source, source + steps) for source in range(f...]
    all_to_all x1, starting transfers between devices: 20.6 us -> 25.8 us  [per_device(): lax.all_to_all(by_head, 'ctx', 0, 0, axis_index_groups=groups, tiled=True)]
    slice x2, local copies, waits for them, and re-layouts: 2.13 us -> 0.01 us  [cross_attention(): table = jnp.concatenate([before[-1:], table[:-1]], axis=0)]
    concatenate x3 -> x1, other arithmetic: 1.99 us -> 0.01 us  [cross_attention(): table = jnp.concatenate([before[-1:], table[:-1]], axis=0)]
    pallas_call x1, Pallas kernels: 15.8 us -> 17.4 us  [cross_attention(): pl.pallas_call(functools.partial(cross_kernel, HEAD_DIM ** (-0.5) * LOG2E...]
    ppermute x5, starting transfers between devices: 11.2 us -> 9.59 us  [swapped(): lax.ppermute(value, axis, [(source, source ^ bit) for source in range(cou...]
    ppermute x5, waiting for transfers between devices: 1.54 us -> 0.01 us  [swapped(): lax.ppermute(value, axis, [(source, source ^ bit) for source in range(cou...]
  transfers between devices with their start and end apart: 14 -> 14, of which waited for: 4 -> 5; matrix products, arithmetic and copies ran while one was open for 8% -> 2% of each run, Pallas kernels for 29% -> 29%
where the time goes in v1:
time: 142 us; the launch traced here: 141 us
  starting transfers between devices  65.9 us (46%)
  Pallas kernels  45.5 us (32%)
  waiting for transfers between devices  24.1 us (17%)
  local copies, waits for them, and re-layouts  3.23 us (2%)
  other arithmetic  2.33 us (2%)
    all_to_all x1, starting transfers between devices, per_device(): lax.all_to_all(by_head, 'ctx', 0, 0, axis_index_groups=groups, tiled=True)  25.8 us
    ppermute x6, starting transfers between devices, shifted(): lax.ppermute(value, axis, [(source, source + steps) for source in range(f...  19.2 us
    ppermute x6, waiting for transfers between devices, shifted(): lax.ppermute(value, axis, [(source, source + steps) for source in range(f...  18.2 us
    pallas_call x1, Pallas kernels, cross_attention(): pl.pallas_call(functools.partial(cross_kernel, HEAD_DIM ** (-0.5) * LOG2E...  17.4 us
    ppermute x5, starting transfers between devices, swapped(): lax.ppermute(value, axis, [(source, source ^ bit) for source in range(cou...  9.59 us
    pallas_call x1, Pallas kernels, self_attention(): pl.pallas_call(functools.partial(previous_kernel, scale), out_shape=jax.S...  7.34 us
    pallas_call x1, Pallas kernels, self_attention(): pl.pallas_call(functools.partial(own_kernel, scale), out_shape=(jax.Shape...  7.22 us
    all_to_all x1, waiting for transfers between devices, self_attention(): lax.all_to_all(packed(queries), 'ctx', 0, 0, axis_index_groups=groups, ti...  5.93 us
  transfers between devices with their start and end apart: 14, of which 5 were waited for; matrix products, arithmetic and copies ran while one was open for 2% of the time, Pallas kernels for 29%

profile of v1, /device:TPU:23, one launch (start us, length us, event | category | flops | bytes accessed | tf_op | source)
XLA Modules:
  0.0 141.3 jit_solution(1598448681559985876)
XLA Ops:
  0.0 0.0 copy-start.9
  0.0 0.0 copy-start.11
  0.0 2.0 %pack.2 = bf16[16,128,128]{2,1,0:T(8,128)(2,1)} custom-call(bf16[128,2048]{1,0:T(8,128)(2,1)} %refs_0_.4), custom_call_target="tpu_custom_call" | custom-call | bytes 1048576 | tf_op jit(solution)/shard_map/pack/pallas_call | solution.py:43
  2.0 5.5 %all-to-all-start = ((bf16[16,128,128]{2,1,0:T(8,128)(2,1)}), bf16[16,128,128]{2,1,0:T(8,128)(2,1)S(1)}, u32[]{:S(2)}, u32[]{:S(2)}) async-start(bf16[16,128,128]{2,1,0:T(8,128)(2,1)} %pack.2), calls=%async_computation | async-start | bytes 1048576 | tf_op jit(solution)/shard_map/all_to_all | solution.py:210
  7.5 2.4 %pack.3 = bf16[16,256,128]{2,1,0:T(8,128)(2,1)} custom-call(bf16[128,2048]{1,0:T(8,128)(2,1)} %refs_0_.5, bf16[128,2048]{1,0:T(8,128)(2,1)} %refs_1_.1), custom_call_target="tpu_custom_call" | custom-call | bytes 2097152 | tf_op jit(solution)/shard_map/pack/pallas_call | solution.py:43
  9.8 5.9 %all-to-all-done.q_ref = bf16[16,128,128]{2,1,0:T(8,128)(2,1)S(1)} async-done(((bf16[16,128,128]{2,1,0:T(8,128)(2,1)}), bf16[16,128,128]{2,1,0:T(8,128)(2,1)S(1)}, u32[]{:S(2)}, u32[]{:S(2)}) %all-to-all-start) | async-done | bytes 524320 | tf_op jit(solution)/shard_map/all_to_all | solution.py:210
  15.8 0.0 copy-start.1
  15.8 5.8 %all-to-all-start.1 = ((bf16[16,256,128]{2,1,0:T(8,128)(2,1)}), bf16[16,256,128]{2,1,0:T(8,128)(2,1)S(1)}, u32[]{:S(2)}, u32[]{:S(2)}) async-start(bf16[16,256,128]{2,1,0:T(8,128)(2,1)} %pack.3), calls=%async_computation.1 | async-start | bytes 2097152 | tf_op jit(solution)/shard_map/all_to_all | solution.py:207
  21.6 3.1 %collective-permute-start.4 = (bf16[128,896]{1,0:T(8,128)(2,1)}, bf16[128,896]{1,0:T(8,128)(2,1)S(1)}, u32[]{:S(2)}, u32[]{:S(2)}) collective-permute-start(bf16[128,896]{1,0:T(8,128)(2,1)} %refs_0_.7), channel_id=1, source_target_pairs={{0,8},{1,9},{2,10},{3,11},{4,12},{5,13},{6,14},{7,15},{8,16},{9,17... | collective-permute-start | bytes 688136 | tf_op jit(solution)/shard_map/ppermute | solution.py:24
  24.7 13.3 %collective-permute-done.4.refs_1_ = bf16[128,896]{1,0:T(8,128)(2,1)S(1)} collective-permute-done((bf16[128,896]{1,0:T(8,128)(2,1)}, bf16[128,896]{1,0:T(8,128)(2,1)S(1)}, u32[]{:S(2)}, u32[]{:S(2)}) %collective-permute-start.4) | collective-permute-done | bytes 229408 | tf_op jit(solution)/shard_map/ppermute | solution.py:24
  38.0 0.0 copy-start.3
  38.0 4.0 %collective-permute-start.5 = (bf16[128,896]{1,0:T(8,128)(2,1)S(1)}, bf16[128,896]{1,0:T(8,128)(2,1)S(1)}, u32[]{:S(2)}, u32[]{:S(2)}) collective-permute-start(bf16[128,896]{1,0:T(8,128)(2,1)S(1)} %collective-permute-done.4.refs_1_), channel_id=1, source_target_pairs={{0,8},{1,9},{2,10},{3,11},{4,12},{5,13},{6,14},{7,15},{8,16},{9,17... | collective-permute-start | bytes 688136 | tf_op jit(solution)/shard_map/ppermute | solution.py:24
  42.0 4.1 %collective-permute-done.5.refs_2_ = bf16[128,896]{1,0:T(8,128)(2,1)S(1)} collective-permute-done((bf16[128,896]{1,0:T(8,128)(2,1)S(1)}, bf16[128,896]{1,0:T(8,128)(2,1)S(1)}, u32[]{:S(2)}, u32[]{:S(2)}) %collective-permute-start.5) | collective-permute-done | bytes 229408 | tf_op jit(solution)/shard_map/ppermute | solution.py:24
  46.0 0.0 copy-start.4
  46.0 1.1 broadcast_select_fusion
  47.1 1.2 pad_maximum_fusion
  48.3 0.3 collective-permute-start.6
  48.6 0.6 collective-permute-start.7
  49.2 1.8 %collective-permute-start.8 = (bf16[256,896]{1,0:T(8,128)(2,1)}, bf16[256,896]{1,0:T(8,128)(2,1)}, u32[]{:S(2)}, u32[]{:S(2)}) collective-permute-start(bf16[256,896]{1,0:T(8,128)(2,1)} %get-tuple-element.12), channel_id=1, source_target_pairs={{0,6},{1,7},{2,4},{3,5},{4,2},{5,3},{6,0},{7,1},{8,14},{9,15},{10,... | collective-permute-start | bytes 1376264 | tf_op jit(solution)/shard_map/ppermute | solution.py:29
  50.9 0.7 slice.17
  51.7 2.5 %collective-permute-start.1 = (bf16[8,128,128]{2,1,0:T(8,128)(2,1)}, bf16[8,128,128]{2,1,0:T(8,128)(2,1)}, u32[]{:S(2)}, u32[]{:S(2)}) collective-permute-start(bf16[8,128,128]{2,1,0:T(8,128)(2,1)} %slice.17), channel_id=1, source_target_pairs={{16,0},{17,1},{18,2},{19,3},{20,4},{21,5},{22,6},{23,7},{24,8},{25... | collective-permute-start | bytes 786440 | tf_op jit(solution)/shard_map/ppermute | solution.py:24
  54.2 0.0 copy-done.9
  54.2 0.0 copy-done.11
  54.2 0.1 multiply_add_fusion
  54.3 7.0 %collective-permute-start.3 = (s32[2,2]{1,0:T(2,128)S(1)}, s32[2,2]{1,0:T(2,128)S(1)}, u32[]{:S(2)}, u32[]{:S(2)}) collective-permute-start(s32[2,2]{1,0:T(2,128)S(1)} %multiply_add_fusion), channel_id=1, source_target_pairs={{0,1},{1,2},{2,3},{3,4},{4,5},{5,6},{6,7},{7,8},{8,9},{9,10},{10,1... | collective-permute-start | bytes 56 | tf_op jit(solution)/shard_map/ppermute | solution.py:24
  61.3 0.0 all-to-all-done.1.kv_ref
  61.3 0.0 copy-start
  61.4 0.6 collective-permute-done.3
  62.0 1.3 collective-permute-start
  63.3 0.0 copy-start.10
  63.3 0.2 collective-permute-done.1.q_ref
  63.6 6.9 %collective-permute-start.9 = (s32[2,2]{1,0:T(2,128)S(1)}, s32[2,2]{1,0:T(2,128)S(1)}, u32[]{:S(2)}, u32[]{:S(2)}) collective-permute-start(s32[2,2]{1,0:T(2,128)S(1)} %pad_add_fusion.table_ref), channel_id=1, source_target_pairs={{0,1},{1,0},{2,3},{3,2},{4,5},{5,4},{6,7},{7,6},{8,9},{9,8},{10,11... | collective-permute-start | bytes 56 | tf_op jit(solution)/shard_map/ppermute | solution.py:29
  70.4 0.0 copy-done
  70.4 3.9 %later.1 = bf16[9,128,128]{2,1,0:T(8,128)(2,1)} custom-call(bf16[8,128,128]{2,1,0:T(8,128)(2,1)} %collective-permute-done.1.q_ref, bf16[16,256,128]{2,1,0:T(8,128)(2,1)} %copy-done), custom_call_target="tpu_custom_call" | custom-call | flops 268435456 | bytes 262144 | tf_op jit(solution)/shard_map/later/pallas_call | solution.py:224
  74.4 0.0 collective-permute-done.9.theirs_ref
  74.4 0.0 copy-start.8
  74.4 1.3 collective-permute-start.2
  75.6 0.0 collective-permute-done.6.refs_3_
  75.7 0.0 copy-start.6
  75.7 0.0 collective-permute-done.7.refs_4_
  75.7 0.0 collective-permute-done.8.refs_5_
  75.7 0.0 copy-done.3
  75.7 0.0 copy-done.4
  75.7 0.0 copy-done.8
  75.7 0.7 copy-done.6
  76.5 2.9 %gather.1 = bf16[512,896]{1,0:T(8,128)(2,1)} custom-call(s32[1]{0:T(128)} %bitcast.1.position_ref, s32[2,2]{1,0:T(2,128)} %copy-done.8, bf16[128,896]{1,0:T(8,128)(2,1)} %refs_0_.7, bf16[128,896]{1,0:T(8,128)(2,1)} %copy-done.3, bf16[128,896]{1,0:T(8,128)(2,1)} %copy-done.4, bf16[256,896]{1,0:T(8,128)(2,1)} %copy-done.6, ...), custom_call_target="tpu_custom_call" | custom-call | bytes 3670016 | tf_op jit(solution)/shard_map/gather/pallas_call | solution.py:382
  79.4 0.1 collective-permute-start.10
  79.5 0.0 copy-done.1
  79.5 7.2 %own.1 = (f32[16,128,128]{2,1,0:T(8,128)}, f32[16,128,128]{2,1,0:T(8,128)}) custom-call(bf16[16,128,128]{2,1,0:T(8,128)(2,1)} %copy-done.1, bf16[16,256,128]{2,1,0:T(8,128)(2,1)} %copy-done), custom_call_target="tpu_custom_call" | custom-call | flops 1073741824 | bytes 1572864 | tf_op jit(solution)/shard_map/own/pallas_call | solution.py:215
  86.7 0.0 collective-permute-done.2.back_ref
  86.7 0.0 copy-start.7
  86.7 0.0 collective-permute-done.kv_ref
  86.7 0.0 copy-start.5
  86.7 0.7 copy-done.7
  87.4 0.2 copy-done.5
  87.6 7.3 %previous.1 = bf16[16,128,128]{2,1,0:T(8,128)(2,1)} custom-call(s32[1]{0:T(128)} %bitcast.flag_ref, bf16[16,128,128]{2,1,0:T(8,128)(2,1)} %copy-done.1, bf16[8,256,128]{2,1,0:T(8,128)(2,1)} %copy-done.5, bf16[9,128,128]{2,1,0:T(8,128)(2,1)} %copy-done.7, f32[16,128,128]{2,1,0:T(8,128)} %get-tuple-element.7.out1_ref, f32[16,128,128]{2,1,0:T(8,128)} %get-tuple-element.8.stat_ref), custom_call_target="tpu_custom_call" | custom-call | flops 805306368 | bytes 2621440 | tf_op jit(solution)/shard_map/previous/pallas_call | solution.py:232
  95.0 25.8 %all-to-all-start.2 = ((bf16[16,128,128]{2,1,0:T(8,128)(2,1)}), bf16[16,128,128]{2,1,0:T(8,128)(2,1)S(1)}, u32[]{:S(2)}, u32[]{:S(2)}) async-start(bf16[16,128,128]{2,1,0:T(8,128)(2,1)} %previous.1), calls=%async_computation.2 | async-start | bytes 1048576 | tf_op jit(solution)/shard_map/all_to_all | solution.py:436
  120.7 0.0 collective-permute-done.10.refs_6_
  120.7 0.0 copy-done.10
  120.8 17.4 %cross.1.cross_ref = f32[128,2048]{1,0:T(8,128)} custom-call(s32[1]{0:T(128)} %bitcast.1.position_ref, s32[2,2]{1,0:T(2,128)} %copy-done.10, bf16[128,896]{1,0:T(8,128)(2,1)} %refs_0_.7, bf16[128,896]{1,0:T(8,128)(2,1)} %copy-done.3, bf16[128,896]{1,0:T(8,128)(2,1)} %copy-done.4, bf16[256,896]{1,0:T(8,128)(2,1)} %copy-done.6, ...), custom_call_target="tpu_custom_call" | custom-call | flops 3758096384 | bytes 9175040 | tf_op jit(solution)/shard_map/cross/pallas_call | solution.py:402
  138.2 0.0 all-to-all-done.2.self_ref
  138.2 0.0 copy-start.2
  138.2 0.8 copy-done.2
  139.0 2.3 %total.1 = bf16[128,2048]{1,0:T(8,128)(2,1)} custom-call(bf16[16,128,128]{2,1,0:T(8,128)(2,1)} %copy-done.2, f32[128,2048]{1,0:T(8,128)} %cross.1.cross_ref), custom_call_target="tpu_custom_call" | custom-call | tf_op jit(solution)/shard_map/total/pallas_call | solution.py:437
  (4 shorter events, 0.1 us)
Async XLA Ops:
  0.0 54.2 %copy-start.9 = (s32[2,2]{1,0:T(2,128)S(1)}, s32[2,2]{1,0:T(2,128)}, u32[]{:S(2)}) copy-start(s32[2,2]{1,0:T(2,128)} %param.15) | copy-start | bytes 52
  0.0 54.2 %copy-start.11 = (s32[2]{0:T(128)S(1)}, s32[2]{0:T(128)}, u32[]{:S(2)}) copy-start(s32[2]{0:T(128)} %param.14) | copy-start | bytes 28
  2.0 13.8 %all-to-all-start = ((bf16[16,128,128]{2,1,0:T(8,128)(2,1)}), bf16[16,128,128]{2,1,0:T(8,128)(2,1)S(1)}, u32[]{:S(2)}, u32[]{:S(2)}) async-start(bf16[16,128,128]{2,1,0:T(8,128)(2,1)} %pack.2), calls=%async_computation | async-start | bytes 1048576 | tf_op jit(solution)/shard_map/all_to_all | solution.py:210
  15.8 63.7 %copy-start.1 = (bf16[16,128,128]{2,1,0:T(8,128)(2,1)}, bf16[16,128,128]{2,1,0:T(8,128)(2,1)S(1)}, u32[]{:S(2)}) copy-start(bf16[16,128,128]{2,1,0:T(8,128)(2,1)S(1)} %all-to-all-done.q_ref) | copy-start | bytes 1572868
  15.8 45.5 %all-to-all-start.1 = ((bf16[16,256,128]{2,1,0:T(8,128)(2,1)}), bf16[16,256,128]{2,1,0:T(8,128)(2,1)S(1)}, u32[]{:S(2)}, u32[]{:S(2)}) async-start(bf16[16,256,128]{2,1,0:T(8,128)(2,1)} %pack.3), calls=%async_computation.1 | async-start | bytes 2097152 | tf_op jit(solution)/shard_map/all_to_all | solution.py:207
  21.6 16.4 %collective-permute-start.4 = (bf16[128,896]{1,0:T(8,128)(2,1)}, bf16[128,896]{1,0:T(8,128)(2,1)S(1)}, u32[]{:S(2)}, u32[]{:S(2)}) collective-permute-start(bf16[128,896]{1,0:T(8,128)(2,1)} %refs_0_.7), channel_id=1, source_target_pairs={{0,8},{1,9},{2,10},{3,11},{4,12},{5,13},{6,14},{7,15},{8,16},{9,17... | collective-permute-start | bytes 688136 | tf_op jit(solution)/shard_map/ppermute | solution.py:24
  38.0 37.7 %copy-start.3 = (bf16[128,896]{1,0:T(8,128)(2,1)}, bf16[128,896]{1,0:T(8,128)(2,1)S(1)}, u32[]{:S(2)}) copy-start(bf16[128,896]{1,0:T(8,128)(2,1)S(1)} %collective-permute-done.4.refs_1_) | copy-start | bytes 688132
  38.0 8.1 %collective-permute-start.5 = (bf16[128,896]{1,0:T(8,128)(2,1)S(1)}, bf16[128,896]{1,0:T(8,128)(2,1)S(1)}, u32[]{:S(2)}, u32[]{:S(2)}) collective-permute-start(bf16[128,896]{1,0:T(8,128)(2,1)S(1)} %collective-permute-done.4.refs_1_), channel_id=1, source_target_pairs={{0,8},{1,9},{2,10},{3,11},{4,12},{5,13},{6,14},{7,15},{8,16},{9,17... | collective-permute-start | bytes 688136 | tf_op jit(solution)/shard_map/ppermute | solution.py:24
  46.0 29.7 %copy-start.4 = (bf16[128,896]{1,0:T(8,128)(2,1)}, bf16[128,896]{1,0:T(8,128)(2,1)S(1)}, u32[]{:S(2)}) copy-start(bf16[128,896]{1,0:T(8,128)(2,1)S(1)} %collective-permute-done.5.refs_2_) | copy-start | bytes 688132
  48.3 27.4 %collective-permute-start.6 = (bf16[256,896]{1,0:T(8,128)(2,1)}, bf16[256,896]{1,0:T(8,128)(2,1)S(1)}, u32[]{:S(2)}, u32[]{:S(2)}) collective-permute-start(bf16[256,896]{1,0:T(8,128)(2,1)} %get-tuple-element.14), channel_id=1, source_target_pairs={{0,2},{1,3},{2,0},{3,1},{4,6},{5,7},{6,4},{7,5},{8,10},{9,11},{10,... | collective-permute-start | bytes 1376264 | tf_op jit(solution)/shard_map/ppermute | solution.py:29
  48.6 27.1 %collective-permute-start.7 = (bf16[256,896]{1,0:T(8,128)(2,1)}, bf16[256,896]{1,0:T(8,128)(2,1)}, u32[]{:S(2)}, u32[]{:S(2)}) collective-permute-start(bf16[256,896]{1,0:T(8,128)(2,1)} %get-tuple-element.13), channel_id=1, source_target_pairs={{0,4},{1,5},{2,6},{3,7},{4,0},{5,1},{6,2},{7,3},{8,12},{9,13},{10,... | collective-permute-start | bytes 1376264 | tf_op jit(solution)/shard_map/ppermute | solution.py:29
  49.2 26.5 %collective-permute-start.8 = (bf16[256,896]{1,0:T(8,128)(2,1)}, bf16[256,896]{1,0:T(8,128)(2,1)}, u32[]{:S(2)}, u32[]{:S(2)}) collective-permute-start(bf16[256,896]{1,0:T(8,128)(2,1)} %get-tuple-element.12), channel_id=1, source_target_pairs={{0,6},{1,7},{2,4},{3,5},{4,2},{5,3},{6,0},{7,1},{8,14},{9,15},{10,... | collective-permute-start | bytes 1376264 | tf_op jit(solution)/shard_map/ppermute | solution.py:29
  51.7 11.9 %collective-permute-start.1 = (bf16[8,128,128]{2,1,0:T(8,128)(2,1)}, bf16[8,128,128]{2,1,0:T(8,128)(2,1)}, u32[]{:S(2)}, u32[]{:S(2)}) collective-permute-start(bf16[8,128,128]{2,1,0:T(8,128)(2,1)} %slice.17), channel_id=1, source_target_pairs={{16,0},{17,1},{18,2},{19,3},{20,4},{21,5},{22,6},{23,7},{24,8},{25... | collective-permute-start | bytes 786440 | tf_op jit(solution)/shard_map/ppermute | solution.py:24
  54.3 7.7 %collective-permute-start.3 = (s32[2,2]{1,0:T(2,128)S(1)}, s32[2,2]{1,0:T(2,128)S(1)}, u32[]{:S(2)}, u32[]{:S(2)}) collective-permute-start(s32[2,2]{1,0:T(2,128)S(1)} %multiply_add_fusion), channel_id=1, source_target_pairs={{0,1},{1,2},{2,3},{3,4},{4,5},{5,6},{6,7},{7,8},{8,9},{9,10},{10,1... | collective-permute-start | bytes 56 | tf_op jit(solution)/shard_map/ppermute | solution.py:24
  61.3 9.1 %copy-start = (bf16[16,256,128]{2,1,0:T(8,128)(2,1)}, bf16[16,256,128]{2,1,0:T(8,128)(2,1)S(1)}, u32[]{:S(2)}) copy-start(bf16[16,256,128]{2,1,0:T(8,128)(2,1)S(1)} %all-to-all-done.1.kv_ref) | copy-start | bytes 3145732
  62.0 24.7 %collective-permute-start = (bf16[8,256,128]{2,1,0:T(8,128)(2,1)S(1)}, bf16[8,256,128]{2,1,0:T(8,128)(2,1)S(1)}, u32[]{:S(2)}, u32[]{:S(2)}) collective-permute-start(bf16[8,256,128]{2,1,0:T(8,128)(2,1)S(1)} %slice.16), channel_id=1, source_target_pairs={{0,16},{1,17},{2,18},{3,19},{4,20},{5,21},{6,22},{7,23},{8,24},{9,... | collective-permute-start | bytes 1572872 | tf_op jit(solution)/shard_map/ppermute | solution.py:24
  63.3 57.4 %copy-start.10 = (s32[2,2]{1,0:T(2,128)}, s32[2,2]{1,0:T(2,128)S(1)}, u32[]{:S(2)}) copy-start(s32[2,2]{1,0:T(2,128)S(1)} %pad_add_fusion.table_ref) | copy-start | bytes 52
  63.6 10.8 %collective-permute-start.9 = (s32[2,2]{1,0:T(2,128)S(1)}, s32[2,2]{1,0:T(2,128)S(1)}, u32[]{:S(2)}, u32[]{:S(2)}) collective-permute-start(s32[2,2]{1,0:T(2,128)S(1)} %pad_add_fusion.table_ref), channel_id=1, source_target_pairs={{0,1},{1,0},{2,3},{3,2},{4,5},{5,4},{6,7},{7,6},{8,9},{9,8},{10,11... | collective-permute-start | bytes 56 | tf_op jit(solution)/shard_map/ppermute | solution.py:29
  74.4 1.4 copy-start.8
  74.4 12.4 %collective-permute-start.2 = (bf16[9,128,128]{2,1,0:T(8,128)(2,1)}, bf16[9,128,128]{2,1,0:T(8,128)(2,1)S(1)}, u32[]{:S(2)}, u32[]{:S(2)}) collective-permute-start(bf16[9,128,128]{2,1,0:T(8,128)(2,1)} %later.1), channel_id=1, source_target_pairs={{0,16},{1,17},{2,18},{3,19},{4,20},{5,21},{6,22},{7,23},{8,24},{9,... | collective-permute-start | bytes 884744 | tf_op jit(solution)/shard_map/ppermute | solution.py:24
  75.7 0.8 copy-start.6
  79.4 41.3 %collective-permute-start.10 = (bf16[512,896]{1,0:T(8,128)(2,1)}, bf16[512,896]{1,0:T(8,128)(2,1)}, u32[]{:S(2)}, u32[]{:S(2)}) collective-permute-start(bf16[512,896]{1,0:T(8,128)(2,1)} %gather.1), channel_id=1, source_target_pairs={{0,1},{1,0},{2,3},{3,2},{4,5},{5,4},{6,7},{7,6},{8,9},{9,8},{10,11... | collective-permute-start | bytes 2752520 | tf_op jit(solution)/shard_map/ppermute | solution.py:29
  86.7 0.7 copy-start.7
  86.7 0.9 copy-start.5
  95.0 43.2 %all-to-all-start.2 = ((bf16[16,128,128]{2,1,0:T(8,128)(2,1)}), bf16[16,128,128]{2,1,0:T(8,128)(2,1)S(1)}, u32[]{:S(2)}, u32[]{:S(2)}) async-start(bf16[16,128,128]{2,1,0:T(8,128)(2,1)} %previous.1), calls=%async_computation.2 | async-start | bytes 1048576 | tf_op jit(solution)/shard_map/all_to_all | solution.py:436
  138.2 0.8 copy-start.2

commit v2 on v1

--- a/solution.py
+++ b/solution.py
@@ -12,7 +12,7 @@
 HEAD_DIM = 128
 SPAN = 64
 PLANE = 8
-LEFT = 8
+LEFT = 12
 
 MASKED_SCORE = -1e30
 LOG2E = 1.4426950408889634
@@ -285,22 +285,37 @@
             pltpu.make_async_copy(in_refs[0].at[0:size, :], targets[n], sems.at[n]).wait()
 
 
-def cross_kernel(scale, span_count, position_ref, table_ref, *refs):
-    *in_refs, theirs_ref, q_ref, weight_ref, out_ref, rows_ref, weights_ref, sems, weight_sems = refs
+def absorb_kernel(q_ref, weight_ref, out_ref, weights_ref, sems):
     rows, width = q_ref.shape
+    span_count = out_ref.shape[0]
     span = rows // span_count
-    steps, _, _, block = weights_ref.shape
-    weight_copies = [
-        [
-            pltpu.make_async_copy(
-                weight_ref.at[:, n * width + g * block : n * width + (g + 1) * block],
-                weights_ref.at[g, n],
-                weight_sems.at[g, n],
-            )
-            for n in range(2)
-        ]
+    steps, _, block = weights_ref.shape
+    copies = [
+        pltpu.make_async_copy(
+            weight_ref.at[:, g * block : (g + 1) * block], weights_ref.at[g], sems.at[g]
+        )
         for g in range(steps)
     ]
+    for copy in copies:
+        copy.start()
+    for head in range(width // HEAD_DIM):
+        g, first = divmod(head * HEAD_DIM, block)
+        if first == 0:
+            copies[g].wait()
+        lanes = slice(head * HEAD_DIM, (head + 1) * HEAD_DIM)
+        product = scores_of(q_ref[:, lanes], weights_ref[g, :, first : first + HEAD_DIM])
+        product = product.astype(out_ref.dtype)
+        for c in range(span_count):
+            out_ref[c, head * span : (head + 1) * span, :] = product[c * span : (c + 1) * span]
+
+
+def cross_kernel(scale, position_ref, table_ref, *refs):
+    *in_refs, theirs_ref, asks_ref, weight_ref, out_ref = refs[:-6]
+    rows_ref, all_asks_ref, weights_ref, sems, ask_sems, weight_sems = refs[-6:]
+    rows, width = out_ref.shape
+    steps, span_count, asked, _ = all_asks_ref.shape
+    span = rows // span_count
+    block = weights_ref.shape[2]
     pieces = wanted_pieces(table_ref, position_ref[0], span_count)
     targets = [rows_ref.at[n * span : (n + 1) * span, :] for n in range(len(pieces))]
     held = sum(ref.shape[0] for ref in in_refs) // rows
@@ -312,48 +327,47 @@
             source = theirs_ref.at[n * span : (n + 1) * span, :]
             pltpu.make_async_copy(source, targets[n], sems.at[n]).start()
 
+    ask_copies = [
+        pltpu.make_async_copy(
+            asks_ref.at[:, g * asked : (g + 1) * asked, :], all_asks_ref.at[g], ask_sems.at[g]
+        )
+        for g in range(steps)
+    ]
+    weight_copies = [
+        pltpu.make_async_copy(
+            weight_ref.at[:, width + g * block : width + (g + 1) * block],
+            weights_ref.at[g],
+            weight_sems.at[g],
+        )
+        for g in range(steps)
+    ]
     for g in range(steps):
-        for copy in weight_copies[g]:
-            copy.start()
+        ask_copies[g].start()
+        weight_copies[g].start()
     for n in range(len(pieces)):
         pltpu.make_async_copy(theirs_ref.at[0:span, :], targets[n], sems.at[n]).wait()
 
     keys_of_span = rows_ref.shape[0] // span_count
-    slot = lax.broadcasted_iota(jnp.int32, (span, keys_of_span), 1) // (2 * span)
+    slot = lax.broadcasted_iota(jnp.int32, (asked, keys_of_span), 1) // (2 * span)
     counts = [table_ref[c, 0] % 4 for c in range(span_count)]
-    valid = [slot < count for count in counts]
-    none = [jnp.where(count > 0, 0.0, 1.0) for count in counts]
-
-    def attend(g, keys, values):
+    for g in range(steps):
+        ask_copies[g].wait()
+        means = []
+        for c in range(span_count):
+            keys = rows_ref[c * keys_of_span : (c + 1) * keys_of_span, :]
+            s = jnp.where(slot < counts[c], scores_of(all_asks_ref[g, c], keys), MASKED_SCORE)
+            p = jnp.exp2((s - jnp.max(s, axis=1, keepdims=True)) * scale)
+            inverse = jnp.where(counts[c] > 0, 1.0 / jnp.sum(p, axis=1, keepdims=True), 0.0)
+            mean = jnp.dot(p.astype(jnp.bfloat16), keys, preferred_element_type=jnp.float32)
+            means.append((mean * inverse).astype(jnp.bfloat16))
+        weight_copies[g].wait()
         for h in range(block // HEAD_DIM):
+            mean = jnp.concatenate([m[h * span : (h + 1) * span] for m in means], axis=0)
             inner = slice(h * HEAD_DIM, (h + 1) * HEAD_DIM)
             lanes = slice(g * block + h * HEAD_DIM, g * block + (h + 1) * HEAD_DIM)
-            for c in range(span_count):
-                here = slice(c * keys_of_span, (c + 1) * keys_of_span)
-                mine = slice(c * span, (c + 1) * span)
-                s = jnp.where(valid[c], scores_of(q_ref[mine, lanes], keys[here, inner]), MASKED_SCORE)
-                largest = jnp.max(s, axis=1, keepdims=True)
-                p = jnp.where(valid[c], jnp.exp2((s - largest) * scale), 0.0)
-                total = jnp.sum(p, axis=1, keepdims=True) + none[c]
-                o = jnp.dot(
-                    p.astype(jnp.bfloat16), values[here, inner], preferred_element_type=jnp.float32
-                )
-                out_ref[mine, lanes] = o * (1.0 / total)
-
-    waiting = None
-    for g in range(steps):
-        for copy in weight_copies[g]:
-            copy.wait()
-        projected = [
-            jnp.dot(
-                rows_ref[...], weights_ref[g, n], preferred_element_type=jnp.float32
-            ).astype(jnp.bfloat16)
-            for n in range(2)
-        ]
-        if waiting is not None:
-            attend(*waiting)
-        waiting = (g, *projected)
-    attend(*waiting)
+            out_ref[:, lanes] = jnp.dot(
+                mean, weights_ref[g, :, inner], preferred_element_type=jnp.float32
+            )
 
 
 def cross_attention(cross_queries, encoded, weight, counts, sources, position):
@@ -392,27 +406,46 @@
     )(where, their_table, *held)
     theirs = swapped(theirs, "ctx", 1)
 
+    heads = width // HEAD_DIM
     block = 4 * HEAD_DIM
     steps = width // block
+    asks = pl.pallas_call(
+        absorb_kernel,
+        out_shape=jax.ShapeDtypeStruct((span_count, heads * SPAN, depth), jnp.bfloat16),
+        in_specs=[vmem, anywhere],
+        out_specs=vmem,
+        scratch_shapes=[
+            pltpu.VMEM((steps, depth, block), weight.dtype),
+            pltpu.SemaphoreType.DMA((steps,)),
+        ],
+        cost_estimate=pl.CostEstimate(
+            flops=2 * rows * depth * width, bytes_accessed=2 * weight.size, transcendentals=0
+        ),
+        name="absorb",
+    )(cross_queries, weight)
+    block = 8 * HEAD_DIM
+    steps = width // block
     cost = pl.CostEstimate(
-        flops=2 * picked * depth * 2 * width,
-        bytes_accessed=weight.size * 2 + picked * depth * 4,
-        transcendentals=picked * SPAN * HEADS,
+        flops=4 * picked * depth * heads * SPAN + 2 * rows * depth * width,
+        bytes_accessed=weight.size + asks.size * 2 + picked * depth * 4,
+        transcendentals=picked * SPAN * heads,
     )
     return pl.pallas_call(
-        functools.partial(cross_kernel, HEAD_DIM ** (-0.5) * LOG2E, span_count),
+        functools.partial(cross_kernel, HEAD_DIM ** (-0.5) * LOG2E),
         out_shape=jax.ShapeDtypeStruct((rows, width), jnp.float32),
-        in_specs=[smem] * 2 + [anywhere] * (len(held) + 1) + [vmem, anywhere],
+        in_specs=[smem] * 2 + [anywhere] * (len(held) + 3),
         out_specs=vmem,
         scratch_shapes=[
             pltpu.VMEM((picked, depth), encoded.dtype),
-            pltpu.VMEM((steps, 2, depth, block), weight.dtype),
+            pltpu.VMEM((steps, span_count, heads * SPAN // steps, depth), asks.dtype),
+            pltpu.VMEM((steps, depth, block), weight.dtype),
             pltpu.SemaphoreType.DMA((pieces,)),
-            pltpu.SemaphoreType.DMA((steps, 2)),
+            pltpu.SemaphoreType.DMA((steps,)),
+            pltpu.SemaphoreType.DMA((steps,)),
         ],
         cost_estimate=cost,
         name="cross",
-    )(where, table, *held, theirs, cross_queries, weight)
+    )(where, table, *held, theirs, asks, weight)
 
 
 def sum_kernel(self_ref, cross_ref, out_ref):

time: 142 us -> 128 us (0.901)
  starting transfers between devices: 65.9 us -> 39.9 us
  waiting for transfers between devices: 24.1 us -> 33.6 us
  local copies, waits for them, and re-layouts: 3.23 us -> 5.6 us
    all_to_all x1, starting transfers between devices: 25.8 us -> 8.98 us  [per_device(): lax.all_to_all(by_head, 'ctx', 0, 0, axis_index_groups=groups, tiled=True)]
    ppermute x6, waiting for transfers between devices: 18.2 us -> 27.6 us  [shifted(): lax.ppermute(value, axis, [(source, source + steps) for source in range(f...]
    pallas_call x1, Pallas kernels: 17.4 us -> 10.5 us  [cross_attention(): pl.pallas_call(functools.partial(cross_kernel, HEAD_DIM ** (-0.5) * LOG2E...]
    pallas_call x0 -> x1, Pallas kernels: none -> 5.82 us  [cross_attention(): pl.pallas_call(absorb_kernel, out_shape=jax.ShapeDtypeStruct((span_count,...]
    ppermute x6, starting transfers between devices: 19.2 us -> 14.3 us  [shifted(): lax.ppermute(value, axis, [(source, source + steps) for source in range(f...]
    ppermute x5, starting transfers between devices: 9.59 us -> 5.23 us  [swapped(): lax.ppermute(value, axis, [(source, source ^ bit) for source in range(cou...]
    unnamed x24 -> x30, local copies, waits for them, and re-layouts: 2.45 us -> 4.6 us
  transfers between devices with their start and end apart: 14 -> 14, of which waited for: 5 -> 6; matrix products, arithmetic and copies ran while one was open for 2% -> 3% of each run, Pallas kernels for 29% -> 32%
where the time goes in v2:
time: 128 us; the launch traced here: 127 us
  Pallas kernels  45.5 us (36%)
  starting transfers between devices  39.9 us (31%)
  waiting for transfers between devices  33.6 us (26%)
  local copies, waits for them, and re-layouts  5.6 us (4%)
  other arithmetic  2.34 us (2%)
    ppermute x6, waiting for transfers between devices, shifted(): lax.ppermute(value, axis, [(source, source + steps) for source in range(f...  27.6 us
    ppermute x6, starting transfers between devices, shifted(): lax.ppermute(value, axis, [(source, source + steps) for source in range(f...  14.3 us
    pallas_call x1, Pallas kernels, cross_attention(): pl.pallas_call(functools.partial(cross_kernel, HEAD_DIM ** (-0.5) * LOG2E...  10.5 us
    all_to_all x1, starting transfers between devices, per_device(): lax.all_to_all(by_head, 'ctx', 0, 0, axis_index_groups=groups, tiled=True)  8.98 us
    pallas_call x1, Pallas kernels, self_attention(): pl.pallas_call(functools.partial(own_kernel, scale), out_shape=(jax.Shape...  7.18 us
    pallas_call x1, Pallas kernels, self_attention(): pl.pallas_call(functools.partial(previous_kernel, scale), out_shape=jax.S...  7.16 us
    all_to_all x1, waiting for transfers between devices, self_attention(): lax.all_to_all(packed(queries), 'ctx', 0, 0, axis_index_groups=groups, ti...  5.94 us
    pallas_call x1, Pallas kernels, cross_attention(): pl.pallas_call(absorb_kernel, out_shape=jax.ShapeDtypeStruct((span_count,...  5.82 us
  transfers between devices with their start and end apart: 14, of which 6 were waited for; matrix products, arithmetic and copies ran while one was open for 3% of the time, Pallas kernels for 32%

profile of v2, /device:TPU:23, one launch (start us, length us, event | category | flops | bytes accessed | tf_op | source)
XLA Modules:
  0.0 127.2 jit_solution(2947868010954475422)
XLA Ops:
  0.0 0.0 copy-start.14
  0.0 0.0 copy-start.13
  0.0 2.0 %pack.2 = bf16[16,128,128]{2,1,0:T(8,128)(2,1)} custom-call(bf16[128,2048]{1,0:T(8,128)(2,1)} %refs_0_.4), custom_call_target="tpu_custom_call" | custom-call | bytes 1048576 | tf_op jit(solution)/shard_map/pack/pallas_call | solution.py:43
  2.0 5.5 %all-to-all-start = ((bf16[16,128,128]{2,1,0:T(8,128)(2,1)}), bf16[16,128,128]{2,1,0:T(8,128)(2,1)S(1)}, u32[]{:S(2)}, u32[]{:S(2)}) async-start(bf16[16,128,128]{2,1,0:T(8,128)(2,1)} %pack.2), calls=%async_computation | async-start | bytes 1048576 | tf_op jit(solution)/shard_map/all_to_all | solution.py:210
  7.5 2.4 %pack.3 = bf16[16,256,128]{2,1,0:T(8,128)(2,1)} custom-call(bf16[128,2048]{1,0:T(8,128)(2,1)} %refs_0_.5, bf16[128,2048]{1,0:T(8,128)(2,1)} %refs_1_.1), custom_call_target="tpu_custom_call" | custom-call | bytes 2097152 | tf_op jit(solution)/shard_map/pack/pallas_call | solution.py:43
  9.8 5.9 %all-to-all-done.q_ref = bf16[16,128,128]{2,1,0:T(8,128)(2,1)S(1)} async-done(((bf16[16,128,128]{2,1,0:T(8,128)(2,1)}), bf16[16,128,128]{2,1,0:T(8,128)(2,1)S(1)}, u32[]{:S(2)}, u32[]{:S(2)}) %all-to-all-start) | async-done | bytes 524320 | tf_op jit(solution)/shard_map/all_to_all | solution.py:210
  15.8 5.8 %all-to-all-start.1 = ((bf16[16,256,128]{2,1,0:T(8,128)(2,1)}), bf16[16,256,128]{2,1,0:T(8,128)(2,1)S(1)}, u32[]{:S(2)}, u32[]{:S(2)}) async-start(bf16[16,256,128]{2,1,0:T(8,128)(2,1)} %pack.3), calls=%async_computation.1 | async-start | bytes 2097152 | tf_op jit(solution)/shard_map/all_to_all | solution.py:207
  21.6 3.1 %collective-permute-start.4 = (bf16[128,896]{1,0:T(8,128)(2,1)}, bf16[128,896]{1,0:T(8,128)(2,1)S(1)}, u32[]{:S(2)}, u32[]{:S(2)}) collective-permute-start(bf16[128,896]{1,0:T(8,128)(2,1)} %refs_0_.7), channel_id=1, source_target_pairs={{0,8},{1,9},{2,10},{3,11},{4,12},{5,13},{6,14},{7,15},{8,16},{9,17... | collective-permute-start | bytes 688136 | tf_op jit(solution)/shard_map/ppermute | solution.py:24
  24.7 13.3 %collective-permute-done.4.refs_1_ = bf16[128,896]{1,0:T(8,128)(2,1)S(1)} collective-permute-done((bf16[128,896]{1,0:T(8,128)(2,1)}, bf16[128,896]{1,0:T(8,128)(2,1)S(1)}, u32[]{:S(2)}, u32[]{:S(2)}) %collective-permute-start.4) | collective-permute-done | bytes 229408 | tf_op jit(solution)/shard_map/ppermute | solution.py:24
  38.0 4.0 %collective-permute-start.5 = (bf16[128,896]{1,0:T(8,128)(2,1)S(1)}, bf16[128,896]{1,0:T(8,128)(2,1)S(1)}, u32[]{:S(2)}, u32[]{:S(2)}) collective-permute-start(bf16[128,896]{1,0:T(8,128)(2,1)S(1)} %collective-permute-done.4.refs_1_), channel_id=1, source_target_pairs={{0,8},{1,9},{2,10},{3,11},{4,12},{5,13},{6,14},{7,15},{8,16},{9,17... | collective-permute-start | bytes 688136 | tf_op jit(solution)/shard_map/ppermute | solution.py:24
  42.0 2.7 %collective-permute-start.1 = (bf16[12,128,128]{2,1,0:T(8,128)(2,1)S(1)}, bf16[12,128,128]{2,1,0:T(8,128)(2,1)}, u32[]{:S(2)}, u32[]{:S(2)}) collective-permute-start(bf16[12,128,128]{2,1,0:T(8,128)(2,1)S(1)} %slice.17), channel_id=1, source_target_pairs={{16,0},{17,1},{18,2},{19,3},{20,4},{21,5},{22,6},{23,7},{24,8},{25... | collective-permute-start | bytes 1179656 | tf_op jit(solution)/shard_map/ppermute | solution.py:24
  44.8 1.3 %collective-permute-done.5.refs_2_ = bf16[128,896]{1,0:T(8,128)(2,1)S(1)} collective-permute-done((bf16[128,896]{1,0:T(8,128)(2,1)S(1)}, bf16[128,896]{1,0:T(8,128)(2,1)S(1)}, u32[]{:S(2)}, u32[]{:S(2)}) %collective-permute-start.5) | collective-permute-done | bytes 229408 | tf_op jit(solution)/shard_map/ppermute | solution.py:24
  46.0 1.1 broadcast_select_fusion
  47.1 1.2 pad_maximum_fusion
  48.3 0.3 collective-permute-start.6
  48.6 0.6 collective-permute-start.7
  49.2 1.8 %collective-permute-start.8 = (bf16[256,896]{1,0:T(8,128)(2,1)}, bf16[256,896]{1,0:T(8,128)(2,1)S(1)}, u32[]{:S(2)}, u32[]{:S(2)}) collective-permute-start(bf16[256,896]{1,0:T(8,128)(2,1)} %get-tuple-element.12), channel_id=1, source_target_pairs={{0,6},{1,7},{2,4},{3,5},{4,2},{5,3},{6,0},{7,1},{8,14},{9,15},{10,... | collective-permute-start | bytes 1376264 | tf_op jit(solution)/shard_map/ppermute | solution.py:29
  51.0 10.1 %collective-permute-done.1.q_ref = bf16[12,128,128]{2,1,0:T(8,128)(2,1)} collective-permute-done((bf16[12,128,128]{2,1,0:T(8,128)(2,1)S(1)}, bf16[12,128,128]{2,1,0:T(8,128)(2,1)}, u32[]{:S(2)}, u32[]{:S(2)}) %collective-permute-start.1) | collective-permute-done | bytes 393248 | tf_op jit(solution)/shard_map/ppermute | solution.py:24
  61.0 0.0 all-to-all-done.1.kv_ref
  61.0 1.0 copy-done.7
  62.0 5.3 %later.1 = bf16[13,128,128]{2,1,0:T(8,128)(2,1)} custom-call(bf16[12,128,128]{2,1,0:T(8,128)(2,1)} %collective-permute-done.1.q_ref, bf16[16,256,128]{2,1,0:T(8,128)(2,1)} %copy-done.7), custom_call_target="tpu_custom_call" | custom-call | flops 603979776 | bytes 393216 | tf_op jit(solution)/shard_map/later/pallas_call | solution.py:224
  67.3 1.3 %collective-permute-start.2 = (bf16[13,128,128]{2,1,0:T(8,128)(2,1)}, bf16[13,128,128]{2,1,0:T(8,128)(2,1)S(1)}, u32[]{:S(2)}, u32[]{:S(2)}) collective-permute-start(bf16[13,128,128]{2,1,0:T(8,128)(2,1)} %later.1), channel_id=1, source_target_pairs={{0,16},{1,17},{2,18},{3,19},{4,20},{5,21},{6,22},{7,23},{8,24},{9,... | collective-permute-start | bytes 1277960 | tf_op jit(solution)/shard_map/ppermute | solution.py:24
  68.6 0.0 copy-done.14
  68.6 0.0 copy-done.13
  68.6 0.1 multiply_add_fusion
  68.7 1.9 %collective-permute-start.3 = (s32[2,2]{1,0:T(2,128)S(1)}, s32[2,2]{1,0:T(2,128)S(1)}, u32[]{:S(2)}, u32[]{:S(2)}) collective-permute-start(s32[2,2]{1,0:T(2,128)S(1)} %multiply_add_fusion), channel_id=1, source_target_pairs={{0,1},{1,2},{2,3},{3,4},{4,5},{5,6},{6,7},{7,8},{8,9},{9,10},{10,1... | collective-permute-start | bytes 56 | tf_op jit(solution)/shard_map/ppermute | solution.py:24
  70.6 1.3 %collective-permute-done.3 = s32[2,2]{1,0:T(2,128)S(1)} collective-permute-done((s32[2,2]{1,0:T(2,128)S(1)}, s32[2,2]{1,0:T(2,128)S(1)}, u32[]{:S(2)}, u32[]{:S(2)}) %collective-permute-start.3) | collective-permute-done | bytes 48 | tf_op jit(solution)/shard_map/ppermute | solution.py:24
  72.0 2.4 %collective-permute-start.9 = (s32[2,2]{1,0:T(2,128)S(1)}, s32[2,2]{1,0:T(2,128)S(1)}, u32[]{:S(2)}, u32[]{:S(2)}) collective-permute-start(s32[2,2]{1,0:T(2,128)S(1)} %pad_add_fusion.table_ref), channel_id=1, source_target_pairs={{0,1},{1,0},{2,3},{3,2},{4,5},{5,4},{6,7},{7,6},{8,9},{9,8},{10,11... | collective-permute-start | bytes 56 | tf_op jit(solution)/shard_map/ppermute | solution.py:29
  74.4 1.0 slice.16
  75.3 0.0 collective-permute-done.9.theirs_ref
  75.4 0.0 copy-start.12
  75.4 1.3 %collective-permute-start = (bf16[4,256,128]{2,1,0:T(8,128)(2,1)S(1)}, bf16[4,256,128]{2,1,0:T(8,128)(2,1)S(1)}, u32[]{:S(2)}, u32[]{:S(2)}) collective-permute-start(bf16[4,256,128]{2,1,0:T(8,128)(2,1)S(1)} %slice.16), channel_id=1, source_target_pairs={{0,16},{1,17},{2,18},{3,19},{4,20},{5,21},{6,22},{7,23},{8,24},{9,... | collective-permute-start | bytes 786440 | tf_op jit(solution)/shard_map/ppermute | solution.py:24
  76.7 0.0 collective-permute-done.6.refs_3_
  76.7 0.0 copy-start.4
  76.7 0.0 collective-permute-done.7.refs_4_
  76.7 0.0 copy-start.5
  76.7 0.0 collective-permute-done.8.refs_5_
  76.7 0.0 copy-start.6
  76.7 0.0 copy-done.2
  76.7 0.0 copy-done.3
  76.7 0.0 copy-done.12
  76.8 0.7 copy-done.4
  77.4 0.2 copy-done.5
  77.6 0.1 copy-done.6
  77.8 2.9 %gather.1 = bf16[512,896]{1,0:T(8,128)(2,1)} custom-call(s32[1]{0:T(128)} %bitcast.1.position_ref, s32[2,2]{1,0:T(2,128)} %copy-done.12, bf16[128,896]{1,0:T(8,128)(2,1)} %refs_0_.7, bf16[128,896]{1,0:T(8,128)(2,1)} %copy-done.2, bf16[128,896]{1,0:T(8,128)(2,1)} %copy-done.3, bf16[256,896]{1,0:T(8,128)(2,1)} %copy-done.4, bf16[256,896]{1,0:T(8,128)(2,1)} %copy-done.5, ...), custom_call_target="tpu_custom_call" | custom-call | bytes 3670016 | tf_op jit(solution)/shard_map/gather/pallas_call | solution.py:396
  80.7 0.2 collective-permute-start.10
  80.9 0.0 copy-done
  80.9 7.2 %own.1 = (f32[16,128,128]{2,1,0:T(8,128)}, f32[16,128,128]{2,1,0:T(8,128)}) custom-call(bf16[16,128,128]{2,1,0:T(8,128)(2,1)} %copy-done, bf16[16,256,128]{2,1,0:T(8,128)(2,1)} %copy-done.7), custom_call_target="tpu_custom_call" | custom-call | flops 1073741824 | bytes 1572864 | tf_op jit(solution)/shard_map/own/pallas_call | solution.py:215
  88.1 1.7 %collective-permute-done.kv_ref = bf16[4,256,128]{2,1,0:T(8,128)(2,1)S(1)} collective-permute-done((bf16[4,256,128]{2,1,0:T(8,128)(2,1)S(1)}, bf16[4,256,128]{2,1,0:T(8,128)(2,1)S(1)}, u32[]{:S(2)}, u32[]{:S(2)}) %collective-permute-start) | collective-permute-done | bytes 262176 | tf_op jit(solution)/shard_map/ppermute | solution.py:24
  89.7 0.0 collective-permute-done.2.back_ref
  89.8 0.7 copy-done.10
  90.4 0.2 copy-done.9
  90.6 7.2 %previous.1 = bf16[16,128,128]{2,1,0:T(8,128)(2,1)} custom-call(s32[1]{0:T(128)} %bitcast.flag_ref, bf16[16,128,128]{2,1,0:T(8,128)(2,1)} %copy-done, bf16[4,256,128]{2,1,0:T(8,128)(2,1)} %copy-done.10, bf16[13,128,128]{2,1,0:T(8,128)(2,1)} %copy-done.9, f32[16,128,128]{2,1,0:T(8,128)} %get-tuple-element.7.out1_ref, f32[16,128,128]{2,1,0:T(8,128)} %get-tuple-element.8.stat_ref), custom_call_target="tpu_custom_call" | custom-call | flops 469762048 | bytes 2621440 | tf_op jit(solution)/shard_map/previous/pallas_call | solution.py:232
  97.8 9.0 %all-to-all-start.2 = ((bf16[16,128,128]{2,1,0:T(8,128)(2,1)}), bf16[16,128,128]{2,1,0:T(8,128)(2,1)S(1)}, u32[]{:S(2)}, u32[]{:S(2)}) async-start(bf16[16,128,128]{2,1,0:T(8,128)(2,1)} %previous.1), calls=%async_computation.2 | async-start | bytes 1048576 | tf_op jit(solution)/shard_map/all_to_all | solution.py:469
  106.7 5.8 %absorb.1.refs_7_ = bf16[2,1024,896]{2,1,0:T(8,128)(2,1)} custom-call(bf16[128,2048]{1,0:T(8,128)(2,1)} %q_ref.1, bf16[896,4096]{1,0:T(8,128)(2,1)} %refs_8_.1), custom_call_target="tpu_custom_call" | custom-call | flops 469762048 | bytes 7340032 | tf_op jit(solution)/shard_map/absorb/pallas_call | solution.py:412
  112.6 0.0 copy-done.11
  112.6 0.0 collective-permute-done.10.refs_6_
  112.6 0.0 copy-start.8
  112.6 0.9 copy-done.8
  113.5 10.5 %cross.1.cross_ref = f32[128,2048]{1,0:T(8,128)} custom-call(s32[1]{0:T(128)} %bitcast.1.position_ref, s32[2,2]{1,0:T(2,128)} %copy-done.11, bf16[128,896]{1,0:T(8,128)(2,1)} %refs_0_.7, bf16[128,896]{1,0:T(8,128)(2,1)} %copy-done.2, bf16[128,896]{1,0:T(8,128)(2,1)} %copy-done.3, bf16[256,896]{1,0:T(8,128)(2,1)} %copy-done.4, bf16[256,896]{1,0:T(8,128)(2,1)} %copy-done.5, ...), custom_call_target="tpu_custom_call" | custom-call | flops 2348810240 | bytes 9175040 | tf_op jit(solution)/shard_map/cross/pallas_call | solution.py:433
  124.1 0.0 all-to-all-done.2.self_ref
  124.1 0.0 copy-start.1
  124.1 0.8 copy-done.1
  124.9 2.3 %total.1 = bf16[128,2048]{1,0:T(8,128)(2,1)} custom-call(bf16[16,128,128]{2,1,0:T(8,128)(2,1)} %copy-done.1, f32[128,2048]{1,0:T(8,128)} %cross.1.cross_ref), custom_call_target="tpu_custom_call" | custom-call | tf_op jit(solution)/shard_map/total/pallas_call | solution.py:470
  (11 shorter events, 0.1 us)
Async XLA Ops:
  0.0 68.6 %copy-start.14 = (s32[2]{0:T(128)S(1)}, s32[2]{0:T(128)}, u32[]{:S(2)}) copy-start(s32[2]{0:T(128)} %param.14) | copy-start | bytes 28
  0.0 68.6 %copy-start.13 = (s32[2,2]{1,0:T(2,128)S(1)}, s32[2,2]{1,0:T(2,128)}, u32[]{:S(2)}) copy-start(s32[2,2]{1,0:T(2,128)} %param.15) | copy-start | bytes 52
  2.0 13.8 %all-to-all-start = ((bf16[16,128,128]{2,1,0:T(8,128)(2,1)}), bf16[16,128,128]{2,1,0:T(8,128)(2,1)S(1)}, u32[]{:S(2)}, u32[]{:S(2)}) async-start(bf16[16,128,128]{2,1,0:T(8,128)(2,1)} %pack.2), calls=%async_computation | async-start | bytes 1048576 | tf_op jit(solution)/shard_map/all_to_all | solution.py:210
  15.8 65.1 %copy-start = (bf16[16,128,128]{2,1,0:T(8,128)(2,1)}, bf16[16,128,128]{2,1,0:T(8,128)(2,1)S(1)}, u32[]{:S(2)}) copy-start(bf16[16,128,128]{2,1,0:T(8,128)(2,1)S(1)} %all-to-all-done.q_ref) | copy-start | bytes 1572868
  15.8 45.3 %all-to-all-start.1 = ((bf16[16,256,128]{2,1,0:T(8,128)(2,1)}), bf16[16,256,128]{2,1,0:T(8,128)(2,1)S(1)}, u32[]{:S(2)}, u32[]{:S(2)}) async-start(bf16[16,256,128]{2,1,0:T(8,128)(2,1)} %pack.3), calls=%async_computation.1 | async-start | bytes 2097152 | tf_op jit(solution)/shard_map/all_to_all | solution.py:207
  21.6 16.4 %collective-permute-start.4 = (bf16[128,896]{1,0:T(8,128)(2,1)}, bf16[128,896]{1,0:T(8,128)(2,1)S(1)}, u32[]{:S(2)}, u32[]{:S(2)}) collective-permute-start(bf16[128,896]{1,0:T(8,128)(2,1)} %refs_0_.7), channel_id=1, source_target_pairs={{0,8},{1,9},{2,10},{3,11},{4,12},{5,13},{6,14},{7,15},{8,16},{9,17... | collective-permute-start | bytes 688136 | tf_op jit(solution)/shard_map/ppermute | solution.py:24
  38.0 38.8 %copy-start.2 = (bf16[128,896]{1,0:T(8,128)(2,1)}, bf16[128,896]{1,0:T(8,128)(2,1)S(1)}, u32[]{:S(2)}) copy-start(bf16[128,896]{1,0:T(8,128)(2,1)S(1)} %collective-permute-done.4.refs_1_) | copy-start | bytes 688132
  38.0 8.1 %collective-permute-start.5 = (bf16[128,896]{1,0:T(8,128)(2,1)S(1)}, bf16[128,896]{1,0:T(8,128)(2,1)S(1)}, u32[]{:S(2)}, u32[]{:S(2)}) collective-permute-start(bf16[128,896]{1,0:T(8,128)(2,1)S(1)} %collective-permute-done.4.refs_1_), channel_id=1, source_target_pairs={{0,8},{1,9},{2,10},{3,11},{4,12},{5,13},{6,14},{7,15},{8,16},{9,17... | collective-permute-start | bytes 688136 | tf_op jit(solution)/shard_map/ppermute | solution.py:24
  42.0 19.0 %collective-permute-start.1 = (bf16[12,128,128]{2,1,0:T(8,128)(2,1)S(1)}, bf16[12,128,128]{2,1,0:T(8,128)(2,1)}, u32[]{:S(2)}, u32[]{:S(2)}) collective-permute-start(bf16[12,128,128]{2,1,0:T(8,128)(2,1)S(1)} %slice.17), channel_id=1, source_target_pairs={{16,0},{17,1},{18,2},{19,3},{20,4},{21,5},{22,6},{23,7},{24,8},{25... | collective-permute-start | bytes 1179656 | tf_op jit(solution)/shard_map/ppermute | solution.py:24
  46.0 30.7 %copy-start.3 = (bf16[128,896]{1,0:T(8,128)(2,1)}, bf16[128,896]{1,0:T(8,128)(2,1)S(1)}, u32[]{:S(2)}) copy-start(bf16[128,896]{1,0:T(8,128)(2,1)S(1)} %collective-permute-done.5.refs_2_) | copy-start | bytes 688132
  48.3 28.4 %collective-permute-start.6 = (bf16[256,896]{1,0:T(8,128)(2,1)}, bf16[256,896]{1,0:T(8,128)(2,1)S(1)}, u32[]{:S(2)}, u32[]{:S(2)}) collective-permute-start(bf16[256,896]{1,0:T(8,128)(2,1)} %get-tuple-element.14), channel_id=1, source_target_pairs={{0,2},{1,3},{2,0},{3,1},{4,6},{5,7},{6,4},{7,5},{8,10},{9,11},{10,... | collective-permute-start | bytes 1376264 | tf_op jit(solution)/shard_map/ppermute | solution.py:29
  48.6 28.1 %collective-permute-start.7 = (bf16[256,896]{1,0:T(8,128)(2,1)}, bf16[256,896]{1,0:T(8,128)(2,1)S(1)}, u32[]{:S(2)}, u32[]{:S(2)}) collective-permute-start(bf16[256,896]{1,0:T(8,128)(2,1)} %get-tuple-element.13), channel_id=1, source_target_pairs={{0,4},{1,5},{2,6},{3,7},{4,0},{5,1},{6,2},{7,3},{8,12},{9,13},{10,... | collective-permute-start | bytes 1376264 | tf_op jit(solution)/shard_map/ppermute | solution.py:29
  49.2 27.5 %collective-permute-start.8 = (bf16[256,896]{1,0:T(8,128)(2,1)}, bf16[256,896]{1,0:T(8,128)(2,1)S(1)}, u32[]{:S(2)}, u32[]{:S(2)}) collective-permute-start(bf16[256,896]{1,0:T(8,128)(2,1)} %get-tuple-element.12), channel_id=1, source_target_pairs={{0,6},{1,7},{2,4},{3,5},{4,2},{5,3},{6,0},{7,1},{8,14},{9,15},{10,... | collective-permute-start | bytes 1376264 | tf_op jit(solution)/shard_map/ppermute | solution.py:29
  61.0 1.0 copy-start.7
  67.3 22.4 %collective-permute-start.2 = (bf16[13,128,128]{2,1,0:T(8,128)(2,1)}, bf16[13,128,128]{2,1,0:T(8,128)(2,1)S(1)}, u32[]{:S(2)}, u32[]{:S(2)}) collective-permute-start(bf16[13,128,128]{2,1,0:T(8,128)(2,1)} %later.1), channel_id=1, source_target_pairs={{0,16},{1,17},{2,18},{3,19},{4,20},{5,21},{6,22},{7,23},{8,24},{9,... | collective-permute-start | bytes 1277960 | tf_op jit(solution)/shard_map/ppermute | solution.py:24
  68.7 3.3 %collective-permute-start.3 = (s32[2,2]{1,0:T(2,128)S(1)}, s32[2,2]{1,0:T(2,128)S(1)}, u32[]{:S(2)}, u32[]{:S(2)}) collective-permute-start(s32[2,2]{1,0:T(2,128)S(1)} %multiply_add_fusion), channel_id=1, source_target_pairs={{0,1},{1,2},{2,3},{3,4},{4,5},{5,6},{6,7},{7,8},{8,9},{9,10},{10,1... | collective-permute-start | bytes 56 | tf_op jit(solution)/shard_map/ppermute | solution.py:24
  72.0 40.6 %copy-start.11 = (s32[2,2]{1,0:T(2,128)}, s32[2,2]{1,0:T(2,128)S(1)}, u32[]{:S(2)}) copy-start(s32[2,2]{1,0:T(2,128)S(1)} %pad_add_fusion.table_ref) | copy-start | bytes 52
  72.0 3.4 %collective-permute-start.9 = (s32[2,2]{1,0:T(2,128)S(1)}, s32[2,2]{1,0:T(2,128)S(1)}, u32[]{:S(2)}, u32[]{:S(2)}) collective-permute-start(s32[2,2]{1,0:T(2,128)S(1)} %pad_add_fusion.table_ref), channel_id=1, source_target_pairs={{0,1},{1,0},{2,3},{3,2},{4,5},{5,4},{6,7},{7,6},{8,9},{9,8},{10,11... | collective-permute-start | bytes 56 | tf_op jit(solution)/shard_map/ppermute | solution.py:29
  75.4 1.4 %copy-start.12 = (s32[2,2]{1,0:T(2,128)}, s32[2,2]{1,0:T(2,128)S(1)}, u32[]{:S(2)}) copy-start(s32[2,2]{1,0:T(2,128)S(1)} %collective-permute-done.9.theirs_ref) | copy-start | bytes 52
  75.4 14.4 %collective-permute-start = (bf16[4,256,128]{2,1,0:T(8,128)(2,1)S(1)}, bf16[4,256,128]{2,1,0:T(8,128)(2,1)S(1)}, u32[]{:S(2)}, u32[]{:S(2)}) collective-permute-start(bf16[4,256,128]{2,1,0:T(8,128)(2,1)S(1)} %slice.16), channel_id=1, source_target_pairs={{0,16},{1,17},{2,18},{3,19},{4,20},{5,21},{6,22},{7,23},{8,24},{9,... | collective-permute-start | bytes 786440 | tf_op jit(solution)/shard_map/ppermute | solution.py:24
  76.7 0.8 copy-start.4
  76.7 0.9 copy-start.5
  76.7 1.0 copy-start.6
  80.7 31.9 %collective-permute-start.10 = (bf16[512,896]{1,0:T(8,128)(2,1)}, bf16[512,896]{1,0:T(8,128)(2,1)S(1)}, u32[]{:S(2)}, u32[]{:S(2)}) collective-permute-start(bf16[512,896]{1,0:T(8,128)(2,1)} %gather.1), channel_id=1, source_target_pairs={{0,1},{1,0},{2,3},{3,2},{4,5},{5,4},{6,7},{7,6},{8,9},{9,8},{10,11... | collective-permute-start | bytes 2752520 | tf_op jit(solution)/shard_map/ppermute | solution.py:29
  89.7 0.7 copy-start.10
  89.7 0.8 copy-start.9
  97.8 26.3 %all-to-all-start.2 = ((bf16[16,128,128]{2,1,0:T(8,128)(2,1)}), bf16[16,128,128]{2,1,0:T(8,128)(2,1)S(1)}, u32[]{:S(2)}, u32[]{:S(2)}) async-start(bf16[16,128,128]{2,1,0:T(8,128)(2,1)} %previous.1), calls=%async_computation.2 | async-start | bytes 1048576 | tf_op jit(solution)/shard_map/all_to_all | solution.py:469
  112.6 1.0 copy-start.8
  124.1 0.8 copy-start.1

commit v3 on v2

--- a/solution.py
+++ b/solution.py
@@ -12,7 +12,7 @@
 HEAD_DIM = 128
 SPAN = 64
 PLANE = 8
-LEFT = 12
+LEFT = 8
 
 MASKED_SCORE = -1e30
 LOG2E = 1.4426950408889634
@@ -101,29 +101,31 @@
     return keep(column, row)
 
 
-def own_kernel(scale, q_ref, kv_ref, out_ref, stat_ref):
-    blocks, rows, dim = q_ref.shape
+def own_kernel(scale, x_ref, out_ref, stat_ref):
+    blocks, triple, dim = x_ref.shape
+    rows = triple // 3
     causal = triangle(2 * rows, lambda column, row: column <= row)
     for i in range(0, blocks, 2):
-        pieces = [(taken(kv_ref, i, 2, 0, rows), taken(kv_ref, i, 2, rows, rows), causal)]
-        if i:
-            pieces.append((taken(kv_ref, 0, i, 0, rows), taken(kv_ref, 0, i, rows, rows), None))
-        out, largest, total = softmax_parts(taken(q_ref, i, 2, 0, rows), pieces, scale)
+        spans = [(i, 2, causal)] + ([(0, i, None)] if i else [])
+        pieces = [
+            (taken(x_ref, f, n, rows, rows), taken(x_ref, f, n, 2 * rows, rows), mask)
+            for f, n, mask in spans
+        ]
+        out, largest, total = softmax_parts(taken(x_ref, i, 2, 0, rows), pieces, scale)
         out_ref[i : i + 2] = out.reshape(2, rows, dim)
         stat_ref[i : i + 2] = with_stats(largest, total).reshape(2, rows, 128)
 
 
-def later_kernel(scale, q_ref, kv_ref, out_ref):
+def later_kernel(scale, q_ref, x_ref, out_ref):
     blocks, rows, dim = q_ref.shape
     later = triangle(2 * rows, lambda column, row: column > row)
     out_ref[blocks] = jnp.zeros((rows, dim), out_ref.dtype)
     for i in range(0, blocks, 2):
-        pieces = [(taken(kv_ref, i, 2, 0, rows), taken(kv_ref, i, 2, rows, rows), later)]
-        rest = blocks - i - 2
-        if rest:
-            pieces.append(
-                (taken(kv_ref, i + 2, rest, 0, rows), taken(kv_ref, i + 2, rest, rows, rows), None)
-            )
+        spans = [(i, 2, later)] + ([(i + 2, blocks - i - 2, None)] if i + 2 < blocks else [])
+        pieces = [
+            (taken(x_ref, f, n, rows, rows), taken(x_ref, f, n, 2 * rows, rows), mask)
+            for f, n, mask in spans
+        ]
         out, largest, total = softmax_parts(taken(q_ref, i, 2, 0, rows), pieces, scale)
         out_ref[i : i + 2] = out.reshape(2, rows, dim).astype(out_ref.dtype)
         stat = with_stats(largest, total)
@@ -145,10 +147,29 @@
     return jnp.where(sublane < 64, values[0], values[1]).T
 
 
-def previous_kernel(scale, flag_ref, q_ref, kv_ref, back_ref, out1_ref, stat_ref, out_ref):
+def previous_kernel(scale, flag_ref, *refs):
+    in_refs, out_ref = refs[:5], refs[5]
+    q_ref, kv_ref, back_ref, out1_ref, stat_ref = bufs = refs[6:11]
+    sems = refs[11]
     blocks, rows, dim = q_ref.shape
     sent = back_ref.shape[0] - 1
     later = triangle(2 * rows, lambda column, row: column > row)
+
+    def copy(n, i):
+        if i is None:
+            return pltpu.make_async_copy(in_refs[n], bufs[n], sems.at[n, 0])
+        source = in_refs[n].at[i : i + 2, 0 : bufs[n].shape[1], :]
+        return pltpu.make_async_copy(source, bufs[n].at[i : i + 2], sems.at[n, i // 2])
+
+    whole = [copy(n, None) for n in (1, 2)]
+    paired = {i: [copy(n, i) for n in (0, 3, 4)] for i in range(0, blocks, 2)}
+    order = list(range(0, blocks, 2))[::-1]
+    whole[0].start()
+    for i in order:
+        for c in paired[i]:
+            c.start()
+        if i == order[0]:
+            whole[1].start()
 
     def store(i, parts):
         top = functools.reduce(jnp.maximum, [largest for _, largest, _ in parts])
@@ -163,32 +184,34 @@
 
     @pl.when(flag_ref[0] > 0)
     def _():
-        for i in range(0, blocks, 2):
-            pieces = []
+        whole[0].wait()
+        for i in order:
+            for c in paired[i]:
+                c.wait()
             first = max(i - sent, 0)
-            if i >= sent:
-                pieces.append(
-                    (taken(kv_ref, first, 2, 0, rows), taken(kv_ref, first, 2, rows, rows), later)
-                )
-                first += 2
-            rest = kv_ref.shape[0] - first
-            if rest:
-                pieces.append(
-                    (
-                        taken(kv_ref, first, rest, 0, rows),
-                        taken(kv_ref, first, rest, rows, rows),
-                        None,
-                    )
-                )
+            spans = [(first, 2, later)] if i >= sent else []
+            first += 2 * len(spans)
+            if first < kv_ref.shape[0]:
+                spans.append((first, kv_ref.shape[0] - first, None))
+            pieces = [
+                (taken(kv_ref, f, n, 0, rows), taken(kv_ref, f, n, rows, rows), mask)
+                for f, n, mask in spans
+            ]
             parts = [softmax_parts(taken(q_ref, i, 2, 0, rows), pieces, scale), own_part(i)]
             if i < sent:
+                if i == sent - 2:
+                    whole[1].wait()
                 stat = jnp.concatenate([sent_stats(back_ref, i + n, rows) for n in range(2)], axis=0)
                 parts.append((taken(back_ref, i, 2, 0, rows).astype(jnp.float32), *halves(stat)))
             store(i, parts)
 
     @pl.when(flag_ref[0] == 0)
     def _():
-        for i in range(0, blocks, 2):
+        for c in whole:
+            c.wait()
+        for i in order:
+            for c in paired[i]:
+                c.wait()
             store(i, [own_part(i)])
 
 
@@ -204,12 +227,11 @@
     rows, width = queries.shape
     heads = width // HEAD_DIM
     scale = HEAD_DIM ** (-0.5) * LOG2E
-    kv = lax.all_to_all(
-        packed(keys, values), "ctx", 0, 0, axis_index_groups=groups, tiled=True
+    x = lax.all_to_all(
+        packed(queries, keys, values), "ctx", 0, 0, axis_index_groups=groups, tiled=True
     )
-    q = lax.all_to_all(packed(queries), "ctx", 0, 0, axis_index_groups=groups, tiled=True)
-    arriving = shifted(kv[LEFT:], "ctx", heads)
-    asked = shifted(q[:LEFT], "ctx", -heads)
+    arriving = shifted(x[LEFT:, rows:], "ctx", heads)
+    asked = shifted(x[:LEFT, :rows], "ctx", -heads)
     area = (heads * rows) ** 2 // 2
     small = (LEFT * rows) ** 2 // 2
     out1, stat = pl.pallas_call(
@@ -218,24 +240,33 @@
             jax.ShapeDtypeStruct((heads, rows, HEAD_DIM), jnp.float32),
             jax.ShapeDtypeStruct((heads, rows, 128), jnp.float32),
         ),
-        cost_estimate=estimate(area, (q, kv)),
+        cost_estimate=estimate(area, (x,)),
         name="own",
-    )(q, kv)
+    )(x)
     answer = pl.pallas_call(
         functools.partial(later_kernel, scale),
         out_shape=jax.ShapeDtypeStruct((LEFT + 1, rows, HEAD_DIM), jnp.bfloat16),
         cost_estimate=estimate(small, (asked,)),
         name="later",
-    )(asked, kv)
+    )(asked, x)
     back = shifted(answer, "ctx", heads)
-    vmem = pl.BlockSpec(memory_space=pltpu.VMEM)
     return pl.pallas_call(
         functools.partial(previous_kernel, scale),
         out_shape=jax.ShapeDtypeStruct((heads, rows, HEAD_DIM), jnp.bfloat16),
-        in_specs=[pl.BlockSpec(memory_space=pltpu.SMEM)] + [vmem] * 5,
-        cost_estimate=estimate(area - small, (q, kv, out1, stat)),
+        in_specs=[pl.BlockSpec(memory_space=pltpu.SMEM)]
+        + [pl.BlockSpec(memory_space=pl.ANY)] * 5,
+        out_specs=pl.BlockSpec(memory_space=pltpu.VMEM),
+        scratch_shapes=[
+            pltpu.VMEM((heads, rows, HEAD_DIM), x.dtype),
+            pltpu.VMEM(arriving.shape, arriving.dtype),
+            pltpu.VMEM(back.shape, back.dtype),
+            pltpu.VMEM(out1.shape, out1.dtype),
+            pltpu.VMEM(stat.shape, stat.dtype),
+            pltpu.SemaphoreType.DMA((5, heads // 2)),
+        ],
+        cost_estimate=estimate(area - small, (x, out1, stat)),
         name="previous",
-    )(chunk.reshape(1), q, arriving, back, out1, stat)
+    )(chunk.reshape(1), x, arriving, back, out1, stat)
 
 
 def wanted_pieces(table_ref, position, span_count):

time: 128 us -> 135 us (1.055)
  starting transfers between devices: 39.9 us -> 59.4 us
  waiting for transfers between devices: 33.6 us -> 25 us
  Pallas kernels: 45.5 us -> 43.8 us
  local copies, waits for them, and re-layouts: 5.6 us -> 4.13 us
    all_to_all x1, starting transfers between devices: 8.98 us -> 24.5 us  [per_device(): lax.all_to_all(by_head, 'ctx', 0, 0, axis_index_groups=groups, tiled=True)]
    all_to_all x2 -> x1, waiting for transfers between devices: 5.94 us -> 0.01 us  [self_attention(): lax.all_to_all(packed(queries, keys, values), 'ctx', 0, 0, axis_index_gro...]
    all_to_all x2 -> x1, starting transfers between devices: 11.3 us -> 5.64 us  [self_attention(): lax.all_to_all(packed(queries, keys, values), 'ctx', 0, 0, axis_index_gro...]
    ppermute x5, starting transfers between devices: 5.23 us -> 10.4 us  [swapped(): lax.ppermute(value, axis, [(source, source ^ bit) for source in range(cou...]
    ppermute x6, starting transfers between devices: 14.3 us -> 18.8 us  [shifted(): lax.ppermute(value, axis, [(source, source + steps) for source in range(f...]
    ppermute x6, waiting for transfers between devices: 27.6 us -> 25 us  [shifted(): lax.ppermute(value, axis, [(source, source + steps) for source in range(f...]
    pallas_call x2 -> x1, Pallas kernels: 4.32 us -> 2.87 us  [packed(): pl.pallas_call(pack_kernel, out_shape=jax.ShapeDtypeStruct((width // HEAD...]
    unnamed x30 -> x28, local copies, waits for them, and re-layouts: 4.6 us -> 4.07 us
  transfers between devices with their start and end apart: 14 -> 13, of which waited for: 6 -> 5; matrix products, arithmetic and copies ran while one was open for 3% -> 1% of each run, Pallas kernels for 32% -> 29%
where the time goes in v3:
time: 135 us; the launch traced here: 134 us
  starting transfers between devices  59.4 us (44%)
  Pallas kernels  43.8 us (32%)
  waiting for transfers between devices  25 us (19%)
  local copies, waits for them, and re-layouts  4.13 us (3%)
    ppermute x6, waiting for transfers between devices, shifted(): lax.ppermute(value, axis, [(source, source + steps) for source in range(f...  25 us
    all_to_all x1, starting transfers between devices, per_device(): lax.all_to_all(by_head, 'ctx', 0, 0, axis_index_groups=groups, tiled=True)  24.5 us
    ppermute x6, starting transfers between devices, shifted(): lax.ppermute(value, axis, [(source, source + steps) for source in range(f...  18.8 us
    pallas_call x1, Pallas kernels, cross_attention(): pl.pallas_call(functools.partial(cross_kernel, HEAD_DIM ** (-0.5) * LOG2E...  10.5 us
    ppermute x5, starting transfers between devices, swapped(): lax.ppermute(value, axis, [(source, source ^ bit) for source in range(cou...  10.4 us
    pallas_call x1, Pallas kernels, self_attention(): pl.pallas_call(functools.partial(previous_kernel, scale), out_shape=jax.S...  8.04 us
    pallas_call x1, Pallas kernels, self_attention(): pl.pallas_call(functools.partial(own_kernel, scale), out_shape=(jax.Shape...  7.19 us
    pallas_call x1, Pallas kernels, cross_attention(): pl.pallas_call(absorb_kernel, out_shape=jax.ShapeDtypeStruct((span_count,...  5.81 us
  transfers between devices with their start and end apart: 13, of which 5 were waited for; matrix products, arithmetic and copies ran while one was open for 1% of the time, Pallas kernels for 29%

profile of v3, /device:TPU:23, one launch (start us, length us, event | category | flops | bytes accessed | tf_op | source)
XLA Modules:
  0.0 134.0 jit_solution(10172220308039798187)
XLA Ops:
  0.0 0.0 copy-start.3
  0.0 2.9 %pack.1 = bf16[16,384,128]{2,1,0:T(8,128)(2,1)} custom-call(bf16[128,2048]{1,0:T(8,128)(2,1)} %refs_0_.3, bf16[128,2048]{1,0:T(8,128)(2,1)} %refs_1_.1, bf16[128,2048]{1,0:T(8,128)(2,1)} %refs_2_.1), custom_call_target="tpu_custom_call" | custom-call | bytes 3145728 | tf_op jit(solution)/shard_map/pack/pallas_call | solution.py:43
  2.9 0.0 copy-start.12
  2.9 0.0 copy-start.13
  2.9 5.6 %all-to-all-start = ((bf16[16,384,128]{2,1,0:T(8,128)(2,1)}), bf16[16,384,128]{2,1,0:T(8,128)(2,1)S(1)}, u32[]{:S(2)}, u32[]{:S(2)}) async-start(bf16[16,384,128]{2,1,0:T(8,128)(2,1)} %pack.1), calls=%async_computation | async-start | bytes 3145728 | tf_op jit(solution)/shard_map/all_to_all | solution.py:230
  8.5 0.0 copy-done.3
  8.5 3.1 %collective-permute-start.4 = (bf16[128,896]{1,0:T(8,128)(2,1)S(1)}, bf16[128,896]{1,0:T(8,128)(2,1)S(1)}, u32[]{:S(2)}, u32[]{:S(2)}) collective-permute-start(bf16[128,896]{1,0:T(8,128)(2,1)S(1)} %copy-done.3), channel_id=1, source_target_pairs={{0,8},{1,9},{2,10},{3,11},{4,12},{5,13},{6,14},{7,15},{8,16},{9,17... | collective-permute-start | bytes 688136 | tf_op jit(solution)/shard_map/ppermute | solution.py:24
  11.6 19.5 %collective-permute-done.4.refs_1_ = bf16[128,896]{1,0:T(8,128)(2,1)S(1)} collective-permute-done((bf16[128,896]{1,0:T(8,128)(2,1)S(1)}, bf16[128,896]{1,0:T(8,128)(2,1)S(1)}, u32[]{:S(2)}, u32[]{:S(2)}) %collective-permute-start.4) | collective-permute-done | bytes 229408 | tf_op jit(solution)/shard_map/ppermute | solution.py:24
  31.2 0.0 copy-start.2
  31.2 4.1 %collective-permute-start.5 = (bf16[128,896]{1,0:T(8,128)(2,1)S(1)}, bf16[128,896]{1,0:T(8,128)(2,1)S(1)}, u32[]{:S(2)}, u32[]{:S(2)}) collective-permute-start(bf16[128,896]{1,0:T(8,128)(2,1)S(1)} %collective-permute-done.4.refs_1_), channel_id=1, source_target_pairs={{0,8},{1,9},{2,10},{3,11},{4,12},{5,13},{6,14},{7,15},{8,16},{9,17... | collective-permute-start | bytes 688136 | tf_op jit(solution)/shard_map/ppermute | solution.py:24
  35.3 4.0 %collective-permute-done.5.refs_2_ = bf16[128,896]{1,0:T(8,128)(2,1)S(1)} collective-permute-done((bf16[128,896]{1,0:T(8,128)(2,1)S(1)}, bf16[128,896]{1,0:T(8,128)(2,1)S(1)}, u32[]{:S(2)}, u32[]{:S(2)}) %collective-permute-start.5) | collective-permute-done | bytes 229408 | tf_op jit(solution)/shard_map/ppermute | solution.py:24
  39.2 0.0 copy-start.4
  39.2 0.1 broadcast_select_fusion
  39.3 1.2 pad_maximum_fusion
  40.5 0.2 collective-permute-start.6
  40.7 0.9 collective-permute-start.7
  41.6 1.5 %collective-permute-start.8 = (bf16[256,896]{1,0:T(8,128)(2,1)}, bf16[256,896]{1,0:T(8,128)(2,1)}, u32[]{:S(2)}, u32[]{:S(2)}) collective-permute-start(bf16[256,896]{1,0:T(8,128)(2,1)} %get-tuple-element.12), channel_id=1, source_target_pairs={{0,6},{1,7},{2,4},{3,5},{4,2},{5,3},{6,0},{7,1},{8,14},{9,15},{10,... | collective-permute-start | bytes 1376264 | tf_op jit(solution)/shard_map/ppermute | solution.py:29
  43.2 0.0 all-to-all-done.x_ref.refs_0_
  43.2 0.0 copy-start
  43.2 2.0 %collective-permute-start.1 = (bf16[8,128,128]{2,1,0:T(8,128)(2,1)S(1)}, bf16[8,128,128]{2,1,0:T(8,128)(2,1)S(1)}, u32[]{:S(2)}, u32[]{:S(2)}) collective-permute-start(bf16[8,128,128]{2,1,0:T(8,128)(2,1)S(1)} %slice.17), channel_id=1, source_target_pairs={{16,0},{17,1},{18,2},{19,3},{20,4},{21,5},{22,6},{23,7},{24,8},{25... | collective-permute-start | bytes 786440 | tf_op jit(solution)/shard_map/ppermute | solution.py:24
  45.2 0.0 copy-done.12
  45.2 0.0 copy-done.13
  45.2 0.1 multiply_add_fusion
  45.3 7.1 %collective-permute-start.3 = (s32[2,2]{1,0:T(2,128)S(1)}, s32[2,2]{1,0:T(2,128)S(1)}, u32[]{:S(2)}, u32[]{:S(2)}) collective-permute-start(s32[2,2]{1,0:T(2,128)S(1)} %multiply_add_fusion), channel_id=1, source_target_pairs={{0,1},{1,2},{2,3},{3,4},{4,5},{5,6},{6,7},{7,8},{8,9},{9,10},{10,1... | collective-permute-start | bytes 56 | tf_op jit(solution)/shard_map/ppermute | solution.py:24
  52.4 0.7 collective-permute-done.3
  53.1 1.3 collective-permute-start
  54.4 0.0 copy-start.10
  54.4 0.4 collective-permute-done.1.q_ref
  54.9 0.0 copy-start.9
  54.9 0.7 copy-done.9
  55.6 7.7 %collective-permute-start.9 = (s32[2,2]{1,0:T(2,128)S(1)}, s32[2,2]{1,0:T(2,128)S(1)}, u32[]{:S(2)}, u32[]{:S(2)}) collective-permute-start(s32[2,2]{1,0:T(2,128)S(1)} %pad_add_fusion.table_ref), channel_id=1, source_target_pairs={{0,1},{1,0},{2,3},{3,2},{4,5},{5,4},{6,7},{7,6},{8,9},{9,8},{10,11... | collective-permute-start | bytes 56 | tf_op jit(solution)/shard_map/ppermute | solution.py:29
  63.3 0.0 copy-done
  63.3 4.1 %later.1 = bf16[9,128,128]{2,1,0:T(8,128)(2,1)} custom-call(bf16[8,128,128]{2,1,0:T(8,128)(2,1)} %copy-done.9, bf16[16,384,128]{2,1,0:T(8,128)(2,1)} %copy-done), custom_call_target="tpu_custom_call" | custom-call | flops 268435456 | bytes 262144 | tf_op jit(solution)/shard_map/later/pallas_call | solution.py:246
  67.4 0.0 collective-permute-done.9.theirs_ref
  67.4 0.0 copy-start.11
  67.4 1.3 collective-permute-start.2
  68.7 0.0 collective-permute-done.6.refs_3_
  68.7 0.0 copy-start.5
  68.7 0.0 collective-permute-done.7.refs_4_
  68.7 0.0 copy-start.6
  68.7 0.0 collective-permute-done.8.refs_5_
  68.7 0.0 copy-done.2
  68.8 0.0 copy-done.4
  68.8 0.0 copy-done.11
  68.8 0.7 copy-done.5
  69.5 0.2 copy-done.6
  69.6 2.9 %gather.1 = bf16[512,896]{1,0:T(8,128)(2,1)} custom-call(s32[1]{0:T(128)} %bitcast.1.position_ref, s32[2,2]{1,0:T(2,128)} %copy-done.11, bf16[128,896]{1,0:T(8,128)(2,1)} %refs_0_.5, bf16[128,896]{1,0:T(8,128)(2,1)} %copy-done.2, bf16[128,896]{1,0:T(8,128)(2,1)} %copy-done.4, bf16[256,896]{1,0:T(8,128)(2,1)} %copy-done.5, bf16[256,896]{1,0:T(8,128)(2,1)} %copy-done.6, ...), custom_call_target="tpu_custom_call" | custom-call | bytes 3670016 | tf_op jit(solution)/shard_map/gather/pallas_call | solution.py:427
  72.6 0.1 collective-permute-start.10
  72.7 7.2 %own.1 = (f32[16,128,128]{2,1,0:T(8,128)}, f32[16,128,128]{2,1,0:T(8,128)}) custom-call(bf16[16,384,128]{2,1,0:T(8,128)(2,1)} %copy-done), custom_call_target="tpu_custom_call" | custom-call | flops 1073741824 | bytes 1572864 | tf_op jit(solution)/shard_map/own/pallas_call | solution.py:237
  79.9 0.0 collective-permute-done.refs_1_
  79.9 0.4 collective-permute-done.2.refs_2_
  80.3 0.7 copy-done.8
  81.0 8.0 %previous.1 = bf16[16,128,128]{2,1,0:T(8,128)(2,1)} custom-call(s32[1]{0:T(128)} %bitcast.flag_ref, bf16[16,384,128]{2,1,0:T(8,128)(2,1)} %copy-done, bf16[8,256,128]{2,1,0:T(8,128)(2,1)} %collective-permute-done.refs_1_, bf16[9,128,128]{2,1,0:T(8,128)(2,1)} %copy-done.8, f32[16,128,128]{2,1,0:T(8,128)} %get-tuple-element.7.refs_3_, ...), custom_call_target="tpu_custom_call" | custom-call | flops 805306368 | bytes 2621440 | tf_op jit(solution)/shard_map/previous/pallas_call | solution.py:253
  89.0 24.5 %all-to-all-start.1 = ((bf16[16,128,128]{2,1,0:T(8,128)(2,1)}), bf16[16,128,128]{2,1,0:T(8,128)(2,1)S(1)}, u32[]{:S(2)}, u32[]{:S(2)}) async-start(bf16[16,128,128]{2,1,0:T(8,128)(2,1)} %previous.1), calls=%async_computation.1 | async-start | bytes 1048576 | tf_op jit(solution)/shard_map/all_to_all | solution.py:500
  113.6 5.8 %absorb.1.refs_7_ = bf16[2,1024,896]{2,1,0:T(8,128)(2,1)} custom-call(bf16[128,2048]{1,0:T(8,128)(2,1)} %q_ref.1, bf16[896,4096]{1,0:T(8,128)(2,1)} %refs_8_.1), custom_call_target="tpu_custom_call" | custom-call | flops 469762048 | bytes 7340032 | tf_op jit(solution)/shard_map/absorb/pallas_call | solution.py:443
  119.4 0.0 copy-done.10
  119.4 0.0 collective-permute-done.10.refs_6_
  119.4 0.0 copy-start.7
  119.4 0.9 copy-done.7
  120.3 10.5 %cross.1.cross_ref = f32[128,2048]{1,0:T(8,128)} custom-call(s32[1]{0:T(128)} %bitcast.1.position_ref, s32[2,2]{1,0:T(2,128)} %copy-done.10, bf16[128,896]{1,0:T(8,128)(2,1)} %refs_0_.5, bf16[128,896]{1,0:T(8,128)(2,1)} %copy-done.2, bf16[128,896]{1,0:T(8,128)(2,1)} %copy-done.4, bf16[256,896]{1,0:T(8,128)(2,1)} %copy-done.5, bf16[256,896]{1,0:T(8,128)(2,1)} %copy-done.6, ...), custom_call_target="tpu_custom_call" | custom-call | flops 2348810240 | bytes 9175040 | tf_op jit(solution)/shard_map/cross/pallas_call | solution.py:464
  130.9 0.0 all-to-all-done.1.self_ref
  130.9 0.0 copy-start.1
  130.9 0.8 copy-done.1
  131.7 2.3 %total.1 = bf16[128,2048]{1,0:T(8,128)(2,1)} custom-call(bf16[16,128,128]{2,1,0:T(8,128)(2,1)} %copy-done.1, f32[128,2048]{1,0:T(8,128)} %cross.1.cross_ref), custom_call_target="tpu_custom_call" | custom-call | tf_op jit(solution)/shard_map/total/pallas_call | solution.py:501
  (6 shorter events, 0.1 us)
Async XLA Ops:
  0.0 8.5 %copy-start.3 = (bf16[128,896]{1,0:T(8,128)(2,1)S(1)}, bf16[128,896]{1,0:T(8,128)(2,1)}, u32[]{:S(2)}) copy-start(bf16[128,896]{1,0:T(8,128)(2,1)} %refs_0_.5) | copy-start | bytes 688132
  2.9 42.3 %copy-start.12 = (s32[2,2]{1,0:T(2,128)S(1)}, s32[2,2]{1,0:T(2,128)}, u32[]{:S(2)}) copy-start(s32[2,2]{1,0:T(2,128)} %param.15) | copy-start | bytes 52
  2.9 42.3 %copy-start.13 = (s32[2]{0:T(128)S(1)}, s32[2]{0:T(128)}, u32[]{:S(2)}) copy-start(s32[2]{0:T(128)} %param.14) | copy-start | bytes 28
  2.9 40.3 %all-to-all-start = ((bf16[16,384,128]{2,1,0:T(8,128)(2,1)}), bf16[16,384,128]{2,1,0:T(8,128)(2,1)S(1)}, u32[]{:S(2)}, u32[]{:S(2)}) async-start(bf16[16,384,128]{2,1,0:T(8,128)(2,1)} %pack.1), calls=%async_computation | async-start | bytes 3145728 | tf_op jit(solution)/shard_map/all_to_all | solution.py:230
  8.5 22.6 %collective-permute-start.4 = (bf16[128,896]{1,0:T(8,128)(2,1)S(1)}, bf16[128,896]{1,0:T(8,128)(2,1)S(1)}, u32[]{:S(2)}, u32[]{:S(2)}) collective-permute-start(bf16[128,896]{1,0:T(8,128)(2,1)S(1)} %copy-done.3), channel_id=1, source_target_pairs={{0,8},{1,9},{2,10},{3,11},{4,12},{5,13},{6,14},{7,15},{8,16},{9,17... | collective-permute-start | bytes 688136 | tf_op jit(solution)/shard_map/ppermute | solution.py:24
  31.2 37.6 %copy-start.2 = (bf16[128,896]{1,0:T(8,128)(2,1)}, bf16[128,896]{1,0:T(8,128)(2,1)S(1)}, u32[]{:S(2)}) copy-start(bf16[128,896]{1,0:T(8,128)(2,1)S(1)} %collective-permute-done.4.refs_1_) | copy-start | bytes 688132
  31.2 8.1 %collective-permute-start.5 = (bf16[128,896]{1,0:T(8,128)(2,1)S(1)}, bf16[128,896]{1,0:T(8,128)(2,1)S(1)}, u32[]{:S(2)}, u32[]{:S(2)}) collective-permute-start(bf16[128,896]{1,0:T(8,128)(2,1)S(1)} %collective-permute-done.4.refs_1_), channel_id=1, source_target_pairs={{0,8},{1,9},{2,10},{3,11},{4,12},{5,13},{6,14},{7,15},{8,16},{9,17... | collective-permute-start | bytes 688136 | tf_op jit(solution)/shard_map/ppermute | solution.py:24
  39.2 29.5 %copy-start.4 = (bf16[128,896]{1,0:T(8,128)(2,1)}, bf16[128,896]{1,0:T(8,128)(2,1)S(1)}, u32[]{:S(2)}) copy-start(bf16[128,896]{1,0:T(8,128)(2,1)S(1)} %collective-permute-done.5.refs_2_) | copy-start | bytes 688132
  40.5 28.2 %collective-permute-start.6 = (bf16[256,896]{1,0:T(8,128)(2,1)}, bf16[256,896]{1,0:T(8,128)(2,1)S(1)}, u32[]{:S(2)}, u32[]{:S(2)}) collective-permute-start(bf16[256,896]{1,0:T(8,128)(2,1)} %get-tuple-element.14), channel_id=1, source_target_pairs={{0,2},{1,3},{2,0},{3,1},{4,6},{5,7},{6,4},{7,5},{8,10},{9,11},{10,... | collective-permute-start | bytes 1376264 | tf_op jit(solution)/shard_map/ppermute | solution.py:29
  40.7 28.0 %collective-permute-start.7 = (bf16[256,896]{1,0:T(8,128)(2,1)}, bf16[256,896]{1,0:T(8,128)(2,1)S(1)}, u32[]{:S(2)}, u32[]{:S(2)}) collective-permute-start(bf16[256,896]{1,0:T(8,128)(2,1)} %get-tuple-element.13), channel_id=1, source_target_pairs={{0,4},{1,5},{2,6},{3,7},{4,0},{5,1},{6,2},{7,3},{8,12},{9,13},{10,... | collective-permute-start | bytes 1376264 | tf_op jit(solution)/shard_map/ppermute | solution.py:29
  41.6 27.1 %collective-permute-start.8 = (bf16[256,896]{1,0:T(8,128)(2,1)}, bf16[256,896]{1,0:T(8,128)(2,1)}, u32[]{:S(2)}, u32[]{:S(2)}) collective-permute-start(bf16[256,896]{1,0:T(8,128)(2,1)} %get-tuple-element.12), channel_id=1, source_target_pairs={{0,6},{1,7},{2,4},{3,5},{4,2},{5,3},{6,0},{7,1},{8,14},{9,15},{10,... | collective-permute-start | bytes 1376264 | tf_op jit(solution)/shard_map/ppermute | solution.py:29
  43.2 20.1 %copy-start = (bf16[16,384,128]{2,1,0:T(8,128)(2,1)}, bf16[16,384,128]{2,1,0:T(8,128)(2,1)S(1)}, u32[]{:S(2)}) copy-start(bf16[16,384,128]{2,1,0:T(8,128)(2,1)S(1)} %all-to-all-done.x_ref.refs_0_) | copy-start | bytes 4718596
  43.2 11.7 %collective-permute-start.1 = (bf16[8,128,128]{2,1,0:T(8,128)(2,1)S(1)}, bf16[8,128,128]{2,1,0:T(8,128)(2,1)S(1)}, u32[]{:S(2)}, u32[]{:S(2)}) collective-permute-start(bf16[8,128,128]{2,1,0:T(8,128)(2,1)S(1)} %slice.17), channel_id=1, source_target_pairs={{16,0},{17,1},{18,2},{19,3},{20,4},{21,5},{22,6},{23,7},{24,8},{25... | collective-permute-start | bytes 786440 | tf_op jit(solution)/shard_map/ppermute | solution.py:24
  45.3 7.8 %collective-permute-start.3 = (s32[2,2]{1,0:T(2,128)S(1)}, s32[2,2]{1,0:T(2,128)S(1)}, u32[]{:S(2)}, u32[]{:S(2)}) collective-permute-start(s32[2,2]{1,0:T(2,128)S(1)} %multiply_add_fusion), channel_id=1, source_target_pairs={{0,1},{1,2},{2,3},{3,4},{4,5},{5,6},{6,7},{7,8},{8,9},{9,10},{10,1... | collective-permute-start | bytes 56 | tf_op jit(solution)/shard_map/ppermute | solution.py:24
  53.1 26.8 %collective-permute-start = (bf16[8,256,128]{2,1,0:T(8,128)(2,1)S(1)}, bf16[8,256,128]{2,1,0:T(8,128)(2,1)}, u32[]{:S(2)}, u32[]{:S(2)}) collective-permute-start(bf16[8,256,128]{2,1,0:T(8,128)(2,1)S(1)} %slice.16), channel_id=1, source_target_pairs={{0,16},{1,17},{2,18},{3,19},{4,20},{5,21},{6,22},{7,23},{8,24},{9,... | collective-permute-start | bytes 1572872 | tf_op jit(solution)/shard_map/ppermute | solution.py:24
  54.4 65.0 %copy-start.10 = (s32[2,2]{1,0:T(2,128)}, s32[2,2]{1,0:T(2,128)S(1)}, u32[]{:S(2)}) copy-start(s32[2,2]{1,0:T(2,128)S(1)} %pad_add_fusion.table_ref) | copy-start | bytes 52
  54.9 0.7 copy-start.9
  55.6 11.8 %collective-permute-start.9 = (s32[2,2]{1,0:T(2,128)S(1)}, s32[2,2]{1,0:T(2,128)S(1)}, u32[]{:S(2)}, u32[]{:S(2)}) collective-permute-start(s32[2,2]{1,0:T(2,128)S(1)} %pad_add_fusion.table_ref), channel_id=1, source_target_pairs={{0,1},{1,0},{2,3},{3,2},{4,5},{5,4},{6,7},{7,6},{8,9},{9,8},{10,11... | collective-permute-start | bytes 56 | tf_op jit(solution)/shard_map/ppermute | solution.py:29
  67.4 1.4 %copy-start.11 = (s32[2,2]{1,0:T(2,128)}, s32[2,2]{1,0:T(2,128)S(1)}, u32[]{:S(2)}) copy-start(s32[2,2]{1,0:T(2,128)S(1)} %collective-permute-done.9.theirs_ref) | copy-start | bytes 52
  67.4 12.9 %collective-permute-start.2 = (bf16[9,128,128]{2,1,0:T(8,128)(2,1)}, bf16[9,128,128]{2,1,0:T(8,128)(2,1)S(1)}, u32[]{:S(2)}, u32[]{:S(2)}) collective-permute-start(bf16[9,128,128]{2,1,0:T(8,128)(2,1)} %later.1), channel_id=1, source_target_pairs={{0,16},{1,17},{2,18},{3,19},{4,20},{5,21},{6,22},{7,23},{8,24},{9,... | collective-permute-start | bytes 884744 | tf_op jit(solution)/shard_map/ppermute | solution.py:24
  68.7 0.8 copy-start.5
  68.7 0.9 copy-start.6
  72.6 46.8 %collective-permute-start.10 = (bf16[512,896]{1,0:T(8,128)(2,1)}, bf16[512,896]{1,0:T(8,128)(2,1)S(1)}, u32[]{:S(2)}, u32[]{:S(2)}) collective-permute-start(bf16[512,896]{1,0:T(8,128)(2,1)} %gather.1), channel_id=1, source_target_pairs={{0,1},{1,0},{2,3},{3,2},{4,5},{5,4},{6,7},{7,6},{8,9},{9,8},{10,11... | collective-permute-start | bytes 2752520 | tf_op jit(solution)/shard_map/ppermute | solution.py:29
  80.3 0.7 copy-start.8
  89.0 41.8 %all-to-all-start.1 = ((bf16[16,128,128]{2,1,0:T(8,128)(2,1)}), bf16[16,128,128]{2,1,0:T(8,128)(2,1)S(1)}, u32[]{:S(2)}, u32[]{:S(2)}) async-start(bf16[16,128,128]{2,1,0:T(8,128)(2,1)} %previous.1), calls=%async_computation.1 | async-start | bytes 1048576 | tf_op jit(solution)/shard_map/all_to_all | solution.py:500
  119.4 0.9 copy-start.7
  130.9 0.8 copy-start.1

commit v4 on v3

--- a/solution.py
+++ b/solution.py
@@ -147,49 +147,36 @@
     return jnp.where(sublane < 64, values[0], values[1]).T
 
 
-def previous_kernel(scale, flag_ref, *refs):
-    in_refs, out_ref = refs[:5], refs[5]
-    q_ref, kv_ref, back_ref, out1_ref, stat_ref = bufs = refs[6:11]
-    sems = refs[11]
+def merged(parts, scale):
+    top = functools.reduce(jnp.maximum, [largest for _, largest, _ in parts])
+    weights = [jnp.exp2((largest - top) * scale) for _, largest, _ in parts]
+    total = sum(w * t for w, (_, _, t) in zip(weights, parts))
+    return sum(w * out for w, (out, _, _) in zip(weights, parts)), top, total
+
+
+def previous_kernel(scale, flag_ref, q_ref, kv_ref, out1_ref, stat1_ref, out_ref, part_ref, stat_ref):
     blocks, rows, dim = q_ref.shape
-    sent = back_ref.shape[0] - 1
+    waiting = part_ref.shape[0]
     later = triangle(2 * rows, lambda column, row: column > row)
 
-    def copy(n, i):
-        if i is None:
-            return pltpu.make_async_copy(in_refs[n], bufs[n], sems.at[n, 0])
-        source = in_refs[n].at[i : i + 2, 0 : bufs[n].shape[1], :]
-        return pltpu.make_async_copy(source, bufs[n].at[i : i + 2], sems.at[n, i // 2])
-
-    whole = [copy(n, None) for n in (1, 2)]
-    paired = {i: [copy(n, i) for n in (0, 3, 4)] for i in range(0, blocks, 2)}
-    order = list(range(0, blocks, 2))[::-1]
-    whole[0].start()
-    for i in order:
-        for c in paired[i]:
-            c.start()
-        if i == order[0]:
-            whole[1].start()
-
-    def store(i, parts):
-        top = functools.reduce(jnp.maximum, [largest for _, largest, _ in parts])
-        weights = [jnp.exp2((largest - top) * scale) for _, largest, _ in parts]
-        inverse = 1.0 / sum(w * total for w, (_, _, total) in zip(weights, parts))
-        merged = sum((w * inverse) * out for w, (out, _, _) in zip(weights, parts))
-        out_ref[i : i + 2] = merged.reshape(2, rows, dim).astype(out_ref.dtype)
-
     def own_part(i):
-        stat = stat_ref[i : i + 2].reshape(2 * rows, 128)
+        stat = stat1_ref[i : i + 2].reshape(2 * rows, 128)
         return (out1_ref[i : i + 2].reshape(2 * rows, dim), *halves(stat))
+
+    def store(i, part):
+        out, largest, total = part
+        if i < waiting:
+            part_ref[i : i + 2] = out.reshape(2, rows, dim)
+            stat_ref[i : i + 2] = with_stats(largest, total).reshape(2, rows, 128)
+        else:
+            out = out * (1.0 / total)
+            out_ref[i : i + 2] = out.reshape(2, rows, dim).astype(out_ref.dtype)
 
     @pl.when(flag_ref[0] > 0)
     def _():
-        whole[0].wait()
-        for i in order:
-            for c in paired[i]:
-                c.wait()
-            first = max(i - sent, 0)
-            spans = [(first, 2, later)] if i >= sent else []
+        for i in range(0, blocks, 2):
+            first = max(i - waiting, 0)
+            spans = [(first, 2, later)] if i >= waiting else []
             first += 2 * len(spans)
             if first < kv_ref.shape[0]:
                 spans.append((first, kv_ref.shape[0] - first, None))
@@ -197,22 +184,32 @@
                 (taken(kv_ref, f, n, 0, rows), taken(kv_ref, f, n, rows, rows), mask)
                 for f, n, mask in spans
             ]
-            parts = [softmax_parts(taken(q_ref, i, 2, 0, rows), pieces, scale), own_part(i)]
-            if i < sent:
-                if i == sent - 2:
-                    whole[1].wait()
-                stat = jnp.concatenate([sent_stats(back_ref, i + n, rows) for n in range(2)], axis=0)
-                parts.append((taken(back_ref, i, 2, 0, rows).astype(jnp.float32), *halves(stat)))
-            store(i, parts)
+            part = softmax_parts(taken(q_ref, i, 2, 0, rows), pieces, scale)
+            store(i, merged([part, own_part(i)], scale))
 
     @pl.when(flag_ref[0] == 0)
     def _():
-        for c in whole:
-            c.wait()
-        for i in order:
-            for c in paired[i]:
-                c.wait()
-            store(i, [own_part(i)])
+        part_ref[...] = out1_ref[0:waiting]
+        stat_ref[...] = stat1_ref[0:waiting]
+        for i in range(waiting, blocks, 2):
+            store(i, own_part(i))
+
+
+def merge_kernel(scale, flag_ref, part_ref, stat_ref, back_ref, rest_ref, out_ref, done_ref, sem):
+    del rest_ref
+    blocks, rows, dim = part_ref.shape
+    for i in range(0, blocks, 2):
+        stat = stat_ref[i : i + 2].reshape(2 * rows, 128)
+        parts = [(part_ref[i : i + 2].reshape(2 * rows, dim), *halves(stat))]
+        stat = jnp.concatenate([sent_stats(back_ref, i + n, rows) for n in range(2)], axis=0)
+        largest, total = halves(stat)
+        largest = jnp.where(flag_ref[0] > 0, largest, MASKED_SCORE)
+        parts.append((taken(back_ref, i, 2, 0, rows).astype(jnp.float32), largest, total))
+        out, _, total = merged(parts, scale)
+        done_ref[i : i + 2] = (out * (1.0 / total)).reshape(2, rows, dim).astype(done_ref.dtype)
+    copy = pltpu.make_async_copy(done_ref, out_ref.at[0:blocks], sem)
+    copy.start()
+    copy.wait()
 
 
 def estimate(area, arrays):
@@ -243,30 +240,50 @@
         cost_estimate=estimate(area, (x,)),
         name="own",
     )(x)
+    smem = pl.BlockSpec(memory_space=pltpu.SMEM)
+
+    def first_blocks(count, height):
+        return pl.BlockSpec((count, height, HEAD_DIM), lambda *_: (0, 0, 0))
+
     answer = pl.pallas_call(
         functools.partial(later_kernel, scale),
         out_shape=jax.ShapeDtypeStruct((LEFT + 1, rows, HEAD_DIM), jnp.bfloat16),
+        grid=(1,),
+        in_specs=[first_blocks(LEFT, rows), first_blocks(LEFT, 3 * rows)],
+        out_specs=first_blocks(LEFT + 1, rows),
         cost_estimate=estimate(small, (asked,)),
         name="later",
     )(asked, x)
     back = shifted(answer, "ctx", heads)
-    return pl.pallas_call(
+    flag = chunk.reshape(1)
+    all_blocks = first_blocks(heads, rows)
+    rest, part, stat = pl.pallas_call(
         functools.partial(previous_kernel, scale),
-        out_shape=jax.ShapeDtypeStruct((heads, rows, HEAD_DIM), jnp.bfloat16),
-        in_specs=[pl.BlockSpec(memory_space=pltpu.SMEM)]
-        + [pl.BlockSpec(memory_space=pl.ANY)] * 5,
-        out_specs=pl.BlockSpec(memory_space=pltpu.VMEM),
-        scratch_shapes=[
-            pltpu.VMEM((heads, rows, HEAD_DIM), x.dtype),
-            pltpu.VMEM(arriving.shape, arriving.dtype),
-            pltpu.VMEM(back.shape, back.dtype),
-            pltpu.VMEM(out1.shape, out1.dtype),
-            pltpu.VMEM(stat.shape, stat.dtype),
-            pltpu.SemaphoreType.DMA((5, heads // 2)),
-        ],
+        out_shape=(
+            jax.ShapeDtypeStruct((heads, rows, HEAD_DIM), jnp.bfloat16),
+            jax.ShapeDtypeStruct((LEFT, rows, HEAD_DIM), jnp.float32),
+            jax.ShapeDtypeStruct((LEFT, rows, 128), jnp.float32),
+        ),
+        grid=(1,),
+        in_specs=[smem, all_blocks, first_blocks(heads - LEFT, 2 * rows), all_blocks, all_blocks],
+        out_specs=(all_blocks, first_blocks(LEFT, rows), first_blocks(LEFT, rows)),
         cost_estimate=estimate(area - small, (x, out1, stat)),
         name="previous",
-    )(chunk.reshape(1), x, arriving, back, out1, stat)
+    )(flag, x, arriving, out1, stat)
+    vmem, anywhere = (pl.BlockSpec(memory_space=m) for m in (pltpu.VMEM, pl.ANY))
+    return pl.pallas_call(
+        functools.partial(merge_kernel, scale),
+        out_shape=jax.ShapeDtypeStruct(rest.shape, rest.dtype),
+        in_specs=[smem, vmem, vmem, vmem, anywhere],
+        out_specs=anywhere,
+        input_output_aliases={4: 0},
+        scratch_shapes=[
+            pltpu.VMEM((LEFT, rows, HEAD_DIM), rest.dtype),
+            pltpu.SemaphoreType.DMA(()),
+        ],
+        cost_estimate=estimate(0, (part, stat, back)),
+        name="merge",
+    )(flag, part, stat, back, rest)
 
 
 def wanted_pieces(table_ref, position, span_count):

time: 135 us -> 136 us (level)
  starting transfers between devices: 59.4 us -> 52.2 us
  Pallas kernels: 43.8 us -> 47.9 us
  waiting for transfers between devices: 25 us -> 27.4 us
  local copies, waits for them, and re-layouts: 4.13 us -> 5.74 us
    all_to_all x1, starting transfers between devices: 24.5 us -> 13.3 us  [per_device(): lax.all_to_all(by_head, 'ctx', 0, 0, axis_index_groups=groups, tiled=True)]
    pallas_call x1 -> x2, Pallas kernels: 8.04 us -> 12.5 us  [the longest x1 9.55 us: self_attention(): pl.pallas_call(functools.partial(previous_kernel, scale), out_shape=(jax....]
    ppermute x6, starting transfers between devices: 18.8 us -> 22.8 us  [shifted(): lax.ppermute(value, axis, [(source, source + steps) for source in range(f...]
    ppermute x6, waiting for transfers between devices: 25 us -> 27.4 us  [shifted(): lax.ppermute(value, axis, [(source, source + steps) for source in range(f...]
    unnamed x28 -> x30, local copies, waits for them, and re-layouts: 4.07 us -> 4.84 us
  transfers between devices with their start and end apart: 13 -> 13, of which waited for: 5 -> 4; matrix products, arithmetic and copies ran while one was open for 1% -> 2% of each run, Pallas kernels for 29% -> 32%
where the time goes in v4:
time: 136 us; the launch traced here: 135 us
  starting transfers between devices  52.2 us (38%)
  Pallas kernels  47.9 us (35%)
  waiting for transfers between devices  27.4 us (20%)
  local copies, waits for them, and re-layouts  5.74 us (4%)
    ppermute x6, waiting for transfers between devices, shifted(): lax.ppermute(value, axis, [(source, source + steps) for source in range(f...  27.4 us
    ppermute x6, starting transfers between devices, shifted(): lax.ppermute(value, axis, [(source, source + steps) for source in range(f...  22.8 us
    all_to_all x1, starting transfers between devices, per_device(): lax.all_to_all(by_head, 'ctx', 0, 0, axis_index_groups=groups, tiled=True)  13.3 us
    pallas_call x1, Pallas kernels, cross_attention(): pl.pallas_call(functools.partial(cross_kernel, HEAD_DIM ** (-0.5) * LOG2E...  10.5 us
    ppermute x5, starting transfers between devices, swapped(): lax.ppermute(value, axis, [(source, source ^ bit) for source in range(cou...  10.4 us
    pallas_call x1, Pallas kernels, self_attention(): pl.pallas_call(functools.partial(previous_kernel, scale), out_shape=(jax....  9.55 us
    pallas_call x1, Pallas kernels, self_attention(): pl.pallas_call(functools.partial(own_kernel, scale), out_shape=(jax.Shape...  7.19 us
    pallas_call x1, Pallas kernels, cross_attention(): pl.pallas_call(absorb_kernel, out_shape=jax.ShapeDtypeStruct((span_count,...  5.82 us
  transfers between devices with their start and end apart: 13, of which 4 were waited for; matrix products, arithmetic and copies ran while one was open for 2% of the time, Pallas kernels for 32%

profile of v4, /device:TPU:23, one launch (start us, length us, event | category | flops | bytes accessed | tf_op | source)
XLA Modules:
  0.0 134.8 jit_solution(618231358518486222)
XLA Ops:
  0.0 0.0 copy-start.3
  0.0 2.9 %pack.1 = bf16[16,384,128]{2,1,0:T(8,128)(2,1)} custom-call(bf16[128,2048]{1,0:T(8,128)(2,1)} %refs_0_.3, bf16[128,2048]{1,0:T(8,128)(2,1)} %refs_1_.1, bf16[128,2048]{1,0:T(8,128)(2,1)} %refs_2_.1), custom_call_target="tpu_custom_call" | custom-call | bytes 3145728 | tf_op jit(solution)/shard_map/pack/pallas_call | solution.py:43
  2.9 0.0 copy-start.13
  2.9 0.0 copy-start.14
  2.9 5.6 %all-to-all-start = ((bf16[16,384,128]{2,1,0:T(8,128)(2,1)}), bf16[16,384,128]{2,1,0:T(8,128)(2,1)S(1)}, u32[]{:S(2)}, u32[]{:S(2)}) async-start(bf16[16,384,128]{2,1,0:T(8,128)(2,1)} %pack.1), calls=%async_computation | async-start | bytes 3145728 | tf_op jit(solution)/shard_map/all_to_all | solution.py:227
  8.5 0.0 copy-done.3
  8.5 3.1 %collective-permute-start.4 = (bf16[128,896]{1,0:T(8,128)(2,1)S(1)}, bf16[128,896]{1,0:T(8,128)(2,1)S(1)}, u32[]{:S(2)}, u32[]{:S(2)}) collective-permute-start(bf16[128,896]{1,0:T(8,128)(2,1)S(1)} %copy-done.3), channel_id=1, source_target_pairs={{0,8},{1,9},{2,10},{3,11},{4,12},{5,13},{6,14},{7,15},{8,16},{9,17... | collective-permute-start | bytes 688136 | tf_op jit(solution)/shard_map/ppermute | solution.py:24
  11.6 19.5 %collective-permute-done.4.refs_1_ = bf16[128,896]{1,0:T(8,128)(2,1)S(1)} collective-permute-done((bf16[128,896]{1,0:T(8,128)(2,1)S(1)}, bf16[128,896]{1,0:T(8,128)(2,1)S(1)}, u32[]{:S(2)}, u32[]{:S(2)}) %collective-permute-start.4) | collective-permute-done | bytes 229408 | tf_op jit(solution)/shard_map/ppermute | solution.py:24
  31.1 0.0 copy-start.2
  31.1 4.1 %collective-permute-start.5 = (bf16[128,896]{1,0:T(8,128)(2,1)S(1)}, bf16[128,896]{1,0:T(8,128)(2,1)S(1)}, u32[]{:S(2)}, u32[]{:S(2)}) collective-permute-start(bf16[128,896]{1,0:T(8,128)(2,1)S(1)} %collective-permute-done.4.refs_1_), channel_id=1, source_target_pairs={{0,8},{1,9},{2,10},{3,11},{4,12},{5,13},{6,14},{7,15},{8,16},{9,17... | collective-permute-start | bytes 688136 | tf_op jit(solution)/shard_map/ppermute | solution.py:24
  35.3 4.0 %collective-permute-done.5.refs_2_ = bf16[128,896]{1,0:T(8,128)(2,1)S(1)} collective-permute-done((bf16[128,896]{1,0:T(8,128)(2,1)S(1)}, bf16[128,896]{1,0:T(8,128)(2,1)S(1)}, u32[]{:S(2)}, u32[]{:S(2)}) %collective-permute-start.5) | collective-permute-done | bytes 229408 | tf_op jit(solution)/shard_map/ppermute | solution.py:24
  39.2 0.0 copy-start.4
  39.2 0.1 broadcast_select_fusion
  39.3 1.1 pad_maximum_fusion
  40.4 0.2 collective-permute-start.6
  40.7 0.9 collective-permute-start.7
  41.6 1.5 %collective-permute-start.8 = (bf16[256,896]{1,0:T(8,128)(2,1)}, bf16[256,896]{1,0:T(8,128)(2,1)}, u32[]{:S(2)}, u32[]{:S(2)}) collective-permute-start(bf16[256,896]{1,0:T(8,128)(2,1)} %get-tuple-element.18), channel_id=1, source_target_pairs={{0,6},{1,7},{2,4},{3,5},{4,2},{5,3},{6,0},{7,1},{8,14},{9,15},{10,... | collective-permute-start | bytes 1376264 | tf_op jit(solution)/shard_map/ppermute | solution.py:29
  43.1 0.0 all-to-all-done.x_ref.q_ref
  43.1 0.9 slice.16
  44.0 1.3 collective-permute-start
  45.3 0.0 copy-done.13
  45.3 0.0 copy-done.14
  45.3 0.1 multiply_add_fusion
  45.3 6.8 %collective-permute-start.3 = (s32[2,2]{1,0:T(2,128)S(1)}, s32[2,2]{1,0:T(2,128)S(1)}, u32[]{:S(2)}, u32[]{:S(2)}) collective-permute-start(s32[2,2]{1,0:T(2,128)S(1)} %multiply_add_fusion), channel_id=1, source_target_pairs={{0,1},{1,2},{2,3},{3,4},{4,5},{5,6},{6,7},{7,8},{8,9},{9,10},{10,1... | collective-permute-start | bytes 56 | tf_op jit(solution)/shard_map/ppermute | solution.py:24
  52.2 0.7 collective-permute-done.3
  52.9 6.3 %collective-permute-start.1 = (bf16[8,128,128]{2,1,0:T(8,128)(2,1)S(1)}, bf16[8,128,128]{2,1,0:T(8,128)(2,1)S(1)}, u32[]{:S(2)}, u32[]{:S(2)}) collective-permute-start(bf16[8,128,128]{2,1,0:T(8,128)(2,1)S(1)} %slice.17), channel_id=1, source_target_pairs={{16,0},{17,1},{18,2},{19,3},{20,4},{21,5},{22,6},{23,7},{24,8},{25... | collective-permute-start | bytes 786440 | tf_op jit(solution)/shard_map/ppermute | solution.py:24
  59.2 0.0 copy-start.11
  59.2 3.2 %collective-permute-done.1.q_ref = bf16[8,128,128]{2,1,0:T(8,128)(2,1)S(1)} collective-permute-done((bf16[8,128,128]{2,1,0:T(8,128)(2,1)S(1)}, bf16[8,128,128]{2,1,0:T(8,128)(2,1)S(1)}, u32[]{:S(2)}, u32[]{:S(2)}) %collective-permute-start.1) | collective-permute-done | bytes 262176 | tf_op jit(solution)/shard_map/ppermute | solution.py:24
  62.4 0.7 copy-done.10
  63.1 7.6 %collective-permute-start.9 = (s32[2,2]{1,0:T(2,128)S(1)}, s32[2,2]{1,0:T(2,128)S(1)}, u32[]{:S(2)}, u32[]{:S(2)}) collective-permute-start(s32[2,2]{1,0:T(2,128)S(1)} %pad_add_fusion.table_ref), channel_id=1, source_target_pairs={{0,1},{1,0},{2,3},{3,2},{4,5},{5,4},{6,7},{7,6},{8,9},{9,8},{10,11... | collective-permute-start | bytes 56 | tf_op jit(solution)/shard_map/ppermute | solution.py:29
  70.8 0.0 copy-done
  70.8 3.9 %later.1 = bf16[9,128,128]{2,1,0:T(8,128)(2,1)} custom-call(bf16[8,128,128]{2,1,0:T(8,128)(2,1)} %copy-done.10, bf16[16,384,128]{2,1,0:T(8,128)(2,1)} %copy-done), custom_call_target="tpu_custom_call" | custom-call | flops 268435456 | bytes 262144 | tf_op jit(solution)/shard_map/later/pallas_call | solution.py:248
  74.6 0.0 collective-permute-done.9.theirs_ref
  74.6 1.3 collective-permute-start.2
  75.9 0.0 collective-permute-done.6.refs_3_
  76.0 0.0 copy-start.5
  76.0 0.0 collective-permute-done.7.refs_4_
  76.0 0.0 copy-start.6
  76.0 0.0 collective-permute-done.8.refs_5_
  76.0 0.0 copy-done.2
  76.0 0.0 copy-done.4
  76.0 0.0 copy-done.12
  76.0 0.7 copy-done.5
  76.7 0.2 copy-done.6
  76.9 2.9 %gather.1 = bf16[512,896]{1,0:T(8,128)(2,1)} custom-call(s32[1]{0:T(128)} %bitcast.1.position_ref, s32[2,2]{1,0:T(2,128)} %copy-done.12, bf16[128,896]{1,0:T(8,128)(2,1)} %refs_0_.5, bf16[128,896]{1,0:T(8,128)(2,1)} %copy-done.2, bf16[128,896]{1,0:T(8,128)(2,1)} %copy-done.4, bf16[256,896]{1,0:T(8,128)(2,1)} %copy-done.5, bf16[256,896]{1,0:T(8,128)(2,1)} %copy-done.6, ...), custom_call_target="tpu_custom_call" | custom-call | bytes 3670016 | tf_op jit(solution)/shard_map/gather/pallas_call | solution.py:444
  79.8 0.1 collective-permute-start.10
  79.9 7.2 %own.1 = (f32[16,128,128]{2,1,0:T(8,128)}, f32[16,128,128]{2,1,0:T(8,128)}) custom-call(bf16[16,384,128]{2,1,0:T(8,128)(2,1)} %copy-done), custom_call_target="tpu_custom_call" | custom-call | flops 1073741824 | bytes 1572864 | tf_op jit(solution)/shard_map/own/pallas_call | solution.py:234
  87.1 0.0 collective-permute-done.kv_ref
  87.1 0.8 copy-done.8
  87.9 9.6 %previous.1 = (bf16[16,128,128]{2,1,0:T(8,128)(2,1)}, f32[8,128,128]{2,1,0:T(8,128)}, f32[8,128,128]{2,1,0:T(8,128)}) custom-call(s32[1]{0:T(128)} %bitcast.flag_ref, bf16[16,384,128]{2,1,0:T(8,128)(2,1)} %copy-done, bf16[8,256,128]{2,1,0:T(8,128)(2,1)} %copy-done.8, f32[16,128,128]{2,1,0:T(8,128)} %get-tuple-element.10.out1_ref, ...), custom_call_target="tpu_custom_call" | custom-call | flops 805306368 | bytes 2621440 | tf_op jit(solution)/shard_map/previous/pallas_call | solution.py:260
  97.5 0.0 collective-permute-done.2.back_ref
  97.5 0.7 copy-done.9
  98.2 2.9 %merge.1 = bf16[16,128,128]{2,1,0:T(8,128)(2,1)} custom-call(s32[1]{0:T(128)} %bitcast.flag_ref, f32[8,128,128]{2,1,0:T(8,128)} %get-tuple-element.12.part_ref, f32[8,128,128]{2,1,0:T(8,128)} %get-tuple-element.13.stat_ref, bf16[9,128,128]{2,1,0:T(8,128)(2,1)} %copy-done.9, ...), custom_call_target="tpu_custom_call", output_to_operand_aliasing={{}: (4, {})} | custom-call | bytes 819200 | tf_op jit(solution)/shard_map/merge/pallas_call | solution.py:274
  101.1 13.3 %all-to-all-start.1 = ((bf16[16,128,128]{2,1,0:T(8,128)(2,1)}), bf16[16,128,128]{2,1,0:T(8,128)(2,1)S(1)}, u32[]{:S(2)}, u32[]{:S(2)}) async-start(bf16[16,128,128]{2,1,0:T(8,128)(2,1)} %merge.1), calls=%async_computation.1 | async-start | bytes 1048576 | tf_op jit(solution)/shard_map/all_to_all | solution.py:517
  114.4 5.8 %absorb.1.refs_7_ = bf16[2,1024,896]{2,1,0:T(8,128)(2,1)} custom-call(bf16[128,2048]{1,0:T(8,128)(2,1)} %q_ref.1, bf16[896,4096]{1,0:T(8,128)(2,1)} %refs_8_.1), custom_call_target="tpu_custom_call" | custom-call | flops 469762048 | bytes 7340032 | tf_op jit(solution)/shard_map/absorb/pallas_call | solution.py:460
  120.3 0.0 copy-done.11
  120.3 0.0 collective-permute-done.10.refs_6_
  120.3 0.0 copy-start.7
  120.3 0.9 copy-done.7
  121.2 10.5 %cross.1.cross_ref = f32[128,2048]{1,0:T(8,128)} custom-call(s32[1]{0:T(128)} %bitcast.1.position_ref, s32[2,2]{1,0:T(2,128)} %copy-done.11, bf16[128,896]{1,0:T(8,128)(2,1)} %refs_0_.5, bf16[128,896]{1,0:T(8,128)(2,1)} %copy-done.2, bf16[128,896]{1,0:T(8,128)(2,1)} %copy-done.4, bf16[256,896]{1,0:T(8,128)(2,1)} %copy-done.5, bf16[256,896]{1,0:T(8,128)(2,1)} %copy-done.6, ...), custom_call_target="tpu_custom_call" | custom-call | flops 2348810240 | bytes 9175040 | tf_op jit(solution)/shard_map/cross/pallas_call | solution.py:481
  131.7 0.0 all-to-all-done.1.self_ref
  131.7 0.0 copy-start.1
  131.7 0.8 copy-done.1
  132.5 2.3 %total.1 = bf16[128,2048]{1,0:T(8,128)(2,1)} custom-call(bf16[16,128,128]{2,1,0:T(8,128)(2,1)} %copy-done.1, f32[128,2048]{1,0:T(8,128)} %cross.1.cross_ref), custom_call_target="tpu_custom_call" | custom-call | tf_op jit(solution)/shard_map/total/pallas_call | solution.py:518
  (9 shorter events, 0.0 us)
Async XLA Ops:
  0.0 8.5 %copy-start.3 = (bf16[128,896]{1,0:T(8,128)(2,1)S(1)}, bf16[128,896]{1,0:T(8,128)(2,1)}, u32[]{:S(2)}) copy-start(bf16[128,896]{1,0:T(8,128)(2,1)} %refs_0_.5) | copy-start | bytes 688132
  2.9 42.4 %copy-start.13 = (s32[2,2]{1,0:T(2,128)S(1)}, s32[2,2]{1,0:T(2,128)}, u32[]{:S(2)}) copy-start(s32[2,2]{1,0:T(2,128)} %param.15) | copy-start | bytes 52
  2.9 42.4 %copy-start.14 = (s32[2]{0:T(128)S(1)}, s32[2]{0:T(128)}, u32[]{:S(2)}) copy-start(s32[2]{0:T(128)} %param.14) | copy-start | bytes 28
  2.9 40.2 %all-to-all-start = ((bf16[16,384,128]{2,1,0:T(8,128)(2,1)}), bf16[16,384,128]{2,1,0:T(8,128)(2,1)S(1)}, u32[]{:S(2)}, u32[]{:S(2)}) async-start(bf16[16,384,128]{2,1,0:T(8,128)(2,1)} %pack.1), calls=%async_computation | async-start | bytes 3145728 | tf_op jit(solution)/shard_map/all_to_all | solution.py:227
  8.5 22.6 %collective-permute-start.4 = (bf16[128,896]{1,0:T(8,128)(2,1)S(1)}, bf16[128,896]{1,0:T(8,128)(2,1)S(1)}, u32[]{:S(2)}, u32[]{:S(2)}) collective-permute-start(bf16[128,896]{1,0:T(8,128)(2,1)S(1)} %copy-done.3), channel_id=1, source_target_pairs={{0,8},{1,9},{2,10},{3,11},{4,12},{5,13},{6,14},{7,15},{8,16},{9,17... | collective-permute-start | bytes 688136 | tf_op jit(solution)/shard_map/ppermute | solution.py:24
  31.1 44.9 %copy-start.2 = (bf16[128,896]{1,0:T(8,128)(2,1)}, bf16[128,896]{1,0:T(8,128)(2,1)S(1)}, u32[]{:S(2)}) copy-start(bf16[128,896]{1,0:T(8,128)(2,1)S(1)} %collective-permute-done.4.refs_1_) | copy-start | bytes 688132
  31.1 8.1 %collective-permute-start.5 = (bf16[128,896]{1,0:T(8,128)(2,1)S(1)}, bf16[128,896]{1,0:T(8,128)(2,1)S(1)}, u32[]{:S(2)}, u32[]{:S(2)}) collective-permute-start(bf16[128,896]{1,0:T(8,128)(2,1)S(1)} %collective-permute-done.4.refs_1_), channel_id=1, source_target_pairs={{0,8},{1,9},{2,10},{3,11},{4,12},{5,13},{6,14},{7,15},{8,16},{9,17... | collective-permute-start | bytes 688136 | tf_op jit(solution)/shard_map/ppermute | solution.py:24
  39.2 36.8 %copy-start.4 = (bf16[128,896]{1,0:T(8,128)(2,1)}, bf16[128,896]{1,0:T(8,128)(2,1)S(1)}, u32[]{:S(2)}) copy-start(bf16[128,896]{1,0:T(8,128)(2,1)S(1)} %collective-permute-done.5.refs_2_) | copy-start | bytes 688132
  40.4 35.5 %collective-permute-start.6 = (bf16[256,896]{1,0:T(8,128)(2,1)}, bf16[256,896]{1,0:T(8,128)(2,1)S(1)}, u32[]{:S(2)}, u32[]{:S(2)}) collective-permute-start(bf16[256,896]{1,0:T(8,128)(2,1)} %get-tuple-element.20), channel_id=1, source_target_pairs={{0,2},{1,3},{2,0},{3,1},{4,6},{5,7},{6,4},{7,5},{8,10},{9,11},{10,... | collective-permute-start | bytes 1376264 | tf_op jit(solution)/shard_map/ppermute | solution.py:29
  40.7 35.3 %collective-permute-start.7 = (bf16[256,896]{1,0:T(8,128)(2,1)}, bf16[256,896]{1,0:T(8,128)(2,1)S(1)}, u32[]{:S(2)}, u32[]{:S(2)}) collective-permute-start(bf16[256,896]{1,0:T(8,128)(2,1)} %get-tuple-element.19), channel_id=1, source_target_pairs={{0,4},{1,5},{2,6},{3,7},{4,0},{5,1},{6,2},{7,3},{8,12},{9,13},{10,... | collective-permute-start | bytes 1376264 | tf_op jit(solution)/shard_map/ppermute | solution.py:29
  41.6 34.4 %collective-permute-start.8 = (bf16[256,896]{1,0:T(8,128)(2,1)}, bf16[256,896]{1,0:T(8,128)(2,1)}, u32[]{:S(2)}, u32[]{:S(2)}) collective-permute-start(bf16[256,896]{1,0:T(8,128)(2,1)} %get-tuple-element.18), channel_id=1, source_target_pairs={{0,6},{1,7},{2,4},{3,5},{4,2},{5,3},{6,0},{7,1},{8,14},{9,15},{10,... | collective-permute-start | bytes 1376264 | tf_op jit(solution)/shard_map/ppermute | solution.py:29
  43.1 27.7 %copy-start = (bf16[16,384,128]{2,1,0:T(8,128)(2,1)}, bf16[16,384,128]{2,1,0:T(8,128)(2,1)S(1)}, u32[]{:S(2)}) copy-start(bf16[16,384,128]{2,1,0:T(8,128)(2,1)S(1)} %all-to-all-done.x_ref.q_ref) | copy-start | bytes 4718596
  44.0 43.1 %collective-permute-start = (bf16[8,256,128]{2,1,0:T(8,128)(2,1)}, bf16[8,256,128]{2,1,0:T(8,128)(2,1)S(1)}, u32[]{:S(2)}, u32[]{:S(2)}) collective-permute-start(bf16[8,256,128]{2,1,0:T(8,128)(2,1)} %slice.16), channel_id=1, source_target_pairs={{0,16},{1,17},{2,18},{3,19},{4,20},{5,21},{6,22},{7,23},{8,24},{9,... | collective-permute-start | bytes 1572872 | tf_op jit(solution)/shard_map/ppermute | solution.py:24
  45.3 7.5 %collective-permute-start.3 = (s32[2,2]{1,0:T(2,128)S(1)}, s32[2,2]{1,0:T(2,128)S(1)}, u32[]{:S(2)}, u32[]{:S(2)}) collective-permute-start(s32[2,2]{1,0:T(2,128)S(1)} %multiply_add_fusion), channel_id=1, source_target_pairs={{0,1},{1,2},{2,3},{3,4},{4,5},{5,6},{6,7},{7,8},{8,9},{9,10},{10,1... | collective-permute-start | bytes 56 | tf_op jit(solution)/shard_map/ppermute | solution.py:24
  52.9 9.5 %collective-permute-start.1 = (bf16[8,128,128]{2,1,0:T(8,128)(2,1)S(1)}, bf16[8,128,128]{2,1,0:T(8,128)(2,1)S(1)}, u32[]{:S(2)}, u32[]{:S(2)}) collective-permute-start(bf16[8,128,128]{2,1,0:T(8,128)(2,1)S(1)} %slice.17), channel_id=1, source_target_pairs={{16,0},{17,1},{18,2},{19,3},{20,4},{21,5},{22,6},{23,7},{24,8},{25... | collective-permute-start | bytes 786440 | tf_op jit(solution)/shard_map/ppermute | solution.py:24
  59.2 61.1 %copy-start.11 = (s32[2,2]{1,0:T(2,128)}, s32[2,2]{1,0:T(2,128)S(1)}, u32[]{:S(2)}) copy-start(s32[2,2]{1,0:T(2,128)S(1)} %pad_add_fusion.table_ref) | copy-start | bytes 52
  62.4 0.7 copy-start.10
  63.1 11.5 %collective-permute-start.9 = (s32[2,2]{1,0:T(2,128)S(1)}, s32[2,2]{1,0:T(2,128)S(1)}, u32[]{:S(2)}, u32[]{:S(2)}) collective-permute-start(s32[2,2]{1,0:T(2,128)S(1)} %pad_add_fusion.table_ref), channel_id=1, source_target_pairs={{0,1},{1,0},{2,3},{3,2},{4,5},{5,4},{6,7},{7,6},{8,9},{9,8},{10,11... | collective-permute-start | bytes 56 | tf_op jit(solution)/shard_map/ppermute | solution.py:29
  74.6 1.4 %copy-start.12 = (s32[2,2]{1,0:T(2,128)}, s32[2,2]{1,0:T(2,128)S(1)}, u32[]{:S(2)}) copy-start(s32[2,2]{1,0:T(2,128)S(1)} %collective-permute-done.9.theirs_ref) | copy-start | bytes 52
  74.6 22.8 %collective-permute-start.2 = (bf16[9,128,128]{2,1,0:T(8,128)(2,1)}, bf16[9,128,128]{2,1,0:T(8,128)(2,1)S(1)}, u32[]{:S(2)}, u32[]{:S(2)}) collective-permute-start(bf16[9,128,128]{2,1,0:T(8,128)(2,1)} %later.1), channel_id=1, source_target_pairs={{0,16},{1,17},{2,18},{3,19},{4,20},{5,21},{6,22},{7,23},{8,24},{9,... | collective-permute-start | bytes 884744 | tf_op jit(solution)/shard_map/ppermute | solution.py:24
  76.0 0.8 copy-start.5
  76.0 0.9 copy-start.6
  79.8 40.4 %collective-permute-start.10 = (bf16[512,896]{1,0:T(8,128)(2,1)}, bf16[512,896]{1,0:T(8,128)(2,1)S(1)}, u32[]{:S(2)}, u32[]{:S(2)}) collective-permute-start(bf16[512,896]{1,0:T(8,128)(2,1)} %gather.1), channel_id=1, source_target_pairs={{0,1},{1,0},{2,3},{3,2},{4,5},{5,4},{6,7},{7,6},{8,9},{9,8},{10,11... | collective-permute-start | bytes 2752520 | tf_op jit(solution)/shard_map/ppermute | solution.py:29
  87.1 0.8 copy-start.8
  97.5 0.7 copy-start.9
  101.1 30.6 %all-to-all-start.1 = ((bf16[16,128,128]{2,1,0:T(8,128)(2,1)}), bf16[16,128,128]{2,1,0:T(8,128)(2,1)S(1)}, u32[]{:S(2)}, u32[]{:S(2)}) async-start(bf16[16,128,128]{2,1,0:T(8,128)(2,1)} %merge.1), calls=%async_computation.1 | async-start | bytes 1048576 | tf_op jit(solution)/shard_map/all_to_all | solution.py:517
  120.3 1.0 copy-start.7
  131.7 0.8 copy-start.1

commit v5 on v4

--- a/solution.py
+++ b/solution.py
@@ -12,7 +12,6 @@
 HEAD_DIM = 128
 SPAN = 64
 PLANE = 8
-LEFT = 8
 
 MASKED_SCORE = -1e30
 LOG2E = 1.4426950408889634
@@ -56,15 +55,18 @@
     return lax.dot_general(q, k, (((1,), (1,)), ((), ())), preferred_element_type=jnp.float32)
 
 
-def softmax_parts(q, pieces, scale):
+def softmax_parts(q, pieces, scale, start=None):
     scores = []
     for k, _, mask in pieces:
         s = scores_of(q, k)
         scores.append(s if mask is None else jnp.where(mask, s, MASKED_SCORE))
-    largest = functools.reduce(
-        jnp.maximum, [jnp.max(s, axis=1, keepdims=True) for s in scores]
-    )
+    largest = functools.reduce(jnp.maximum, [jnp.max(s, axis=1, keepdims=True) for s in scores])
     total, out = None, None
+    if start is not None:
+        out, before, total = start
+        largest = jnp.maximum(largest, before)
+        weight = jnp.exp2((before - largest) * scale)
+        out, total = out * weight, total * weight
     for s, (_, v, _) in zip(scores, pieces):
         p = jnp.exp2((s - largest) * scale)
         t = jnp.sum(p, axis=1, keepdims=True)
@@ -147,17 +149,21 @@
     return jnp.where(sublane < 64, values[0], values[1]).T
 
 
-def merged(parts, scale):
-    top = functools.reduce(jnp.maximum, [largest for _, largest, _ in parts])
-    weights = [jnp.exp2((largest - top) * scale) for _, largest, _ in parts]
-    total = sum(w * t for w, (_, _, t) in zip(weights, parts))
-    return sum(w * out for w, (out, _, _) in zip(weights, parts)), top, total
-
-
 def previous_kernel(scale, flag_ref, q_ref, kv_ref, out1_ref, stat1_ref, out_ref, part_ref, stat_ref):
     blocks, rows, dim = q_ref.shape
     waiting = part_ref.shape[0]
+    half = rows // 2
     later = triangle(2 * rows, lambda column, row: column > row)
+
+    def arrived(first, count, start):
+        return jnp.concatenate(
+            [
+                kv_ref[place, start : start + half, :]
+                for block in range(first, first + count)
+                for place in (block, waiting + block)
+            ],
+            axis=0,
+        )
 
     def own_part(i):
         stat = stat1_ref[i : i + 2].reshape(2 * rows, 128)
@@ -178,14 +184,10 @@
             first = max(i - waiting, 0)
             spans = [(first, 2, later)] if i >= waiting else []
             first += 2 * len(spans)
-            if first < kv_ref.shape[0]:
-                spans.append((first, kv_ref.shape[0] - first, None))
-            pieces = [
-                (taken(kv_ref, f, n, 0, rows), taken(kv_ref, f, n, rows, rows), mask)
-                for f, n, mask in spans
-            ]
-            part = softmax_parts(taken(q_ref, i, 2, 0, rows), pieces, scale)
-            store(i, merged([part, own_part(i)], scale))
+            if first < waiting:
+                spans.append((first, waiting - first, None))
+            pieces = [(arrived(f, n, 0), arrived(f, n, half), mask) for f, n, mask in spans]
+            store(i, softmax_parts(taken(q_ref, i, 2, 0, rows), pieces, scale, own_part(i)))
 
     @pl.when(flag_ref[0] == 0)
     def _():
@@ -199,14 +201,19 @@
     del rest_ref
     blocks, rows, dim = part_ref.shape
     for i in range(0, blocks, 2):
-        stat = stat_ref[i : i + 2].reshape(2 * rows, 128)
-        parts = [(part_ref[i : i + 2].reshape(2 * rows, dim), *halves(stat))]
+        out1, largest1, total1 = (
+            part_ref[i : i + 2].reshape(2 * rows, dim),
+            *halves(stat_ref[i : i + 2].reshape(2 * rows, 128)),
+        )
         stat = jnp.concatenate([sent_stats(back_ref, i + n, rows) for n in range(2)], axis=0)
-        largest, total = halves(stat)
-        largest = jnp.where(flag_ref[0] > 0, largest, MASKED_SCORE)
-        parts.append((taken(back_ref, i, 2, 0, rows).astype(jnp.float32), largest, total))
-        out, _, total = merged(parts, scale)
-        done_ref[i : i + 2] = (out * (1.0 / total)).reshape(2, rows, dim).astype(done_ref.dtype)
+        largest2, total2 = halves(stat)
+        largest2 = jnp.where(flag_ref[0] > 0, largest2, MASKED_SCORE)
+        top = jnp.maximum(largest1, largest2)
+        a, b = jnp.exp2((largest1 - top) * scale), jnp.exp2((largest2 - top) * scale)
+        inverse = 1.0 / (a * total1 + b * total2)
+        out2 = taken(back_ref, i, 2, 0, rows).astype(jnp.float32)
+        out = out1 * (a * inverse) + out2 * (b * inverse)
+        done_ref[i : i + 2] = out.reshape(2, rows, dim).astype(done_ref.dtype)
     copy = pltpu.make_async_copy(done_ref, out_ref.at[0:blocks], sem)
     copy.start()
     copy.wait()
@@ -220,17 +227,29 @@
     )
 
 
-def self_attention(queries, keys, values, chunk, groups):
+def self_attention(queries, keys, values, chunk, chunk_place, groups):
     rows, width = queries.shape
     heads = width // HEAD_DIM
     scale = HEAD_DIM ** (-0.5) * LOG2E
     x = lax.all_to_all(
         packed(queries, keys, values), "ctx", 0, 0, axis_index_groups=groups, tiled=True
     )
-    arriving = shifted(x[LEFT:, rows:], "ctx", heads)
-    asked = shifted(x[:LEFT, :rows], "ctx", -heads)
+    count, half, left = lax.axis_size("ctx"), rows // 2, heads // 2
+    pieces = []
+    for n in range(2):
+        steps = left * (n + 1)
+        pairs = [(i, i + steps) for i in range(count - steps) if i % heads >= left]
+        part = slice(n * half, (n + 1) * half)
+        pieces.append(
+            lax.ppermute(jnp.concatenate([keys[part], values[part]], axis=0), "ctx", pairs)
+        )
+    raw = jnp.where(chunk_place < left, pieces[0], pieces[1])
+    arriving = lax.all_to_all(
+        packed(raw), "ctx", 0, 0, axis_index_groups=groups, tiled=True
+    )
+    asked = shifted(x[:left, :rows], "ctx", -heads)
     area = (heads * rows) ** 2 // 2
-    small = (LEFT * rows) ** 2 // 2
+    small = (left * rows) ** 2 // 2
     out1, stat = pl.pallas_call(
         functools.partial(own_kernel, scale),
         out_shape=(
@@ -247,10 +266,10 @@
 
     answer = pl.pallas_call(
         functools.partial(later_kernel, scale),
-        out_shape=jax.ShapeDtypeStruct((LEFT + 1, rows, HEAD_DIM), jnp.bfloat16),
+        out_shape=jax.ShapeDtypeStruct((left + 1, rows, HEAD_DIM), jnp.bfloat16),
         grid=(1,),
-        in_specs=[first_blocks(LEFT, rows), first_blocks(LEFT, 3 * rows)],
-        out_specs=first_blocks(LEFT + 1, rows),
+        in_specs=[first_blocks(left, rows), first_blocks(left, 3 * rows)],
+        out_specs=first_blocks(left + 1, rows),
         cost_estimate=estimate(small, (asked,)),
         name="later",
     )(asked, x)
@@ -261,12 +280,18 @@
         functools.partial(previous_kernel, scale),
         out_shape=(
             jax.ShapeDtypeStruct((heads, rows, HEAD_DIM), jnp.bfloat16),
-            jax.ShapeDtypeStruct((LEFT, rows, HEAD_DIM), jnp.float32),
-            jax.ShapeDtypeStruct((LEFT, rows, 128), jnp.float32),
+            jax.ShapeDtypeStruct((left, rows, HEAD_DIM), jnp.float32),
+            jax.ShapeDtypeStruct((left, rows, 128), jnp.float32),
         ),
         grid=(1,),
-        in_specs=[smem, all_blocks, first_blocks(heads - LEFT, 2 * rows), all_blocks, all_blocks],
-        out_specs=(all_blocks, first_blocks(LEFT, rows), first_blocks(LEFT, rows)),
+        in_specs=[
+            smem,
+            all_blocks,
+            all_blocks,
+            all_blocks,
+            all_blocks,
+        ],
+        out_specs=(all_blocks, first_blocks(left, rows), first_blocks(left, rows)),
         cost_estimate=estimate(area - small, (x, out1, stat)),
         name="previous",
     )(flag, x, arriving, out1, stat)
@@ -278,7 +303,7 @@
         out_specs=anywhere,
         input_output_aliases={4: 0},
         scratch_shapes=[
-            pltpu.VMEM((LEFT, rows, HEAD_DIM), rest.dtype),
+            pltpu.VMEM((left, rows, HEAD_DIM), rest.dtype),
             pltpu.SemaphoreType.DMA(()),
         ],
         cost_estimate=estimate(0, (part, stat, back)),
@@ -513,7 +538,9 @@
     cross_part = cross_attention(
         cross_queries, encoded, neighbour_weight, counts, sources, position
     )
-    by_head = self_attention(queries, self_keys, self_values, position // HEADS, groups)
+    by_head = self_attention(
+        queries, self_keys, self_values, position // HEADS, position % HEADS, groups
+    )
     self_part = lax.all_to_all(by_head, "ctx", 0, 0, axis_index_groups=groups, tiled=True)
     return pl.pallas_call(
         sum_kernel,

time: 136 us -> 140 us (1.029)
  waiting for transfers between devices: 27.4 us -> 37.4 us
  starting transfers between devices: 52.2 us -> 44.7 us
  other arithmetic: 1.29 us -> 3.07 us
    ppermute x6 -> x5, starting transfers between devices: 22.8 us -> 12.7 us  [shifted(): lax.ppermute(value, axis, [(source, source + steps) for source in range(f...]
    ppermute x6 -> x5, waiting for transfers between devices: 27.4 us -> 36.6 us  [shifted(): lax.ppermute(value, axis, [(source, source + steps) for source in range(f...]
    all_to_all x0 -> x1, starting transfers between devices: none -> 5.22 us  [self_attention(): lax.all_to_all(packed(raw), 'ctx', 0, 0, axis_index_groups=groups, tiled=...]
    ppermute x5, starting transfers between devices: 10.4 us -> 6.46 us  [swapped(): lax.ppermute(value, axis, [(source, source ^ bit) for source in range(cou...]
    ppermute x0 -> x2, starting transfers between devices: none -> 2.75 us  [self_attention(): lax.ppermute(jnp.concatenate([keys[part], values[part]], axis=0), 'ctx',...]
    pallas_call x1 -> x2, Pallas kernels: 2.86 us -> 4.85 us  [packed(): pl.pallas_call(pack_kernel, out_shape=jax.ShapeDtypeStruct((width // HEAD...]
    pallas_call x1, Pallas kernels: 9.55 us -> 7.7 us  [self_attention(): pl.pallas_call(functools.partial(previous_kernel, scale), out_shape=(jax....]
    all_to_all x1, starting transfers between devices: 13.3 us -> 11.9 us  [per_device(): lax.all_to_all(by_head, 'ctx', 0, 0, axis_index_groups=groups, tiled=True)]
  transfers between devices with their start and end apart: 13 -> 15, of which waited for: 4 -> 4; matrix products, arithmetic and copies ran while one was open for 2% -> 2% of each run, Pallas kernels for 32% -> 31%
where the time goes in v5:
time: 140 us; the launch traced here: 139 us
  Pallas kernels  48.2 us (34%)
  starting transfers between devices  44.7 us (32%)
  waiting for transfers between devices  37.4 us (27%)
  local copies, waits for them, and re-layouts  4.99 us (4%)
  other arithmetic  3.07 us (2%)
    ppermute x5, waiting for transfers between devices, shifted(): lax.ppermute(value, axis, [(source, source + steps) for source in range(f...  36.6 us
    ppermute x5, starting transfers between devices, shifted(): lax.ppermute(value, axis, [(source, source + steps) for source in range(f...  12.7 us
    all_to_all x1, starting transfers between devices, per_device(): lax.all_to_all(by_head, 'ctx', 0, 0, axis_index_groups=groups, tiled=True)  11.9 us
    pallas_call x1, Pallas kernels, cross_attention(): pl.pallas_call(functools.partial(cross_kernel, HEAD_DIM ** (-0.5) * LOG2E...  10.5 us
    pallas_call x1, Pallas kernels, self_attention(): pl.pallas_call(functools.partial(previous_kernel, scale), out_shape=(jax....  7.7 us
    pallas_call x1, Pallas kernels, self_attention(): pl.pallas_call(functools.partial(own_kernel, scale), out_shape=(jax.Shape...  7.21 us
    ppermute x5, starting transfers between devices, swapped(): lax.ppermute(value, axis, [(source, source ^ bit) for source in range(cou...  6.46 us
    pallas_call x1, Pallas kernels, cross_attention(): pl.pallas_call(absorb_kernel, out_shape=jax.ShapeDtypeStruct((span_count,...  5.82 us
  transfers between devices with their start and end apart: 15, of which 4 were waited for; matrix products, arithmetic and copies ran while one was open for 2% of the time, Pallas kernels for 31%

profile of v5, /device:TPU:23, one launch (start us, length us, event | category | flops | bytes accessed | tf_op | source)
XLA Modules:
  0.0 138.6 jit_solution(4963597400580197859)
XLA Ops:
  0.0 2.9 %pack.2 = bf16[16,384,128]{2,1,0:T(8,128)(2,1)} custom-call(bf16[128,2048]{1,0:T(8,128)(2,1)} %refs_0_.3, bf16[128,2048]{1,0:T(8,128)(2,1)} %refs_1_.1, bf16[128,2048]{1,0:T(8,128)(2,1)} %refs_2_.1), custom_call_target="tpu_custom_call" | custom-call | bytes 3145728 | tf_op jit(solution)/shard_map/pack/pallas_call | solution.py:42
  2.9 5.6 %all-to-all-start = ((bf16[16,384,128]{2,1,0:T(8,128)(2,1)}), bf16[16,384,128]{2,1,0:T(8,128)(2,1)S(1)}, u32[]{:S(2)}, u32[]{:S(2)}) async-start(bf16[16,384,128]{2,1,0:T(8,128)(2,1)} %pack.2), calls=%async_computation | async-start | bytes 3145728 | tf_op jit(solution)/shard_map/all_to_all | solution.py:234
  8.6 0.0 copy-done.4
  8.6 0.0 copy-done.3
  8.6 0.1 fusion
  8.7 1.3 collective-permute-start
  10.0 0.8 pad_maximum_fusion.4
  10.8 1.5 %collective-permute-start.1 = (bf16[128,2048]{1,0:T(8,128)(2,1)}, bf16[128,2048]{1,0:T(8,128)(2,1)}, u32[]{:S(2)}, u32[]{:S(2)}) collective-permute-start(bf16[128,2048]{1,0:T(8,128)(2,1)} %pad_maximum_fusion.4), channel_id=1, source_target_pairs={{8,24},{9,25},{10,26},{11,27},{12,28},{13,29},{14,30},{15,31}} | collective-permute-start | bytes 1572872 | tf_op jit(solution)/shard_map/ppermute | solution.py:244
  12.3 0.0 copy-done.6
  12.3 2.3 %collective-permute-start.5 = (bf16[128,896]{1,0:T(8,128)(2,1)S(1)}, bf16[128,896]{1,0:T(8,128)(2,1)S(1)}, u32[]{:S(2)}, u32[]{:S(2)}) collective-permute-start(bf16[128,896]{1,0:T(8,128)(2,1)S(1)} %copy-done.6), channel_id=1, source_target_pairs={{0,8},{1,9},{2,10},{3,11},{4,12},{5,13},{6,14},{7,15},{8,16},{9,17... | collective-permute-start | bytes 688136 | tf_op jit(solution)/shard_map/ppermute | solution.py:23
  14.7 27.7 %collective-permute-done.5.refs_1_ = bf16[128,896]{1,0:T(8,128)(2,1)S(1)} collective-permute-done((bf16[128,896]{1,0:T(8,128)(2,1)S(1)}, bf16[128,896]{1,0:T(8,128)(2,1)S(1)}, u32[]{:S(2)}, u32[]{:S(2)}) %collective-permute-start.5) | collective-permute-done | bytes 229408 | tf_op jit(solution)/shard_map/ppermute | solution.py:23
  42.4 4.1 %collective-permute-start.6 = (bf16[128,896]{1,0:T(8,128)(2,1)S(1)}, bf16[128,896]{1,0:T(8,128)(2,1)S(1)}, u32[]{:S(2)}, u32[]{:S(2)}) collective-permute-start(bf16[128,896]{1,0:T(8,128)(2,1)S(1)} %collective-permute-done.5.refs_1_), channel_id=1, source_target_pairs={{0,8},{1,9},{2,10},{3,11},{4,12},{5,13},{6,14},{7,15},{8,16},{9,17... | collective-permute-start | bytes 688136 | tf_op jit(solution)/shard_map/ppermute | solution.py:23
  46.5 0.0 collective-permute-done
  46.5 0.0 collective-permute-done.1
  46.5 0.9 broadcast_select_fusion.refs_0_
  47.4 1.9 %pack.3 = bf16[16,128,128]{2,1,0:T(8,128)(2,1)} custom-call(bf16[128,2048]{1,0:T(8,128)(2,1)} %broadcast_select_fusion.refs_0_), custom_call_target="tpu_custom_call" | custom-call | bytes 1048576 | tf_op jit(solution)/shard_map/pack/pallas_call | solution.py:42
  49.3 0.0 all-to-all-done.x_ref.q_ref
  49.3 5.2 %all-to-all-start.1 = ((bf16[16,128,128]{2,1,0:T(8,128)(2,1)}), bf16[16,128,128]{2,1,0:T(8,128)(2,1)S(1)}, u32[]{:S(2)}, u32[]{:S(2)}) async-start(bf16[16,128,128]{2,1,0:T(8,128)(2,1)} %pack.3), calls=%async_computation.1 | async-start | bytes 1048576 | tf_op jit(solution)/shard_map/all_to_all | solution.py:247
  54.6 3.1 %collective-permute-start.2 = (bf16[8,128,128]{2,1,0:T(8,128)(2,1)S(1)}, bf16[8,128,128]{2,1,0:T(8,128)(2,1)S(1)}, u32[]{:S(2)}, u32[]{:S(2)}) collective-permute-start(bf16[8,128,128]{2,1,0:T(8,128)(2,1)S(1)} %slice.28), channel_id=1, source_target_pairs={{16,0},{17,1},{18,2},{19,3},{20,4},{21,5},{22,6},{23,7},{24,8},{25... | collective-permute-start | bytes 786440 | tf_op jit(solution)/shard_map/ppermute | solution.py:23
  57.7 0.0 collective-permute-done.6.refs_2_
  57.7 0.0 copy-start.7
  57.7 0.1 broadcast_select_fusion.1
  57.8 1.2 pad_maximum_fusion
  59.0 0.0 copy-done.5
  59.0 0.3 collective-permute-start.7
  59.3 0.1 collective-permute-start.8
  59.4 2.3 %collective-permute-start.9 = (bf16[256,896]{1,0:T(8,128)(2,1)}, bf16[256,896]{1,0:T(8,128)(2,1)}, u32[]{:S(2)}, u32[]{:S(2)}) collective-permute-start(bf16[256,896]{1,0:T(8,128)(2,1)} %get-tuple-element.22), channel_id=1, source_target_pairs={{0,6},{1,7},{2,4},{3,5},{4,2},{5,3},{6,0},{7,1},{8,14},{9,15},{10,... | collective-permute-start | bytes 1376264 | tf_op jit(solution)/shard_map/ppermute | solution.py:28
  61.6 7.0 %collective-permute-done.2.q_ref = bf16[8,128,128]{2,1,0:T(8,128)(2,1)S(1)} collective-permute-done((bf16[8,128,128]{2,1,0:T(8,128)(2,1)S(1)}, bf16[8,128,128]{2,1,0:T(8,128)(2,1)S(1)}, u32[]{:S(2)}, u32[]{:S(2)}) %collective-permute-start.2) | collective-permute-done | bytes 262176 | tf_op jit(solution)/shard_map/ppermute | solution.py:23
  68.6 0.0 copy-done
  68.6 0.7 copy-done.12
  69.3 3.9 %later.1 = bf16[9,128,128]{2,1,0:T(8,128)(2,1)} custom-call(bf16[8,128,128]{2,1,0:T(8,128)(2,1)} %copy-done.12, bf16[16,384,128]{2,1,0:T(8,128)(2,1)} %copy-done), custom_call_target="tpu_custom_call" | custom-call | flops 268435456 | bytes 262144 | tf_op jit(solution)/shard_map/later/pallas_call | solution.py:267
  73.2 1.3 collective-permute-start.3
  74.5 0.0 copy-done.15
  74.5 0.0 copy-done.16
  74.5 0.1 multiply_add_fusion
  74.6 1.9 %collective-permute-start.4 = (s32[2,2]{1,0:T(2,128)S(1)}, s32[2,2]{1,0:T(2,128)S(1)}, u32[]{:S(2)}, u32[]{:S(2)}) collective-permute-start(s32[2,2]{1,0:T(2,128)S(1)} %multiply_add_fusion), channel_id=1, source_target_pairs={{0,1},{1,2},{2,3},{3,4},{4,5},{5,6},{6,7},{7,8},{8,9},{9,10},{10,1... | collective-permute-start | bytes 56 | tf_op jit(solution)/shard_map/ppermute | solution.py:23
  76.5 1.9 %collective-permute-done.4 = s32[2,2]{1,0:T(2,128)S(1)} collective-permute-done((s32[2,2]{1,0:T(2,128)S(1)}, s32[2,2]{1,0:T(2,128)S(1)}, u32[]{:S(2)}, u32[]{:S(2)}) %collective-permute-start.4) | collective-permute-done | bytes 48 | tf_op jit(solution)/shard_map/ppermute | solution.py:23
  78.4 3.5 %collective-permute-start.10 = (s32[2,2]{1,0:T(2,128)S(1)}, s32[2,2]{1,0:T(2,128)S(1)}, u32[]{:S(2)}, u32[]{:S(2)}) collective-permute-start(s32[2,2]{1,0:T(2,128)S(1)} %pad_add_fusion.table_ref), channel_id=1, source_target_pairs={{0,1},{1,0},{2,3},{3,2},{4,5},{5,4},{6,7},{7,6},{8,9},{9,8},{10,11... | collective-permute-start | bytes 56 | tf_op jit(solution)/shard_map/ppermute | solution.py:28
  81.9 0.8 collective-permute-done.10.theirs_ref
  82.7 0.0 collective-permute-done.7.refs_3_
  82.7 0.0 collective-permute-done.8.refs_4_
  82.7 0.0 copy-start.9
  82.7 0.0 collective-permute-done.9.refs_5_
  82.7 0.0 copy-done.7
  82.7 0.5 copy-done.14
  83.3 0.2 copy-done.8
  83.5 0.2 copy-done.9
  83.6 2.9 %gather.1 = bf16[512,896]{1,0:T(8,128)(2,1)} custom-call(s32[1]{0:T(128)} %bitcast.1.position_ref, s32[2,2]{1,0:T(2,128)} %copy-done.14, bf16[128,896]{1,0:T(8,128)(2,1)} %refs_0_.5, bf16[128,896]{1,0:T(8,128)(2,1)} %copy-done.5, bf16[128,896]{1,0:T(8,128)(2,1)} %copy-done.7, bf16[256,896]{1,0:T(8,128)(2,1)} %copy-done.8, bf16[256,896]{1,0:T(8,128)(2,1)} %copy-done.9, ...), custom_call_target="tpu_custom_call" | custom-call | bytes 3670016 | tf_op jit(solution)/shard_map/gather/pallas_call | solution.py:469
  86.6 0.4 collective-permute-start.11
  86.9 7.2 %own.1 = (f32[16,128,128]{2,1,0:T(8,128)}, f32[16,128,128]{2,1,0:T(8,128)}) custom-call(bf16[16,384,128]{2,1,0:T(8,128)(2,1)} %copy-done), custom_call_target="tpu_custom_call" | custom-call | flops 1073741824 | bytes 1572864 | tf_op jit(solution)/shard_map/own/pallas_call | solution.py:253
  94.1 0.0 all-to-all-done.1.kv_ref
  94.2 0.8 copy-done.1
  94.9 7.7 %previous.1 = (bf16[16,128,128]{2,1,0:T(8,128)(2,1)}, f32[8,128,128]{2,1,0:T(8,128)}, f32[8,128,128]{2,1,0:T(8,128)}) custom-call(s32[1]{0:T(128)} %bitcast.flag_ref, bf16[16,384,128]{2,1,0:T(8,128)(2,1)} %copy-done, bf16[16,128,128]{2,1,0:T(8,128)(2,1)} %copy-done.1, f32[16,128,128]{2,1,0:T(8,128)} %get-tuple-element.10.out1_ref, ...), custom_call_target="tpu_custom_call" | custom-call | flops 805306368 | bytes 2621440 | tf_op jit(solution)/shard_map/previous/pallas_call | solution.py:279
  102.6 0.0 collective-permute-done.3.back_ref
  102.7 0.7 copy-done.11
  103.4 2.9 %merge.1 = bf16[16,128,128]{2,1,0:T(8,128)(2,1)} custom-call(s32[1]{0:T(128)} %bitcast.flag_ref, f32[8,128,128]{2,1,0:T(8,128)} %get-tuple-element.12.part_ref, f32[8,128,128]{2,1,0:T(8,128)} %get-tuple-element.13.stat_ref, bf16[9,128,128]{2,1,0:T(8,128)(2,1)} %copy-done.11, ...), custom_call_target="tpu_custom_call", output_to_operand_aliasing={{}: (4, {})} | custom-call | bytes 819200 | tf_op jit(solution)/shard_map/merge/pallas_call | solution.py:299
  106.3 11.9 %all-to-all-start.2 = ((bf16[16,128,128]{2,1,0:T(8,128)(2,1)}), bf16[16,128,128]{2,1,0:T(8,128)(2,1)S(1)}, u32[]{:S(2)}, u32[]{:S(2)}) async-start(bf16[16,128,128]{2,1,0:T(8,128)(2,1)} %merge.1), calls=%async_computation.2 | async-start | bytes 1048576 | tf_op jit(solution)/shard_map/all_to_all | solution.py:544
  118.2 5.8 %absorb.1.refs_7_ = bf16[2,1024,896]{2,1,0:T(8,128)(2,1)} custom-call(bf16[128,2048]{1,0:T(8,128)(2,1)} %q_ref.1, bf16[896,4096]{1,0:T(8,128)(2,1)} %refs_8_.1), custom_call_target="tpu_custom_call" | custom-call | flops 469762048 | bytes 7340032 | tf_op jit(solution)/shard_map/absorb/pallas_call | solution.py:485
  124.0 0.0 collective-permute-done.11.refs_6_
  124.0 1.0 copy-done.10
  125.0 10.5 %cross.1.cross_ref = f32[128,2048]{1,0:T(8,128)} custom-call(s32[1]{0:T(128)} %bitcast.1.position_ref, s32[2,2]{1,0:T(2,128)} %copy-done.13, bf16[128,896]{1,0:T(8,128)(2,1)} %refs_0_.5, bf16[128,896]{1,0:T(8,128)(2,1)} %copy-done.5, bf16[128,896]{1,0:T(8,128)(2,1)} %copy-done.7, bf16[256,896]{1,0:T(8,128)(2,1)} %copy-done.8, bf16[256,896]{1,0:T(8,128)(2,1)} %copy-done.9, ...), custom_call_target="tpu_custom_call" | custom-call | flops 2348810240 | bytes 9175040 | tf_op jit(solution)/shard_map/cross/pallas_call | solution.py:506
  135.5 0.0 all-to-all-done.2.self_ref
  135.5 0.8 copy-done.2
  136.3 2.3 %total.1 = bf16[128,2048]{1,0:T(8,128)(2,1)} custom-call(bf16[16,128,128]{2,1,0:T(8,128)(2,1)} %copy-done.2, f32[128,2048]{1,0:T(8,128)} %cross.1.cross_ref), custom_call_target="tpu_custom_call" | custom-call | tf_op jit(solution)/shard_map/total/pallas_call | solution.py:545
  (21 shorter events, 0.1 us)
Async XLA Ops:
  0.0 8.6 %copy-start.4 = (bf16[128,2048]{1,0:T(8,128)(2,1)S(1)}, bf16[128,2048]{1,0:T(8,128)(2,1)}, u32[]{:S(2)}) copy-start(bf16[128,2048]{1,0:T(8,128)(2,1)} %refs_2_.1) | copy-start | bytes 1572868
  0.0 8.6 %copy-start.3 = (bf16[128,2048]{1,0:T(8,128)(2,1)S(1)}, bf16[128,2048]{1,0:T(8,128)(2,1)}, u32[]{:S(2)}) copy-start(bf16[128,2048]{1,0:T(8,128)(2,1)} %refs_1_.1) | copy-start | bytes 1572868
  2.9 9.4 %copy-start.6 = (bf16[128,896]{1,0:T(8,128)(2,1)S(1)}, bf16[128,896]{1,0:T(8,128)(2,1)}, u32[]{:S(2)}) copy-start(bf16[128,896]{1,0:T(8,128)(2,1)} %refs_0_.5) | copy-start | bytes 688132
  2.9 46.4 %all-to-all-start = ((bf16[16,384,128]{2,1,0:T(8,128)(2,1)}), bf16[16,384,128]{2,1,0:T(8,128)(2,1)S(1)}, u32[]{:S(2)}, u32[]{:S(2)}) async-start(bf16[16,384,128]{2,1,0:T(8,128)(2,1)} %pack.2), calls=%async_computation | async-start | bytes 3145728 | tf_op jit(solution)/shard_map/all_to_all | solution.py:234
  8.7 37.8 %collective-permute-start = (bf16[128,2048]{1,0:T(8,128)(2,1)S(1)}, bf16[128,2048]{1,0:T(8,128)(2,1)S(1)}, u32[]{:S(2)}, u32[]{:S(2)}) collective-permute-start(bf16[128,2048]{1,0:T(8,128)(2,1)S(1)} %pad_maximum_fusion.3), channel_id=1, source_target_pairs={{8,16},{9,17},{10,18},{11,19},{12,20},{13,21},{14,22},{15,23}} | collective-permute-start | bytes 1572872 | tf_op jit(solution)/shard_map/ppermute | solution.py:244
  10.8 35.7 %collective-permute-start.1 = (bf16[128,2048]{1,0:T(8,128)(2,1)}, bf16[128,2048]{1,0:T(8,128)(2,1)}, u32[]{:S(2)}, u32[]{:S(2)}) collective-permute-start(bf16[128,2048]{1,0:T(8,128)(2,1)} %pad_maximum_fusion.4), channel_id=1, source_target_pairs={{8,24},{9,25},{10,26},{11,27},{12,28},{13,29},{14,30},{15,31}} | collective-permute-start | bytes 1572872 | tf_op jit(solution)/shard_map/ppermute | solution.py:244
  12.3 30.1 %collective-permute-start.5 = (bf16[128,896]{1,0:T(8,128)(2,1)S(1)}, bf16[128,896]{1,0:T(8,128)(2,1)S(1)}, u32[]{:S(2)}, u32[]{:S(2)}) collective-permute-start(bf16[128,896]{1,0:T(8,128)(2,1)S(1)} %copy-done.6), channel_id=1, source_target_pairs={{0,8},{1,9},{2,10},{3,11},{4,12},{5,13},{6,14},{7,15},{8,16},{9,17... | collective-permute-start | bytes 688136 | tf_op jit(solution)/shard_map/ppermute | solution.py:23
  42.4 16.6 %copy-start.5 = (bf16[128,896]{1,0:T(8,128)(2,1)}, bf16[128,896]{1,0:T(8,128)(2,1)S(1)}, u32[]{:S(2)}) copy-start(bf16[128,896]{1,0:T(8,128)(2,1)S(1)} %collective-permute-done.5.refs_1_) | copy-start | bytes 688132
  42.4 15.3 %collective-permute-start.6 = (bf16[128,896]{1,0:T(8,128)(2,1)S(1)}, bf16[128,896]{1,0:T(8,128)(2,1)S(1)}, u32[]{:S(2)}, u32[]{:S(2)}) collective-permute-start(bf16[128,896]{1,0:T(8,128)(2,1)S(1)} %collective-permute-done.5.refs_1_), channel_id=1, source_target_pairs={{0,8},{1,9},{2,10},{3,11},{4,12},{5,13},{6,14},{7,15},{8,16},{9,17... | collective-permute-start | bytes 688136 | tf_op jit(solution)/shard_map/ppermute | solution.py:23
  49.3 25.2 %copy-start.15 = (s32[2,2]{1,0:T(2,128)S(1)}, s32[2,2]{1,0:T(2,128)}, u32[]{:S(2)}) copy-start(s32[2,2]{1,0:T(2,128)} %param.15) | copy-start | bytes 52
  49.3 25.2 %copy-start.16 = (s32[2]{0:T(128)S(1)}, s32[2]{0:T(128)}, u32[]{:S(2)}) copy-start(s32[2]{0:T(128)} %param.14) | copy-start | bytes 28
  49.3 19.3 %copy-start = (bf16[16,384,128]{2,1,0:T(8,128)(2,1)}, bf16[16,384,128]{2,1,0:T(8,128)(2,1)S(1)}, u32[]{:S(2)}) copy-start(bf16[16,384,128]{2,1,0:T(8,128)(2,1)S(1)} %all-to-all-done.x_ref.q_ref) | copy-start | bytes 4718596
  49.3 44.8 %all-to-all-start.1 = ((bf16[16,128,128]{2,1,0:T(8,128)(2,1)}), bf16[16,128,128]{2,1,0:T(8,128)(2,1)S(1)}, u32[]{:S(2)}, u32[]{:S(2)}) async-start(bf16[16,128,128]{2,1,0:T(8,128)(2,1)} %pack.3), calls=%async_computation.1 | async-start | bytes 1048576 | tf_op jit(solution)/shard_map/all_to_all | solution.py:247
  54.6 14.0 %collective-permute-start.2 = (bf16[8,128,128]{2,1,0:T(8,128)(2,1)S(1)}, bf16[8,128,128]{2,1,0:T(8,128)(2,1)S(1)}, u32[]{:S(2)}, u32[]{:S(2)}) collective-permute-start(bf16[8,128,128]{2,1,0:T(8,128)(2,1)S(1)} %slice.28), channel_id=1, source_target_pairs={{16,0},{17,1},{18,2},{19,3},{20,4},{21,5},{22,6},{23,7},{24,8},{25... | collective-permute-start | bytes 786440 | tf_op jit(solution)/shard_map/ppermute | solution.py:23
  57.7 25.0 %copy-start.7 = (bf16[128,896]{1,0:T(8,128)(2,1)}, bf16[128,896]{1,0:T(8,128)(2,1)S(1)}, u32[]{:S(2)}) copy-start(bf16[128,896]{1,0:T(8,128)(2,1)S(1)} %collective-permute-done.6.refs_2_) | copy-start | bytes 688132
  59.0 23.7 %collective-permute-start.7 = (bf16[256,896]{1,0:T(8,128)(2,1)}, bf16[256,896]{1,0:T(8,128)(2,1)S(1)}, u32[]{:S(2)}, u32[]{:S(2)}) collective-permute-start(bf16[256,896]{1,0:T(8,128)(2,1)} %get-tuple-element.24), channel_id=1, source_target_pairs={{0,2},{1,3},{2,0},{3,1},{4,6},{5,7},{6,4},{7,5},{8,10},{9,11},{10,... | collective-permute-start | bytes 1376264 | tf_op jit(solution)/shard_map/ppermute | solution.py:28
  59.3 23.4 %collective-permute-start.8 = (bf16[256,896]{1,0:T(8,128)(2,1)}, bf16[256,896]{1,0:T(8,128)(2,1)S(1)}, u32[]{:S(2)}, u32[]{:S(2)}) collective-permute-start(bf16[256,896]{1,0:T(8,128)(2,1)} %get-tuple-element.23), channel_id=1, source_target_pairs={{0,4},{1,5},{2,6},{3,7},{4,0},{5,1},{6,2},{7,3},{8,12},{9,13},{10,... | collective-permute-start | bytes 1376264 | tf_op jit(solution)/shard_map/ppermute | solution.py:28
  59.4 23.3 %collective-permute-start.9 = (bf16[256,896]{1,0:T(8,128)(2,1)}, bf16[256,896]{1,0:T(8,128)(2,1)}, u32[]{:S(2)}, u32[]{:S(2)}) collective-permute-start(bf16[256,896]{1,0:T(8,128)(2,1)} %get-tuple-element.22), channel_id=1, source_target_pairs={{0,6},{1,7},{2,4},{3,5},{4,2},{5,3},{6,0},{7,1},{8,14},{9,15},{10,... | collective-permute-start | bytes 1376264 | tf_op jit(solution)/shard_map/ppermute | solution.py:28
  68.6 0.7 copy-start.12
  73.2 29.4 %collective-permute-start.3 = (bf16[9,128,128]{2,1,0:T(8,128)(2,1)}, bf16[9,128,128]{2,1,0:T(8,128)(2,1)S(1)}, u32[]{:S(2)}, u32[]{:S(2)}) collective-permute-start(bf16[9,128,128]{2,1,0:T(8,128)(2,1)} %later.1), channel_id=1, source_target_pairs={{0,16},{1,17},{2,18},{3,19},{4,20},{5,21},{6,22},{7,23},{8,24},{9,... | collective-permute-start | bytes 884744 | tf_op jit(solution)/shard_map/ppermute | solution.py:23
  74.6 3.8 %collective-permute-start.4 = (s32[2,2]{1,0:T(2,128)S(1)}, s32[2,2]{1,0:T(2,128)S(1)}, u32[]{:S(2)}, u32[]{:S(2)}) collective-permute-start(s32[2,2]{1,0:T(2,128)S(1)} %multiply_add_fusion), channel_id=1, source_target_pairs={{0,1},{1,2},{2,3},{3,4},{4,5},{5,6},{6,7},{7,8},{8,9},{9,10},{10,1... | collective-permute-start | bytes 56 | tf_op jit(solution)/shard_map/ppermute | solution.py:23
  78.4 24.2 %copy-start.13 = (s32[2,2]{1,0:T(2,128)}, s32[2,2]{1,0:T(2,128)S(1)}, u32[]{:S(2)}) copy-start(s32[2,2]{1,0:T(2,128)S(1)} %pad_add_fusion.table_ref) | copy-start | bytes 52
  78.4 4.3 %collective-permute-start.10 = (s32[2,2]{1,0:T(2,128)S(1)}, s32[2,2]{1,0:T(2,128)S(1)}, u32[]{:S(2)}, u32[]{:S(2)}) collective-permute-start(s32[2,2]{1,0:T(2,128)S(1)} %pad_add_fusion.table_ref), channel_id=1, source_target_pairs={{0,1},{1,0},{2,3},{3,2},{4,5},{5,4},{6,7},{7,6},{8,9},{9,8},{10,11... | collective-permute-start | bytes 56 | tf_op jit(solution)/shard_map/ppermute | solution.py:28
  82.7 0.6 copy-start.14
  82.7 0.8 copy-start.8
  82.7 0.9 copy-start.9
  86.6 37.4 %collective-permute-start.11 = (bf16[512,896]{1,0:T(8,128)(2,1)}, bf16[512,896]{1,0:T(8,128)(2,1)S(1)}, u32[]{:S(2)}, u32[]{:S(2)}) collective-permute-start(bf16[512,896]{1,0:T(8,128)(2,1)} %gather.1), channel_id=1, source_target_pairs={{0,1},{1,0},{2,3},{3,2},{4,5},{5,4},{6,7},{7,6},{8,9},{9,8},{10,11... | collective-permute-start | bytes 2752520 | tf_op jit(solution)/shard_map/ppermute | solution.py:28
  94.1 0.8 copy-start.1
  102.6 0.7 copy-start.11
  106.3 29.2 %all-to-all-start.2 = ((bf16[16,128,128]{2,1,0:T(8,128)(2,1)}), bf16[16,128,128]{2,1,0:T(8,128)(2,1)S(1)}, u32[]{:S(2)}, u32[]{:S(2)}) async-start(bf16[16,128,128]{2,1,0:T(8,128)(2,1)} %merge.1), calls=%async_computation.2 | async-start | bytes 1048576 | tf_op jit(solution)/shard_map/all_to_all | solution.py:544
  124.0 1.0 copy-start.10
  135.5 0.8 copy-start.2

commit v6 on v4

--- a/solution.py
+++ b/solution.py
@@ -56,15 +56,18 @@
     return lax.dot_general(q, k, (((1,), (1,)), ((), ())), preferred_element_type=jnp.float32)
 
 
-def softmax_parts(q, pieces, scale):
+def softmax_parts(q, pieces, scale, start=None):
     scores = []
     for k, _, mask in pieces:
         s = scores_of(q, k)
         scores.append(s if mask is None else jnp.where(mask, s, MASKED_SCORE))
-    largest = functools.reduce(
-        jnp.maximum, [jnp.max(s, axis=1, keepdims=True) for s in scores]
-    )
+    largest = functools.reduce(jnp.maximum, [jnp.max(s, axis=1, keepdims=True) for s in scores])
     total, out = None, None
+    if start is not None:
+        out, before, total = start
+        largest = jnp.maximum(largest, before)
+        weight = jnp.exp2((before - largest) * scale)
+        out, total = out * weight, total * weight
     for s, (_, v, _) in zip(scores, pieces):
         p = jnp.exp2((s - largest) * scale)
         t = jnp.sum(p, axis=1, keepdims=True)
@@ -101,29 +104,28 @@
     return keep(column, row)
 
 
-def own_kernel(scale, x_ref, out_ref, stat_ref):
-    blocks, triple, dim = x_ref.shape
-    rows = triple // 3
+def own_kernel(scale, q_ref, kv_ref, out_ref, stat_ref):
+    blocks, rows, dim = q_ref.shape
     causal = triangle(2 * rows, lambda column, row: column <= row)
     for i in range(0, blocks, 2):
         spans = [(i, 2, causal)] + ([(0, i, None)] if i else [])
         pieces = [
-            (taken(x_ref, f, n, rows, rows), taken(x_ref, f, n, 2 * rows, rows), mask)
+            (taken(kv_ref, f, n, 0, rows), taken(kv_ref, f, n, rows, rows), mask)
             for f, n, mask in spans
         ]
-        out, largest, total = softmax_parts(taken(x_ref, i, 2, 0, rows), pieces, scale)
+        out, largest, total = softmax_parts(taken(q_ref, i, 2, 0, rows), pieces, scale)
         out_ref[i : i + 2] = out.reshape(2, rows, dim)
         stat_ref[i : i + 2] = with_stats(largest, total).reshape(2, rows, 128)
 
 
-def later_kernel(scale, q_ref, x_ref, out_ref):
+def later_kernel(scale, q_ref, kv_ref, out_ref):
     blocks, rows, dim = q_ref.shape
     later = triangle(2 * rows, lambda column, row: column > row)
     out_ref[blocks] = jnp.zeros((rows, dim), out_ref.dtype)
     for i in range(0, blocks, 2):
         spans = [(i, 2, later)] + ([(i + 2, blocks - i - 2, None)] if i + 2 < blocks else [])
         pieces = [
-            (taken(x_ref, f, n, rows, rows), taken(x_ref, f, n, 2 * rows, rows), mask)
+            (taken(kv_ref, f, n, 0, rows), taken(kv_ref, f, n, rows, rows), mask)
             for f, n, mask in spans
         ]
         out, largest, total = softmax_parts(taken(q_ref, i, 2, 0, rows), pieces, scale)
@@ -145,13 +147,6 @@
         values.append(three[0:1] + three[1:2] + three[2:3])
     sublane = lax.broadcasted_iota(jnp.int32, (rows, 128), 0)
     return jnp.where(sublane < 64, values[0], values[1]).T
-
-
-def merged(parts, scale):
-    top = functools.reduce(jnp.maximum, [largest for _, largest, _ in parts])
-    weights = [jnp.exp2((largest - top) * scale) for _, largest, _ in parts]
-    total = sum(w * t for w, (_, _, t) in zip(weights, parts))
-    return sum(w * out for w, (out, _, _) in zip(weights, parts)), top, total
 
 
 def previous_kernel(scale, flag_ref, q_ref, kv_ref, out1_ref, stat1_ref, out_ref, part_ref, stat_ref):
@@ -184,8 +179,7 @@
                 (taken(kv_ref, f, n, 0, rows), taken(kv_ref, f, n, rows, rows), mask)
                 for f, n, mask in spans
             ]
-            part = softmax_parts(taken(q_ref, i, 2, 0, rows), pieces, scale)
-            store(i, merged([part, own_part(i)], scale))
+            store(i, softmax_parts(taken(q_ref, i, 2, 0, rows), pieces, scale, own_part(i)))
 
     @pl.when(flag_ref[0] == 0)
     def _():
@@ -199,14 +193,19 @@
     del rest_ref
     blocks, rows, dim = part_ref.shape
     for i in range(0, blocks, 2):
-        stat = stat_ref[i : i + 2].reshape(2 * rows, 128)
-        parts = [(part_ref[i : i + 2].reshape(2 * rows, dim), *halves(stat))]
+        out1, largest1, total1 = (
+            part_ref[i : i + 2].reshape(2 * rows, dim),
+            *halves(stat_ref[i : i + 2].reshape(2 * rows, 128)),
+        )
         stat = jnp.concatenate([sent_stats(back_ref, i + n, rows) for n in range(2)], axis=0)
-        largest, total = halves(stat)
-        largest = jnp.where(flag_ref[0] > 0, largest, MASKED_SCORE)
-        parts.append((taken(back_ref, i, 2, 0, rows).astype(jnp.float32), largest, total))
-        out, _, total = merged(parts, scale)
-        done_ref[i : i + 2] = (out * (1.0 / total)).reshape(2, rows, dim).astype(done_ref.dtype)
+        largest2, total2 = halves(stat)
+        largest2 = jnp.where(flag_ref[0] > 0, largest2, MASKED_SCORE)
+        top = jnp.maximum(largest1, largest2)
+        a, b = jnp.exp2((largest1 - top) * scale), jnp.exp2((largest2 - top) * scale)
+        inverse = 1.0 / (a * total1 + b * total2)
+        out2 = taken(back_ref, i, 2, 0, rows).astype(jnp.float32)
+        out = out1 * (a * inverse) + out2 * (b * inverse)
+        done_ref[i : i + 2] = out.reshape(2, rows, dim).astype(done_ref.dtype)
     copy = pltpu.make_async_copy(done_ref, out_ref.at[0:blocks], sem)
     copy.start()
     copy.wait()
@@ -224,11 +223,12 @@
     rows, width = queries.shape
     heads = width // HEAD_DIM
     scale = HEAD_DIM ** (-0.5) * LOG2E
-    x = lax.all_to_all(
-        packed(queries, keys, values), "ctx", 0, 0, axis_index_groups=groups, tiled=True
+    kv = lax.all_to_all(
+        packed(keys, values), "ctx", 0, 0, axis_index_groups=groups, tiled=True
     )
-    arriving = shifted(x[LEFT:, rows:], "ctx", heads)
-    asked = shifted(x[:LEFT, :rows], "ctx", -heads)
+    arriving = shifted(kv[LEFT:], "ctx", heads)
+    q = lax.all_to_all(packed(queries), "ctx", 0, 0, axis_index_groups=groups, tiled=True)
+    asked = shifted(q[:LEFT], "ctx", -heads)
     area = (heads * rows) ** 2 // 2
     small = (LEFT * rows) ** 2 // 2
     out1, stat = pl.pallas_call(
@@ -237,9 +237,9 @@
             jax.ShapeDtypeStruct((heads, rows, HEAD_DIM), jnp.float32),
             jax.ShapeDtypeStruct((heads, rows, 128), jnp.float32),
         ),
-        cost_estimate=estimate(area, (x,)),
+        cost_estimate=estimate(area, (q, kv)),
         name="own",
-    )(x)
+    )(q, kv)
     smem = pl.BlockSpec(memory_space=pltpu.SMEM)
 
     def first_blocks(count, height):
@@ -249,11 +249,11 @@
         functools.partial(later_kernel, scale),
         out_shape=jax.ShapeDtypeStruct((LEFT + 1, rows, HEAD_DIM), jnp.bfloat16),
         grid=(1,),
-        in_specs=[first_blocks(LEFT, rows), first_blocks(LEFT, 3 * rows)],
+        in_specs=[first_blocks(LEFT, rows), first_blocks(LEFT, 2 * rows)],
         out_specs=first_blocks(LEFT + 1, rows),
         cost_estimate=estimate(small, (asked,)),
         name="later",
-    )(asked, x)
+    )(asked, kv)
     back = shifted(answer, "ctx", heads)
     flag = chunk.reshape(1)
     all_blocks = first_blocks(heads, rows)
@@ -267,9 +267,9 @@
         grid=(1,),
         in_specs=[smem, all_blocks, first_blocks(heads - LEFT, 2 * rows), all_blocks, all_blocks],
         out_specs=(all_blocks, first_blocks(LEFT, rows), first_blocks(LEFT, rows)),
-        cost_estimate=estimate(area - small, (x, out1, stat)),
+        cost_estimate=estimate(area - small, (q, kv, out1, stat)),
         name="previous",
-    )(flag, x, arriving, out1, stat)
+    )(flag, q, arriving, out1, stat)
     vmem, anywhere = (pl.BlockSpec(memory_space=m) for m in (pltpu.VMEM, pl.ANY))
     return pl.pallas_call(
         functools.partial(merge_kernel, scale),

time: 136 us -> 132 us (0.971)
  waiting for transfers between devices: 27.4 us -> 20.1 us
  starting transfers between devices: 52.2 us -> 57 us
  local copies, waits for them, and re-layouts: 5.74 us -> 3.63 us
    ppermute x6, waiting for transfers between devices: 27.4 us -> 10.7 us  [shifted(): lax.ppermute(value, axis, [(source, source + steps) for source in range(f...]
    all_to_all x1 -> x2, waiting for transfers between devices: 0.01 us -> 9.39 us  [the longest x1 9.38 us: self_attention(): lax.all_to_all(packed(keys, values), 'ctx', 0, 0, axis_index_groups=group...]
    all_to_all x1 -> x2, starting transfers between devices: 5.64 us -> 10.7 us  [the longest x1 5.51 us: self_attention(): lax.all_to_all(packed(keys, values), 'ctx', 0, 0, axis_index_groups=group...]
    unnamed x30 -> x26, local copies, waits for them, and re-layouts: 4.84 us -> 2.77 us
    pallas_call x1, Pallas kernels: 9.55 us -> 7.65 us  [self_attention(): pl.pallas_call(functools.partial(previous_kernel, scale), out_shape=(jax....]
    pallas_call x1 -> x2, Pallas kernels: 2.86 us -> 4.31 us  [packed(): pl.pallas_call(pack_kernel, out_shape=jax.ShapeDtypeStruct((width // HEAD...]
  transfers between devices with their start and end apart: 13 -> 14, of which waited for: 4 -> 4; matrix products, arithmetic and copies ran while one was open for 2% -> 2% of each run, Pallas kernels for 32% -> 33%
where the time goes in v6:
time: 132 us; the launch traced here: 131 us
  starting transfers between devices  57 us (43%)
  Pallas kernels  47.5 us (36%)
  waiting for transfers between devices  20.1 us (15%)
  local copies, waits for them, and re-layouts  3.63 us (3%)
  other arithmetic  2.37 us (2%)
    ppermute x6, starting transfers between devices, shifted(): lax.ppermute(value, axis, [(source, source + steps) for source in range(f...  23.4 us
    all_to_all x1, starting transfers between devices, per_device(): lax.all_to_all(by_head, 'ctx', 0, 0, axis_index_groups=groups, tiled=True)  12.4 us
    ppermute x6, waiting for transfers between devices, shifted(): lax.ppermute(value, axis, [(source, source + steps) for source in range(f...  10.7 us
    pallas_call x1, Pallas kernels, cross_attention(): pl.pallas_call(functools.partial(cross_kernel, HEAD_DIM ** (-0.5) * LOG2E...  10.6 us
    ppermute x5, starting transfers between devices, swapped(): lax.ppermute(value, axis, [(source, source ^ bit) for source in range(cou...  10.4 us
    all_to_all x1, waiting for transfers between devices, self_attention(): lax.all_to_all(packed(keys, values), 'ctx', 0, 0, axis_index_groups=group...  9.38 us
    pallas_call x1, Pallas kernels, self_attention(): pl.pallas_call(functools.partial(previous_kernel, scale), out_shape=(jax....  7.65 us
    pallas_call x1, Pallas kernels, self_attention(): pl.pallas_call(functools.partial(own_kernel, scale), out_shape=(jax.Shape...  7.17 us
  transfers between devices with their start and end apart: 14, of which 4 were waited for; matrix products, arithmetic and copies ran while one was open for 2% of the time, Pallas kernels for 33%

profile of v6, /device:TPU:23, one launch (start us, length us, event | category | flops | bytes accessed | tf_op | source)
XLA Modules:
  0.0 130.9 jit_solution(4768868791634748405)
XLA Ops:
  0.0 0.0 copy-start.12
  0.0 0.0 copy-start.11
  0.0 2.4 %pack.3 = bf16[16,256,128]{2,1,0:T(8,128)(2,1)} custom-call(bf16[128,2048]{1,0:T(8,128)(2,1)} %refs_0_.5, bf16[128,2048]{1,0:T(8,128)(2,1)} %refs_1_.1), custom_call_target="tpu_custom_call" | custom-call | bytes 2097152 | tf_op jit(solution)/shard_map/pack/pallas_call | solution.py:43
  2.4 5.5 %all-to-all-start.1 = ((bf16[16,256,128]{2,1,0:T(8,128)(2,1)}), bf16[16,256,128]{2,1,0:T(8,128)(2,1)S(1)}, u32[]{:S(2)}, u32[]{:S(2)}) async-start(bf16[16,256,128]{2,1,0:T(8,128)(2,1)} %pack.3), calls=%async_computation.1 | async-start | bytes 2097152 | tf_op jit(solution)/shard_map/all_to_all | solution.py:226
  7.9 3.1 %collective-permute-start.4 = (bf16[128,896]{1,0:T(8,128)(2,1)}, bf16[128,896]{1,0:T(8,128)(2,1)S(1)}, u32[]{:S(2)}, u32[]{:S(2)}) collective-permute-start(bf16[128,896]{1,0:T(8,128)(2,1)} %refs_0_.7), channel_id=1, source_target_pairs={{0,8},{1,9},{2,10},{3,11},{4,12},{5,13},{6,14},{7,15},{8,16},{9,17... | collective-permute-start | bytes 688136 | tf_op jit(solution)/shard_map/ppermute | solution.py:24
  11.0 1.9 %pack.2 = bf16[16,128,128]{2,1,0:T(8,128)(2,1)} custom-call(bf16[128,2048]{1,0:T(8,128)(2,1)} %refs_0_.4), custom_call_target="tpu_custom_call" | custom-call | bytes 1048576 | tf_op jit(solution)/shard_map/pack/pallas_call | solution.py:43
  12.9 9.4 %all-to-all-done.1.kv_ref = bf16[16,256,128]{2,1,0:T(8,128)(2,1)S(1)} async-done(((bf16[16,256,128]{2,1,0:T(8,128)(2,1)}), bf16[16,256,128]{2,1,0:T(8,128)(2,1)S(1)}, u32[]{:S(2)}, u32[]{:S(2)}) %all-to-all-start.1) | async-done | bytes 1048608 | tf_op jit(solution)/shard_map/all_to_all | solution.py:226
  22.3 5.2 %all-to-all-start = ((bf16[16,128,128]{2,1,0:T(8,128)(2,1)}), bf16[16,128,128]{2,1,0:T(8,128)(2,1)S(1)}, u32[]{:S(2)}, u32[]{:S(2)}) async-start(bf16[16,128,128]{2,1,0:T(8,128)(2,1)} %pack.2), calls=%async_computation | async-start | bytes 1048576 | tf_op jit(solution)/shard_map/all_to_all | solution.py:230
  27.5 0.0 collective-permute-done.4.refs_1_
  27.5 0.0 copy-start.3
  27.5 3.1 %collective-permute-start.5 = (bf16[128,896]{1,0:T(8,128)(2,1)S(1)}, bf16[128,896]{1,0:T(8,128)(2,1)S(1)}, u32[]{:S(2)}, u32[]{:S(2)}) collective-permute-start(bf16[128,896]{1,0:T(8,128)(2,1)S(1)} %collective-permute-done.4.refs_1_), channel_id=1, source_target_pairs={{0,8},{1,9},{2,10},{3,11},{4,12},{5,13},{6,14},{7,15},{8,16},{9,17... | collective-permute-start | bytes 688136 | tf_op jit(solution)/shard_map/ppermute | solution.py:24
  30.7 7.5 %collective-permute-done.5.refs_2_ = bf16[128,896]{1,0:T(8,128)(2,1)S(1)} collective-permute-done((bf16[128,896]{1,0:T(8,128)(2,1)S(1)}, bf16[128,896]{1,0:T(8,128)(2,1)S(1)}, u32[]{:S(2)}, u32[]{:S(2)}) %collective-permute-start.5) | collective-permute-done | bytes 229408 | tf_op jit(solution)/shard_map/ppermute | solution.py:24
  38.2 1.1 broadcast_select_fusion
  39.3 1.2 pad_maximum_fusion
  40.5 0.3 collective-permute-start.6
  40.8 0.4 collective-permute-start.7
  41.1 2.0 %collective-permute-start.8 = (bf16[256,896]{1,0:T(8,128)(2,1)}, bf16[256,896]{1,0:T(8,128)(2,1)S(1)}, u32[]{:S(2)}, u32[]{:S(2)}) collective-permute-start(bf16[256,896]{1,0:T(8,128)(2,1)} %get-tuple-element.18), channel_id=1, source_target_pairs={{0,6},{1,7},{2,4},{3,5},{4,2},{5,3},{6,0},{7,1},{8,14},{9,15},{10,... | collective-permute-start | bytes 1376264 | tf_op jit(solution)/shard_map/ppermute | solution.py:29
  43.1 0.8 slice.16
  44.0 1.3 collective-permute-start
  45.3 0.0 copy-done.12
  45.3 0.0 copy-done.11
  45.3 0.1 multiply_add_fusion
  45.4 5.6 %collective-permute-start.3 = (s32[2,2]{1,0:T(2,128)S(1)}, s32[2,2]{1,0:T(2,128)S(1)}, u32[]{:S(2)}, u32[]{:S(2)}) collective-permute-start(s32[2,2]{1,0:T(2,128)S(1)} %multiply_add_fusion), channel_id=1, source_target_pairs={{0,1},{1,2},{2,3},{3,4},{4,5},{5,6},{6,7},{7,8},{8,9},{9,10},{10,1... | collective-permute-start | bytes 56 | tf_op jit(solution)/shard_map/ppermute | solution.py:24
  51.0 0.0 all-to-all-done.q_ref
  51.0 0.0 copy-start.1
  51.0 0.7 collective-permute-done.3
  51.7 9.0 %collective-permute-start.1 = (bf16[8,128,128]{2,1,0:T(8,128)(2,1)S(1)}, bf16[8,128,128]{2,1,0:T(8,128)(2,1)}, u32[]{:S(2)}, u32[]{:S(2)}) collective-permute-start(bf16[8,128,128]{2,1,0:T(8,128)(2,1)S(1)} %slice.17), channel_id=1, source_target_pairs={{16,0},{17,1},{18,2},{19,3},{20,4},{21,5},{22,6},{23,7},{24,8},{25... | collective-permute-start | bytes 786440 | tf_op jit(solution)/shard_map/ppermute | solution.py:24
  60.7 2.5 %collective-permute-done.1.q_ref = bf16[8,128,128]{2,1,0:T(8,128)(2,1)} collective-permute-done((bf16[8,128,128]{2,1,0:T(8,128)(2,1)S(1)}, bf16[8,128,128]{2,1,0:T(8,128)(2,1)}, u32[]{:S(2)}, u32[]{:S(2)}) %collective-permute-start.1) | collective-permute-done | bytes 262176 | tf_op jit(solution)/shard_map/ppermute | solution.py:24
  63.3 7.7 %collective-permute-start.9 = (s32[2,2]{1,0:T(2,128)S(1)}, s32[2,2]{1,0:T(2,128)S(1)}, u32[]{:S(2)}, u32[]{:S(2)}) collective-permute-start(s32[2,2]{1,0:T(2,128)S(1)} %pad_add_fusion.table_ref), channel_id=1, source_target_pairs={{0,1},{1,0},{2,3},{3,2},{4,5},{5,4},{6,7},{7,6},{8,9},{9,8},{10,11... | collective-permute-start | bytes 56 | tf_op jit(solution)/shard_map/ppermute | solution.py:29
  71.0 0.0 copy-done
  71.0 3.8 %later.1 = bf16[9,128,128]{2,1,0:T(8,128)(2,1)} custom-call(bf16[8,128,128]{2,1,0:T(8,128)(2,1)} %collective-permute-done.1.q_ref, bf16[16,256,128]{2,1,0:T(8,128)(2,1)} %copy-done), custom_call_target="tpu_custom_call" | custom-call | flops 268435456 | bytes 262144 | tf_op jit(solution)/shard_map/later/pallas_call | solution.py:248
  74.7 0.0 collective-permute-done.9.theirs_ref
  74.8 1.3 collective-permute-start.2
  76.1 0.0 collective-permute-done.6.refs_3_
  76.1 0.0 copy-start.5
  76.1 0.0 collective-permute-done.7.refs_4_
  76.1 0.0 copy-start.6
  76.1 0.0 collective-permute-done.8.refs_5_
  76.1 0.0 copy-start.7
  76.1 0.0 copy-done.3
  76.1 0.0 copy-done.4
  76.1 0.0 copy-done.10
  76.1 0.7 copy-done.5
  76.8 0.2 copy-done.6
  77.0 0.2 copy-done.7
  77.2 2.9 %gather.1 = bf16[512,896]{1,0:T(8,128)(2,1)} custom-call(s32[1]{0:T(128)} %bitcast.1.position_ref, s32[2,2]{1,0:T(2,128)} %copy-done.10, bf16[128,896]{1,0:T(8,128)(2,1)} %refs_0_.7, bf16[128,896]{1,0:T(8,128)(2,1)} %copy-done.3, bf16[128,896]{1,0:T(8,128)(2,1)} %copy-done.4, bf16[256,896]{1,0:T(8,128)(2,1)} %copy-done.5, bf16[256,896]{1,0:T(8,128)(2,1)} %copy-done.6, ...), custom_call_target="tpu_custom_call" | custom-call | bytes 3670016 | tf_op jit(solution)/shard_map/gather/pallas_call | solution.py:444
  80.1 0.1 collective-permute-start.10
  80.2 0.0 copy-done.1
  80.2 7.2 %own.1 = (f32[16,128,128]{2,1,0:T(8,128)}, f32[16,128,128]{2,1,0:T(8,128)}) custom-call(bf16[16,128,128]{2,1,0:T(8,128)(2,1)} %copy-done.1, bf16[16,256,128]{2,1,0:T(8,128)(2,1)} %copy-done), custom_call_target="tpu_custom_call" | custom-call | flops 1073741824 | bytes 1572864 | tf_op jit(solution)/shard_map/own/pallas_call | solution.py:234
  87.4 0.0 collective-permute-done.kv_ref
  87.4 7.7 %previous.1 = (bf16[16,128,128]{2,1,0:T(8,128)(2,1)}, f32[8,128,128]{2,1,0:T(8,128)}, f32[8,128,128]{2,1,0:T(8,128)}) custom-call(s32[1]{0:T(128)} %bitcast.flag_ref, bf16[16,128,128]{2,1,0:T(8,128)(2,1)} %copy-done.1, bf16[8,256,128]{2,1,0:T(8,128)(2,1)} %collective-permute-done.kv_ref, f32[16,128,128]{2,1,0:T(8,128)} %get-tuple-element.10.out1_ref, ...), custom_call_target="tpu_custom_call" | custom-call | flops 805306368 | bytes 2621440 | tf_op jit(solution)/shard_map/previous/pallas_call | solution.py:260
  95.0 0.0 collective-permute-done.2.back_ref
  95.0 2.9 %merge.1 = bf16[16,128,128]{2,1,0:T(8,128)(2,1)} custom-call(s32[1]{0:T(128)} %bitcast.flag_ref, f32[8,128,128]{2,1,0:T(8,128)} %get-tuple-element.12.part_ref, f32[8,128,128]{2,1,0:T(8,128)} %get-tuple-element.13.stat_ref, bf16[9,128,128]{2,1,0:T(8,128)(2,1)} %collective-permute-done.2.back_ref, ...), custom_call_target="tpu_custom_call", output_to_operand_aliasing={{}: (4, {})} | custom-call | bytes 819200 | tf_op jit(solution)/shard_map/merge/pallas_call | solution.py:274
  97.9 0.0 copy-done.9
  98.0 12.4 %all-to-all-start.2 = ((bf16[16,128,128]{2,1,0:T(8,128)(2,1)}), bf16[16,128,128]{2,1,0:T(8,128)(2,1)S(1)}, u32[]{:S(2)}, u32[]{:S(2)}) async-start(bf16[16,128,128]{2,1,0:T(8,128)(2,1)} %merge.1), calls=%async_computation.2 | async-start | bytes 1048576 | tf_op jit(solution)/shard_map/all_to_all | solution.py:517
  110.4 5.8 %absorb.1.refs_7_ = bf16[2,1024,896]{2,1,0:T(8,128)(2,1)} custom-call(bf16[128,2048]{1,0:T(8,128)(2,1)} %q_ref.1, bf16[896,4096]{1,0:T(8,128)(2,1)} %refs_8_.1), custom_call_target="tpu_custom_call" | custom-call | flops 469762048 | bytes 7340032 | tf_op jit(solution)/shard_map/absorb/pallas_call | solution.py:460
  116.2 0.0 collective-permute-done.10.refs_6_
  116.2 0.0 copy-start.8
  116.2 0.9 copy-done.8
  117.2 10.6 %cross.1.cross_ref = f32[128,2048]{1,0:T(8,128)} custom-call(s32[1]{0:T(128)} %bitcast.1.position_ref, s32[2,2]{1,0:T(2,128)} %copy-done.9, bf16[128,896]{1,0:T(8,128)(2,1)} %refs_0_.7, bf16[128,896]{1,0:T(8,128)(2,1)} %copy-done.3, bf16[128,896]{1,0:T(8,128)(2,1)} %copy-done.4, bf16[256,896]{1,0:T(8,128)(2,1)} %copy-done.5, bf16[256,896]{1,0:T(8,128)(2,1)} %copy-done.6, ...), custom_call_target="tpu_custom_call" | custom-call | flops 2348810240 | bytes 9175040 | tf_op jit(solution)/shard_map/cross/pallas_call | solution.py:481
  127.8 0.0 all-to-all-done.2.self_ref
  127.8 0.0 copy-start.2
  127.8 0.8 copy-done.2
  128.6 2.3 %total.1 = bf16[128,2048]{1,0:T(8,128)(2,1)} custom-call(bf16[16,128,128]{2,1,0:T(8,128)(2,1)} %copy-done.2, f32[128,2048]{1,0:T(8,128)} %cross.1.cross_ref), custom_call_target="tpu_custom_call" | custom-call | tf_op jit(solution)/shard_map/total/pallas_call | solution.py:518
  (8 shorter events, 0.0 us)
Async XLA Ops:
  0.0 45.3 %copy-start.12 = (s32[2]{0:T(128)S(1)}, s32[2]{0:T(128)}, u32[]{:S(2)}) copy-start(s32[2]{0:T(128)} %param.14) | copy-start | bytes 28
  0.0 45.3 %copy-start.11 = (s32[2,2]{1,0:T(2,128)S(1)}, s32[2,2]{1,0:T(2,128)}, u32[]{:S(2)}) copy-start(s32[2,2]{1,0:T(2,128)} %param.15) | copy-start | bytes 52
  2.4 19.9 %all-to-all-start.1 = ((bf16[16,256,128]{2,1,0:T(8,128)(2,1)}), bf16[16,256,128]{2,1,0:T(8,128)(2,1)S(1)}, u32[]{:S(2)}, u32[]{:S(2)}) async-start(bf16[16,256,128]{2,1,0:T(8,128)(2,1)} %pack.3), calls=%async_computation.1 | async-start | bytes 2097152 | tf_op jit(solution)/shard_map/all_to_all | solution.py:226
  7.9 19.6 %collective-permute-start.4 = (bf16[128,896]{1,0:T(8,128)(2,1)}, bf16[128,896]{1,0:T(8,128)(2,1)S(1)}, u32[]{:S(2)}, u32[]{:S(2)}) collective-permute-start(bf16[128,896]{1,0:T(8,128)(2,1)} %refs_0_.7), channel_id=1, source_target_pairs={{0,8},{1,9},{2,10},{3,11},{4,12},{5,13},{6,14},{7,15},{8,16},{9,17... | collective-permute-start | bytes 688136 | tf_op jit(solution)/shard_map/ppermute | solution.py:24
  22.3 48.7 %copy-start = (bf16[16,256,128]{2,1,0:T(8,128)(2,1)}, bf16[16,256,128]{2,1,0:T(8,128)(2,1)S(1)}, u32[]{:S(2)}) copy-start(bf16[16,256,128]{2,1,0:T(8,128)(2,1)S(1)} %all-to-all-done.1.kv_ref) | copy-start | bytes 3145732
  22.3 28.6 %all-to-all-start = ((bf16[16,128,128]{2,1,0:T(8,128)(2,1)}), bf16[16,128,128]{2,1,0:T(8,128)(2,1)S(1)}, u32[]{:S(2)}, u32[]{:S(2)}) async-start(bf16[16,128,128]{2,1,0:T(8,128)(2,1)} %pack.2), calls=%async_computation | async-start | bytes 1048576 | tf_op jit(solution)/shard_map/all_to_all | solution.py:230
  27.5 48.6 %copy-start.3 = (bf16[128,896]{1,0:T(8,128)(2,1)}, bf16[128,896]{1,0:T(8,128)(2,1)S(1)}, u32[]{:S(2)}) copy-start(bf16[128,896]{1,0:T(8,128)(2,1)S(1)} %collective-permute-done.4.refs_1_) | copy-start | bytes 688132
  27.5 10.7 %collective-permute-start.5 = (bf16[128,896]{1,0:T(8,128)(2,1)S(1)}, bf16[128,896]{1,0:T(8,128)(2,1)S(1)}, u32[]{:S(2)}, u32[]{:S(2)}) collective-permute-start(bf16[128,896]{1,0:T(8,128)(2,1)S(1)} %collective-permute-done.4.refs_1_), channel_id=1, source_target_pairs={{0,8},{1,9},{2,10},{3,11},{4,12},{5,13},{6,14},{7,15},{8,16},{9,17... | collective-permute-start | bytes 688136 | tf_op jit(solution)/shard_map/ppermute | solution.py:24
  38.2 37.9 %copy-start.4 = (bf16[128,896]{1,0:T(8,128)(2,1)}, bf16[128,896]{1,0:T(8,128)(2,1)S(1)}, u32[]{:S(2)}) copy-start(bf16[128,896]{1,0:T(8,128)(2,1)S(1)} %collective-permute-done.5.refs_2_) | copy-start | bytes 688132
  40.5 35.6 %collective-permute-start.6 = (bf16[256,896]{1,0:T(8,128)(2,1)}, bf16[256,896]{1,0:T(8,128)(2,1)S(1)}, u32[]{:S(2)}, u32[]{:S(2)}) collective-permute-start(bf16[256,896]{1,0:T(8,128)(2,1)} %get-tuple-element.20), channel_id=1, source_target_pairs={{0,2},{1,3},{2,0},{3,1},{4,6},{5,7},{6,4},{7,5},{8,10},{9,11},{10,... | collective-permute-start | bytes 1376264 | tf_op jit(solution)/shard_map/ppermute | solution.py:29
  40.8 35.3 %collective-permute-start.7 = (bf16[256,896]{1,0:T(8,128)(2,1)}, bf16[256,896]{1,0:T(8,128)(2,1)S(1)}, u32[]{:S(2)}, u32[]{:S(2)}) collective-permute-start(bf16[256,896]{1,0:T(8,128)(2,1)} %get-tuple-element.19), channel_id=1, source_target_pairs={{0,4},{1,5},{2,6},{3,7},{4,0},{5,1},{6,2},{7,3},{8,12},{9,13},{10,... | collective-permute-start | bytes 1376264 | tf_op jit(solution)/shard_map/ppermute | solution.py:29
  41.1 35.0 %collective-permute-start.8 = (bf16[256,896]{1,0:T(8,128)(2,1)}, bf16[256,896]{1,0:T(8,128)(2,1)S(1)}, u32[]{:S(2)}, u32[]{:S(2)}) collective-permute-start(bf16[256,896]{1,0:T(8,128)(2,1)} %get-tuple-element.18), channel_id=1, source_target_pairs={{0,6},{1,7},{2,4},{3,5},{4,2},{5,3},{6,0},{7,1},{8,14},{9,15},{10,... | collective-permute-start | bytes 1376264 | tf_op jit(solution)/shard_map/ppermute | solution.py:29
  44.0 43.4 %collective-permute-start = (bf16[8,256,128]{2,1,0:T(8,128)(2,1)}, bf16[8,256,128]{2,1,0:T(8,128)(2,1)}, u32[]{:S(2)}, u32[]{:S(2)}) collective-permute-start(bf16[8,256,128]{2,1,0:T(8,128)(2,1)} %slice.16), channel_id=1, source_target_pairs={{0,16},{1,17},{2,18},{3,19},{4,20},{5,21},{6,22},{7,23},{8,24},{9,... | collective-permute-start | bytes 1572872 | tf_op jit(solution)/shard_map/ppermute | solution.py:24
  45.4 6.3 %collective-permute-start.3 = (s32[2,2]{1,0:T(2,128)S(1)}, s32[2,2]{1,0:T(2,128)S(1)}, u32[]{:S(2)}, u32[]{:S(2)}) collective-permute-start(s32[2,2]{1,0:T(2,128)S(1)} %multiply_add_fusion), channel_id=1, source_target_pairs={{0,1},{1,2},{2,3},{3,4},{4,5},{5,6},{6,7},{7,8},{8,9},{9,10},{10,1... | collective-permute-start | bytes 56 | tf_op jit(solution)/shard_map/ppermute | solution.py:24
  51.0 29.2 %copy-start.1 = (bf16[16,128,128]{2,1,0:T(8,128)(2,1)}, bf16[16,128,128]{2,1,0:T(8,128)(2,1)S(1)}, u32[]{:S(2)}) copy-start(bf16[16,128,128]{2,1,0:T(8,128)(2,1)S(1)} %all-to-all-done.q_ref) | copy-start | bytes 1572868
  51.7 11.6 %collective-permute-start.1 = (bf16[8,128,128]{2,1,0:T(8,128)(2,1)S(1)}, bf16[8,128,128]{2,1,0:T(8,128)(2,1)}, u32[]{:S(2)}, u32[]{:S(2)}) collective-permute-start(bf16[8,128,128]{2,1,0:T(8,128)(2,1)S(1)} %slice.17), channel_id=1, source_target_pairs={{16,0},{17,1},{18,2},{19,3},{20,4},{21,5},{22,6},{23,7},{24,8},{25... | collective-permute-start | bytes 786440 | tf_op jit(solution)/shard_map/ppermute | solution.py:24
  60.7 37.2 %copy-start.9 = (s32[2,2]{1,0:T(2,128)}, s32[2,2]{1,0:T(2,128)S(1)}, u32[]{:S(2)}) copy-start(s32[2,2]{1,0:T(2,128)S(1)} %pad_add_fusion.table_ref) | copy-start | bytes 52
  63.3 11.5 %collective-permute-start.9 = (s32[2,2]{1,0:T(2,128)S(1)}, s32[2,2]{1,0:T(2,128)S(1)}, u32[]{:S(2)}, u32[]{:S(2)}) collective-permute-start(s32[2,2]{1,0:T(2,128)S(1)} %pad_add_fusion.table_ref), channel_id=1, source_target_pairs={{0,1},{1,0},{2,3},{3,2},{4,5},{5,4},{6,7},{7,6},{8,9},{9,8},{10,11... | collective-permute-start | bytes 56 | tf_op jit(solution)/shard_map/ppermute | solution.py:29
  74.7 1.4 %copy-start.10 = (s32[2,2]{1,0:T(2,128)}, s32[2,2]{1,0:T(2,128)S(1)}, u32[]{:S(2)}) copy-start(s32[2,2]{1,0:T(2,128)S(1)} %collective-permute-done.9.theirs_ref) | copy-start | bytes 52
  74.8 20.3 %collective-permute-start.2 = (bf16[9,128,128]{2,1,0:T(8,128)(2,1)}, bf16[9,128,128]{2,1,0:T(8,128)(2,1)}, u32[]{:S(2)}, u32[]{:S(2)}) collective-permute-start(bf16[9,128,128]{2,1,0:T(8,128)(2,1)} %later.1), channel_id=1, source_target_pairs={{0,16},{1,17},{2,18},{3,19},{4,20},{5,21},{6,22},{7,23},{8,24},{9,... | collective-permute-start | bytes 884744 | tf_op jit(solution)/shard_map/ppermute | solution.py:24
  76.1 0.8 copy-start.5
  76.1 0.9 copy-start.6
  76.1 1.0 copy-start.7
  80.1 36.1 %collective-permute-start.10 = (bf16[512,896]{1,0:T(8,128)(2,1)}, bf16[512,896]{1,0:T(8,128)(2,1)S(1)}, u32[]{:S(2)}, u32[]{:S(2)}) collective-permute-start(bf16[512,896]{1,0:T(8,128)(2,1)} %gather.1), channel_id=1, source_target_pairs={{0,1},{1,0},{2,3},{3,2},{4,5},{5,4},{6,7},{7,6},{8,9},{9,8},{10,11... | collective-permute-start | bytes 2752520 | tf_op jit(solution)/shard_map/ppermute | solution.py:29
  98.0 29.8 %all-to-all-start.2 = ((bf16[16,128,128]{2,1,0:T(8,128)(2,1)}), bf16[16,128,128]{2,1,0:T(8,128)(2,1)S(1)}, u32[]{:S(2)}, u32[]{:S(2)}) async-start(bf16[16,128,128]{2,1,0:T(8,128)(2,1)} %merge.1), calls=%async_computation.2 | async-start | bytes 1048576 | tf_op jit(solution)/shard_map/all_to_all | solution.py:517
  116.2 1.0 copy-start.8
  127.8 0.8 copy-start.2

commit v7 on v6

--- a/solution.py
+++ b/solution.py
@@ -12,7 +12,7 @@
 HEAD_DIM = 128
 SPAN = 64
 PLANE = 8
-LEFT = 8
+LEFT = 12
 
 MASKED_SCORE = -1e30
 LOG2E = 1.4426950408889634
@@ -286,7 +286,7 @@
     )(flag, part, stat, back, rest)
 
 
-def wanted_pieces(table_ref, position, span_count):
+def wanted_pieces(table_ref, position, span_count, held):
     pieces = []
     place, plane = position % PLANE, position // PLANE
     for c in range(span_count):
@@ -297,10 +297,9 @@
                 relative = (block % PLANE) ^ place
                 away = plane - block // PLANE
                 column = relative // 2
-                index = jnp.where(
-                    column == 0, away, 1 + 2 * column + jnp.where(away == 1, 0, 1)
-                )
-                pieces.append((relative % 2 == 0, index, (source + later) % span_count))
+                index = jnp.where(column == 0, away, 1 + 2 * column + jnp.where(away == 1, 0, 1))
+                index = jnp.clip(index, 0, held - 1) + held * (relative % 2)
+                pieces.append((index, (source + later) % span_count))
     return pieces
 
 
@@ -316,21 +315,6 @@
             pltpu.make_async_copy(ref.at[pl.ds(start, size), :], target, sem).start()
 
         first += count
-
-
-def gather_kernel(span_count, position_ref, theirs_ref, *refs):
-    *in_refs, out_ref, sems = refs
-    rows = in_refs[0].shape[0]
-    pieces = wanted_pieces(theirs_ref, position_ref[0], span_count)
-    size = out_ref.shape[0] // len(pieces)
-    targets = [out_ref.at[n * size : (n + 1) * size, :] for n in range(len(pieces))]
-    for n, (here, index, half) in enumerate(pieces):
-        fetch(in_refs, rows, jnp.where(here, index, -1), half, targets[n], sems.at[n])
-    for n, (here, _, _) in enumerate(pieces):
-
-        @pl.when(here)
-        def _(n=n):
-            pltpu.make_async_copy(in_refs[0].at[0:size, :], targets[n], sems.at[n]).wait()
 
 
 def absorb_kernel(q_ref, weight_ref, out_ref, weights_ref, sems):
@@ -358,63 +342,84 @@
 
 
 def cross_kernel(scale, position_ref, table_ref, *refs):
-    *in_refs, theirs_ref, asks_ref, weight_ref, out_ref = refs[:-6]
-    rows_ref, all_asks_ref, weights_ref, sems, ask_sems, weight_sems = refs[-6:]
-    rows, width = out_ref.shape
+    *in_refs, asks_ref, out_ref = refs[:-6]
+    rows_ref, all_asks_ref, means_ref, sems, ask_sems, mean_sems = refs[-6:]
     steps, span_count, asked, _ = all_asks_ref.shape
+    rows = in_refs[0].shape[0]
     span = rows // span_count
-    block = weights_ref.shape[2]
-    pieces = wanted_pieces(table_ref, position_ref[0], span_count)
+    held = sum(ref.shape[0] for ref in in_refs) // rows // 2
+    pieces = wanted_pieces(table_ref, position_ref[0], span_count, held)
     targets = [rows_ref.at[n * span : (n + 1) * span, :] for n in range(len(pieces))]
-    held = sum(ref.shape[0] for ref in in_refs) // rows
-    for n, (here, index, half) in enumerate(pieces):
-        fetch(in_refs, rows, jnp.where(here, index, held), half, targets[n], sems.at[n])
-
-        @pl.when(jnp.logical_not(here))
-        def _(n=n):
-            source = theirs_ref.at[n * span : (n + 1) * span, :]
-            pltpu.make_async_copy(source, targets[n], sems.at[n]).start()
-
+    for n, (index, half) in enumerate(pieces):
+        fetch(in_refs, rows, index, half, targets[n], sems.at[n])
     ask_copies = [
         pltpu.make_async_copy(
             asks_ref.at[:, g * asked : (g + 1) * asked, :], all_asks_ref.at[g], ask_sems.at[g]
         )
         for g in range(steps)
     ]
-    weight_copies = [
+    height = means_ref.shape[1]
+    mean_copies = [
         pltpu.make_async_copy(
-            weight_ref.at[:, width + g * block : width + (g + 1) * block],
-            weights_ref.at[g],
-            weight_sems.at[g],
+            means_ref.at[g], out_ref.at[g * height : (g + 1) * height, :], mean_sems.at[g]
         )
         for g in range(steps)
     ]
-    for g in range(steps):
-        ask_copies[g].start()
-        weight_copies[g].start()
+    for copy in ask_copies:
+        copy.start()
     for n in range(len(pieces)):
-        pltpu.make_async_copy(theirs_ref.at[0:span, :], targets[n], sems.at[n]).wait()
+        pltpu.make_async_copy(in_refs[0].at[0:span, :], targets[n], sems.at[n]).wait()
 
     keys_of_span = rows_ref.shape[0] // span_count
     slot = lax.broadcasted_iota(jnp.int32, (asked, keys_of_span), 1) // (2 * span)
-    counts = [table_ref[c, 0] % 4 for c in range(span_count)]
     for g in range(steps):
         ask_copies[g].wait()
-        means = []
         for c in range(span_count):
+            count = table_ref[c, 0] % 4
             keys = rows_ref[c * keys_of_span : (c + 1) * keys_of_span, :]
-            s = jnp.where(slot < counts[c], scores_of(all_asks_ref[g, c], keys), MASKED_SCORE)
+            s = jnp.where(slot < count, scores_of(all_asks_ref[g, c], keys), MASKED_SCORE)
             p = jnp.exp2((s - jnp.max(s, axis=1, keepdims=True)) * scale)
-            inverse = jnp.where(counts[c] > 0, 1.0 / jnp.sum(p, axis=1, keepdims=True), 0.0)
+            inverse = jnp.where(count > 0, 1.0 / jnp.sum(p, axis=1, keepdims=True), 0.0)
             mean = jnp.dot(p.astype(jnp.bfloat16), keys, preferred_element_type=jnp.float32)
-            means.append((mean * inverse).astype(jnp.bfloat16))
-        weight_copies[g].wait()
+            mean = (mean * inverse).astype(jnp.bfloat16)
+            for h in range(asked // span):
+                place = h * rows + c * span
+                means_ref[g, place : place + span, :] = mean[h * span : (h + 1) * span]
+        mean_copies[g].start()
+    for copy in mean_copies:
+        copy.wait()
+
+
+def values_kernel(means_ref, weight_ref, out_ref, all_means_ref, weights_ref, sems):
+    rows, width = out_ref.shape
+    steps, _, block = weights_ref.shape
+    height = all_means_ref.shape[1]
+    copies = [
+        (
+            pltpu.make_async_copy(
+                means_ref.at[g * height : (g + 1) * height, :], all_means_ref.at[g], sems.at[0, g]
+            ),
+            pltpu.make_async_copy(
+                weight_ref.at[:, width + g * block : width + (g + 1) * block],
+                weights_ref.at[g],
+                sems.at[1, g],
+            ),
+        )
+        for g in range(steps)
+    ]
+    for pair in copies:
+        for copy in pair:
+            copy.start()
+    for g in range(steps):
+        for copy in copies[g]:
+            copy.wait()
         for h in range(block // HEAD_DIM):
-            mean = jnp.concatenate([m[h * span : (h + 1) * span] for m in means], axis=0)
             inner = slice(h * HEAD_DIM, (h + 1) * HEAD_DIM)
             lanes = slice(g * block + h * HEAD_DIM, g * block + (h + 1) * HEAD_DIM)
             out_ref[:, lanes] = jnp.dot(
-                mean, weights_ref[g, :, inner], preferred_element_type=jnp.float32
+                all_means_ref[g, h * rows : (h + 1) * rows, :],
+                weights_ref[g, :, inner],
+                preferred_element_type=jnp.float32,
             )
 
 
@@ -422,39 +427,25 @@
     rows, width = cross_queries.shape
     span_count = counts.shape[0]
     depth = encoded.shape[1]
+    heads = width // HEAD_DIM
     place = position % PLANE
     one_back = shifted(encoded, "ctx", PLANE)
     table = sources * 4 + counts[:, None]
     before = shifted(table, "ctx", 1)
     table = jnp.concatenate([before[-1:], table[:-1]], axis=0)
-    their_table = swapped(table, "ctx", 1)
     two_back = shifted(one_back, "ctx", PLANE)
-
+    far = [swapped(jnp.concatenate([encoded, one_back, two_back], axis=0), "ctx", 1)]
     near = []
     for bit in (2, 4, 6):
         other = jnp.where(place < (place ^ bit), encoded, two_back)
         near.append(swapped(jnp.concatenate([one_back, other], axis=0), "ctx", bit))
-
-    held = [encoded, one_back, two_back, *near]
-    where = position.reshape(1)
+        far.append(swapped(near[-1], "ctx", 1))
+
+    held = [encoded, one_back, two_back, *near, *far]
     picked = span_count * 4 * SPAN
     pieces = picked // SPAN
     smem, anywhere = (pl.BlockSpec(memory_space=m) for m in (pltpu.SMEM, pl.ANY))
     vmem = pl.BlockSpec(memory_space=pltpu.VMEM)
-    theirs = pl.pallas_call(
-        functools.partial(gather_kernel, span_count),
-        out_shape=jax.ShapeDtypeStruct((picked, depth), encoded.dtype),
-        in_specs=[smem] * 2 + [anywhere] * len(held),
-        out_specs=vmem,
-        scratch_shapes=[pltpu.SemaphoreType.DMA((pieces,))],
-        cost_estimate=pl.CostEstimate(
-            flops=0, bytes_accessed=8 * picked * depth, transcendentals=0
-        ),
-        name="gather",
-    )(where, their_table, *held)
-    theirs = swapped(theirs, "ctx", 1)
-
-    heads = width // HEAD_DIM
     block = 4 * HEAD_DIM
     steps = width // block
     asks = pl.pallas_call(
@@ -471,29 +462,46 @@
         ),
         name="absorb",
     )(cross_queries, weight)
-    block = 8 * HEAD_DIM
-    steps = width // block
-    cost = pl.CostEstimate(
-        flops=4 * picked * depth * heads * SPAN + 2 * rows * depth * width,
-        bytes_accessed=weight.size + asks.size * 2 + picked * depth * 4,
-        transcendentals=picked * SPAN * heads,
-    )
+    halves_of_heads = 2
+    means = pl.pallas_call(
+        functools.partial(cross_kernel, HEAD_DIM ** (-0.5) * LOG2E),
+        out_shape=jax.ShapeDtypeStruct((heads * rows, depth), jnp.bfloat16),
+        in_specs=[smem] * 2 + [anywhere] * (len(held) + 1),
+        out_specs=anywhere,
+        scratch_shapes=[
+            pltpu.VMEM((picked, depth), encoded.dtype),
+            pltpu.VMEM(
+                (halves_of_heads, span_count, heads * SPAN // halves_of_heads, depth), asks.dtype
+            ),
+            pltpu.VMEM((halves_of_heads, heads * rows // halves_of_heads, depth), jnp.bfloat16),
+            pltpu.SemaphoreType.DMA((pieces,)),
+            pltpu.SemaphoreType.DMA((halves_of_heads,)),
+            pltpu.SemaphoreType.DMA((halves_of_heads,)),
+        ],
+        cost_estimate=pl.CostEstimate(
+            flops=4 * picked * depth * heads * SPAN,
+            bytes_accessed=asks.size * 4 + picked * depth * 2,
+            transcendentals=picked * SPAN * heads,
+        ),
+        name="cross",
+    )(position.reshape(1), table, *held, asks)
     return pl.pallas_call(
-        functools.partial(cross_kernel, HEAD_DIM ** (-0.5) * LOG2E),
+        values_kernel,
         out_shape=jax.ShapeDtypeStruct((rows, width), jnp.float32),
-        in_specs=[smem] * 2 + [anywhere] * (len(held) + 3),
+        in_specs=[anywhere] * 2,
         out_specs=vmem,
         scratch_shapes=[
-            pltpu.VMEM((picked, depth), encoded.dtype),
-            pltpu.VMEM((steps, span_count, heads * SPAN // steps, depth), asks.dtype),
+            pltpu.VMEM((steps, heads * rows // steps, depth), jnp.bfloat16),
             pltpu.VMEM((steps, depth, block), weight.dtype),
-            pltpu.SemaphoreType.DMA((pieces,)),
-            pltpu.SemaphoreType.DMA((steps,)),
-            pltpu.SemaphoreType.DMA((steps,)),
+            pltpu.SemaphoreType.DMA((2, steps)),
         ],
-        cost_estimate=cost,
-        name="cross",
-    )(where, table, *held, theirs, asks, weight)
+        cost_estimate=pl.CostEstimate(
+            flops=2 * rows * depth * width,
+            bytes_accessed=weight.size + means.size * 2,
+            transcendentals=0,
+        ),
+        name="values",
+    )(means, weight)
 
 
 def sum_kernel(self_ref, cross_ref, out_ref):

time: 132 us -> 116 us (0.88)
  starting transfers between devices: 57 us -> 42.4 us
  waiting for transfers between devices: 20.1 us -> 17.1 us
    all_to_all x1, waiting for transfers between devices: 9.38 us -> 0.01 us  [self_attention(): lax.all_to_all(packed(keys, values), 'ctx', 0, 0, axis_index_groups=group...]
    ppermute x6, starting transfers between devices: 23.4 us -> 15.2 us  [shifted(): lax.ppermute(value, axis, [(source, source + steps) for source in range(f...]
    ppermute x5 -> x7, starting transfers between devices: 10.4 us -> 3.74 us  [swapped(): lax.ppermute(value, axis, [(source, source ^ bit) for source in range(cou...]
    all_to_all x1, waiting for transfers between devices: 0.01 us -> 5.95 us  [self_attention(): lax.all_to_all(packed(queries), 'ctx', 0, 0, axis_index_groups=groups, ti...]
    pallas_call x1, Pallas kernels: 10.6 us -> 8.51 us  [cross_attention(): pl.pallas_call(functools.partial(cross_kernel, HEAD_DIM ** (-0.5) * LOG2E...]
    pallas_call x1, Pallas kernels: 2.93 us -> 4.57 us  [cross_attention(): pl.pallas_call(values_kernel, out_shape=jax.ShapeDtypeStruct((rows, width...]
    pallas_call x1, Pallas kernels: 3.75 us -> 5.16 us  [self_attention(): pl.pallas_call(functools.partial(later_kernel, scale), out_shape=jax.Shap...]
    unnamed x26 -> x30, local copies, waits for them, and re-layouts: 2.77 us -> 3.91 us
  transfers between devices with their start and end apart: 14 -> 16, of which waited for: 4 -> 2; matrix products, arithmetic and copies ran while one was open for 2% -> 2% of each run, Pallas kernels for 33% -> 38%
where the time goes in v7:
time: 116 us; the launch traced here: 115 us
  Pallas kernels  48.2 us (42%)
  starting transfers between devices  42.4 us (37%)
  waiting for transfers between devices  17.1 us (15%)
  local copies, waits for them, and re-layouts  4.69 us (4%)
  other arithmetic  1.95 us (2%)
    ppermute x6, starting transfers between devices, shifted(): lax.ppermute(value, axis, [(source, source + steps) for source in range(f...  15.2 us
    all_to_all x1, starting transfers between devices, per_device(): lax.all_to_all(by_head, 'ctx', 0, 0, axis_index_groups=groups, tiled=True)  12.2 us
    ppermute x6, waiting for transfers between devices, shifted(): lax.ppermute(value, axis, [(source, source + steps) for source in range(f...  11.1 us
    pallas_call x1, Pallas kernels, cross_attention(): pl.pallas_call(functools.partial(cross_kernel, HEAD_DIM ** (-0.5) * LOG2E...  8.51 us
    pallas_call x1, Pallas kernels, self_attention(): pl.pallas_call(functools.partial(own_kernel, scale), out_shape=(jax.Shape...  7.18 us
    pallas_call x1, Pallas kernels, self_attention(): pl.pallas_call(functools.partial(previous_kernel, scale), out_shape=(jax....  6.7 us
    all_to_all x1, waiting for transfers between devices, self_attention(): lax.all_to_all(packed(queries), 'ctx', 0, 0, axis_index_groups=groups, ti...  5.95 us
    pallas_call x1, Pallas kernels, cross_attention(): pl.pallas_call(absorb_kernel, out_shape=jax.ShapeDtypeStruct((span_count,...  5.85 us
  transfers between devices with their start and end apart: 16, of which 2 were waited for; matrix products, arithmetic and copies ran while one was open for 2% of the time, Pallas kernels for 38%

profile of v7, /device:TPU:23, one launch (start us, length us, event | category | flops | bytes accessed | tf_op | source)
XLA Modules:
  0.0 114.6 jit_solution(18424171452433032163)
XLA Ops:
  0.0 1.9 %pack.2 = bf16[16,128,128]{2,1,0:T(8,128)(2,1)} custom-call(bf16[128,2048]{1,0:T(8,128)(2,1)} %refs_0_.3), custom_call_target="tpu_custom_call" | custom-call | bytes 1048576 | tf_op jit(solution)/shard_map/pack/pallas_call | solution.py:43
  1.9 5.5 %all-to-all-start = ((bf16[16,128,128]{2,1,0:T(8,128)(2,1)}), bf16[16,128,128]{2,1,0:T(8,128)(2,1)S(1)}, u32[]{:S(2)}, u32[]{:S(2)}) async-start(bf16[16,128,128]{2,1,0:T(8,128)(2,1)} %pack.2), calls=%async_computation | async-start | bytes 1048576 | tf_op jit(solution)/shard_map/all_to_all | solution.py:230
  7.4 2.4 %pack.3 = bf16[16,256,128]{2,1,0:T(8,128)(2,1)} custom-call(bf16[128,2048]{1,0:T(8,128)(2,1)} %refs_0_.4, bf16[128,2048]{1,0:T(8,128)(2,1)} %refs_1_.1), custom_call_target="tpu_custom_call" | custom-call | bytes 2097152 | tf_op jit(solution)/shard_map/pack/pallas_call | solution.py:43
  9.8 5.9 %all-to-all-done.q_ref = bf16[16,128,128]{2,1,0:T(8,128)(2,1)S(1)} async-done(((bf16[16,128,128]{2,1,0:T(8,128)(2,1)}), bf16[16,128,128]{2,1,0:T(8,128)(2,1)S(1)}, u32[]{:S(2)}, u32[]{:S(2)}) %all-to-all-start) | async-done | bytes 524320 | tf_op jit(solution)/shard_map/all_to_all | solution.py:230
  15.7 5.8 %all-to-all-start.1 = ((bf16[16,256,128]{2,1,0:T(8,128)(2,1)}), bf16[16,256,128]{2,1,0:T(8,128)(2,1)S(1)}, u32[]{:S(2)}, u32[]{:S(2)}) async-start(bf16[16,256,128]{2,1,0:T(8,128)(2,1)} %pack.3), calls=%async_computation.1 | async-start | bytes 2097152 | tf_op jit(solution)/shard_map/all_to_all | solution.py:226
  21.5 0.0 copy-done.3
  21.5 3.1 %collective-permute-start.4 = (bf16[128,896]{1,0:T(8,128)(2,1)S(1)}, bf16[128,896]{1,0:T(8,128)(2,1)S(1)}, u32[]{:S(2)}, u32[]{:S(2)}) collective-permute-start(bf16[128,896]{1,0:T(8,128)(2,1)S(1)} %copy-done.3), channel_id=1, source_target_pairs={{0,8},{1,9},{2,10},{3,11},{4,12},{5,13},{6,14},{7,15},{8,16},{9,17... | collective-permute-start | bytes 688136 | tf_op jit(solution)/shard_map/ppermute | solution.py:24
  24.7 0.0 copy-done
  24.7 2.0 %collective-permute-start.1 = (bf16[12,128,128]{2,1,0:T(8,128)(2,1)S(1)}, bf16[12,128,128]{2,1,0:T(8,128)(2,1)S(1)}, u32[]{:S(2)}, u32[]{:S(2)}) collective-permute-start(bf16[12,128,128]{2,1,0:T(8,128)(2,1)S(1)} %slice.17), channel_id=1, source_target_pairs={{16,0},{17,1},{18,2},{19,3},{20,4},{21,5},{22,6},{23,7},{24,8},{25... | collective-permute-start | bytes 1179656 | tf_op jit(solution)/shard_map/ppermute | solution.py:24
  26.7 11.1 %collective-permute-done.4.refs_1_ = bf16[128,896]{1,0:T(8,128)(2,1)S(1)} collective-permute-done((bf16[128,896]{1,0:T(8,128)(2,1)S(1)}, bf16[128,896]{1,0:T(8,128)(2,1)S(1)}, u32[]{:S(2)}, u32[]{:S(2)}) %collective-permute-start.4) | collective-permute-done | bytes 229408 | tf_op jit(solution)/shard_map/ppermute | solution.py:24
  37.8 4.1 %collective-permute-start.5 = (bf16[128,896]{1,0:T(8,128)(2,1)S(1)}, bf16[128,896]{1,0:T(8,128)(2,1)S(1)}, u32[]{:S(2)}, u32[]{:S(2)}) collective-permute-start(bf16[128,896]{1,0:T(8,128)(2,1)S(1)} %collective-permute-done.4.refs_1_), channel_id=1, source_target_pairs={{0,8},{1,9},{2,10},{3,11},{4,12},{5,13},{6,14},{7,15},{8,16},{9,17... | collective-permute-start | bytes 688136 | tf_op jit(solution)/shard_map/ppermute | solution.py:24
  42.0 0.0 all-to-all-done.1.kv_ref
  42.0 0.0 copy-start.5
  42.0 0.8 slice.16
  42.7 1.3 %collective-permute-start = (bf16[4,256,128]{2,1,0:T(8,128)(2,1)}, bf16[4,256,128]{2,1,0:T(8,128)(2,1)S(1)}, u32[]{:S(2)}, u32[]{:S(2)}) collective-permute-start(bf16[4,256,128]{2,1,0:T(8,128)(2,1)} %slice.16), channel_id=1, source_target_pairs={{0,16},{1,17},{2,18},{3,19},{4,20},{5,21},{6,22},{7,23},{8,24},{9,... | collective-permute-start | bytes 786440 | tf_op jit(solution)/shard_map/ppermute | solution.py:24
  44.0 0.0 collective-permute-done.1.q_ref
  44.0 0.0 copy-done.5
  44.0 0.0 copy-start.14
  44.1 0.7 copy-done.14
  44.8 5.2 %later.1 = bf16[13,128,128]{2,1,0:T(8,128)(2,1)} custom-call(bf16[12,128,128]{2,1,0:T(8,128)(2,1)} %copy-done.14, bf16[16,256,128]{2,1,0:T(8,128)(2,1)} %copy-done.5), custom_call_target="tpu_custom_call" | custom-call | flops 603979776 | bytes 393216 | tf_op jit(solution)/shard_map/later/pallas_call | solution.py:248
  50.0 1.3 %collective-permute-start.2 = (bf16[13,128,128]{2,1,0:T(8,128)(2,1)}, bf16[13,128,128]{2,1,0:T(8,128)(2,1)S(1)}, u32[]{:S(2)}, u32[]{:S(2)}) collective-permute-start(bf16[13,128,128]{2,1,0:T(8,128)(2,1)} %later.1), channel_id=1, source_target_pairs={{0,16},{1,17},{2,18},{3,19},{4,20},{5,21},{6,22},{7,23},{8,24},{9,... | collective-permute-start | bytes 1277960 | tf_op jit(solution)/shard_map/ppermute | solution.py:24
  51.2 0.0 collective-permute-done.5.refs_2_
  51.3 0.0 copy-start.4
  51.3 0.1 broadcast_select_fusion
  51.3 1.2 %pad_maximum_fusion.1 = (bf16[256,896]{1,0:T(8,128)(2,1)}, bf16[256,896]{1,0:T(8,128)(2,1)}, bf16[256,896]{1,0:T(8,128)(2,1)}) fusion(bf16[128,896]{1,0:T(8,128)(2,1)S(1)} %collective-permute-done.4.refs_1_, bf16[128,896]{1,0:T(8,128)(2,1)S(1)} %get-tuple-element.15, bf16[128,896]{1,0:T(8,128)(2,1)S(1)} %get-tuple-element.16, ...), kind=kLoop, calls=%fused_computation.1 | loop fusion | flops 2293760 | bytes 2293760 | tf_op jit(solution)/shard_map/concatenate | solution.py:441
  52.5 0.3 collective-permute-start.6
  52.8 0.3 collective-permute-start.7
  53.1 2.0 %collective-permute-start.8 = (bf16[256,896]{1,0:T(8,128)(2,1)}, bf16[256,896]{1,0:T(8,128)(2,1)S(1)}, u32[]{:S(2)}, u32[]{:S(2)}) collective-permute-start(bf16[256,896]{1,0:T(8,128)(2,1)} %get-tuple-element.18), channel_id=1, source_target_pairs={{0,6},{1,7},{2,4},{3,5},{4,2},{5,3},{6,0},{7,1},{8,14},{9,15},{10,... | collective-permute-start | bytes 1376264 | tf_op jit(solution)/shard_map/ppermute | solution.py:29
  55.2 7.2 %own.1 = (f32[16,128,128]{2,1,0:T(8,128)}, f32[16,128,128]{2,1,0:T(8,128)}) custom-call(bf16[16,128,128]{2,1,0:T(8,128)(2,1)} %copy-done, bf16[16,256,128]{2,1,0:T(8,128)(2,1)} %copy-done.5), custom_call_target="tpu_custom_call" | custom-call | flops 1073741824 | bytes 1572864 | tf_op jit(solution)/shard_map/own/pallas_call | solution.py:234
  62.3 0.0 collective-permute-done.kv_ref
  62.3 0.7 copy-done.11
  63.0 6.7 %previous.1 = (bf16[16,128,128]{2,1,0:T(8,128)(2,1)}, f32[12,128,128]{2,1,0:T(8,128)}, f32[12,128,128]{2,1,0:T(8,128)}) custom-call(s32[1]{0:T(128)} %bitcast.flag_ref, bf16[16,128,128]{2,1,0:T(8,128)(2,1)} %copy-done, bf16[4,256,128]{2,1,0:T(8,128)(2,1)} %copy-done.11, f32[16,128,128]{2,1,0:T(8,128)} %get-tuple-element.10.out1_ref, ...), custom_call_target="tpu_custom_call" | custom-call | flops 469762048 | bytes 2621440 | tf_op jit(solution)/shard_map/previous/pallas_call | solution.py:260
  69.8 0.0 collective-permute-done.2.back_ref
  69.8 0.8 copy-done.10
  70.5 3.6 %merge.1 = bf16[16,128,128]{2,1,0:T(8,128)(2,1)} custom-call(s32[1]{0:T(128)} %bitcast.flag_ref, f32[12,128,128]{2,1,0:T(8,128)} %get-tuple-element.12.part_ref, f32[12,128,128]{2,1,0:T(8,128)} %get-tuple-element.13.stat_ref, bf16[13,128,128]{2,1,0:T(8,128)(2,1)} %copy-done.10, ...), custom_call_target="tpu_custom_call", output_to_operand_aliasing={{}: (4, {})} | custom-call | bytes 1212416 | tf_op jit(solution)/shard_map/merge/pallas_call | solution.py:274
  74.1 0.0 copy-start.12
  74.1 0.0 copy-start.13
  74.2 12.2 %all-to-all-start.2 = ((bf16[16,128,128]{2,1,0:T(8,128)(2,1)}), bf16[16,128,128]{2,1,0:T(8,128)(2,1)S(1)}, u32[]{:S(2)}, u32[]{:S(2)}) async-start(bf16[16,128,128]{2,1,0:T(8,128)(2,1)} %merge.1), calls=%async_computation.2 | async-start | bytes 1048576 | tf_op jit(solution)/shard_map/all_to_all | solution.py:525
  86.4 0.0 copy-done.2
  86.4 0.0 copy-done.4
  86.4 0.1 pad_maximum_fusion
  86.4 0.5 collective-permute-start.9
  86.9 0.0 collective-permute-done.6.refs_3_
  86.9 0.1 collective-permute-start.10
  87.0 0.0 collective-permute-done.7.refs_4_
  87.0 0.4 collective-permute-start.11
  87.4 0.0 collective-permute-done.8.refs_5_
  87.4 0.1 collective-permute-start.12
  87.5 0.0 copy-done.12
  87.5 0.1 multiply_add_fusion
  87.6 3.4 %collective-permute-start.3 = (s32[2,2]{1,0:T(2,128)S(1)}, s32[2,2]{1,0:T(2,128)S(1)}, u32[]{:S(2)}, u32[]{:S(2)}) collective-permute-start(s32[2,2]{1,0:T(2,128)S(1)} %multiply_add_fusion), channel_id=1, source_target_pairs={{0,1},{1,2},{2,3},{3,4},{4,5},{5,6},{6,7},{7,8},{8,9},{9,10},{10,1... | collective-permute-start | bytes 56 | tf_op jit(solution)/shard_map/ppermute | solution.py:24
  91.0 5.9 %absorb.1.refs_10_ = bf16[2,1024,896]{2,1,0:T(8,128)(2,1)} custom-call(bf16[128,2048]{1,0:T(8,128)(2,1)} %q_ref.1, bf16[896,4096]{1,0:T(8,128)(2,1)} %weight_ref.3), custom_call_target="tpu_custom_call" | custom-call | flops 469762048 | bytes 7340032 | tf_op jit(solution)/shard_map/absorb/pallas_call | solution.py:451
  96.9 0.0 collective-permute-done.3
  96.9 0.6 pad_add_fusion.table_ref
  97.5 0.0 collective-permute-done.9.refs_6_
  97.5 0.0 collective-permute-done.10.refs_7_
  97.5 0.0 collective-permute-done.11.refs_8_
  97.5 0.0 collective-permute-done.12.refs_9_
  97.5 0.9 copy-done.6
  98.4 8.5 %cross.1.means_ref = bf16[2048,896]{1,0:T(8,128)(2,1)} custom-call(s32[1]{0:T(128)} %bitcast.1.position_ref, s32[2,2]{1,0:T(2,128)} %pad_add_fusion.table_ref, bf16[128,896]{1,0:T(8,128)(2,1)} %refs_0_.5, bf16[128,896]{1,0:T(8,128)(2,1)} %copy-done.2, bf16[128,896]{1,0:T(8,128)(2,1)} %copy-done.4, bf16[256,896]{1,0:T(8,128)(2,1)} %copy-done.7, ...), custom_call_target="tpu_custom_call" | custom-call | flops 1879048192 | bytes 8257536 | tf_op jit(solution)/shard_map/cross/pallas_call | solution.py:466
  106.9 4.6 %values.1.cross_ref = f32[128,2048]{1,0:T(8,128)} custom-call(bf16[2048,896]{1,0:T(8,128)(2,1)} %cross.1.means_ref, bf16[896,4096]{1,0:T(8,128)(2,1)} %weight_ref.3), custom_call_target="tpu_custom_call" | custom-call | flops 469762048 | bytes 7340032 | tf_op jit(solution)/shard_map/values/pallas_call | solution.py:488
  111.5 0.0 all-to-all-done.2.self_ref
  111.5 0.8 copy-done.1
  112.3 2.3 %total.1 = bf16[128,2048]{1,0:T(8,128)(2,1)} custom-call(bf16[16,128,128]{2,1,0:T(8,128)(2,1)} %copy-done.1, f32[128,2048]{1,0:T(8,128)} %values.1.cross_ref), custom_call_target="tpu_custom_call" | custom-call | tf_op jit(solution)/shard_map/total/pallas_call | solution.py:526
  (17 shorter events, 0.1 us)
Async XLA Ops:
  1.9 13.8 %all-to-all-start = ((bf16[16,128,128]{2,1,0:T(8,128)(2,1)}), bf16[16,128,128]{2,1,0:T(8,128)(2,1)S(1)}, u32[]{:S(2)}, u32[]{:S(2)}) async-start(bf16[16,128,128]{2,1,0:T(8,128)(2,1)} %pack.2), calls=%async_computation | async-start | bytes 1048576 | tf_op jit(solution)/shard_map/all_to_all | solution.py:230
  9.8 11.7 %copy-start.3 = (bf16[128,896]{1,0:T(8,128)(2,1)S(1)}, bf16[128,896]{1,0:T(8,128)(2,1)}, u32[]{:S(2)}) copy-start(bf16[128,896]{1,0:T(8,128)(2,1)} %refs_0_.5) | copy-start | bytes 688132
  15.7 9.0 %copy-start = (bf16[16,128,128]{2,1,0:T(8,128)(2,1)}, bf16[16,128,128]{2,1,0:T(8,128)(2,1)S(1)}, u32[]{:S(2)}) copy-start(bf16[16,128,128]{2,1,0:T(8,128)(2,1)S(1)} %all-to-all-done.q_ref) | copy-start | bytes 1572868
  15.7 26.2 %all-to-all-start.1 = ((bf16[16,256,128]{2,1,0:T(8,128)(2,1)}), bf16[16,256,128]{2,1,0:T(8,128)(2,1)S(1)}, u32[]{:S(2)}, u32[]{:S(2)}) async-start(bf16[16,256,128]{2,1,0:T(8,128)(2,1)} %pack.3), calls=%async_computation.1 | async-start | bytes 2097152 | tf_op jit(solution)/shard_map/all_to_all | solution.py:226
  21.5 16.3 %collective-permute-start.4 = (bf16[128,896]{1,0:T(8,128)(2,1)S(1)}, bf16[128,896]{1,0:T(8,128)(2,1)S(1)}, u32[]{:S(2)}, u32[]{:S(2)}) collective-permute-start(bf16[128,896]{1,0:T(8,128)(2,1)S(1)} %copy-done.3), channel_id=1, source_target_pairs={{0,8},{1,9},{2,10},{3,11},{4,12},{5,13},{6,14},{7,15},{8,16},{9,17... | collective-permute-start | bytes 688136 | tf_op jit(solution)/shard_map/ppermute | solution.py:24
  24.7 19.3 %collective-permute-start.1 = (bf16[12,128,128]{2,1,0:T(8,128)(2,1)S(1)}, bf16[12,128,128]{2,1,0:T(8,128)(2,1)S(1)}, u32[]{:S(2)}, u32[]{:S(2)}) collective-permute-start(bf16[12,128,128]{2,1,0:T(8,128)(2,1)S(1)} %slice.17), channel_id=1, source_target_pairs={{16,0},{17,1},{18,2},{19,3},{20,4},{21,5},{22,6},{23,7},{24,8},{25... | collective-permute-start | bytes 1179656 | tf_op jit(solution)/shard_map/ppermute | solution.py:24
  37.8 48.5 %copy-start.2 = (bf16[128,896]{1,0:T(8,128)(2,1)}, bf16[128,896]{1,0:T(8,128)(2,1)S(1)}, u32[]{:S(2)}) copy-start(bf16[128,896]{1,0:T(8,128)(2,1)S(1)} %collective-permute-done.4.refs_1_) | copy-start | bytes 688132
  37.8 13.4 %collective-permute-start.5 = (bf16[128,896]{1,0:T(8,128)(2,1)S(1)}, bf16[128,896]{1,0:T(8,128)(2,1)S(1)}, u32[]{:S(2)}, u32[]{:S(2)}) collective-permute-start(bf16[128,896]{1,0:T(8,128)(2,1)S(1)} %collective-permute-done.4.refs_1_), channel_id=1, source_target_pairs={{0,8},{1,9},{2,10},{3,11},{4,12},{5,13},{6,14},{7,15},{8,16},{9,17... | collective-permute-start | bytes 688136 | tf_op jit(solution)/shard_map/ppermute | solution.py:24
  42.0 2.1 %copy-start.5 = (bf16[16,256,128]{2,1,0:T(8,128)(2,1)}, bf16[16,256,128]{2,1,0:T(8,128)(2,1)S(1)}, u32[]{:S(2)}) copy-start(bf16[16,256,128]{2,1,0:T(8,128)(2,1)S(1)} %all-to-all-done.1.kv_ref) | copy-start | bytes 3145732
  42.7 19.6 %collective-permute-start = (bf16[4,256,128]{2,1,0:T(8,128)(2,1)}, bf16[4,256,128]{2,1,0:T(8,128)(2,1)S(1)}, u32[]{:S(2)}, u32[]{:S(2)}) collective-permute-start(bf16[4,256,128]{2,1,0:T(8,128)(2,1)} %slice.16), channel_id=1, source_target_pairs={{0,16},{1,17},{2,18},{3,19},{4,20},{5,21},{6,22},{7,23},{8,24},{9,... | collective-permute-start | bytes 786440 | tf_op jit(solution)/shard_map/ppermute | solution.py:24
  44.0 0.7 copy-start.14
  50.0 19.8 %collective-permute-start.2 = (bf16[13,128,128]{2,1,0:T(8,128)(2,1)}, bf16[13,128,128]{2,1,0:T(8,128)(2,1)S(1)}, u32[]{:S(2)}, u32[]{:S(2)}) collective-permute-start(bf16[13,128,128]{2,1,0:T(8,128)(2,1)} %later.1), channel_id=1, source_target_pairs={{0,16},{1,17},{2,18},{3,19},{4,20},{5,21},{6,22},{7,23},{8,24},{9,... | collective-permute-start | bytes 1277960 | tf_op jit(solution)/shard_map/ppermute | solution.py:24
  51.3 35.1 %copy-start.4 = (bf16[128,896]{1,0:T(8,128)(2,1)}, bf16[128,896]{1,0:T(8,128)(2,1)S(1)}, u32[]{:S(2)}) copy-start(bf16[128,896]{1,0:T(8,128)(2,1)S(1)} %collective-permute-done.5.refs_2_) | copy-start | bytes 688132
  52.5 34.4 %collective-permute-start.6 = (bf16[256,896]{1,0:T(8,128)(2,1)}, bf16[256,896]{1,0:T(8,128)(2,1)S(1)}, u32[]{:S(2)}, u32[]{:S(2)}) collective-permute-start(bf16[256,896]{1,0:T(8,128)(2,1)} %get-tuple-element.20), channel_id=1, source_target_pairs={{0,2},{1,3},{2,0},{3,1},{4,6},{5,7},{6,4},{7,5},{8,10},{9,11},{10,... | collective-permute-start | bytes 1376264 | tf_op jit(solution)/shard_map/ppermute | solution.py:29
  52.8 34.2 %collective-permute-start.7 = (bf16[256,896]{1,0:T(8,128)(2,1)}, bf16[256,896]{1,0:T(8,128)(2,1)S(1)}, u32[]{:S(2)}, u32[]{:S(2)}) collective-permute-start(bf16[256,896]{1,0:T(8,128)(2,1)} %get-tuple-element.19), channel_id=1, source_target_pairs={{0,4},{1,5},{2,6},{3,7},{4,0},{5,1},{6,2},{7,3},{8,12},{9,13},{10,... | collective-permute-start | bytes 1376264 | tf_op jit(solution)/shard_map/ppermute | solution.py:29
  53.1 34.3 %collective-permute-start.8 = (bf16[256,896]{1,0:T(8,128)(2,1)}, bf16[256,896]{1,0:T(8,128)(2,1)S(1)}, u32[]{:S(2)}, u32[]{:S(2)}) collective-permute-start(bf16[256,896]{1,0:T(8,128)(2,1)} %get-tuple-element.18), channel_id=1, source_target_pairs={{0,6},{1,7},{2,4},{3,5},{4,2},{5,3},{6,0},{7,1},{8,14},{9,15},{10,... | collective-permute-start | bytes 1376264 | tf_op jit(solution)/shard_map/ppermute | solution.py:29
  62.3 0.7 copy-start.11
  69.8 0.8 copy-start.10
  74.1 13.4 %copy-start.12 = (s32[2,2]{1,0:T(2,128)S(1)}, s32[2,2]{1,0:T(2,128)}, u32[]{:S(2)}) copy-start(s32[2,2]{1,0:T(2,128)} %param.15) | copy-start | bytes 52
  74.1 13.4 %copy-start.13 = (s32[2]{0:T(128)S(1)}, s32[2]{0:T(128)}, u32[]{:S(2)}) copy-start(s32[2]{0:T(128)} %param.14) | copy-start | bytes 28
  74.2 37.3 %all-to-all-start.2 = ((bf16[16,128,128]{2,1,0:T(8,128)(2,1)}), bf16[16,128,128]{2,1,0:T(8,128)(2,1)S(1)}, u32[]{:S(2)}, u32[]{:S(2)}) async-start(bf16[16,128,128]{2,1,0:T(8,128)(2,1)} %merge.1), calls=%async_computation.2 | async-start | bytes 1048576 | tf_op jit(solution)/shard_map/all_to_all | solution.py:525
  86.4 11.1 %collective-permute-start.9 = (bf16[384,896]{1,0:T(8,128)(2,1)S(1)}, bf16[384,896]{1,0:T(8,128)(2,1)S(1)}, u32[]{:S(2)}, u32[]{:S(2)}) collective-permute-start(bf16[384,896]{1,0:T(8,128)(2,1)S(1)} %pad_maximum_fusion), channel_id=1, source_target_pairs={{0,1},{1,0},{2,3},{3,2},{4,5},{5,4},{6,7},{7,6},{8,9},{9,8},{10,11... | collective-permute-start | bytes 2064392 | tf_op jit(solution)/shard_map/ppermute | solution.py:29
  86.9 10.0 %copy-start.7 = (bf16[256,896]{1,0:T(8,128)(2,1)}, bf16[256,896]{1,0:T(8,128)(2,1)S(1)}, u32[]{:S(2)}) copy-start(bf16[256,896]{1,0:T(8,128)(2,1)S(1)} %collective-permute-done.6.refs_3_) | copy-start | bytes 1376260
  86.9 10.6 %collective-permute-start.10 = (bf16[256,896]{1,0:T(8,128)(2,1)S(1)}, bf16[256,896]{1,0:T(8,128)(2,1)}, u32[]{:S(2)}, u32[]{:S(2)}) collective-permute-start(bf16[256,896]{1,0:T(8,128)(2,1)S(1)} %collective-permute-done.6.refs_3_), channel_id=1, source_target_pairs={{0,1},{1,0},{2,3},{3,2},{4,5},{5,4},{6,7},{7,6},{8,9},{9,8},{10,11... | collective-permute-start | bytes 1376264 | tf_op jit(solution)/shard_map/ppermute | solution.py:29
  87.0 9.8 %copy-start.8 = (bf16[256,896]{1,0:T(8,128)(2,1)}, bf16[256,896]{1,0:T(8,128)(2,1)S(1)}, u32[]{:S(2)}) copy-start(bf16[256,896]{1,0:T(8,128)(2,1)S(1)} %collective-permute-done.7.refs_4_) | copy-start | bytes 1376260
  87.0 10.5 %collective-permute-start.11 = (bf16[256,896]{1,0:T(8,128)(2,1)S(1)}, bf16[256,896]{1,0:T(8,128)(2,1)}, u32[]{:S(2)}, u32[]{:S(2)}) collective-permute-start(bf16[256,896]{1,0:T(8,128)(2,1)S(1)} %collective-permute-done.7.refs_4_), channel_id=1, source_target_pairs={{0,1},{1,0},{2,3},{3,2},{4,5},{5,4},{6,7},{7,6},{8,9},{9,8},{10,11... | collective-permute-start | bytes 1376264 | tf_op jit(solution)/shard_map/ppermute | solution.py:29
  87.4 9.5 %copy-start.9 = (bf16[256,896]{1,0:T(8,128)(2,1)}, bf16[256,896]{1,0:T(8,128)(2,1)S(1)}, u32[]{:S(2)}) copy-start(bf16[256,896]{1,0:T(8,128)(2,1)S(1)} %collective-permute-done.8.refs_5_) | copy-start | bytes 1376260
  87.4 10.1 %collective-permute-start.12 = (bf16[256,896]{1,0:T(8,128)(2,1)S(1)}, bf16[256,896]{1,0:T(8,128)(2,1)}, u32[]{:S(2)}, u32[]{:S(2)}) collective-permute-start(bf16[256,896]{1,0:T(8,128)(2,1)S(1)} %collective-permute-done.8.refs_5_), channel_id=1, source_target_pairs={{0,1},{1,0},{2,3},{3,2},{4,5},{5,4},{6,7},{7,6},{8,9},{9,8},{10,11... | collective-permute-start | bytes 1376264 | tf_op jit(solution)/shard_map/ppermute | solution.py:29
  87.6 9.3 %collective-permute-start.3 = (s32[2,2]{1,0:T(2,128)S(1)}, s32[2,2]{1,0:T(2,128)S(1)}, u32[]{:S(2)}, u32[]{:S(2)}) collective-permute-start(s32[2,2]{1,0:T(2,128)S(1)} %multiply_add_fusion), channel_id=1, source_target_pairs={{0,1},{1,2},{2,3},{3,4},{4,5},{5,6},{6,7},{7,8},{8,9},{9,10},{10,1... | collective-permute-start | bytes 56 | tf_op jit(solution)/shard_map/ppermute | solution.py:24
  97.5 0.9 copy-start.6
  111.5 0.8 copy-start.1

commit v8 on v7

--- a/solution.py
+++ b/solution.py
@@ -12,7 +12,7 @@
 HEAD_DIM = 128
 SPAN = 64
 PLANE = 8
-LEFT = 12
+LEFT = 8
 
 MASKED_SCORE = -1e30
 LOG2E = 1.4426950408889634
@@ -149,29 +149,34 @@
     return jnp.where(sublane < 64, values[0], values[1]).T
 
 
-def previous_kernel(scale, flag_ref, q_ref, kv_ref, out1_ref, stat1_ref, out_ref, part_ref, stat_ref):
+def previous_kernel(scale, flag_ref, q_ref, kv_ref, back_ref, out1_ref, stat1_ref, out_ref):
     blocks, rows, dim = q_ref.shape
-    waiting = part_ref.shape[0]
+    sent = back_ref.shape[0] - 1
     later = triangle(2 * rows, lambda column, row: column > row)
 
     def own_part(i):
         stat = stat1_ref[i : i + 2].reshape(2 * rows, 128)
         return (out1_ref[i : i + 2].reshape(2 * rows, dim), *halves(stat))
 
+    def with_sent(i):
+        out1, largest1, total1 = own_part(i)
+        stat = jnp.concatenate([sent_stats(back_ref, i + n, rows) for n in range(2)], axis=0)
+        largest2, total2 = halves(stat)
+        top = jnp.maximum(largest1, largest2)
+        a, b = jnp.exp2((largest1 - top) * scale), jnp.exp2((largest2 - top) * scale)
+        out2 = taken(back_ref, i, 2, 0, rows).astype(jnp.float32)
+        return out1 * a + out2 * b, top, total1 * a + total2 * b
+
     def store(i, part):
-        out, largest, total = part
-        if i < waiting:
-            part_ref[i : i + 2] = out.reshape(2, rows, dim)
-            stat_ref[i : i + 2] = with_stats(largest, total).reshape(2, rows, 128)
-        else:
-            out = out * (1.0 / total)
-            out_ref[i : i + 2] = out.reshape(2, rows, dim).astype(out_ref.dtype)
+        out, _, total = part
+        out = out * (1.0 / total)
+        out_ref[i : i + 2] = out.reshape(2, rows, dim).astype(out_ref.dtype)
 
     @pl.when(flag_ref[0] > 0)
     def _():
         for i in range(0, blocks, 2):
-            first = max(i - waiting, 0)
-            spans = [(first, 2, later)] if i >= waiting else []
+            first = max(i - sent, 0)
+            spans = [(first, 2, later)] if i >= sent else []
             first += 2 * len(spans)
             if first < kv_ref.shape[0]:
                 spans.append((first, kv_ref.shape[0] - first, None))
@@ -179,36 +184,13 @@
                 (taken(kv_ref, f, n, 0, rows), taken(kv_ref, f, n, rows, rows), mask)
                 for f, n, mask in spans
             ]
-            store(i, softmax_parts(taken(q_ref, i, 2, 0, rows), pieces, scale, own_part(i)))
+            start = with_sent(i) if i < sent else own_part(i)
+            store(i, softmax_parts(taken(q_ref, i, 2, 0, rows), pieces, scale, start))
 
     @pl.when(flag_ref[0] == 0)
     def _():
-        part_ref[...] = out1_ref[0:waiting]
-        stat_ref[...] = stat1_ref[0:waiting]
-        for i in range(waiting, blocks, 2):
+        for i in range(0, blocks, 2):
             store(i, own_part(i))
-
-
-def merge_kernel(scale, flag_ref, part_ref, stat_ref, back_ref, rest_ref, out_ref, done_ref, sem):
-    del rest_ref
-    blocks, rows, dim = part_ref.shape
-    for i in range(0, blocks, 2):
-        out1, largest1, total1 = (
-            part_ref[i : i + 2].reshape(2 * rows, dim),
-            *halves(stat_ref[i : i + 2].reshape(2 * rows, 128)),
-        )
-        stat = jnp.concatenate([sent_stats(back_ref, i + n, rows) for n in range(2)], axis=0)
-        largest2, total2 = halves(stat)
-        largest2 = jnp.where(flag_ref[0] > 0, largest2, MASKED_SCORE)
-        top = jnp.maximum(largest1, largest2)
-        a, b = jnp.exp2((largest1 - top) * scale), jnp.exp2((largest2 - top) * scale)
-        inverse = 1.0 / (a * total1 + b * total2)
-        out2 = taken(back_ref, i, 2, 0, rows).astype(jnp.float32)
-        out = out1 * (a * inverse) + out2 * (b * inverse)
-        done_ref[i : i + 2] = out.reshape(2, rows, dim).astype(done_ref.dtype)
-    copy = pltpu.make_async_copy(done_ref, out_ref.at[0:blocks], sem)
-    copy.start()
-    copy.wait()
 
 
 def estimate(area, arrays):
@@ -256,34 +238,14 @@
     )(asked, kv)
     back = shifted(answer, "ctx", heads)
     flag = chunk.reshape(1)
-    all_blocks = first_blocks(heads, rows)
-    rest, part, stat = pl.pallas_call(
+    vmem = pl.BlockSpec(memory_space=pltpu.VMEM)
+    return pl.pallas_call(
         functools.partial(previous_kernel, scale),
-        out_shape=(
-            jax.ShapeDtypeStruct((heads, rows, HEAD_DIM), jnp.bfloat16),
-            jax.ShapeDtypeStruct((LEFT, rows, HEAD_DIM), jnp.float32),
-            jax.ShapeDtypeStruct((LEFT, rows, 128), jnp.float32),
-        ),
-        grid=(1,),
-        in_specs=[smem, all_blocks, first_blocks(heads - LEFT, 2 * rows), all_blocks, all_blocks],
-        out_specs=(all_blocks, first_blocks(LEFT, rows), first_blocks(LEFT, rows)),
+        out_shape=jax.ShapeDtypeStruct((heads, rows, HEAD_DIM), jnp.bfloat16),
+        in_specs=[smem] + [vmem] * 5,
         cost_estimate=estimate(area - small, (q, kv, out1, stat)),
         name="previous",
-    )(flag, q, arriving, out1, stat)
-    vmem, anywhere = (pl.BlockSpec(memory_space=m) for m in (pltpu.VMEM, pl.ANY))
-    return pl.pallas_call(
-        functools.partial(merge_kernel, scale),
-        out_shape=jax.ShapeDtypeStruct(rest.shape, rest.dtype),
-        in_specs=[smem, vmem, vmem, vmem, anywhere],
-        out_specs=anywhere,
-        input_output_aliases={4: 0},
-        scratch_shapes=[
-            pltpu.VMEM((LEFT, rows, HEAD_DIM), rest.dtype),
-            pltpu.SemaphoreType.DMA(()),
-        ],
-        cost_estimate=estimate(0, (part, stat, back)),
-        name="merge",
-    )(flag, part, stat, back, rest)
+    )(flag, q, arriving, back, out1, stat)
 
 
 def wanted_pieces(table_ref, position, span_count, held):
@@ -504,14 +466,6 @@
     )(means, weight)
 
 
-def sum_kernel(self_ref, cross_ref, out_ref):
-    for head in range(self_ref.shape[0]):
-        lanes = slice(head * HEAD_DIM, (head + 1) * HEAD_DIM)
-        out_ref[:, lanes] = (self_ref[head].astype(jnp.float32) + cross_ref[:, lanes]).astype(
-            out_ref.dtype
-        )
-
-
 def per_device(
     queries, self_keys, self_values, cross_queries, encoded, neighbour_weight, counts, sources
 ):
@@ -523,11 +477,8 @@
     )
     by_head = self_attention(queries, self_keys, self_values, position // HEADS, groups)
     self_part = lax.all_to_all(by_head, "ctx", 0, 0, axis_index_groups=groups, tiled=True)
-    return pl.pallas_call(
-        sum_kernel,
-        out_shape=jax.ShapeDtypeStruct(queries.shape, jnp.bfloat16),
-        name="total",
-    )(self_part, cross_part)
+    self_part = jnp.moveaxis(self_part.astype(jnp.float32), 0, 1).reshape(queries.shape)
+    return (self_part + cross_part).astype(jnp.bfloat16)
 
 
 def solution(mesh):

time: 116 us -> 125 us (1.078)
  starting transfers between devices: 42.4 us -> 54 us
  Pallas kernels: 48.2 us -> 42.1 us
  waiting for transfers between devices: 17.1 us -> 21 us
  other arithmetic: 1.95 us -> 4.05 us
  local copies, waits for them, and re-layouts: 4.69 us -> 2.94 us
    all_to_all x1, starting transfers between devices: 12.2 us -> 22.9 us  [per_device(): lax.all_to_all(by_head, 'ctx', 0, 0, axis_index_groups=groups, tiled=True)]
    pallas_call x3 -> x1, Pallas kernels: 12.6 us -> 7.89 us  [self_attention(): pl.pallas_call(functools.partial(previous_kernel, scale), out_shape=jax.S...]
    ppermute x6, waiting for transfers between devices: 11.1 us -> 15 us  [shifted(): lax.ppermute(value, axis, [(source, source + steps) for source in range(f...]
    convert_element_type x0 -> x1, other arithmetic: none -> 2.12 us  [per_device(): return (self_part + cross_part).astype(jnp.bfloat16)]
    unnamed x30 -> x26, local copies, waits for them, and re-layouts: 3.91 us -> 2.19 us
    pallas_call x1, Pallas kernels: 5.16 us -> 3.75 us  [self_attention(): pl.pallas_call(functools.partial(later_kernel, scale), out_shape=jax.Shap...]
  transfers between devices with their start and end apart: 16 -> 16, of which waited for: 2 -> 3; matrix products, arithmetic and copies ran while one was open for 2% -> 2% of each run, Pallas kernels for 38% -> 32%
where the time goes in v8:
time: 125 us; the launch traced here: 124 us
  starting transfers between devices  54 us (43%)
  Pallas kernels  42.1 us (34%)
  waiting for transfers between devices  21 us (17%)
  other arithmetic  4.05 us (3%)
  local copies, waits for them, and re-layouts  2.94 us (2%)
    all_to_all x1, starting transfers between devices, per_device(): lax.all_to_all(by_head, 'ctx', 0, 0, axis_index_groups=groups, tiled=True)  22.9 us
    ppermute x6, starting transfers between devices, shifted(): lax.ppermute(value, axis, [(source, source + steps) for source in range(f...  16.1 us
    ppermute x6, waiting for transfers between devices, shifted(): lax.ppermute(value, axis, [(source, source + steps) for source in range(f...  15 us
    pallas_call x1, Pallas kernels, cross_attention(): pl.pallas_call(functools.partial(cross_kernel, HEAD_DIM ** (-0.5) * LOG2E...  8.51 us
    pallas_call x1, Pallas kernels, self_attention(): pl.pallas_call(functools.partial(previous_kernel, scale), out_shape=jax.S...  7.89 us
    pallas_call x1, Pallas kernels, self_attention(): pl.pallas_call(functools.partial(own_kernel, scale), out_shape=(jax.Shape...  7.18 us
    all_to_all x1, waiting for transfers between devices, self_attention(): lax.all_to_all(packed(queries), 'ctx', 0, 0, axis_index_groups=groups, ti...  5.93 us
    pallas_call x1, Pallas kernels, cross_attention(): pl.pallas_call(absorb_kernel, out_shape=jax.ShapeDtypeStruct((span_count,...  5.87 us
  transfers between devices with their start and end apart: 16, of which 3 were waited for; matrix products, arithmetic and copies ran while one was open for 2% of the time, Pallas kernels for 32%

profile of v8, /device:TPU:23, one launch (start us, length us, event | category | flops | bytes accessed | tf_op | source)
XLA Modules:
  0.0 124.3 jit_solution(4288624010671551610)
XLA Ops:
  0.0 1.9 %pack.2 = bf16[16,128,128]{2,1,0:T(8,128)(2,1)} custom-call(bf16[128,2048]{1,0:T(8,128)(2,1)} %refs_0_.3), custom_call_target="tpu_custom_call" | custom-call | bytes 1048576 | tf_op jit(solution)/shard_map/pack/pallas_call | solution.py:43
  1.9 5.5 %all-to-all-start = ((bf16[16,128,128]{2,1,0:T(8,128)(2,1)}), bf16[16,128,128]{2,1,0:T(8,128)(2,1)S(1)}, u32[]{:S(2)}, u32[]{:S(2)}) async-start(bf16[16,128,128]{2,1,0:T(8,128)(2,1)} %pack.2), calls=%async_computation | async-start | bytes 1048576 | tf_op jit(solution)/shard_map/all_to_all | solution.py:212
  7.4 2.4 %pack.3 = bf16[16,256,128]{2,1,0:T(8,128)(2,1)} custom-call(bf16[128,2048]{1,0:T(8,128)(2,1)} %refs_0_.4, bf16[128,2048]{1,0:T(8,128)(2,1)} %refs_1_.1), custom_call_target="tpu_custom_call" | custom-call | bytes 2097152 | tf_op jit(solution)/shard_map/pack/pallas_call | solution.py:43
  9.8 5.9 %all-to-all-done.q_ref = bf16[16,128,128]{2,1,0:T(8,128)(2,1)S(1)} async-done(((bf16[16,128,128]{2,1,0:T(8,128)(2,1)}), bf16[16,128,128]{2,1,0:T(8,128)(2,1)S(1)}, u32[]{:S(2)}, u32[]{:S(2)}) %all-to-all-start) | async-done | bytes 524320 | tf_op jit(solution)/shard_map/all_to_all | solution.py:212
  15.7 5.8 %all-to-all-start.1 = ((bf16[16,256,128]{2,1,0:T(8,128)(2,1)}), bf16[16,256,128]{2,1,0:T(8,128)(2,1)S(1)}, u32[]{:S(2)}, u32[]{:S(2)}) async-start(bf16[16,256,128]{2,1,0:T(8,128)(2,1)} %pack.3), calls=%async_computation.1 | async-start | bytes 2097152 | tf_op jit(solution)/shard_map/all_to_all | solution.py:208
  21.5 0.0 copy-done.3
  21.5 3.1 %collective-permute-start.4 = (bf16[128,896]{1,0:T(8,128)(2,1)S(1)}, bf16[128,896]{1,0:T(8,128)(2,1)S(1)}, u32[]{:S(2)}, u32[]{:S(2)}) collective-permute-start(bf16[128,896]{1,0:T(8,128)(2,1)S(1)} %copy-done.3), channel_id=1, source_target_pairs={{0,8},{1,9},{2,10},{3,11},{4,12},{5,13},{6,14},{7,15},{8,16},{9,17... | collective-permute-start | bytes 688136 | tf_op jit(solution)/shard_map/ppermute | solution.py:24
  24.7 0.7 slice.17
  25.4 2.7 %collective-permute-start.1 = (bf16[8,128,128]{2,1,0:T(8,128)(2,1)}, bf16[8,128,128]{2,1,0:T(8,128)(2,1)}, u32[]{:S(2)}, u32[]{:S(2)}) collective-permute-start(bf16[8,128,128]{2,1,0:T(8,128)(2,1)} %slice.17), channel_id=1, source_target_pairs={{16,0},{17,1},{18,2},{19,3},{20,4},{21,5},{22,6},{23,7},{24,8},{25... | collective-permute-start | bytes 786440 | tf_op jit(solution)/shard_map/ppermute | solution.py:24
  28.1 9.8 %collective-permute-done.4.refs_1_ = bf16[128,896]{1,0:T(8,128)(2,1)S(1)} collective-permute-done((bf16[128,896]{1,0:T(8,128)(2,1)S(1)}, bf16[128,896]{1,0:T(8,128)(2,1)S(1)}, u32[]{:S(2)}, u32[]{:S(2)}) %collective-permute-start.4) | collective-permute-done | bytes 229408 | tf_op jit(solution)/shard_map/ppermute | solution.py:24
  37.8 4.1 %collective-permute-start.5 = (bf16[128,896]{1,0:T(8,128)(2,1)S(1)}, bf16[128,896]{1,0:T(8,128)(2,1)S(1)}, u32[]{:S(2)}, u32[]{:S(2)}) collective-permute-start(bf16[128,896]{1,0:T(8,128)(2,1)S(1)} %collective-permute-done.4.refs_1_), channel_id=1, source_target_pairs={{0,8},{1,9},{2,10},{3,11},{4,12},{5,13},{6,14},{7,15},{8,16},{9,17... | collective-permute-start | bytes 688136 | tf_op jit(solution)/shard_map/ppermute | solution.py:24
  42.0 0.0 all-to-all-done.1.kv_ref
  42.0 0.0 copy-start
  42.0 0.0 copy-done.1
  42.0 1.3 %collective-permute-start = (bf16[8,256,128]{2,1,0:T(8,128)(2,1)S(1)}, bf16[8,256,128]{2,1,0:T(8,128)(2,1)S(1)}, u32[]{:S(2)}, u32[]{:S(2)}) collective-permute-start(bf16[8,256,128]{2,1,0:T(8,128)(2,1)S(1)} %slice.16), channel_id=1, source_target_pairs={{0,16},{1,17},{2,18},{3,19},{4,20},{5,21},{6,22},{7,23},{8,24},{9,... | collective-permute-start | bytes 1572872 | tf_op jit(solution)/shard_map/ppermute | solution.py:24
  43.3 0.0 collective-permute-done.1.q_ref
  43.3 0.0 copy-done
  43.4 3.7 %later.1 = bf16[9,128,128]{2,1,0:T(8,128)(2,1)} custom-call(bf16[8,128,128]{2,1,0:T(8,128)(2,1)} %collective-permute-done.1.q_ref, bf16[16,256,128]{2,1,0:T(8,128)(2,1)} %copy-done), custom_call_target="tpu_custom_call" | custom-call | flops 268435456 | bytes 262144 | tf_op jit(solution)/shard_map/later/pallas_call | solution.py:230
  47.1 1.3 %collective-permute-start.2 = (bf16[9,128,128]{2,1,0:T(8,128)(2,1)}, bf16[9,128,128]{2,1,0:T(8,128)(2,1)S(1)}, u32[]{:S(2)}, u32[]{:S(2)}) collective-permute-start(bf16[9,128,128]{2,1,0:T(8,128)(2,1)} %later.1), channel_id=1, source_target_pairs={{0,16},{1,17},{2,18},{3,19},{4,20},{5,21},{6,22},{7,23},{8,24},{9,... | collective-permute-start | bytes 884744 | tf_op jit(solution)/shard_map/ppermute | solution.py:24
  48.4 0.0 collective-permute-done.5.refs_2_
  48.4 0.0 copy-start.4
  48.4 0.1 broadcast_select_fusion
  48.5 1.2 pad_maximum_fusion.1
  49.7 0.3 collective-permute-start.6
  50.0 0.3 collective-permute-start.7
  50.3 2.0 %collective-permute-start.8 = (bf16[256,896]{1,0:T(8,128)(2,1)}, bf16[256,896]{1,0:T(8,128)(2,1)}, u32[]{:S(2)}, u32[]{:S(2)}) collective-permute-start(bf16[256,896]{1,0:T(8,128)(2,1)} %get-tuple-element.12), channel_id=1, source_target_pairs={{0,6},{1,7},{2,4},{3,5},{4,2},{5,3},{6,0},{7,1},{8,14},{9,15},{10,... | collective-permute-start | bytes 1376264 | tf_op jit(solution)/shard_map/ppermute | solution.py:29
  52.3 7.2 %own.1 = (f32[16,128,128]{2,1,0:T(8,128)}, f32[16,128,128]{2,1,0:T(8,128)}) custom-call(bf16[16,128,128]{2,1,0:T(8,128)(2,1)} %copy-done.1, bf16[16,256,128]{2,1,0:T(8,128)(2,1)} %copy-done), custom_call_target="tpu_custom_call" | custom-call | flops 1073741824 | bytes 1572864 | tf_op jit(solution)/shard_map/own/pallas_call | solution.py:216
  59.5 5.3 %collective-permute-done.2.back_ref = bf16[9,128,128]{2,1,0:T(8,128)(2,1)S(1)} collective-permute-done((bf16[9,128,128]{2,1,0:T(8,128)(2,1)}, bf16[9,128,128]{2,1,0:T(8,128)(2,1)S(1)}, u32[]{:S(2)}, u32[]{:S(2)}) %collective-permute-start.2) | collective-permute-done | bytes 294944 | tf_op jit(solution)/shard_map/ppermute | solution.py:24
  64.8 0.0 collective-permute-done.kv_ref
  64.8 0.7 copy-done.10
  65.5 0.2 copy-done.6
  65.7 7.9 %previous.1 = bf16[16,128,128]{2,1,0:T(8,128)(2,1)} custom-call(s32[1]{0:T(128)} %bitcast.flag_ref, bf16[16,128,128]{2,1,0:T(8,128)(2,1)} %copy-done.1, bf16[8,256,128]{2,1,0:T(8,128)(2,1)} %copy-done.6, bf16[9,128,128]{2,1,0:T(8,128)(2,1)} %copy-done.10, f32[16,128,128]{2,1,0:T(8,128)} %get-tuple-element.7.out1_ref, f32[16,128,128]{2,1,0:T(8,128)} %get-tuple-element.8.stat1_ref), custom_call_target="tpu_custom_call" | custom-call | flops 805306368 | bytes 2621440 | tf_op jit(solution)/shard_map/previous/pallas_call | solution.py:242
  73.6 22.9 %all-to-all-start.2 = ((bf16[16,128,128]{2,1,0:T(8,128)(2,1)}), bf16[16,128,128]{2,1,0:T(8,128)(2,1)S(1)}, u32[]{:S(2)}, u32[]{:S(2)}) async-start(bf16[16,128,128]{2,1,0:T(8,128)(2,1)} %previous.1), calls=%async_computation.2 | async-start | bytes 1048576 | tf_op jit(solution)/shard_map/all_to_all | solution.py:479
  96.5 0.0 copy-done.2
  96.5 0.0 copy-done.4
  96.5 0.1 pad_maximum_fusion
  96.6 0.5 collective-permute-start.9
  97.0 0.0 collective-permute-done.6.refs_3_
  97.0 0.1 collective-permute-start.10
  97.2 0.0 collective-permute-done.7.refs_4_
  97.2 0.4 collective-permute-start.11
  97.6 0.0 collective-permute-done.8.refs_5_
  97.6 0.1 collective-permute-start.12
  97.7 0.0 copy-done.11
  97.7 0.0 copy-done.12
  97.7 0.1 multiply_add_fusion
  97.8 3.6 %collective-permute-start.3 = (s32[2,2]{1,0:T(2,128)S(1)}, s32[2,2]{1,0:T(2,128)S(1)}, u32[]{:S(2)}, u32[]{:S(2)}) collective-permute-start(s32[2,2]{1,0:T(2,128)S(1)} %multiply_add_fusion), channel_id=1, source_target_pairs={{0,1},{1,2},{2,3},{3,4},{4,5},{5,6},{6,7},{7,8},{8,9},{9,10},{10,1... | collective-permute-start | bytes 56 | tf_op jit(solution)/shard_map/ppermute | solution.py:24
  101.4 5.9 %absorb.1.refs_10_ = bf16[2,1024,896]{2,1,0:T(8,128)(2,1)} custom-call(bf16[128,2048]{1,0:T(8,128)(2,1)} %q_ref.1, bf16[896,4096]{1,0:T(8,128)(2,1)} %weight_ref.3), custom_call_target="tpu_custom_call" | custom-call | flops 469762048 | bytes 7340032 | tf_op jit(solution)/shard_map/absorb/pallas_call | solution.py:413
  107.2 0.0 collective-permute-done.3
  107.3 0.5 pad_add_fusion.table_ref
  107.8 0.0 collective-permute-done.9.refs_6_
  107.8 0.0 collective-permute-done.10.refs_7_
  107.8 0.0 copy-start.7
  107.8 0.0 collective-permute-done.11.refs_8_
  107.8 0.0 copy-start.8
  107.8 0.0 collective-permute-done.12.refs_9_
  107.8 0.8 copy-done.5
  108.7 0.1 copy-done.7
  108.8 0.2 copy-done.8
  109.0 0.1 copy-done.9
  109.1 8.5 %cross.1.means_ref = bf16[2048,896]{1,0:T(8,128)(2,1)} custom-call(s32[1]{0:T(128)} %bitcast.2.position_ref, s32[2,2]{1,0:T(2,128)} %pad_add_fusion.table_ref, bf16[128,896]{1,0:T(8,128)(2,1)} %refs_0_.5, bf16[128,896]{1,0:T(8,128)(2,1)} %copy-done.2, bf16[128,896]{1,0:T(8,128)(2,1)} %copy-done.4, bf16[256,896]{1,0:T(8,128)(2,1)} %collective-permute-done.6.refs_3_, ...), custom_call_target="tpu_custom_call" | custom-call | flops 1879048192 | bytes 8257536 | tf_op jit(solution)/shard_map/cross/pallas_call | solution.py:428
  117.6 4.6 %values.1 = f32[128,2048]{1,0:T(8,128)} custom-call(bf16[2048,896]{1,0:T(8,128)(2,1)} %cross.1.means_ref, bf16[896,4096]{1,0:T(8,128)(2,1)} %weight_ref.3), custom_call_target="tpu_custom_call" | custom-call | flops 469762048 | bytes 7340032 | tf_op jit(solution)/shard_map/values/pallas_call | solution.py:450
  122.2 0.0 all-to-all-done.2
  122.2 2.1 %fusion = bf16[128,2048]{1,0:T(8,128)(2,1)} fusion(f32[128,2048]{1,0:T(8,128)} %values.1, bf16[16,128,128]{2,1,0:T(8,128)(2,1)S(1)} %all-to-all-done.2), kind=kLoop, calls=%fused_computation.1 | loop fusion | flops 786432 | bytes 2097152 | tf_op jit(solution)/shard_map/convert_element_type | solution.py:481
  (12 shorter events, 0.1 us)
Async XLA Ops:
  1.9 13.8 %all-to-all-start = ((bf16[16,128,128]{2,1,0:T(8,128)(2,1)}), bf16[16,128,128]{2,1,0:T(8,128)(2,1)S(1)}, u32[]{:S(2)}, u32[]{:S(2)}) async-start(bf16[16,128,128]{2,1,0:T(8,128)(2,1)} %pack.2), calls=%async_computation | async-start | bytes 1048576 | tf_op jit(solution)/shard_map/all_to_all | solution.py:212
  9.8 11.7 %copy-start.3 = (bf16[128,896]{1,0:T(8,128)(2,1)S(1)}, bf16[128,896]{1,0:T(8,128)(2,1)}, u32[]{:S(2)}) copy-start(bf16[128,896]{1,0:T(8,128)(2,1)} %refs_0_.5) | copy-start | bytes 688132
  15.7 26.3 %copy-start.1 = (bf16[16,128,128]{2,1,0:T(8,128)(2,1)}, bf16[16,128,128]{2,1,0:T(8,128)(2,1)S(1)}, u32[]{:S(2)}) copy-start(bf16[16,128,128]{2,1,0:T(8,128)(2,1)S(1)} %all-to-all-done.q_ref) | copy-start | bytes 1572868
  15.7 26.2 %all-to-all-start.1 = ((bf16[16,256,128]{2,1,0:T(8,128)(2,1)}), bf16[16,256,128]{2,1,0:T(8,128)(2,1)S(1)}, u32[]{:S(2)}, u32[]{:S(2)}) async-start(bf16[16,256,128]{2,1,0:T(8,128)(2,1)} %pack.3), calls=%async_computation.1 | async-start | bytes 2097152 | tf_op jit(solution)/shard_map/all_to_all | solution.py:208
  21.5 16.3 %collective-permute-start.4 = (bf16[128,896]{1,0:T(8,128)(2,1)S(1)}, bf16[128,896]{1,0:T(8,128)(2,1)S(1)}, u32[]{:S(2)}, u32[]{:S(2)}) collective-permute-start(bf16[128,896]{1,0:T(8,128)(2,1)S(1)} %copy-done.3), channel_id=1, source_target_pairs={{0,8},{1,9},{2,10},{3,11},{4,12},{5,13},{6,14},{7,15},{8,16},{9,17... | collective-permute-start | bytes 688136 | tf_op jit(solution)/shard_map/ppermute | solution.py:24
  25.4 17.9 %collective-permute-start.1 = (bf16[8,128,128]{2,1,0:T(8,128)(2,1)}, bf16[8,128,128]{2,1,0:T(8,128)(2,1)}, u32[]{:S(2)}, u32[]{:S(2)}) collective-permute-start(bf16[8,128,128]{2,1,0:T(8,128)(2,1)} %slice.17), channel_id=1, source_target_pairs={{16,0},{17,1},{18,2},{19,3},{20,4},{21,5},{22,6},{23,7},{24,8},{25... | collective-permute-start | bytes 786440 | tf_op jit(solution)/shard_map/ppermute | solution.py:24
  37.8 58.7 %copy-start.2 = (bf16[128,896]{1,0:T(8,128)(2,1)}, bf16[128,896]{1,0:T(8,128)(2,1)S(1)}, u32[]{:S(2)}) copy-start(bf16[128,896]{1,0:T(8,128)(2,1)S(1)} %collective-permute-done.4.refs_1_) | copy-start | bytes 688132
  37.8 10.6 %collective-permute-start.5 = (bf16[128,896]{1,0:T(8,128)(2,1)S(1)}, bf16[128,896]{1,0:T(8,128)(2,1)S(1)}, u32[]{:S(2)}, u32[]{:S(2)}) collective-permute-start(bf16[128,896]{1,0:T(8,128)(2,1)S(1)} %collective-permute-done.4.refs_1_), channel_id=1, source_target_pairs={{0,8},{1,9},{2,10},{3,11},{4,12},{5,13},{6,14},{7,15},{8,16},{9,17... | collective-permute-start | bytes 688136 | tf_op jit(solution)/shard_map/ppermute | solution.py:24
  42.0 1.4 %copy-start = (bf16[16,256,128]{2,1,0:T(8,128)(2,1)}, bf16[16,256,128]{2,1,0:T(8,128)(2,1)S(1)}, u32[]{:S(2)}) copy-start(bf16[16,256,128]{2,1,0:T(8,128)(2,1)S(1)} %all-to-all-done.1.kv_ref) | copy-start | bytes 3145732
  42.0 22.8 %collective-permute-start = (bf16[8,256,128]{2,1,0:T(8,128)(2,1)S(1)}, bf16[8,256,128]{2,1,0:T(8,128)(2,1)S(1)}, u32[]{:S(2)}, u32[]{:S(2)}) collective-permute-start(bf16[8,256,128]{2,1,0:T(8,128)(2,1)S(1)} %slice.16), channel_id=1, source_target_pairs={{0,16},{1,17},{2,18},{3,19},{4,20},{5,21},{6,22},{7,23},{8,24},{9,... | collective-permute-start | bytes 1572872 | tf_op jit(solution)/shard_map/ppermute | solution.py:24
  47.1 17.7 %collective-permute-start.2 = (bf16[9,128,128]{2,1,0:T(8,128)(2,1)}, bf16[9,128,128]{2,1,0:T(8,128)(2,1)S(1)}, u32[]{:S(2)}, u32[]{:S(2)}) collective-permute-start(bf16[9,128,128]{2,1,0:T(8,128)(2,1)} %later.1), channel_id=1, source_target_pairs={{0,16},{1,17},{2,18},{3,19},{4,20},{5,21},{6,22},{7,23},{8,24},{9,... | collective-permute-start | bytes 884744 | tf_op jit(solution)/shard_map/ppermute | solution.py:24
  48.4 48.1 %copy-start.4 = (bf16[128,896]{1,0:T(8,128)(2,1)}, bf16[128,896]{1,0:T(8,128)(2,1)S(1)}, u32[]{:S(2)}) copy-start(bf16[128,896]{1,0:T(8,128)(2,1)S(1)} %collective-permute-done.5.refs_2_) | copy-start | bytes 688132
  49.7 47.3 %collective-permute-start.6 = (bf16[256,896]{1,0:T(8,128)(2,1)}, bf16[256,896]{1,0:T(8,128)(2,1)}, u32[]{:S(2)}, u32[]{:S(2)}) collective-permute-start(bf16[256,896]{1,0:T(8,128)(2,1)} %get-tuple-element.14), channel_id=1, source_target_pairs={{0,2},{1,3},{2,0},{3,1},{4,6},{5,7},{6,4},{7,5},{8,10},{9,11},{10,... | collective-permute-start | bytes 1376264 | tf_op jit(solution)/shard_map/ppermute | solution.py:29
  50.0 47.2 %collective-permute-start.7 = (bf16[256,896]{1,0:T(8,128)(2,1)}, bf16[256,896]{1,0:T(8,128)(2,1)}, u32[]{:S(2)}, u32[]{:S(2)}) collective-permute-start(bf16[256,896]{1,0:T(8,128)(2,1)} %get-tuple-element.13), channel_id=1, source_target_pairs={{0,4},{1,5},{2,6},{3,7},{4,0},{5,1},{6,2},{7,3},{8,12},{9,13},{10,... | collective-permute-start | bytes 1376264 | tf_op jit(solution)/shard_map/ppermute | solution.py:29
  50.3 47.3 %collective-permute-start.8 = (bf16[256,896]{1,0:T(8,128)(2,1)}, bf16[256,896]{1,0:T(8,128)(2,1)}, u32[]{:S(2)}, u32[]{:S(2)}) collective-permute-start(bf16[256,896]{1,0:T(8,128)(2,1)} %get-tuple-element.12), channel_id=1, source_target_pairs={{0,6},{1,7},{2,4},{3,5},{4,2},{5,3},{6,0},{7,1},{8,14},{9,15},{10,... | collective-permute-start | bytes 1376264 | tf_op jit(solution)/shard_map/ppermute | solution.py:29
  64.8 0.7 copy-start.10
  64.8 0.9 copy-start.6
  73.6 24.1 %copy-start.11 = (s32[2,2]{1,0:T(2,128)S(1)}, s32[2,2]{1,0:T(2,128)}, u32[]{:S(2)}) copy-start(s32[2,2]{1,0:T(2,128)} %param.15) | copy-start | bytes 52
  73.6 24.1 %copy-start.12 = (s32[2]{0:T(128)S(1)}, s32[2]{0:T(128)}, u32[]{:S(2)}) copy-start(s32[2]{0:T(128)} %param.14) | copy-start | bytes 28
  73.6 48.6 %all-to-all-start.2 = ((bf16[16,128,128]{2,1,0:T(8,128)(2,1)}), bf16[16,128,128]{2,1,0:T(8,128)(2,1)S(1)}, u32[]{:S(2)}, u32[]{:S(2)}) async-start(bf16[16,128,128]{2,1,0:T(8,128)(2,1)} %previous.1), calls=%async_computation.2 | async-start | bytes 1048576 | tf_op jit(solution)/shard_map/all_to_all | solution.py:479
  96.6 11.2 %collective-permute-start.9 = (bf16[384,896]{1,0:T(8,128)(2,1)S(1)}, bf16[384,896]{1,0:T(8,128)(2,1)S(1)}, u32[]{:S(2)}, u32[]{:S(2)}) collective-permute-start(bf16[384,896]{1,0:T(8,128)(2,1)S(1)} %pad_maximum_fusion), channel_id=1, source_target_pairs={{0,1},{1,0},{2,3},{3,2},{4,5},{5,4},{6,7},{7,6},{8,9},{9,8},{10,11... | collective-permute-start | bytes 2064392 | tf_op jit(solution)/shard_map/ppermute | solution.py:29
  97.0 10.7 %collective-permute-start.10 = (bf16[256,896]{1,0:T(8,128)(2,1)}, bf16[256,896]{1,0:T(8,128)(2,1)S(1)}, u32[]{:S(2)}, u32[]{:S(2)}) collective-permute-start(bf16[256,896]{1,0:T(8,128)(2,1)} %collective-permute-done.6.refs_3_), channel_id=1, source_target_pairs={{0,1},{1,0},{2,3},{3,2},{4,5},{5,4},{6,7},{7,6},{8,9},{9,8},{10,11... | collective-permute-start | bytes 1376264 | tf_op jit(solution)/shard_map/ppermute | solution.py:29
  97.2 10.6 %collective-permute-start.11 = (bf16[256,896]{1,0:T(8,128)(2,1)}, bf16[256,896]{1,0:T(8,128)(2,1)S(1)}, u32[]{:S(2)}, u32[]{:S(2)}) collective-permute-start(bf16[256,896]{1,0:T(8,128)(2,1)} %collective-permute-done.7.refs_4_), channel_id=1, source_target_pairs={{0,1},{1,0},{2,3},{3,2},{4,5},{5,4},{6,7},{7,6},{8,9},{9,8},{10,11... | collective-permute-start | bytes 1376264 | tf_op jit(solution)/shard_map/ppermute | solution.py:29
  97.6 10.3 %collective-permute-start.12 = (bf16[256,896]{1,0:T(8,128)(2,1)}, bf16[256,896]{1,0:T(8,128)(2,1)S(1)}, u32[]{:S(2)}, u32[]{:S(2)}) collective-permute-start(bf16[256,896]{1,0:T(8,128)(2,1)} %collective-permute-done.8.refs_5_), channel_id=1, source_target_pairs={{0,1},{1,0},{2,3},{3,2},{4,5},{5,4},{6,7},{7,6},{8,9},{9,8},{10,11... | collective-permute-start | bytes 1376264 | tf_op jit(solution)/shard_map/ppermute | solution.py:29
  97.8 9.5 %collective-permute-start.3 = (s32[2,2]{1,0:T(2,128)S(1)}, s32[2,2]{1,0:T(2,128)S(1)}, u32[]{:S(2)}, u32[]{:S(2)}) collective-permute-start(s32[2,2]{1,0:T(2,128)S(1)} %multiply_add_fusion), channel_id=1, source_target_pairs={{0,1},{1,2},{2,3},{3,4},{4,5},{5,6},{6,7},{7,8},{8,9},{9,10},{10,1... | collective-permute-start | bytes 56 | tf_op jit(solution)/shard_map/ppermute | solution.py:24
  107.8 0.9 copy-start.5
  107.8 1.0 copy-start.7
  107.8 1.1 copy-start.8
  107.8 1.3 %copy-start.9 = (bf16[256,896]{1,0:T(8,128)(2,1)}, bf16[256,896]{1,0:T(8,128)(2,1)S(1)}, u32[]{:S(2)}) copy-start(bf16[256,896]{1,0:T(8,128)(2,1)S(1)} %collective-permute-done.12.refs_9_) | copy-start | bytes 1376260

commit v9 on v7

--- a/solution.py
+++ b/solution.py
@@ -12,7 +12,7 @@
 HEAD_DIM = 128
 SPAN = 64
 PLANE = 8
-LEFT = 12
+LEFT = 8
 
 MASKED_SCORE = -1e30
 LOG2E = 1.4426950408889634
@@ -504,14 +504,6 @@
     )(means, weight)
 
 
-def sum_kernel(self_ref, cross_ref, out_ref):
-    for head in range(self_ref.shape[0]):
-        lanes = slice(head * HEAD_DIM, (head + 1) * HEAD_DIM)
-        out_ref[:, lanes] = (self_ref[head].astype(jnp.float32) + cross_ref[:, lanes]).astype(
-            out_ref.dtype
-        )
-
-
 def per_device(
     queries, self_keys, self_values, cross_queries, encoded, neighbour_weight, counts, sources
 ):
@@ -523,11 +515,8 @@
     )
     by_head = self_attention(queries, self_keys, self_values, position // HEADS, groups)
     self_part = lax.all_to_all(by_head, "ctx", 0, 0, axis_index_groups=groups, tiled=True)
-    return pl.pallas_call(
-        sum_kernel,
-        out_shape=jax.ShapeDtypeStruct(queries.shape, jnp.bfloat16),
-        name="total",
-    )(self_part, cross_part)
+    self_part = jnp.moveaxis(self_part.astype(jnp.float32), 0, 1).reshape(queries.shape)
+    return (self_part + cross_part).astype(jnp.bfloat16)
 
 
 def solution(mesh):

time: 116 us -> 126 us (1.086)
  waiting for transfers between devices: 17.1 us -> 28.8 us
  Pallas kernels: 48.2 us -> 44.8 us
  other arithmetic: 1.95 us -> 4.01 us
    ppermute x6, waiting for transfers between devices: 11.1 us -> 22.8 us  [shifted(): lax.ppermute(value, axis, [(source, source + steps) for source in range(f...]
    pallas_call x1 -> x0, Pallas kernels: 2.32 us -> none  [per_device(): pl.pallas_call(sum_kernel, out_shape=jax.ShapeDtypeStruct(queries.shape,...]
    convert_element_type x0 -> x1, other arithmetic: none -> 2.12 us  [per_device(): return (self_part + cross_part).astype(jnp.bfloat16)]
    pallas_call x1, Pallas kernels: 5.16 us -> 3.73 us  [self_attention(): pl.pallas_call(functools.partial(later_kernel, scale), out_shape=jax.Shap...]
    unnamed x30 -> x26, local copies, waits for them, and re-layouts: 3.91 us -> 2.79 us
  transfers between devices with their start and end apart: 16 -> 16, of which waited for: 2 -> 3; matrix products, arithmetic and copies ran while one was open for 2% -> 2% of each run, Pallas kernels for 38% -> 34%
where the time goes in v9:
time: 126 us; the launch traced here: 125 us
  Pallas kernels  44.8 us (36%)
  starting transfers between devices  43.3 us (34%)
  waiting for transfers between devices  28.8 us (23%)
  other arithmetic  4.01 us (3%)
  local copies, waits for them, and re-layouts  3.55 us (3%)
    ppermute x6, waiting for transfers between devices, shifted(): lax.ppermute(value, axis, [(source, source + steps) for source in range(f...  22.8 us
    ppermute x6, starting transfers between devices, shifted(): lax.ppermute(value, axis, [(source, source + steps) for source in range(f...  15.8 us
    all_to_all x1, starting transfers between devices, per_device(): lax.all_to_all(by_head, 'ctx', 0, 0, axis_index_groups=groups, tiled=True)  12.5 us
    pallas_call x1, Pallas kernels, cross_attention(): pl.pallas_call(functools.partial(cross_kernel, HEAD_DIM ** (-0.5) * LOG2E...  8.58 us
    pallas_call x1, Pallas kernels, self_attention(): pl.pallas_call(functools.partial(previous_kernel, scale), out_shape=(jax....  7.7 us
    pallas_call x1, Pallas kernels, self_attention(): pl.pallas_call(functools.partial(own_kernel, scale), out_shape=(jax.Shape...  7.17 us
    all_to_all x1, waiting for transfers between devices, self_attention(): lax.all_to_all(packed(queries), 'ctx', 0, 0, axis_index_groups=groups, ti...  5.94 us
    pallas_call x1, Pallas kernels, cross_attention(): pl.pallas_call(absorb_kernel, out_shape=jax.ShapeDtypeStruct((span_count,...  5.86 us
  transfers between devices with their start and end apart: 16, of which 3 were waited for; matrix products, arithmetic and copies ran while one was open for 2% of the time, Pallas kernels for 34%

profile of v9, /device:TPU:23, one launch (start us, length us, event | category | flops | bytes accessed | tf_op | source)
XLA Modules:
  0.0 124.8 jit_solution(8439775094316747818)
XLA Ops:
  0.0 1.9 %pack.2 = bf16[16,128,128]{2,1,0:T(8,128)(2,1)} custom-call(bf16[128,2048]{1,0:T(8,128)(2,1)} %refs_0_.3), custom_call_target="tpu_custom_call" | custom-call | bytes 1048576 | tf_op jit(solution)/shard_map/pack/pallas_call | solution.py:43
  1.9 5.5 %all-to-all-start = ((bf16[16,128,128]{2,1,0:T(8,128)(2,1)}), bf16[16,128,128]{2,1,0:T(8,128)(2,1)S(1)}, u32[]{:S(2)}, u32[]{:S(2)}) async-start(bf16[16,128,128]{2,1,0:T(8,128)(2,1)} %pack.2), calls=%async_computation | async-start | bytes 1048576 | tf_op jit(solution)/shard_map/all_to_all | solution.py:230
  7.4 2.4 %pack.3 = bf16[16,256,128]{2,1,0:T(8,128)(2,1)} custom-call(bf16[128,2048]{1,0:T(8,128)(2,1)} %refs_0_.4, bf16[128,2048]{1,0:T(8,128)(2,1)} %refs_1_.1), custom_call_target="tpu_custom_call" | custom-call | bytes 2097152 | tf_op jit(solution)/shard_map/pack/pallas_call | solution.py:43
  9.8 5.9 %all-to-all-done.q_ref = bf16[16,128,128]{2,1,0:T(8,128)(2,1)S(1)} async-done(((bf16[16,128,128]{2,1,0:T(8,128)(2,1)}), bf16[16,128,128]{2,1,0:T(8,128)(2,1)S(1)}, u32[]{:S(2)}, u32[]{:S(2)}) %all-to-all-start) | async-done | bytes 524320 | tf_op jit(solution)/shard_map/all_to_all | solution.py:230
  15.7 5.8 %all-to-all-start.1 = ((bf16[16,256,128]{2,1,0:T(8,128)(2,1)}), bf16[16,256,128]{2,1,0:T(8,128)(2,1)S(1)}, u32[]{:S(2)}, u32[]{:S(2)}) async-start(bf16[16,256,128]{2,1,0:T(8,128)(2,1)} %pack.3), calls=%async_computation.1 | async-start | bytes 2097152 | tf_op jit(solution)/shard_map/all_to_all | solution.py:226
  21.5 0.0 copy-done.3
  21.5 3.1 %collective-permute-start.4 = (bf16[128,896]{1,0:T(8,128)(2,1)S(1)}, bf16[128,896]{1,0:T(8,128)(2,1)S(1)}, u32[]{:S(2)}, u32[]{:S(2)}) collective-permute-start(bf16[128,896]{1,0:T(8,128)(2,1)S(1)} %copy-done.3), channel_id=1, source_target_pairs={{0,8},{1,9},{2,10},{3,11},{4,12},{5,13},{6,14},{7,15},{8,16},{9,17... | collective-permute-start | bytes 688136 | tf_op jit(solution)/shard_map/ppermute | solution.py:24
  24.7 13.1 %collective-permute-done.4.refs_1_ = bf16[128,896]{1,0:T(8,128)(2,1)S(1)} collective-permute-done((bf16[128,896]{1,0:T(8,128)(2,1)S(1)}, bf16[128,896]{1,0:T(8,128)(2,1)S(1)}, u32[]{:S(2)}, u32[]{:S(2)}) %collective-permute-start.4) | collective-permute-done | bytes 229408 | tf_op jit(solution)/shard_map/ppermute | solution.py:24
  37.8 4.1 %collective-permute-start.5 = (bf16[128,896]{1,0:T(8,128)(2,1)S(1)}, bf16[128,896]{1,0:T(8,128)(2,1)S(1)}, u32[]{:S(2)}, u32[]{:S(2)}) collective-permute-start(bf16[128,896]{1,0:T(8,128)(2,1)S(1)} %collective-permute-done.4.refs_1_), channel_id=1, source_target_pairs={{0,8},{1,9},{2,10},{3,11},{4,12},{5,13},{6,14},{7,15},{8,16},{9,17... | collective-permute-start | bytes 688136 | tf_op jit(solution)/shard_map/ppermute | solution.py:24
  41.9 0.7 slice.17
  42.7 2.7 %collective-permute-start.1 = (bf16[8,128,128]{2,1,0:T(8,128)(2,1)}, bf16[8,128,128]{2,1,0:T(8,128)(2,1)}, u32[]{:S(2)}, u32[]{:S(2)}) collective-permute-start(bf16[8,128,128]{2,1,0:T(8,128)(2,1)} %slice.17), channel_id=1, source_target_pairs={{16,0},{17,1},{18,2},{19,3},{20,4},{21,5},{22,6},{23,7},{24,8},{25... | collective-permute-start | bytes 786440 | tf_op jit(solution)/shard_map/ppermute | solution.py:24
  45.3 0.0 all-to-all-done.1.kv_ref
  45.4 0.0 copy-done.1
  45.4 1.3 %collective-permute-start = (bf16[8,256,128]{2,1,0:T(8,128)(2,1)S(1)}, bf16[8,256,128]{2,1,0:T(8,128)(2,1)S(1)}, u32[]{:S(2)}, u32[]{:S(2)}) collective-permute-start(bf16[8,256,128]{2,1,0:T(8,128)(2,1)S(1)} %slice.16), channel_id=1, source_target_pairs={{0,16},{1,17},{2,18},{3,19},{4,20},{5,21},{6,22},{7,23},{8,24},{9,... | collective-permute-start | bytes 1572872 | tf_op jit(solution)/shard_map/ppermute | solution.py:24
  46.7 0.0 collective-permute-done.5.refs_2_
  46.7 0.0 copy-start.4
  46.7 0.1 broadcast_select_fusion
  46.8 9.7 %collective-permute-done.1.q_ref = bf16[8,128,128]{2,1,0:T(8,128)(2,1)} collective-permute-done((bf16[8,128,128]{2,1,0:T(8,128)(2,1)}, bf16[8,128,128]{2,1,0:T(8,128)(2,1)}, u32[]{:S(2)}, u32[]{:S(2)}) %collective-permute-start.1) | collective-permute-done | bytes 262176 | tf_op jit(solution)/shard_map/ppermute | solution.py:24
  56.5 0.0 copy-done
  56.5 3.7 %later.1 = bf16[9,128,128]{2,1,0:T(8,128)(2,1)} custom-call(bf16[8,128,128]{2,1,0:T(8,128)(2,1)} %collective-permute-done.1.q_ref, bf16[16,256,128]{2,1,0:T(8,128)(2,1)} %copy-done), custom_call_target="tpu_custom_call" | custom-call | flops 268435456 | bytes 262144 | tf_op jit(solution)/shard_map/later/pallas_call | solution.py:248
  60.2 1.3 %collective-permute-start.2 = (bf16[9,128,128]{2,1,0:T(8,128)(2,1)}, bf16[9,128,128]{2,1,0:T(8,128)(2,1)S(1)}, u32[]{:S(2)}, u32[]{:S(2)}) collective-permute-start(bf16[9,128,128]{2,1,0:T(8,128)(2,1)} %later.1), channel_id=1, source_target_pairs={{0,16},{1,17},{2,18},{3,19},{4,20},{5,21},{6,22},{7,23},{8,24},{9,... | collective-permute-start | bytes 884744 | tf_op jit(solution)/shard_map/ppermute | solution.py:24
  61.5 1.1 pad_maximum_fusion.1
  62.6 0.3 collective-permute-start.6
  62.9 0.4 collective-permute-start.7
  63.3 2.0 %collective-permute-start.8 = (bf16[256,896]{1,0:T(8,128)(2,1)}, bf16[256,896]{1,0:T(8,128)(2,1)}, u32[]{:S(2)}, u32[]{:S(2)}) collective-permute-start(bf16[256,896]{1,0:T(8,128)(2,1)} %get-tuple-element.18), channel_id=1, source_target_pairs={{0,6},{1,7},{2,4},{3,5},{4,2},{5,3},{6,0},{7,1},{8,14},{9,15},{10,... | collective-permute-start | bytes 1376264 | tf_op jit(solution)/shard_map/ppermute | solution.py:29
  65.3 7.2 %own.1 = (f32[16,128,128]{2,1,0:T(8,128)}, f32[16,128,128]{2,1,0:T(8,128)}) custom-call(bf16[16,128,128]{2,1,0:T(8,128)(2,1)} %copy-done.1, bf16[16,256,128]{2,1,0:T(8,128)(2,1)} %copy-done), custom_call_target="tpu_custom_call" | custom-call | flops 1073741824 | bytes 1572864 | tf_op jit(solution)/shard_map/own/pallas_call | solution.py:234
  72.4 0.0 collective-permute-done.kv_ref
  72.5 0.8 copy-done.6
  73.2 7.7 %previous.1 = (bf16[16,128,128]{2,1,0:T(8,128)(2,1)}, f32[8,128,128]{2,1,0:T(8,128)}, f32[8,128,128]{2,1,0:T(8,128)}) custom-call(s32[1]{0:T(128)} %bitcast.flag_ref, bf16[16,128,128]{2,1,0:T(8,128)(2,1)} %copy-done.1, bf16[8,256,128]{2,1,0:T(8,128)(2,1)} %copy-done.6, f32[16,128,128]{2,1,0:T(8,128)} %get-tuple-element.10.out1_ref, ...), custom_call_target="tpu_custom_call" | custom-call | flops 805306368 | bytes 2621440 | tf_op jit(solution)/shard_map/previous/pallas_call | solution.py:260
  80.9 0.0 collective-permute-done.2.back_ref
  80.9 0.7 copy-done.10
  81.7 2.9 %merge.1 = bf16[16,128,128]{2,1,0:T(8,128)(2,1)} custom-call(s32[1]{0:T(128)} %bitcast.flag_ref, f32[8,128,128]{2,1,0:T(8,128)} %get-tuple-element.12.part_ref, f32[8,128,128]{2,1,0:T(8,128)} %get-tuple-element.13.stat_ref, bf16[9,128,128]{2,1,0:T(8,128)(2,1)} %copy-done.10, ...), custom_call_target="tpu_custom_call", output_to_operand_aliasing={{}: (4, {})} | custom-call | bytes 819200 | tf_op jit(solution)/shard_map/merge/pallas_call | solution.py:274
  84.6 0.0 copy-start.11
  84.6 0.0 copy-start.12
  84.6 12.5 %all-to-all-start.2 = ((bf16[16,128,128]{2,1,0:T(8,128)(2,1)}), bf16[16,128,128]{2,1,0:T(8,128)(2,1)S(1)}, u32[]{:S(2)}, u32[]{:S(2)}) async-start(bf16[16,128,128]{2,1,0:T(8,128)(2,1)} %merge.1), calls=%async_computation.2 | async-start | bytes 1048576 | tf_op jit(solution)/shard_map/all_to_all | solution.py:517
  97.1 0.0 copy-done.2
  97.1 0.0 copy-done.4
  97.1 0.1 pad_maximum_fusion
  97.2 0.5 collective-permute-start.9
  97.6 0.0 collective-permute-done.6.refs_3_
  97.6 0.1 collective-permute-start.10
  97.8 0.0 collective-permute-done.7.refs_4_
  97.8 0.4 collective-permute-start.11
  98.2 0.0 collective-permute-done.8.refs_5_
  98.2 0.1 collective-permute-start.12
  98.3 0.0 copy-done.11
  98.3 0.1 multiply_add_fusion
  98.4 3.4 %collective-permute-start.3 = (s32[2,2]{1,0:T(2,128)S(1)}, s32[2,2]{1,0:T(2,128)S(1)}, u32[]{:S(2)}, u32[]{:S(2)}) collective-permute-start(s32[2,2]{1,0:T(2,128)S(1)} %multiply_add_fusion), channel_id=1, source_target_pairs={{0,1},{1,2},{2,3},{3,4},{4,5},{5,6},{6,7},{7,8},{8,9},{9,10},{10,1... | collective-permute-start | bytes 56 | tf_op jit(solution)/shard_map/ppermute | solution.py:24
  101.7 5.9 %absorb.1.refs_10_ = bf16[2,1024,896]{2,1,0:T(8,128)(2,1)} custom-call(bf16[128,2048]{1,0:T(8,128)(2,1)} %q_ref.1, bf16[896,4096]{1,0:T(8,128)(2,1)} %weight_ref.3), custom_call_target="tpu_custom_call" | custom-call | flops 469762048 | bytes 7340032 | tf_op jit(solution)/shard_map/absorb/pallas_call | solution.py:451
  107.6 0.0 collective-permute-done.3
  107.6 0.5 pad_add_fusion.table_ref
  108.2 0.0 collective-permute-done.9.refs_6_
  108.2 0.0 collective-permute-done.10.refs_7_
  108.2 0.0 copy-start.7
  108.2 0.0 collective-permute-done.11.refs_8_
  108.2 0.0 collective-permute-done.12.refs_9_
  108.2 0.8 copy-done.5
  109.1 0.1 copy-done.7
  109.2 0.2 copy-done.8
  109.3 0.1 copy-done.9
  109.5 8.6 %cross.1.means_ref = bf16[2048,896]{1,0:T(8,128)(2,1)} custom-call(s32[1]{0:T(128)} %bitcast.2.position_ref, s32[2,2]{1,0:T(2,128)} %pad_add_fusion.table_ref, bf16[128,896]{1,0:T(8,128)(2,1)} %refs_0_.5, bf16[128,896]{1,0:T(8,128)(2,1)} %copy-done.2, bf16[128,896]{1,0:T(8,128)(2,1)} %copy-done.4, bf16[256,896]{1,0:T(8,128)(2,1)} %collective-permute-done.6.refs_3_, ...), custom_call_target="tpu_custom_call" | custom-call | flops 1879048192 | bytes 8257536 | tf_op jit(solution)/shard_map/cross/pallas_call | solution.py:466
  118.1 4.6 %values.1 = f32[128,2048]{1,0:T(8,128)} custom-call(bf16[2048,896]{1,0:T(8,128)(2,1)} %cross.1.means_ref, bf16[896,4096]{1,0:T(8,128)(2,1)} %weight_ref.3), custom_call_target="tpu_custom_call" | custom-call | flops 469762048 | bytes 7340032 | tf_op jit(solution)/shard_map/values/pallas_call | solution.py:488
  122.6 0.0 all-to-all-done.2
  122.6 2.1 %fusion = bf16[128,2048]{1,0:T(8,128)(2,1)} fusion(f32[128,2048]{1,0:T(8,128)} %values.1, bf16[16,128,128]{2,1,0:T(8,128)(2,1)S(1)} %all-to-all-done.2), kind=kLoop, calls=%fused_computation.1 | loop fusion | flops 786432 | bytes 2097152 | tf_op jit(solution)/shard_map/convert_element_type | solution.py:519
  (13 shorter events, 0.1 us)
Async XLA Ops:
  1.9 13.8 %all-to-all-start = ((bf16[16,128,128]{2,1,0:T(8,128)(2,1)}), bf16[16,128,128]{2,1,0:T(8,128)(2,1)S(1)}, u32[]{:S(2)}, u32[]{:S(2)}) async-start(bf16[16,128,128]{2,1,0:T(8,128)(2,1)} %pack.2), calls=%async_computation | async-start | bytes 1048576 | tf_op jit(solution)/shard_map/all_to_all | solution.py:230
  9.8 11.7 %copy-start.3 = (bf16[128,896]{1,0:T(8,128)(2,1)S(1)}, bf16[128,896]{1,0:T(8,128)(2,1)}, u32[]{:S(2)}) copy-start(bf16[128,896]{1,0:T(8,128)(2,1)} %refs_0_.5) | copy-start | bytes 688132
  15.7 29.6 %copy-start.1 = (bf16[16,128,128]{2,1,0:T(8,128)(2,1)}, bf16[16,128,128]{2,1,0:T(8,128)(2,1)S(1)}, u32[]{:S(2)}) copy-start(bf16[16,128,128]{2,1,0:T(8,128)(2,1)S(1)} %all-to-all-done.q_ref) | copy-start | bytes 1572868
  15.7 29.6 %all-to-all-start.1 = ((bf16[16,256,128]{2,1,0:T(8,128)(2,1)}), bf16[16,256,128]{2,1,0:T(8,128)(2,1)S(1)}, u32[]{:S(2)}, u32[]{:S(2)}) async-start(bf16[16,256,128]{2,1,0:T(8,128)(2,1)} %pack.3), calls=%async_computation.1 | async-start | bytes 2097152 | tf_op jit(solution)/shard_map/all_to_all | solution.py:226
  21.5 16.3 %collective-permute-start.4 = (bf16[128,896]{1,0:T(8,128)(2,1)S(1)}, bf16[128,896]{1,0:T(8,128)(2,1)S(1)}, u32[]{:S(2)}, u32[]{:S(2)}) collective-permute-start(bf16[128,896]{1,0:T(8,128)(2,1)S(1)} %copy-done.3), channel_id=1, source_target_pairs={{0,8},{1,9},{2,10},{3,11},{4,12},{5,13},{6,14},{7,15},{8,16},{9,17... | collective-permute-start | bytes 688136 | tf_op jit(solution)/shard_map/ppermute | solution.py:24
  37.8 59.3 %copy-start.2 = (bf16[128,896]{1,0:T(8,128)(2,1)}, bf16[128,896]{1,0:T(8,128)(2,1)S(1)}, u32[]{:S(2)}) copy-start(bf16[128,896]{1,0:T(8,128)(2,1)S(1)} %collective-permute-done.4.refs_1_) | copy-start | bytes 688132
  37.8 8.9 %collective-permute-start.5 = (bf16[128,896]{1,0:T(8,128)(2,1)S(1)}, bf16[128,896]{1,0:T(8,128)(2,1)S(1)}, u32[]{:S(2)}, u32[]{:S(2)}) collective-permute-start(bf16[128,896]{1,0:T(8,128)(2,1)S(1)} %collective-permute-done.4.refs_1_), channel_id=1, source_target_pairs={{0,8},{1,9},{2,10},{3,11},{4,12},{5,13},{6,14},{7,15},{8,16},{9,17... | collective-permute-start | bytes 688136 | tf_op jit(solution)/shard_map/ppermute | solution.py:24
  42.7 13.8 %collective-permute-start.1 = (bf16[8,128,128]{2,1,0:T(8,128)(2,1)}, bf16[8,128,128]{2,1,0:T(8,128)(2,1)}, u32[]{:S(2)}, u32[]{:S(2)}) collective-permute-start(bf16[8,128,128]{2,1,0:T(8,128)(2,1)} %slice.17), channel_id=1, source_target_pairs={{16,0},{17,1},{18,2},{19,3},{20,4},{21,5},{22,6},{23,7},{24,8},{25... | collective-permute-start | bytes 786440 | tf_op jit(solution)/shard_map/ppermute | solution.py:24
  45.3 11.1 %copy-start = (bf16[16,256,128]{2,1,0:T(8,128)(2,1)}, bf16[16,256,128]{2,1,0:T(8,128)(2,1)S(1)}, u32[]{:S(2)}) copy-start(bf16[16,256,128]{2,1,0:T(8,128)(2,1)S(1)} %all-to-all-done.1.kv_ref) | copy-start | bytes 3145732
  45.4 27.1 %collective-permute-start = (bf16[8,256,128]{2,1,0:T(8,128)(2,1)S(1)}, bf16[8,256,128]{2,1,0:T(8,128)(2,1)S(1)}, u32[]{:S(2)}, u32[]{:S(2)}) collective-permute-start(bf16[8,256,128]{2,1,0:T(8,128)(2,1)S(1)} %slice.16), channel_id=1, source_target_pairs={{0,16},{1,17},{2,18},{3,19},{4,20},{5,21},{6,22},{7,23},{8,24},{9,... | collective-permute-start | bytes 1572872 | tf_op jit(solution)/shard_map/ppermute | solution.py:24
  46.7 50.4 %copy-start.4 = (bf16[128,896]{1,0:T(8,128)(2,1)}, bf16[128,896]{1,0:T(8,128)(2,1)S(1)}, u32[]{:S(2)}) copy-start(bf16[128,896]{1,0:T(8,128)(2,1)S(1)} %collective-permute-done.5.refs_2_) | copy-start | bytes 688132
  60.2 20.7 %collective-permute-start.2 = (bf16[9,128,128]{2,1,0:T(8,128)(2,1)}, bf16[9,128,128]{2,1,0:T(8,128)(2,1)S(1)}, u32[]{:S(2)}, u32[]{:S(2)}) collective-permute-start(bf16[9,128,128]{2,1,0:T(8,128)(2,1)} %later.1), channel_id=1, source_target_pairs={{0,16},{1,17},{2,18},{3,19},{4,20},{5,21},{6,22},{7,23},{8,24},{9,... | collective-permute-start | bytes 884744 | tf_op jit(solution)/shard_map/ppermute | solution.py:24
  62.6 35.0 %collective-permute-start.6 = (bf16[256,896]{1,0:T(8,128)(2,1)}, bf16[256,896]{1,0:T(8,128)(2,1)}, u32[]{:S(2)}, u32[]{:S(2)}) collective-permute-start(bf16[256,896]{1,0:T(8,128)(2,1)} %get-tuple-element.20), channel_id=1, source_target_pairs={{0,2},{1,3},{2,0},{3,1},{4,6},{5,7},{6,4},{7,5},{8,10},{9,11},{10,... | collective-permute-start | bytes 1376264 | tf_op jit(solution)/shard_map/ppermute | solution.py:29
  62.9 34.9 %collective-permute-start.7 = (bf16[256,896]{1,0:T(8,128)(2,1)}, bf16[256,896]{1,0:T(8,128)(2,1)}, u32[]{:S(2)}, u32[]{:S(2)}) collective-permute-start(bf16[256,896]{1,0:T(8,128)(2,1)} %get-tuple-element.19), channel_id=1, source_target_pairs={{0,4},{1,5},{2,6},{3,7},{4,0},{5,1},{6,2},{7,3},{8,12},{9,13},{10,... | collective-permute-start | bytes 1376264 | tf_op jit(solution)/shard_map/ppermute | solution.py:29
  63.3 34.9 %collective-permute-start.8 = (bf16[256,896]{1,0:T(8,128)(2,1)}, bf16[256,896]{1,0:T(8,128)(2,1)}, u32[]{:S(2)}, u32[]{:S(2)}) collective-permute-start(bf16[256,896]{1,0:T(8,128)(2,1)} %get-tuple-element.18), channel_id=1, source_target_pairs={{0,6},{1,7},{2,4},{3,5},{4,2},{5,3},{6,0},{7,1},{8,14},{9,15},{10,... | collective-permute-start | bytes 1376264 | tf_op jit(solution)/shard_map/ppermute | solution.py:29
  72.5 0.8 copy-start.6
  80.9 0.7 copy-start.10
  84.6 13.7 %copy-start.11 = (s32[2,2]{1,0:T(2,128)S(1)}, s32[2,2]{1,0:T(2,128)}, u32[]{:S(2)}) copy-start(s32[2,2]{1,0:T(2,128)} %param.15) | copy-start | bytes 52
  84.6 13.7 %copy-start.12 = (s32[2]{0:T(128)S(1)}, s32[2]{0:T(128)}, u32[]{:S(2)}) copy-start(s32[2]{0:T(128)} %param.14) | copy-start | bytes 28
  84.6 38.0 %all-to-all-start.2 = ((bf16[16,128,128]{2,1,0:T(8,128)(2,1)}), bf16[16,128,128]{2,1,0:T(8,128)(2,1)S(1)}, u32[]{:S(2)}, u32[]{:S(2)}) async-start(bf16[16,128,128]{2,1,0:T(8,128)(2,1)} %merge.1), calls=%async_computation.2 | async-start | bytes 1048576 | tf_op jit(solution)/shard_map/all_to_all | solution.py:517
  97.2 11.0 %collective-permute-start.9 = (bf16[384,896]{1,0:T(8,128)(2,1)S(1)}, bf16[384,896]{1,0:T(8,128)(2,1)S(1)}, u32[]{:S(2)}, u32[]{:S(2)}) collective-permute-start(bf16[384,896]{1,0:T(8,128)(2,1)S(1)} %pad_maximum_fusion), channel_id=1, source_target_pairs={{0,1},{1,0},{2,3},{3,2},{4,5},{5,4},{6,7},{7,6},{8,9},{9,8},{10,11... | collective-permute-start | bytes 2064392 | tf_op jit(solution)/shard_map/ppermute | solution.py:29
  97.6 10.5 %collective-permute-start.10 = (bf16[256,896]{1,0:T(8,128)(2,1)}, bf16[256,896]{1,0:T(8,128)(2,1)S(1)}, u32[]{:S(2)}, u32[]{:S(2)}) collective-permute-start(bf16[256,896]{1,0:T(8,128)(2,1)} %collective-permute-done.6.refs_3_), channel_id=1, source_target_pairs={{0,1},{1,0},{2,3},{3,2},{4,5},{5,4},{6,7},{7,6},{8,9},{9,8},{10,11... | collective-permute-start | bytes 1376264 | tf_op jit(solution)/shard_map/ppermute | solution.py:29
  97.8 10.4 %collective-permute-start.11 = (bf16[256,896]{1,0:T(8,128)(2,1)}, bf16[256,896]{1,0:T(8,128)(2,1)S(1)}, u32[]{:S(2)}, u32[]{:S(2)}) collective-permute-start(bf16[256,896]{1,0:T(8,128)(2,1)} %collective-permute-done.7.refs_4_), channel_id=1, source_target_pairs={{0,1},{1,0},{2,3},{3,2},{4,5},{5,4},{6,7},{7,6},{8,9},{9,8},{10,11... | collective-permute-start | bytes 1376264 | tf_op jit(solution)/shard_map/ppermute | solution.py:29
  98.2 10.1 %collective-permute-start.12 = (bf16[256,896]{1,0:T(8,128)(2,1)}, bf16[256,896]{1,0:T(8,128)(2,1)S(1)}, u32[]{:S(2)}, u32[]{:S(2)}) collective-permute-start(bf16[256,896]{1,0:T(8,128)(2,1)} %collective-permute-done.8.refs_5_), channel_id=1, source_target_pairs={{0,1},{1,0},{2,3},{3,2},{4,5},{5,4},{6,7},{7,6},{8,9},{9,8},{10,11... | collective-permute-start | bytes 1376264 | tf_op jit(solution)/shard_map/ppermute | solution.py:29
  98.4 9.3 %collective-permute-start.3 = (s32[2,2]{1,0:T(2,128)S(1)}, s32[2,2]{1,0:T(2,128)S(1)}, u32[]{:S(2)}, u32[]{:S(2)}) collective-permute-start(s32[2,2]{1,0:T(2,128)S(1)} %multiply_add_fusion), channel_id=1, source_target_pairs={{0,1},{1,2},{2,3},{3,4},{4,5},{5,6},{6,7},{7,8},{8,9},{9,10},{10,1... | collective-permute-start | bytes 56 | tf_op jit(solution)/shard_map/ppermute | solution.py:24
  108.2 0.9 copy-start.5
  108.2 1.0 copy-start.7
  108.2 1.1 copy-start.8
  108.2 1.3 %copy-start.9 = (bf16[256,896]{1,0:T(8,128)(2,1)}, bf16[256,896]{1,0:T(8,128)(2,1)S(1)}, u32[]{:S(2)}) copy-start(bf16[256,896]{1,0:T(8,128)(2,1)S(1)} %collective-permute-done.12.refs_9_) | copy-start | bytes 1376260

commit v10 on v9

--- a/solution.py
+++ b/solution.py
@@ -158,14 +158,17 @@
         stat = stat1_ref[i : i + 2].reshape(2 * rows, 128)
         return (out1_ref[i : i + 2].reshape(2 * rows, dim), *halves(stat))
 
+    def finish(i, part):
+        out, _, total = part
+        out = out * (1.0 / total)
+        out_ref[i : i + 2] = out.reshape(2, rows, dim).astype(out_ref.dtype)
+
     def store(i, part):
+        if i >= waiting:
+            return finish(i, part)
         out, largest, total = part
-        if i < waiting:
-            part_ref[i : i + 2] = out.reshape(2, rows, dim)
-            stat_ref[i : i + 2] = with_stats(largest, total).reshape(2, rows, 128)
-        else:
-            out = out * (1.0 / total)
-            out_ref[i : i + 2] = out.reshape(2, rows, dim).astype(out_ref.dtype)
+        part_ref[i : i + 2] = out.reshape(2, rows, dim)
+        stat_ref[i : i + 2] = with_stats(largest, total).reshape(2, rows, 128)
 
     @pl.when(flag_ref[0] > 0)
     def _():
@@ -183,32 +186,32 @@
 
     @pl.when(flag_ref[0] == 0)
     def _():
-        part_ref[...] = out1_ref[0:waiting]
-        stat_ref[...] = stat1_ref[0:waiting]
-        for i in range(waiting, blocks, 2):
-            store(i, own_part(i))
+        for i in range(0, blocks, 2):
+            finish(i, own_part(i))
 
 
 def merge_kernel(scale, flag_ref, part_ref, stat_ref, back_ref, rest_ref, out_ref, done_ref, sem):
     del rest_ref
     blocks, rows, dim = part_ref.shape
-    for i in range(0, blocks, 2):
-        out1, largest1, total1 = (
-            part_ref[i : i + 2].reshape(2 * rows, dim),
-            *halves(stat_ref[i : i + 2].reshape(2 * rows, 128)),
-        )
-        stat = jnp.concatenate([sent_stats(back_ref, i + n, rows) for n in range(2)], axis=0)
-        largest2, total2 = halves(stat)
-        largest2 = jnp.where(flag_ref[0] > 0, largest2, MASKED_SCORE)
-        top = jnp.maximum(largest1, largest2)
-        a, b = jnp.exp2((largest1 - top) * scale), jnp.exp2((largest2 - top) * scale)
-        inverse = 1.0 / (a * total1 + b * total2)
-        out2 = taken(back_ref, i, 2, 0, rows).astype(jnp.float32)
-        out = out1 * (a * inverse) + out2 * (b * inverse)
-        done_ref[i : i + 2] = out.reshape(2, rows, dim).astype(done_ref.dtype)
-    copy = pltpu.make_async_copy(done_ref, out_ref.at[0:blocks], sem)
-    copy.start()
-    copy.wait()
+
+    @pl.when(flag_ref[0] > 0)
+    def _():
+        for i in range(0, blocks, 2):
+            out1, largest1, total1 = (
+                part_ref[i : i + 2].reshape(2 * rows, dim),
+                *halves(stat_ref[i : i + 2].reshape(2 * rows, 128)),
+            )
+            stat = jnp.concatenate([sent_stats(back_ref, i + n, rows) for n in range(2)], axis=0)
+            largest2, total2 = halves(stat)
+            top = jnp.maximum(largest1, largest2)
+            a, b = jnp.exp2((largest1 - top) * scale), jnp.exp2((largest2 - top) * scale)
+            inverse = 1.0 / (a * total1 + b * total2)
+            out2 = taken(back_ref, i, 2, 0, rows).astype(jnp.float32)
+            out = out1 * (a * inverse) + out2 * (b * inverse)
+            done_ref[i : i + 2] = out.reshape(2, rows, dim).astype(done_ref.dtype)
+        copy = pltpu.make_async_copy(done_ref, out_ref.at[0:blocks], sem)
+        copy.start()
+        copy.wait()
 
 
 def estimate(area, arrays):

time: 126 us -> 126 us (level)
  no operation moved by 1% of the time
where the time goes in v10:
time: 126 us; the launch traced here: 125 us
  Pallas kernels  44.8 us (36%)
  starting transfers between devices  43.3 us (34%)
  waiting for transfers between devices  28.8 us (23%)
  other arithmetic  4.01 us (3%)
  local copies, waits for them, and re-layouts  3.55 us (3%)
    ppermute x6, waiting for transfers between devices, shifted(): lax.ppermute(value, axis, [(source, source + steps) for source in range(f...  22.8 us
    ppermute x6, starting transfers between devices, shifted(): lax.ppermute(value, axis, [(source, source + steps) for source in range(f...  15.8 us
    all_to_all x1, starting transfers between devices, per_device(): lax.all_to_all(by_head, 'ctx', 0, 0, axis_index_groups=groups, tiled=True)  12.5 us
    pallas_call x1, Pallas kernels, cross_attention(): pl.pallas_call(functools.partial(cross_kernel, HEAD_DIM ** (-0.5) * LOG2E...  8.58 us
    pallas_call x1, Pallas kernels, self_attention(): pl.pallas_call(functools.partial(previous_kernel, scale), out_shape=(jax....  7.7 us
    pallas_call x1, Pallas kernels, self_attention(): pl.pallas_call(functools.partial(own_kernel, scale), out_shape=(jax.Shape...  7.17 us
    all_to_all x1, waiting for transfers between devices, self_attention(): lax.all_to_all(packed(queries), 'ctx', 0, 0, axis_index_groups=groups, ti...  5.94 us
    pallas_call x1, Pallas kernels, cross_attention(): pl.pallas_call(absorb_kernel, out_shape=jax.ShapeDtypeStruct((span_count,...  5.86 us
  transfers between devices with their start and end apart: 16, of which 3 were waited for; matrix products, arithmetic and copies ran while one was open for 2% of the time, Pallas kernels for 34%

profile of v10, /device:TPU:23, one launch (start us, length us, event | category | flops | bytes accessed | tf_op | source)
XLA Modules:
  0.0 124.8 jit_solution(5596798580086509008)
XLA Ops:
  0.0 1.9 %pack.2 = bf16[16,128,128]{2,1,0:T(8,128)(2,1)} custom-call(bf16[128,2048]{1,0:T(8,128)(2,1)} %refs_0_.3), custom_call_target="tpu_custom_call" | custom-call | bytes 1048576 | tf_op jit(solution)/shard_map/pack/pallas_call | solution.py:43
  1.9 5.5 %all-to-all-start = ((bf16[16,128,128]{2,1,0:T(8,128)(2,1)}), bf16[16,128,128]{2,1,0:T(8,128)(2,1)S(1)}, u32[]{:S(2)}, u32[]{:S(2)}) async-start(bf16[16,128,128]{2,1,0:T(8,128)(2,1)} %pack.2), calls=%async_computation | async-start | bytes 1048576 | tf_op jit(solution)/shard_map/all_to_all | solution.py:233
  7.4 2.4 %pack.3 = bf16[16,256,128]{2,1,0:T(8,128)(2,1)} custom-call(bf16[128,2048]{1,0:T(8,128)(2,1)} %refs_0_.4, bf16[128,2048]{1,0:T(8,128)(2,1)} %refs_1_.1), custom_call_target="tpu_custom_call" | custom-call | bytes 2097152 | tf_op jit(solution)/shard_map/pack/pallas_call | solution.py:43
  9.8 5.9 %all-to-all-done.q_ref = bf16[16,128,128]{2,1,0:T(8,128)(2,1)S(1)} async-done(((bf16[16,128,128]{2,1,0:T(8,128)(2,1)}), bf16[16,128,128]{2,1,0:T(8,128)(2,1)S(1)}, u32[]{:S(2)}, u32[]{:S(2)}) %all-to-all-start) | async-done | bytes 524320 | tf_op jit(solution)/shard_map/all_to_all | solution.py:233
  15.7 5.8 %all-to-all-start.1 = ((bf16[16,256,128]{2,1,0:T(8,128)(2,1)}), bf16[16,256,128]{2,1,0:T(8,128)(2,1)S(1)}, u32[]{:S(2)}, u32[]{:S(2)}) async-start(bf16[16,256,128]{2,1,0:T(8,128)(2,1)} %pack.3), calls=%async_computation.1 | async-start | bytes 2097152 | tf_op jit(solution)/shard_map/all_to_all | solution.py:229
  21.5 0.0 copy-done.3
  21.5 3.1 %collective-permute-start.4 = (bf16[128,896]{1,0:T(8,128)(2,1)S(1)}, bf16[128,896]{1,0:T(8,128)(2,1)S(1)}, u32[]{:S(2)}, u32[]{:S(2)}) collective-permute-start(bf16[128,896]{1,0:T(8,128)(2,1)S(1)} %copy-done.3), channel_id=1, source_target_pairs={{0,8},{1,9},{2,10},{3,11},{4,12},{5,13},{6,14},{7,15},{8,16},{9,17... | collective-permute-start | bytes 688136 | tf_op jit(solution)/shard_map/ppermute | solution.py:24
  24.7 13.1 %collective-permute-done.4.refs_1_ = bf16[128,896]{1,0:T(8,128)(2,1)S(1)} collective-permute-done((bf16[128,896]{1,0:T(8,128)(2,1)S(1)}, bf16[128,896]{1,0:T(8,128)(2,1)S(1)}, u32[]{:S(2)}, u32[]{:S(2)}) %collective-permute-start.4) | collective-permute-done | bytes 229408 | tf_op jit(solution)/shard_map/ppermute | solution.py:24
  37.8 4.1 %collective-permute-start.5 = (bf16[128,896]{1,0:T(8,128)(2,1)S(1)}, bf16[128,896]{1,0:T(8,128)(2,1)S(1)}, u32[]{:S(2)}, u32[]{:S(2)}) collective-permute-start(bf16[128,896]{1,0:T(8,128)(2,1)S(1)} %collective-permute-done.4.refs_1_), channel_id=1, source_target_pairs={{0,8},{1,9},{2,10},{3,11},{4,12},{5,13},{6,14},{7,15},{8,16},{9,17... | collective-permute-start | bytes 688136 | tf_op jit(solution)/shard_map/ppermute | solution.py:24
  41.9 0.7 slice.17
  42.7 2.7 %collective-permute-start.1 = (bf16[8,128,128]{2,1,0:T(8,128)(2,1)}, bf16[8,128,128]{2,1,0:T(8,128)(2,1)}, u32[]{:S(2)}, u32[]{:S(2)}) collective-permute-start(bf16[8,128,128]{2,1,0:T(8,128)(2,1)} %slice.17), channel_id=1, source_target_pairs={{16,0},{17,1},{18,2},{19,3},{20,4},{21,5},{22,6},{23,7},{24,8},{25... | collective-permute-start | bytes 786440 | tf_op jit(solution)/shard_map/ppermute | solution.py:24
  45.3 0.0 all-to-all-done.1.kv_ref
  45.4 0.0 copy-done.1
  45.4 1.3 %collective-permute-start = (bf16[8,256,128]{2,1,0:T(8,128)(2,1)S(1)}, bf16[8,256,128]{2,1,0:T(8,128)(2,1)S(1)}, u32[]{:S(2)}, u32[]{:S(2)}) collective-permute-start(bf16[8,256,128]{2,1,0:T(8,128)(2,1)S(1)} %slice.16), channel_id=1, source_target_pairs={{0,16},{1,17},{2,18},{3,19},{4,20},{5,21},{6,22},{7,23},{8,24},{9,... | collective-permute-start | bytes 1572872 | tf_op jit(solution)/shard_map/ppermute | solution.py:24
  46.7 0.0 collective-permute-done.5.refs_2_
  46.7 0.0 copy-start.4
  46.7 0.1 broadcast_select_fusion
  46.8 9.7 %collective-permute-done.1.q_ref = bf16[8,128,128]{2,1,0:T(8,128)(2,1)} collective-permute-done((bf16[8,128,128]{2,1,0:T(8,128)(2,1)}, bf16[8,128,128]{2,1,0:T(8,128)(2,1)}, u32[]{:S(2)}, u32[]{:S(2)}) %collective-permute-start.1) | collective-permute-done | bytes 262176 | tf_op jit(solution)/shard_map/ppermute | solution.py:24
  56.5 0.0 copy-done
  56.5 3.7 %later.1 = bf16[9,128,128]{2,1,0:T(8,128)(2,1)} custom-call(bf16[8,128,128]{2,1,0:T(8,128)(2,1)} %collective-permute-done.1.q_ref, bf16[16,256,128]{2,1,0:T(8,128)(2,1)} %copy-done), custom_call_target="tpu_custom_call" | custom-call | flops 268435456 | bytes 262144 | tf_op jit(solution)/shard_map/later/pallas_call | solution.py:251
  60.2 1.3 %collective-permute-start.2 = (bf16[9,128,128]{2,1,0:T(8,128)(2,1)}, bf16[9,128,128]{2,1,0:T(8,128)(2,1)S(1)}, u32[]{:S(2)}, u32[]{:S(2)}) collective-permute-start(bf16[9,128,128]{2,1,0:T(8,128)(2,1)} %later.1), channel_id=1, source_target_pairs={{0,16},{1,17},{2,18},{3,19},{4,20},{5,21},{6,22},{7,23},{8,24},{9,... | collective-permute-start | bytes 884744 | tf_op jit(solution)/shard_map/ppermute | solution.py:24
  61.5 1.1 pad_maximum_fusion.1
  62.6 0.3 collective-permute-start.6
  62.9 0.4 collective-permute-start.7
  63.3 2.0 %collective-permute-start.8 = (bf16[256,896]{1,0:T(8,128)(2,1)}, bf16[256,896]{1,0:T(8,128)(2,1)}, u32[]{:S(2)}, u32[]{:S(2)}) collective-permute-start(bf16[256,896]{1,0:T(8,128)(2,1)} %get-tuple-element.18), channel_id=1, source_target_pairs={{0,6},{1,7},{2,4},{3,5},{4,2},{5,3},{6,0},{7,1},{8,14},{9,15},{10,... | collective-permute-start | bytes 1376264 | tf_op jit(solution)/shard_map/ppermute | solution.py:29
  65.3 7.2 %own.1 = (f32[16,128,128]{2,1,0:T(8,128)}, f32[16,128,128]{2,1,0:T(8,128)}) custom-call(bf16[16,128,128]{2,1,0:T(8,128)(2,1)} %copy-done.1, bf16[16,256,128]{2,1,0:T(8,128)(2,1)} %copy-done), custom_call_target="tpu_custom_call" | custom-call | flops 1073741824 | bytes 1572864 | tf_op jit(solution)/shard_map/own/pallas_call | solution.py:237
  72.4 0.0 collective-permute-done.kv_ref
  72.5 0.8 copy-done.6
  73.2 7.7 %previous.1 = (bf16[16,128,128]{2,1,0:T(8,128)(2,1)}, f32[8,128,128]{2,1,0:T(8,128)}, f32[8,128,128]{2,1,0:T(8,128)}) custom-call(s32[1]{0:T(128)} %bitcast.flag_ref, bf16[16,128,128]{2,1,0:T(8,128)(2,1)} %copy-done.1, bf16[8,256,128]{2,1,0:T(8,128)(2,1)} %copy-done.6, f32[16,128,128]{2,1,0:T(8,128)} %get-tuple-element.10.out1_ref, ...), custom_call_target="tpu_custom_call" | custom-call | flops 805306368 | bytes 2621440 | tf_op jit(solution)/shard_map/previous/pallas_call | solution.py:263
  80.9 0.0 collective-permute-done.2.back_ref
  80.9 0.7 copy-done.10
  81.7 2.9 %merge.1 = bf16[16,128,128]{2,1,0:T(8,128)(2,1)} custom-call(s32[1]{0:T(128)} %bitcast.flag_ref, f32[8,128,128]{2,1,0:T(8,128)} %get-tuple-element.12.part_ref, f32[8,128,128]{2,1,0:T(8,128)} %get-tuple-element.13.stat_ref, bf16[9,128,128]{2,1,0:T(8,128)(2,1)} %copy-done.10, ...), custom_call_target="tpu_custom_call", output_to_operand_aliasing={{}: (4, {})} | custom-call | bytes 819200 | tf_op jit(solution)/shard_map/merge/pallas_call | solution.py:277
  84.6 0.0 copy-start.11
  84.6 0.0 copy-start.12
  84.6 12.5 %all-to-all-start.2 = ((bf16[16,128,128]{2,1,0:T(8,128)(2,1)}), bf16[16,128,128]{2,1,0:T(8,128)(2,1)S(1)}, u32[]{:S(2)}, u32[]{:S(2)}) async-start(bf16[16,128,128]{2,1,0:T(8,128)(2,1)} %merge.1), calls=%async_computation.2 | async-start | bytes 1048576 | tf_op jit(solution)/shard_map/all_to_all | solution.py:520
  97.1 0.0 copy-done.2
  97.1 0.0 copy-done.4
  97.1 0.1 pad_maximum_fusion
  97.2 0.5 collective-permute-start.9
  97.6 0.0 collective-permute-done.6.refs_3_
  97.6 0.1 collective-permute-start.10
  97.8 0.0 collective-permute-done.7.refs_4_
  97.8 0.4 collective-permute-start.11
  98.2 0.0 collective-permute-done.8.refs_5_
  98.2 0.1 collective-permute-start.12
  98.3 0.0 copy-done.11
  98.3 0.1 multiply_add_fusion
  98.4 3.4 %collective-permute-start.3 = (s32[2,2]{1,0:T(2,128)S(1)}, s32[2,2]{1,0:T(2,128)S(1)}, u32[]{:S(2)}, u32[]{:S(2)}) collective-permute-start(s32[2,2]{1,0:T(2,128)S(1)} %multiply_add_fusion), channel_id=1, source_target_pairs={{0,1},{1,2},{2,3},{3,4},{4,5},{5,6},{6,7},{7,8},{8,9},{9,10},{10,1... | collective-permute-start | bytes 56 | tf_op jit(solution)/shard_map/ppermute | solution.py:24
  101.7 5.9 %absorb.1.refs_10_ = bf16[2,1024,896]{2,1,0:T(8,128)(2,1)} custom-call(bf16[128,2048]{1,0:T(8,128)(2,1)} %q_ref.1, bf16[896,4096]{1,0:T(8,128)(2,1)} %weight_ref.3), custom_call_target="tpu_custom_call" | custom-call | flops 469762048 | bytes 7340032 | tf_op jit(solution)/shard_map/absorb/pallas_call | solution.py:454
  107.6 0.0 collective-permute-done.3
  107.6 0.5 pad_add_fusion.table_ref
  108.2 0.0 collective-permute-done.9.refs_6_
  108.2 0.0 collective-permute-done.10.refs_7_
  108.2 0.0 copy-start.7
  108.2 0.0 collective-permute-done.11.refs_8_
  108.2 0.0 collective-permute-done.12.refs_9_
  108.2 0.8 copy-done.5
  109.1 0.1 copy-done.7
  109.2 0.2 copy-done.8
  109.3 0.1 copy-done.9
  109.5 8.6 %cross.1.means_ref = bf16[2048,896]{1,0:T(8,128)(2,1)} custom-call(s32[1]{0:T(128)} %bitcast.2.position_ref, s32[2,2]{1,0:T(2,128)} %pad_add_fusion.table_ref, bf16[128,896]{1,0:T(8,128)(2,1)} %refs_0_.5, bf16[128,896]{1,0:T(8,128)(2,1)} %copy-done.2, bf16[128,896]{1,0:T(8,128)(2,1)} %copy-done.4, bf16[256,896]{1,0:T(8,128)(2,1)} %collective-permute-done.6.refs_3_, ...), custom_call_target="tpu_custom_call" | custom-call | flops 1879048192 | bytes 8257536 | tf_op jit(solution)/shard_map/cross/pallas_call | solution.py:469
  118.1 4.6 %values.1 = f32[128,2048]{1,0:T(8,128)} custom-call(bf16[2048,896]{1,0:T(8,128)(2,1)} %cross.1.means_ref, bf16[896,4096]{1,0:T(8,128)(2,1)} %weight_ref.3), custom_call_target="tpu_custom_call" | custom-call | flops 469762048 | bytes 7340032 | tf_op jit(solution)/shard_map/values/pallas_call | solution.py:491
  122.6 0.0 all-to-all-done.2
  122.6 2.1 %fusion = bf16[128,2048]{1,0:T(8,128)(2,1)} fusion(f32[128,2048]{1,0:T(8,128)} %values.1, bf16[16,128,128]{2,1,0:T(8,128)(2,1)S(1)} %all-to-all-done.2), kind=kLoop, calls=%fused_computation.1 | loop fusion | flops 786432 | bytes 2097152 | tf_op jit(solution)/shard_map/convert_element_type | solution.py:522
  (13 shorter events, 0.1 us)
Async XLA Ops:
  1.9 13.8 %all-to-all-start = ((bf16[16,128,128]{2,1,0:T(8,128)(2,1)}), bf16[16,128,128]{2,1,0:T(8,128)(2,1)S(1)}, u32[]{:S(2)}, u32[]{:S(2)}) async-start(bf16[16,128,128]{2,1,0:T(8,128)(2,1)} %pack.2), calls=%async_computation | async-start | bytes 1048576 | tf_op jit(solution)/shard_map/all_to_all | solution.py:233
  9.8 11.7 %copy-start.3 = (bf16[128,896]{1,0:T(8,128)(2,1)S(1)}, bf16[128,896]{1,0:T(8,128)(2,1)}, u32[]{:S(2)}) copy-start(bf16[128,896]{1,0:T(8,128)(2,1)} %refs_0_.5) | copy-start | bytes 688132
  15.7 29.6 %copy-start.1 = (bf16[16,128,128]{2,1,0:T(8,128)(2,1)}, bf16[16,128,128]{2,1,0:T(8,128)(2,1)S(1)}, u32[]{:S(2)}) copy-start(bf16[16,128,128]{2,1,0:T(8,128)(2,1)S(1)} %all-to-all-done.q_ref) | copy-start | bytes 1572868
  15.7 29.6 %all-to-all-start.1 = ((bf16[16,256,128]{2,1,0:T(8,128)(2,1)}), bf16[16,256,128]{2,1,0:T(8,128)(2,1)S(1)}, u32[]{:S(2)}, u32[]{:S(2)}) async-start(bf16[16,256,128]{2,1,0:T(8,128)(2,1)} %pack.3), calls=%async_computation.1 | async-start | bytes 2097152 | tf_op jit(solution)/shard_map/all_to_all | solution.py:229
  21.5 16.3 %collective-permute-start.4 = (bf16[128,896]{1,0:T(8,128)(2,1)S(1)}, bf16[128,896]{1,0:T(8,128)(2,1)S(1)}, u32[]{:S(2)}, u32[]{:S(2)}) collective-permute-start(bf16[128,896]{1,0:T(8,128)(2,1)S(1)} %copy-done.3), channel_id=1, source_target_pairs={{0,8},{1,9},{2,10},{3,11},{4,12},{5,13},{6,14},{7,15},{8,16},{9,17... | collective-permute-start | bytes 688136 | tf_op jit(solution)/shard_map/ppermute | solution.py:24
  37.8 59.3 %copy-start.2 = (bf16[128,896]{1,0:T(8,128)(2,1)}, bf16[128,896]{1,0:T(8,128)(2,1)S(1)}, u32[]{:S(2)}) copy-start(bf16[128,896]{1,0:T(8,128)(2,1)S(1)} %collective-permute-done.4.refs_1_) | copy-start | bytes 688132
  37.8 8.9 %collective-permute-start.5 = (bf16[128,896]{1,0:T(8,128)(2,1)S(1)}, bf16[128,896]{1,0:T(8,128)(2,1)S(1)}, u32[]{:S(2)}, u32[]{:S(2)}) collective-permute-start(bf16[128,896]{1,0:T(8,128)(2,1)S(1)} %collective-permute-done.4.refs_1_), channel_id=1, source_target_pairs={{0,8},{1,9},{2,10},{3,11},{4,12},{5,13},{6,14},{7,15},{8,16},{9,17... | collective-permute-start | bytes 688136 | tf_op jit(solution)/shard_map/ppermute | solution.py:24
  42.7 13.8 %collective-permute-start.1 = (bf16[8,128,128]{2,1,0:T(8,128)(2,1)}, bf16[8,128,128]{2,1,0:T(8,128)(2,1)}, u32[]{:S(2)}, u32[]{:S(2)}) collective-permute-start(bf16[8,128,128]{2,1,0:T(8,128)(2,1)} %slice.17), channel_id=1, source_target_pairs={{16,0},{17,1},{18,2},{19,3},{20,4},{21,5},{22,6},{23,7},{24,8},{25... | collective-permute-start | bytes 786440 | tf_op jit(solution)/shard_map/ppermute | solution.py:24
  45.3 11.1 %copy-start = (bf16[16,256,128]{2,1,0:T(8,128)(2,1)}, bf16[16,256,128]{2,1,0:T(8,128)(2,1)S(1)}, u32[]{:S(2)}) copy-start(bf16[16,256,128]{2,1,0:T(8,128)(2,1)S(1)} %all-to-all-done.1.kv_ref) | copy-start | bytes 3145732
  45.4 27.1 %collective-permute-start = (bf16[8,256,128]{2,1,0:T(8,128)(2,1)S(1)}, bf16[8,256,128]{2,1,0:T(8,128)(2,1)S(1)}, u32[]{:S(2)}, u32[]{:S(2)}) collective-permute-start(bf16[8,256,128]{2,1,0:T(8,128)(2,1)S(1)} %slice.16), channel_id=1, source_target_pairs={{0,16},{1,17},{2,18},{3,19},{4,20},{5,21},{6,22},{7,23},{8,24},{9,... | collective-permute-start | bytes 1572872 | tf_op jit(solution)/shard_map/ppermute | solution.py:24
  46.7 50.4 %copy-start.4 = (bf16[128,896]{1,0:T(8,128)(2,1)}, bf16[128,896]{1,0:T(8,128)(2,1)S(1)}, u32[]{:S(2)}) copy-start(bf16[128,896]{1,0:T(8,128)(2,1)S(1)} %collective-permute-done.5.refs_2_) | copy-start | bytes 688132
  60.2 20.7 %collective-permute-start.2 = (bf16[9,128,128]{2,1,0:T(8,128)(2,1)}, bf16[9,128,128]{2,1,0:T(8,128)(2,1)S(1)}, u32[]{:S(2)}, u32[]{:S(2)}) collective-permute-start(bf16[9,128,128]{2,1,0:T(8,128)(2,1)} %later.1), channel_id=1, source_target_pairs={{0,16},{1,17},{2,18},{3,19},{4,20},{5,21},{6,22},{7,23},{8,24},{9,... | collective-permute-start | bytes 884744 | tf_op jit(solution)/shard_map/ppermute | solution.py:24
  62.6 35.0 %collective-permute-start.6 = (bf16[256,896]{1,0:T(8,128)(2,1)}, bf16[256,896]{1,0:T(8,128)(2,1)}, u32[]{:S(2)}, u32[]{:S(2)}) collective-permute-start(bf16[256,896]{1,0:T(8,128)(2,1)} %get-tuple-element.20), channel_id=1, source_target_pairs={{0,2},{1,3},{2,0},{3,1},{4,6},{5,7},{6,4},{7,5},{8,10},{9,11},{10,... | collective-permute-start | bytes 1376264 | tf_op jit(solution)/shard_map/ppermute | solution.py:29
  62.9 34.9 %collective-permute-start.7 = (bf16[256,896]{1,0:T(8,128)(2,1)}, bf16[256,896]{1,0:T(8,128)(2,1)}, u32[]{:S(2)}, u32[]{:S(2)}) collective-permute-start(bf16[256,896]{1,0:T(8,128)(2,1)} %get-tuple-element.19), channel_id=1, source_target_pairs={{0,4},{1,5},{2,6},{3,7},{4,0},{5,1},{6,2},{7,3},{8,12},{9,13},{10,... | collective-permute-start | bytes 1376264 | tf_op jit(solution)/shard_map/ppermute | solution.py:29
  63.3 34.9 %collective-permute-start.8 = (bf16[256,896]{1,0:T(8,128)(2,1)}, bf16[256,896]{1,0:T(8,128)(2,1)}, u32[]{:S(2)}, u32[]{:S(2)}) collective-permute-start(bf16[256,896]{1,0:T(8,128)(2,1)} %get-tuple-element.18), channel_id=1, source_target_pairs={{0,6},{1,7},{2,4},{3,5},{4,2},{5,3},{6,0},{7,1},{8,14},{9,15},{10,... | collective-permute-start | bytes 1376264 | tf_op jit(solution)/shard_map/ppermute | solution.py:29
  72.5 0.8 copy-start.6
  80.9 0.7 copy-start.10
  84.6 13.7 %copy-start.11 = (s32[2,2]{1,0:T(2,128)S(1)}, s32[2,2]{1,0:T(2,128)}, u32[]{:S(2)}) copy-start(s32[2,2]{1,0:T(2,128)} %param.15) | copy-start | bytes 52
  84.6 13.7 %copy-start.12 = (s32[2]{0:T(128)S(1)}, s32[2]{0:T(128)}, u32[]{:S(2)}) copy-start(s32[2]{0:T(128)} %param.14) | copy-start | bytes 28
  84.6 38.0 %all-to-all-start.2 = ((bf16[16,128,128]{2,1,0:T(8,128)(2,1)}), bf16[16,128,128]{2,1,0:T(8,128)(2,1)S(1)}, u32[]{:S(2)}, u32[]{:S(2)}) async-start(bf16[16,128,128]{2,1,0:T(8,128)(2,1)} %merge.1), calls=%async_computation.2 | async-start | bytes 1048576 | tf_op jit(solution)/shard_map/all_to_all | solution.py:520
  97.2 11.0 %collective-permute-start.9 = (bf16[384,896]{1,0:T(8,128)(2,1)S(1)}, bf16[384,896]{1,0:T(8,128)(2,1)S(1)}, u32[]{:S(2)}, u32[]{:S(2)}) collective-permute-start(bf16[384,896]{1,0:T(8,128)(2,1)S(1)} %pad_maximum_fusion), channel_id=1, source_target_pairs={{0,1},{1,0},{2,3},{3,2},{4,5},{5,4},{6,7},{7,6},{8,9},{9,8},{10,11... | collective-permute-start | bytes 2064392 | tf_op jit(solution)/shard_map/ppermute | solution.py:29
  97.6 10.5 %collective-permute-start.10 = (bf16[256,896]{1,0:T(8,128)(2,1)}, bf16[256,896]{1,0:T(8,128)(2,1)S(1)}, u32[]{:S(2)}, u32[]{:S(2)}) collective-permute-start(bf16[256,896]{1,0:T(8,128)(2,1)} %collective-permute-done.6.refs_3_), channel_id=1, source_target_pairs={{0,1},{1,0},{2,3},{3,2},{4,5},{5,4},{6,7},{7,6},{8,9},{9,8},{10,11... | collective-permute-start | bytes 1376264 | tf_op jit(solution)/shard_map/ppermute | solution.py:29
  97.8 10.4 %collective-permute-start.11 = (bf16[256,896]{1,0:T(8,128)(2,1)}, bf16[256,896]{1,0:T(8,128)(2,1)S(1)}, u32[]{:S(2)}, u32[]{:S(2)}) collective-permute-start(bf16[256,896]{1,0:T(8,128)(2,1)} %collective-permute-done.7.refs_4_), channel_id=1, source_target_pairs={{0,1},{1,0},{2,3},{3,2},{4,5},{5,4},{6,7},{7,6},{8,9},{9,8},{10,11... | collective-permute-start | bytes 1376264 | tf_op jit(solution)/shard_map/ppermute | solution.py:29
  98.2 10.1 %collective-permute-start.12 = (bf16[256,896]{1,0:T(8,128)(2,1)}, bf16[256,896]{1,0:T(8,128)(2,1)S(1)}, u32[]{:S(2)}, u32[]{:S(2)}) collective-permute-start(bf16[256,896]{1,0:T(8,128)(2,1)} %collective-permute-done.8.refs_5_), channel_id=1, source_target_pairs={{0,1},{1,0},{2,3},{3,2},{4,5},{5,4},{6,7},{7,6},{8,9},{9,8},{10,11... | collective-permute-start | bytes 1376264 | tf_op jit(solution)/shard_map/ppermute | solution.py:29
  98.4 9.3 %collective-permute-start.3 = (s32[2,2]{1,0:T(2,128)S(1)}, s32[2,2]{1,0:T(2,128)S(1)}, u32[]{:S(2)}, u32[]{:S(2)}) collective-permute-start(s32[2,2]{1,0:T(2,128)S(1)} %multiply_add_fusion), channel_id=1, source_target_pairs={{0,1},{1,2},{2,3},{3,4},{4,5},{5,6},{6,7},{7,8},{8,9},{9,10},{10,1... | collective-permute-start | bytes 56 | tf_op jit(solution)/shard_map/ppermute | solution.py:24
  108.2 0.9 copy-start.5
  108.2 1.0 copy-start.7
  108.2 1.1 copy-start.8
  108.2 1.3 %copy-start.9 = (bf16[256,896]{1,0:T(8,128)(2,1)}, bf16[256,896]{1,0:T(8,128)(2,1)S(1)}, u32[]{:S(2)}) copy-start(bf16[256,896]{1,0:T(8,128)(2,1)S(1)} %collective-permute-done.12.refs_9_) | copy-start | bytes 1376260
